TPU v7x, 32 devices: a whole 2x2x4 slice. The times are simulated.
32 devices in a mesh: blk: 16 (over z, y, x), tp: 2 (over core).
Axes of the slice: x: 2, y: 2, z: 4, core: 2. Of those that a mesh axis runs over, the one named last changes fastest.
Arguments:
- tokens: bfloat16 [2048, 1024], P('blk'), may hold values from -6 to 6
- first_gain: float32 [1024], replicated, may hold values from 0.5 to 1.5
- first_bias: float32 [1024], replicated, may hold values from -2 to 2
- second_gain: float32 [1024], replicated, may hold values from 0.5 to 1.5
- second_bias: float32 [1024], replicated, may hold values from -2 to 2
- query_weight: bfloat16 [1024, 1024], P(None, 'tp'), may hold values from -0.1875 to 0.1875
- key_weight: bfloat16 [1024, 1024], P(None, 'tp'), may hold values from -0.1875 to 0.1875
- value_weight: bfloat16 [1024, 1024], P(None, 'tp'), may hold values from -0.1875 to 0.1875
- output_weight: bfloat16 [1024, 1024], P(None, 'tp'), may hold values from -1.5 to 1.5
- up_weight: bfloat16 [1024, 4096], P(None, 'tp'), may hold values from -0.1875 to 0.1875
- down_weight: bfloat16 [1024, 4096], P(None, 'tp'), may hold values from -0.09375 to 0.09375
- cotangent: bfloat16 [2048, 1024], P('blk'), may hold values from -6 to 6
- scene_len: int32 [4], replicated, may hold values from 1 to 1024, 2048 in all
Outputs:
- layer_out: bfloat16 [2048, 1024], P('blk')
- input_grad: float32 [2048, 1024], P('blk')
- first_gain_grad: float32 [1024], replicated
- first_bias_grad: float32 [1024], replicated
- second_gain_grad: float32 [1024], replicated
- second_bias_grad: float32 [1024], replicated
- query_grad: float32 [1024, 1024], P(None, 'tp')
- key_grad: float32 [1024, 1024], P(None, 'tp')
- value_grad: float32 [1024, 1024], P(None, 'tp')
- output_grad: float32 [1024, 1024], P(None, 'tp')
- up_grad: float32 [1024, 4096], P(None, 'tp')
- down_grad: float32 [1024, 4096], P(None, 'tp')
Inputs may be any that keep to these rules, and one draw needn't show every extreme that they name: `scene_len`: 4 lengths in token order that sum to 2048; the longest is exactly 1024.
All inputs are finite; a program needn't handle non-finite values.
Results may differ from a plain program's by a relative error of at most 0.018.
Values may be sent and summed in bfloat16 or wider, within the bound.
No kernel may reach another device: no remote copies, remote signals or barrier semaphores. Data moves between devices by JAX's collectives and lax.ppermute only.
A program may use at most 128 MiB of HBM per device.

v0:
```python
import jax
import jax.numpy as jnp
from jax import lax
from jax.sharding import PartitionSpec as P

HEAD = 64


def from_behind(block, axis, distance):
    devices = range(lax.axis_size(axis))
    route = [((i - distance) % len(devices), i) for i in devices]
    return lax.ppermute(block, axis, route)


def layer_norm(values, gain, bias):
    center = values - jnp.mean(values, axis=-1, keepdims=True)
    spread = jnp.mean(center * center, axis=-1, keepdims=True)
    return center * lax.rsqrt(spread + 1e-05) * gain + bias


def move_grads(grad_keys, grad_values, offset):
    return (
        from_behind(grad_keys.astype(jnp.bfloat16), "blk", offset).astype(grad_keys.dtype),
        from_behind(grad_values.astype(jnp.bfloat16), "blk", offset).astype(grad_values.dtype),
    )


def body(
    tokens,
    first_gain,
    first_bias,
    second_gain,
    second_bias,
    query_weight,
    key_weight,
    value_weight,
    output_weight,
    up_weight,
    down_weight,
    cotangent,
    scene_len,
):
    f32 = jnp.float32
    bf16 = jnp.bfloat16
    count = lax.axis_size("blk")
    place = lax.axis_index("blk")
    rows = tokens.shape[0]
    heads_here = query_weight.shape[1] // HEAD
    scale = HEAD ** (-0.5)
    ends = jnp.cumsum(scene_len)
    contract_last = (((1,), (1,)), ((), ()))
    contract_first = (((0,), (0,)), ((), ()))

    def scene_of(source):
        places = source * rows + jnp.arange(rows, dtype=jnp.int32)
        return jnp.sum((places[:, None] >= ends[None, :]).astype(jnp.int32), axis=1)

    mine = scene_of(place)

    def shares(source):
        other = scene_of(source)
        return jnp.maximum(mine[0], other[0]) <= jnp.minimum(mine[-1], other[-1])

    directions = (1,)
    steps = count - 1

    def source_of(way, turn):
        raw_source = place - way * turn
        return (raw_source % count, jnp.array(True))

    inputs = tokens.astype(f32)
    normed_one = layer_norm(inputs, first_gain, first_bias).astype(bf16)

    def project(weight):
        return jnp.dot(normed_one, weight, preferred_element_type=f32).astype(bf16)

    query = project(query_weight).reshape(rows, heads_here, HEAD)
    keys = project(key_weight).reshape(rows, heads_here, HEAD)
    values = project(value_weight).reshape(rows, heads_here, HEAD)

    def scores_of(key_block, source):
        mask = mine[:, None] == scene_of(source)[None, :]
        scores = jnp.einsum("qhd,khd->hqk", query, key_block, preferred_element_type=f32) * scale
        return (jnp.where(mask[None], scores, -1e30), mask)

    def absorb(state, key_block, value_block, source):
        top, total, summed = state
        scores, mask = scores_of(key_block, source)
        new_top = jnp.maximum(top, jnp.max(scores, axis=2))
        factor = jnp.exp(top - new_top)
        weights = jnp.where(mask[None], jnp.exp(scores - new_top[:, :, None]), 0.0)
        total = total * factor + jnp.sum(weights, axis=2)
        summed = summed * factor.T[:, :, None] + jnp.einsum(
            "hqk,khd->qhd", weights.astype(bf16), value_block, preferred_element_type=f32
        )
        return (new_top, total, summed)

    start = (
        jnp.full((heads_here, rows), -1e30, f32),
        jnp.zeros((heads_here, rows), f32),
        jnp.zeros((rows, heads_here, HEAD), f32),
    )
    state = absorb(start, keys, values, place)
    way = directions[0]

    def turn_forward(turn, carry):
        current, key_block, value_block = carry
        key_block, value_block = from_behind((key_block, value_block), "blk", way)
        source, inside = source_of(way, turn)
        current = lax.cond(
            inside & shares(source),
            lambda held: absorb(held, key_block, value_block, source),
            lambda held: held,
            current,
        )
        return (current, key_block, value_block)

    state, _, _ = lax.fori_loop(1, steps + 1, turn_forward, (state, keys, values))
    top, total, summed = state
    attended = summed / total.T[:, :, None]
    log_total = top + jnp.log(total)
    attended_low = attended.reshape(rows, -1).astype(bf16)
    branch = lax.dot_general(attended_low, output_weight, contract_last, preferred_element_type=f32)
    branch = lax.psum(branch.astype(jnp.bfloat16), "tp").astype(jnp.float32)
    middle = inputs + branch
    normed_two = layer_norm(middle, second_gain, second_bias).astype(bf16)
    before = jnp.dot(normed_two, up_weight, preferred_element_type=f32)
    active = jax.nn.gelu(before, approximate=False).astype(bf16)
    feed = lax.dot_general(active, down_weight, contract_last, preferred_element_type=f32)
    feed = lax.psum(feed.astype(jnp.bfloat16), "tp").astype(jnp.float32)
    layer_out = (middle + feed).astype(bf16)
    grad_out = cotangent.astype(f32)
    down_grad = lax.dot_general(cotangent, active, contract_first, preferred_element_type=f32)
    grad_active = jnp.dot(cotangent, down_weight, preferred_element_type=f32)
    _, gelu_pull = jax.vjp(lambda arg: jax.nn.gelu(arg, approximate=False), before)
    grad_before = gelu_pull(grad_active)[0].astype(bf16)
    up_grad = lax.dot_general(normed_two, grad_before, contract_first, preferred_element_type=f32)
    grad_two = lax.dot_general(grad_before, up_weight, contract_last, preferred_element_type=f32)
    grad_two = lax.psum(grad_two.astype(jnp.bfloat16), "tp").astype(jnp.float32)
    _, second_pull = jax.vjp(layer_norm, middle, second_gain, second_bias)
    grad_middle_norm, second_gain_grad, second_bias_grad = second_pull(grad_two)
    grad_middle = grad_out + grad_middle_norm
    grad_middle_low = grad_middle.astype(bf16)
    output_grad = lax.dot_general(
        grad_middle_low, attended_low, contract_first, preferred_element_type=f32
    )
    grad_attended = jnp.dot(grad_middle_low, output_weight, preferred_element_type=f32).astype(bf16)
    grad_attended = grad_attended.reshape(rows, heads_here, HEAD)
    delta = jnp.sum(grad_attended * attended, axis=2).T

    def backtrack(grads, key_block, value_block, source):
        grad_query, grad_keys, grad_values = grads
        scores, mask = scores_of(key_block, source)
        probs = jnp.where(mask[None], jnp.exp(scores - log_total[:, :, None]), 0.0)
        grad_values = grad_values + jnp.einsum(
            "hqk,qhd->khd", probs.astype(bf16), grad_attended, preferred_element_type=f32
        )
        grad_probs = jnp.einsum(
            "qhd,khd->hqk", grad_attended, value_block, preferred_element_type=f32
        )
        grad_scores = (probs * (grad_probs - delta[:, :, None]) * scale).astype(bf16)
        grad_query = grad_query + jnp.einsum(
            "hqk,khd->qhd", grad_scores, key_block, preferred_element_type=f32
        )
        grad_keys = grad_keys + jnp.einsum(
            "hqk,qhd->khd", grad_scores, query, preferred_element_type=f32
        )
        return (grad_query, grad_keys, grad_values)

    empty = jnp.zeros((rows, heads_here, HEAD), f32)
    grad_query, home_keys, home_values = backtrack((empty, empty, empty), keys, values, place)
    way = directions[0]

    def turn_backward(turn, carry):
        grad_q, key_block, value_block, grad_k, grad_v = carry
        key_block, value_block = from_behind((key_block, value_block), "blk", way)
        grad_k, grad_v = move_grads(grad_k, grad_v, way)
        source, inside = source_of(way, turn)
        grad_q, grad_k, grad_v = lax.cond(
            inside & shares(source),
            lambda held: backtrack(held, key_block, value_block, source),
            lambda held: held,
            (grad_q, grad_k, grad_v),
        )
        return (grad_q, key_block, value_block, grad_k, grad_v)

    grad_query, _, _, moved_keys, moved_values = lax.fori_loop(
        1, steps + 1, turn_backward, (grad_query, keys, values, empty, empty)
    )
    moved_keys, moved_values = move_grads(moved_keys, moved_values, -way * steps)
    home_keys = home_keys + moved_keys
    home_values = home_values + moved_values
    grad_query = grad_query.reshape(rows, -1).astype(bf16)
    grad_keys = home_keys.reshape(rows, -1).astype(bf16)
    grad_values = home_values.reshape(rows, -1).astype(bf16)
    query_grad = lax.dot_general(normed_one, grad_query, contract_first, preferred_element_type=f32)
    key_grad = lax.dot_general(normed_one, grad_keys, contract_first, preferred_element_type=f32)
    value_grad = lax.dot_general(
        normed_one, grad_values, contract_first, preferred_element_type=f32
    )
    grad_one = lax.dot_general(grad_query, query_weight, contract_last, preferred_element_type=f32)
    grad_one = grad_one + lax.dot_general(
        grad_keys, key_weight, contract_last, preferred_element_type=f32
    )
    grad_one = grad_one + lax.dot_general(
        grad_values, value_weight, contract_last, preferred_element_type=f32
    )
    grad_one = lax.psum(grad_one.astype(jnp.bfloat16), "tp").astype(jnp.float32)
    _, first_pull = jax.vjp(layer_norm, inputs, first_gain, first_bias)
    grad_input_norm, first_gain_grad, first_bias_grad = first_pull(grad_one)
    input_grad = grad_middle + grad_input_norm
    norm_grads = jnp.stack(
        [first_gain_grad, first_bias_grad, second_gain_grad, second_bias_grad], axis=1
    )
    summed_parts = (
        lax.psum_scatter(query_grad, "blk", scatter_dimension=0, tiled=True),
        lax.psum_scatter(key_grad, "blk", scatter_dimension=0, tiled=True),
        lax.psum_scatter(value_grad, "blk", scatter_dimension=0, tiled=True),
        lax.psum_scatter(output_grad, "blk", scatter_dimension=0, tiled=True),
        lax.psum_scatter(up_grad, "blk", scatter_dimension=0, tiled=True),
        lax.psum_scatter(down_grad, "blk", scatter_dimension=0, tiled=True),
        lax.psum_scatter(norm_grads, "blk", scatter_dimension=0, tiled=True),
    )
    totals = (
        lax.all_gather(summed_parts[0].astype(jnp.bfloat16), "blk", axis=0, tiled=True).astype(
            jnp.float32
        ),
        lax.all_gather(summed_parts[1].astype(jnp.bfloat16), "blk", axis=0, tiled=True).astype(
            jnp.float32
        ),
        lax.all_gather(summed_parts[2].astype(jnp.bfloat16), "blk", axis=0, tiled=True).astype(
            jnp.float32
        ),
        lax.all_gather(summed_parts[3].astype(jnp.bfloat16), "blk", axis=0, tiled=True).astype(
            jnp.float32
        ),
        lax.all_gather(summed_parts[4].astype(jnp.bfloat16), "blk", axis=0, tiled=True).astype(
            jnp.float32
        ),
        lax.all_gather(summed_parts[5].astype(jnp.bfloat16), "blk", axis=0, tiled=True).astype(
            jnp.float32
        ),
        lax.all_gather(summed_parts[6].astype(jnp.bfloat16), "blk", axis=0, tiled=True).astype(
            jnp.float32
        ),
    )
    return (
        layer_out,
        input_grad,
        totals[6][:, 0],
        totals[6][:, 1],
        totals[6][:, 2],
        totals[6][:, 3],
        totals[0],
        totals[1],
        totals[2],
        totals[3],
        totals[4],
        totals[5],
    )


def solution(mesh):
    return jax.shard_map(
        body,
        mesh=mesh,
        in_specs=(
            P("blk", None),
            P(),
            P(),
            P(),
            P(),
            P(None, "tp"),
            P(None, "tp"),
            P(None, "tp"),
            P(None, "tp"),
            P(None, "tp"),
            P(None, "tp"),
            P("blk", None),
            P(),
        ),
        out_specs=(
            P("blk", None),
            P("blk", None),
            P(),
            P(),
            P(),
            P(),
            P(None, "tp"),
            P(None, "tp"),
            P(None, "tp"),
            P(None, "tp"),
            P(None, "tp"),
            P(None, "tp"),
        ),
        check_vma=False,
    )
```

profile of v0, /device:TPU:0, one launch (start us, length us, event | category | flops | bytes accessed | tf_op | source)
XLA Modules:
  0.0 1685.5 jit_solution(9029390307173838175)
XLA Ops:
  15.7 178.8 %while.46 = (s32[]{:T(128)}, f32[8,128]{1,0:T(8,128)S(1)}, f32[8,128]{1,0:T(8,128)S(1)}, f32[128,8,64]{0,2,1:T(8,128)S(1)}, bf16[128,8,64]{0,2,1:T(8,128)(2,1)},...) while((s32[]{:T(128)}, f32[8,128]{1,0:T(8,128)S(1)}, ...), condition=%wide.region_13.14_spmd, body=%wide.region_6.13_spmd.sunk | while | flops 34887696 | bytes 4199004 | solution.py:118
  15.7 3.0 collective-permute-start
  36.1 3.7 collective-permute-done
  46.9 4.1 collective-permute-done
  57.7 4.2 collective-permute-done
  68.7 4.2 collective-permute-done
  79.6 4.2 collective-permute-done
  90.5 4.2 collective-permute-done
  101.4 4.2 collective-permute-done
  113.4 5.0 collective-permute-done
  118.4 2.8 collective-permute-done.1
  126.6 5.5 collective-permute-done
  139.7 5.5 collective-permute-done
  152.0 4.6 collective-permute-done
  163.4 4.2 collective-permute-done
  174.3 4.2 collective-permute-done
  186.7 4.2 collective-permute-done
  196.5 14.1 all-reduce.5.cloned.1.call-done
  213.1 3.1 fusion.73
  216.2 3.3 add_convert_fusion
  222.7 4.4 convolution_convert_fusion.2
  227.1 15.1 all-reduce.7.cloned.1.call-done
  249.8 240.7 %while.47 = (s32[]{:T(128)}, f32[128,8,64]{0,2,1:T(8,128)S(1)}, bf16[128,8,64]{0,2,1:T(8,128)(2,1)S(1)}, bf16[128,8,64]{0,2,1:T(8,128)(2,1)S(1)}, f32[128,8,64]{...) while((s32[]{:T(128)}, f32[128,8,64]{0,2,1:T(8,128)S(1)}, ...), condition=%wide.region_27.28_spmd, body=%wide.region_22.27_spmd.sunk | while | flops 85543952 | bytes 9614072 | solution.py:187
  271.8 3.3 collective-permute-start.5
  285.5 3.0 collective-permute-start.3
  289.1 4.2 collective-permute-start.5
  303.4 4.2 collective-permute-start.5
  317.2 4.0 collective-permute-start.5
  332.1 3.0 collective-permute-start.5
  345.1 3.5 collective-permute-start.5
  372.7 4.2 collective-permute-start.5
  388.0 4.2 collective-permute-start.5
  404.4 4.2 collective-permute-start.5
  416.3 5.3 collective-permute-start.3
  434.9 4.5 collective-permute-start.3
  452.2 4.1 collective-permute-start.3
  456.8 3.5 collective-permute-start.5
  469.2 2.9 conditional.5
  474.5 5.3 collective-permute-start.5
  487.5 2.9 conditional.5
  492.7 7.9 collective-permute-done.6
  512.0 4.7 convolution_bitcast_fusion.4
  516.6 9.2 copy.115
  526.9 4.8 fusion.72
  535.6 71.4 %reduce-scatter.18.cloned.1.call-done = f32[64,512]{1,0:T(8,128)} async-done(((f32[1024,512]{1,0:T(8,128)}), f32[64,512]{1,0:T(8,128)}) %reduce-scatter.18.cloned.1.call-update) | async-done | bytes 131088 | tf_op jit(solution)/shard_map/reduce_scatter | solution.py:219
  608.6 78.7 %reduce-scatter.12.cloned.1.call-done = f32[64,512]{1,0:T(8,128)} async-done(((f32[1024,512]{1,0:T(8,128)}), f32[64,512]{1,0:T(8,128)}) %reduce-scatter.12.cloned.1.call-update) | async-done | bytes 131088 | tf_op jit(solution)/shard_map/reduce_scatter | solution.py:216
  688.9 78.8 %reduce-scatter.16.cloned.1.call-done = f32[64,512]{1,0:T(8,128)} async-done(((f32[1024,512]{1,0:T(8,128)}), f32[64,512]{1,0:T(8,128)}) %reduce-scatter.16.cloned.1.call-update) | async-done | bytes 131088 | tf_op jit(solution)/shard_map/reduce_scatter | solution.py:218
  769.3 79.2 %reduce-scatter.14.cloned.1.call-done = f32[64,512]{1,0:T(8,128)} async-done(((f32[1024,512]{1,0:T(8,128)}), f32[64,512]{1,0:T(8,128)}) %reduce-scatter.14.cloned.1.call-update) | async-done | bytes 131088 | tf_op jit(solution)/shard_map/reduce_scatter | solution.py:217
  850.1 176.4 %reduce-scatter.24.cloned.1.call-done = f32[64,2048]{1,0:T(8,128)} async-done(((f32[1024,2048]{1,0:T(8,128)}), f32[64,2048]{1,0:T(8,128)}) %reduce-scatter.24.cloned.1.call-update) | async-done | bytes 524304 | tf_op jit(solution)/shard_map/reduce_scatter | solution.py:221
  1028.4 181.4 %reduce-scatter.20.cloned.1.call-done = f32[64,2048]{1,0:T(8,128)} async-done(((f32[1024,2048]{1,0:T(8,128)}), f32[64,2048]{1,0:T(8,128)}) %reduce-scatter.20.cloned.1.call-update) | async-done | bytes 524304 | tf_op jit(solution)/shard_map/reduce_scatter | solution.py:220
  1212.8 78.2 %reduce-scatter.22.cloned.1.call-done = f32[64,4]{1,0:T(8,128)} async-done(((f32[1024,4]{1,0:T(8,128)}), f32[64,4]{1,0:T(8,128)}) %reduce-scatter.22.cloned.1.call-update) | async-done | bytes 1040
  1291.8 36.2 %all-gather = bf16[16,64,4]{1,2,0:T(4,128)(2,1)S(1)} all-gather(bf16[1,64,4]{1,2,0:T(4,128)(2,1)S(1)} %bitcast.144), channel_id=1, replica_groups=mesh['blk'=16,'tp'=2] {'blk'}, dimensions={0}, use_global_device_ids=true | all-gather | bytes 8704 | tf_op jit(solution)/shard_map/all_gather | solution.py:243
  1328.7 16.8 all-gather.14.cloned.1.call-done
  1345.4 2.8 convert_element_type.302
  1348.3 54.5 %all-gather.8.cloned.1.call-done = bf16[1024,512]{1,0:T(8,128)(2,1)} async-done(((bf16[64,512]{1,0:T(8,128)(2,1)}), bf16[1024,512]{1,0:T(8,128)(2,1)}) %all-gather.8.cloned.1.call-update) | async-done | bytes 1048592 | tf_op jit(solution)/shard_map/all_gather | solution.py:225
  1402.7 2.8 convert_element_type.296
  1405.6 54.0 %all-gather.12.cloned.1.call-done = bf16[1024,512]{1,0:T(8,128)(2,1)} async-done(((bf16[64,512]{1,0:T(8,128)(2,1)}), bf16[1024,512]{1,0:T(8,128)(2,1)}) %all-gather.12.cloned.1.call-update) | async-done | bytes 1048592 | tf_op jit(solution)/shard_map/all_gather | solution.py:231
  1459.6 2.8 convert_element_type.300
  1462.4 54.5 %all-gather.10.cloned.1.call-done = bf16[1024,512]{1,0:T(8,128)(2,1)} async-done(((bf16[64,512]{1,0:T(8,128)(2,1)}), bf16[1024,512]{1,0:T(8,128)(2,1)}) %all-gather.10.cloned.1.call-update) | async-done | bytes 1048592 | tf_op jit(solution)/shard_map/all_gather | solution.py:228
  1516.9 2.8 convert_element_type.298
  1519.7 74.7 %all-gather.18.cloned.1.call-done = bf16[1024,2048]{1,0:T(8,128)(2,1)} async-done(((bf16[64,2048]{1,0:T(8,128)(2,1)}), bf16[1024,2048]{1,0:T(8,128)(2,1)}) %all-gather.18.cloned.1.call-update) | async-done | bytes 4194320 | tf_op jit(solution)/shard_map/all_gather | solution.py:240
  1594.4 6.7 convert_element_type.306
  1601.2 71.2 %all-gather.16.cloned.1.call-done = bf16[1024,2048]{1,0:T(8,128)(2,1)} async-done(((bf16[64,2048]{1,0:T(8,128)(2,1)}), bf16[1024,2048]{1,0:T(8,128)(2,1)}) %all-gather.16.cloned.1.call-update) | async-done | bytes 4194320 | tf_op jit(solution)/shard_map/all_gather | solution.py:237
  1672.4 6.7 convert_element_type.304
  (687 shorter events, 268.6 us)
Async XLA Ops:
  7.3 203.3 %all-reduce.5.cloned.1.call-start = ((), (), s32[]{:S(2)}) async-start(), calls=%async_computation.7 | async-start | bytes 524288 | tf_op jit(solution)/shard_map/psum | solution.py:124
  15.7 11.5 collective-permute-start
  30.0 11.3 collective-permute-start.1
  96.8 11.2 collective-permute-start.1
  108.8 12.5 collective-permute-start.1
  122.0 12.3 collective-permute-start.1
  135.1 11.5 collective-permute-start.1
  195.8 46.5 %all-reduce.7.cloned.1.call-start = ((), (), s32[]{:S(2)}) async-start(), calls=%async_computation.8 | async-start | bytes 524288 | tf_op jit(solution)/shard_map/psum | solution.py:139
  222.7 309.1 %all-reduce.9.cloned.1.call-start = ((), (), s32[]{:S(2)}) async-start(), calls=%async_computation.22 | async-start | bytes 1048576 | tf_op jit(solution)/shard_map/psum | solution.py:130
  251.6 11.0 collective-permute-start.3
  253.1 12.2 collective-permute-start.4
  254.6 13.0 collective-permute-start.5
  267.7 12.0 collective-permute-start.2
  268.8 11.8 collective-permute-start.3
  271.2 12.1 collective-permute-start.4
  271.8 13.0 collective-permute-start.5
  284.9 13.0 collective-permute-start.2
  285.5 12.4 collective-permute-start.3
  288.5 11.0 collective-permute-start.4
  289.1 11.9 collective-permute-start.5
  301.1 11.2 collective-permute-start.2
  301.7 11.8 collective-permute-start.3
  302.0 12.9 collective-permute-start.4
  303.4 12.8 collective-permute-start.5
  317.1 12.2 collective-permute-start.4
  317.2 13.5 collective-permute-start.5
  331.5 11.2 collective-permute-start.4
  332.1 12.0 collective-permute-start.5
  345.1 11.9 collective-permute-start.5
  358.8 11.2 collective-permute-start.5
  370.1 11.3 collective-permute-start.2
  372.7 11.5 collective-permute-start.5
  384.2 12.6 collective-permute-start.2
  384.9 12.0 collective-permute-start.3
  388.0 11.3 collective-permute-start.5
  399.4 13.8 collective-permute-start.2
  400.1 13.2 collective-permute-start.3
  404.4 11.2 collective-permute-start.5
  415.7 13.4 collective-permute-start.2
  416.3 12.8 collective-permute-start.3
  422.2 11.9 collective-permute-start.5
  434.9 12.2 collective-permute-start.3
  439.9 11.5 collective-permute-start.5
  451.5 13.4 collective-permute-start.2
  452.2 12.8 collective-permute-start.3
  456.8 12.4 collective-permute-start.5
  472.2 12.2 collective-permute-start.2
  472.9 11.8 collective-permute-start.3
  472.9 13.2 collective-permute-start.4
  474.5 13.0 collective-permute-start.5
  490.6 11.8 collective-permute-start.7
  503.9 103.0 %reduce-scatter.18.cloned.1.call-start = ((), (), s32[]{:S(2)}) async-start(), calls=%async_computation.15 | async-start | bytes 2228224 | tf_op jit(solution)/shard_map/reduce_scatter | solution.py:219
  506.0 181.3 %reduce-scatter.12.cloned.1.call-start = ((), (), s32[]{:S(2)}) async-start(), calls=%async_computation.9 | async-start | bytes 2228224 | tf_op jit(solution)/shard_map/reduce_scatter | solution.py:216
  508.0 259.7 %reduce-scatter.16.cloned.1.call-start = ((), (), s32[]{:S(2)}) async-start(), calls=%async_computation.13 | async-start | bytes 2228224 | tf_op jit(solution)/shard_map/reduce_scatter | solution.py:218
  509.9 338.6 %reduce-scatter.14.cloned.1.call-start = ((), (), s32[]{:S(2)}) async-start(), calls=%async_computation.11 | async-start | bytes 2228224 | tf_op jit(solution)/shard_map/reduce_scatter | solution.py:217
  511.9 514.7 %reduce-scatter.24.cloned.1.call-start = ((), (), s32[]{:S(2)}) async-start(), calls=%async_computation.21 | async-start | bytes 8912896 | tf_op jit(solution)/shard_map/reduce_scatter | solution.py:221
  525.8 684.0 %reduce-scatter.20.cloned.1.call-start = ((), (), s32[]{:S(2)}) async-start(), calls=%async_computation.17 | async-start | bytes 8912896 | tf_op jit(solution)/shard_map/reduce_scatter | solution.py:220
  531.7 759.3 %reduce-scatter.22.cloned.1.call-start = ((), (), s32[]{:S(2)}) async-start(), calls=%async_computation.20 | async-start | bytes 557056
  535.5 809.9 %all-gather.14.cloned.1.call-start = ((), (), s32[]{:S(2)}) async-start(), calls=%async_computation.16 | async-start | bytes 1114112 | tf_op jit(solution)/shard_map/all_gather | solution.py:234
  608.5 794.2 %all-gather.8.cloned.1.call-start = ((), (), s32[]{:S(2)}) async-start(), calls=%async_computation.10 | async-start | bytes 1114112 | tf_op jit(solution)/shard_map/all_gather | solution.py:225
  688.9 770.7 %all-gather.12.cloned.1.call-start = ((), (), s32[]{:S(2)}) async-start(), calls=%async_computation.14 | async-start | bytes 1114112 | tf_op jit(solution)/shard_map/all_gather | solution.py:231
  769.3 747.6 %all-gather.10.cloned.1.call-start = ((), (), s32[]{:S(2)}) async-start(), calls=%async_computation.12 | async-start | bytes 1114112 | tf_op jit(solution)/shard_map/all_gather | solution.py:228
  850.1 744.3 %all-gather.18.cloned.1.call-start = ((), (), s32[]{:S(2)}) async-start(), calls=%async_computation.19 | async-start | bytes 4456448 | tf_op jit(solution)/shard_map/all_gather | solution.py:240
  1028.3 644.0 %all-gather.16.cloned.1.call-start = ((), (), s32[]{:S(2)}) async-start(), calls=%async_computation.18 | async-start | bytes 4456448 | tf_op jit(solution)/shard_map/all_gather | solution.py:237
  (108 other events, 4120.1 us)
Sparse Core Ops, SparseCore 0:
  195.9 14.5 all-reduce.4
  222.8 19.4 all-reduce.6
  504.1 18.4 all-reduce.8
  525.3 81.5 reduce-scatter.17
  609.7 77.4 reduce-scatter.11
  690.1 77.5 reduce-scatter.15
  770.7 77.8 reduce-scatter.13
  851.5 175.0 reduce-scatter.23
  1029.5 180.2 reduce-scatter.19
  1212.0 78.9 reduce-scatter.21
  1293.7 51.6 all-gather.13
  1348.6 54.0 all-gather.7
  1405.5 54.0 all-gather.11
  1462.8 54.0 all-gather.9
  1519.5 74.8 all-gather.17
  1597.6 74.6 all-gather.15
where the time goes:
time: 1690 us
  waiting for transfers between devices  1260 us (75%)
  starting transfers between devices  102 us (6%)
  loops' own time  80.1 us (5%)
  other arithmetic  76.1 us (5%)
  local copies, waits for them, and re-layouts  70.4 us (4%)
  matrix products  47.2 us (3%)
  blocking collectives  36.2 us (2%)
    reduce_scatter x1, waiting for transfers between devices, body(): lax.psum_scatter(up_grad, 'blk', scatter_dimension=0, tiled=True)  181 us
    reduce_scatter x1, waiting for transfers between devices, body(): lax.psum_scatter(down_grad, 'blk', scatter_dimension=0, tiled=True)  176 us
    ppermute x92, waiting for transfers between devices, from_behind(): return lax.ppermute(block, axis, route)  159 us
    ppermute x92, starting transfers between devices, from_behind(): return lax.ppermute(block, axis, route)  101 us
    reduce_scatter x1, waiting for transfers between devices, body(): lax.psum_scatter(key_grad, 'blk', scatter_dimension=0, tiled=True)  79.2 us
    reduce_scatter x1, waiting for transfers between devices, body(): lax.psum_scatter(value_grad, 'blk', scatter_dimension=0, tiled=True)  78.8 us
    reduce_scatter x1, waiting for transfers between devices, body(): lax.psum_scatter(query_grad, 'blk', scatter_dimension=0, tiled=True)  78.7 us
    unnamed x17, waiting for transfers between devices  78.4 us
  transfers between devices with their start and end apart: 108, of which 84 were waited for; matrix products, arithmetic and copies ran while one was open for 8% of the time, Pallas kernels for 0%

commit v1 on v0

--- a/solution.py
+++ b/solution.py
@@ -1,9 +1,16 @@
 import jax
 import jax.numpy as jnp
 from jax import lax
+from jax.experimental import pallas as pl
+from jax.experimental.pallas import tpu as pltpu
 from jax.sharding import PartitionSpec as P
 
 HEAD = 64
+NEG = -1e30
+f32 = jnp.float32
+bf16 = jnp.bfloat16
+LAST = (((1,), (1,)), ((), ()))
+FIRST = (((0,), (0,)), ((), ()))
 
 
 def from_behind(block, axis, distance):
@@ -25,7 +32,7 @@
     )
 
 
-def body(
+def ring_body(
     tokens,
     first_gain,
     first_bias,
@@ -40,8 +47,6 @@
     cotangent,
     scene_len,
 ):
-    f32 = jnp.float32
-    bf16 = jnp.bfloat16
     count = lax.axis_size("blk")
     place = lax.axis_index("blk")
     rows = tokens.shape[0]
@@ -260,7 +265,343 @@
     )
 
 
+def full(shape):
+    return pl.BlockSpec(shape, lambda *_: (0,) * len(shape))
+
+
+def attend_kernel(q_ref, k_ref, v_ref, mine_ref, all_ref, out_ref):
+    lane = lax.broadcasted_iota(jnp.int32, q_ref.shape, 1) // HEAD
+    mask = mine_ref[...] == all_ref[...]
+    parts = []
+    for head in range(2):
+        q = jnp.where(lane == head, q_ref[...], jnp.zeros_like(q_ref[...]))
+        s = lax.dot_general(q, k_ref[...], LAST, preferred_element_type=f32)
+        s = jnp.where(mask, s, NEG)
+        p = jnp.exp(s - jnp.max(s, axis=1, keepdims=True))
+        total = jnp.sum(p, axis=1, keepdims=True)
+        part = jnp.dot(p.astype(bf16), v_ref[...], preferred_element_type=f32)
+        parts.append(part / total)
+    out_ref[...] = jnp.where(lane == 0, parts[0], parts[1]).astype(bf16)
+
+
+def attend(q, k, v, scene_mine, scene_all):
+    rows, width = q.shape
+    total = k.shape[0]
+    pair = 2 * HEAD
+    return pl.pallas_call(
+        attend_kernel,
+        grid=(width // pair,),
+        in_specs=[
+            pl.BlockSpec((rows, pair), lambda i: (0, i)),
+            pl.BlockSpec((total, pair), lambda i: (0, i)),
+            pl.BlockSpec((total, pair), lambda i: (0, i)),
+            full((rows, 1)),
+            full((1, total)),
+        ],
+        out_specs=pl.BlockSpec((rows, pair), lambda i: (0, i)),
+        out_shape=jax.ShapeDtypeStruct((rows, width), bf16),
+        name="attend",
+    )(q, k, v, scene_mine.reshape(rows, 1), scene_all.reshape(1, total))
+
+
+QT = 256
+KT = 512
+
+
+def prepare_kernel(h_ref, row_ref, col_ref, lse_ref, a_ref, k_s):
+    @pl.when(pl.program_id(0) == 0)
+    def _():
+        k_s[...] = h_ref[HEAD : 2 * HEAD, :].T
+
+    at = pl.multiple_of(pl.program_id(0) * QT, QT)
+    q = h_ref[0:HEAD, pl.ds(at, QT)]
+    s = jnp.dot(k_s[...], q, preferred_element_type=f32)
+    s = jnp.where(col_ref[...] == row_ref[...], s, NEG)
+    top = jnp.max(s, axis=0, keepdims=True)
+    p = jnp.exp(s - top)
+    total = jnp.sum(p, axis=0, keepdims=True)
+    a = jnp.dot(h_ref[2 * HEAD :, :], p.astype(bf16), preferred_element_type=f32)
+    a_ref[...] = a / total
+    lse_ref[...] = top + jnp.log(total)
+
+
+def prepare(head, scene_all):
+    total = head.shape[1]
+    return pl.pallas_call(
+        prepare_kernel,
+        grid=(total // QT,),
+        in_specs=[
+            full(head.shape),
+            pl.BlockSpec((1, QT), lambda i: (0, i)),
+            full((total, 1)),
+        ],
+        out_specs=[
+            pl.BlockSpec((1, QT), lambda i: (0, i)),
+            pl.BlockSpec((HEAD, QT), lambda i: (0, i)),
+        ],
+        out_shape=[
+            jax.ShapeDtypeStruct((1, total), f32),
+            jax.ShapeDtypeStruct((HEAD, total), f32),
+        ],
+        scratch_shapes=[pltpu.VMEM((total, HEAD), bf16)],
+        name="prepare",
+    )(head, scene_all.reshape(1, total), scene_all.reshape(total, 1))
+
+
+def back_kernel(h_ref, ga_ref, lse_ref, a_ref, row_ref, col_ref, out_ref, k_s, v_s, gk_s, gv_s):
+    step = pl.program_id(0)
+    total = h_ref.shape[1]
+
+    @pl.when(step == 0)
+    def _():
+        k_s[...] = h_ref[HEAD : 2 * HEAD, :].T
+        v_s[...] = h_ref[2 * HEAD :, :].T
+        gk_s[...] = jnp.zeros_like(gk_s)
+        gv_s[...] = jnp.zeros_like(gv_s)
+
+    at = pl.multiple_of(step * QT, QT)
+    q_t = h_ref[0:HEAD, pl.ds(at, QT)]
+    ga_t = jnp.concatenate([ga_ref[i] for i in range(ga_ref.shape[0])], axis=1)
+    q = q_t.T
+    ga = ga_t.T
+    delta = jnp.sum(ga_t.astype(f32) * a_ref[...], axis=0, keepdims=True)
+    gq = jnp.zeros((HEAD, QT), f32)
+    for j in range(total // KT):
+        keys = slice(j * KT, (j + 1) * KT)
+        s = jnp.dot(k_s[keys, :], q_t, preferred_element_type=f32)
+        p = jnp.where(col_ref[keys, :] == row_ref[...], jnp.exp(s - lse_ref[...]), 0.0)
+        dp = jnp.dot(v_s[keys, :], ga_t, preferred_element_type=f32)
+        ds = (p * (dp - delta)).astype(bf16)
+        gv_s[keys, :] += jnp.dot(p.astype(bf16), ga, preferred_element_type=f32)
+        gk_s[keys, :] += jnp.dot(ds, q, preferred_element_type=f32)
+        gq += jnp.dot(h_ref[HEAD : 2 * HEAD, keys], ds, preferred_element_type=f32)
+    out_ref[0:HEAD, pl.ds(at, QT)] = (gq * HEAD ** (-0.5)).astype(bf16)
+
+    @pl.when(step == pl.num_programs(0) - 1)
+    def _():
+        out_ref[HEAD : 2 * HEAD, :] = gk_s[...].T.astype(bf16)
+        out_ref[2 * HEAD :, :] = gv_s[...].T.astype(bf16)
+
+
+def back(head, ga, lse, a, scene_all):
+    total = head.shape[1]
+    per = QT // ga.shape[2]
+    return pl.pallas_call(
+        back_kernel,
+        grid=(total // QT,),
+        in_specs=[
+            full(head.shape),
+            pl.BlockSpec((per, HEAD, ga.shape[2]), lambda i: (i, 0, 0)),
+            pl.BlockSpec((1, QT), lambda i: (0, i)),
+            pl.BlockSpec((HEAD, QT), lambda i: (0, i)),
+            pl.BlockSpec((1, QT), lambda i: (0, i)),
+            full((total, 1)),
+        ],
+        out_specs=full(head.shape),
+        out_shape=jax.ShapeDtypeStruct(head.shape, bf16),
+        scratch_shapes=[
+            pltpu.VMEM((total, HEAD), bf16),
+            pltpu.VMEM((total, HEAD), bf16),
+            pltpu.VMEM((total, HEAD), f32),
+            pltpu.VMEM((total, HEAD), f32),
+        ],
+        name="back",
+    )(head, ga, lse, a, scene_all.reshape(1, total), scene_all.reshape(total, 1))
+
+
+FT = 256
+TT = 512
+
+
+def gelu_both(pre, grad):
+    half = 0.5 * (1.0 + lax.erf(pre * 0.7071067811865476))
+    slope = half + pre * (jnp.exp(-0.5 * pre * pre) * 0.3989422804014327)
+    return (pre * half).astype(bf16), (grad * slope).astype(bf16)
+
+
+def ffn_kernel(h_ref, g_ref, ht_ref, gt_ref, up_ref, down_ref, up_out, down_out):
+    total = h_ref.shape[0]
+    for j in range(total // TT):
+        rows = slice(j * TT, (j + 1) * TT)
+        pre = jnp.dot(h_ref[rows, :], up_ref[...], preferred_element_type=f32)
+        grad = jnp.dot(g_ref[rows, :], down_ref[...], preferred_element_type=f32)
+        act, grad_pre = gelu_both(pre, grad)
+        up = jnp.dot(ht_ref[:, rows], grad_pre, preferred_element_type=f32)
+        down = jnp.dot(gt_ref[:, rows], act, preferred_element_type=f32)
+        if j == 0:
+            up_out[...] = up
+            down_out[...] = down
+        else:
+            up_out[...] += up
+            down_out[...] += down
+
+
+def ffn_grads(h, xg, h_t, g_t, up_weight, down_weight):
+    total, width = h.shape
+    hidden = up_weight.shape[1]
+    once = pl.Buffered(1)
+    return pl.pallas_call(
+        ffn_kernel,
+        grid=(hidden // FT,),
+        in_specs=[
+            pl.BlockSpec((total, width), lambda i: (0, 0), pipeline_mode=once),
+            pl.BlockSpec((total, width), lambda i: (0, 1), pipeline_mode=once),
+            pl.BlockSpec((width, total), lambda i: (0, 0), pipeline_mode=once),
+            pl.BlockSpec((width, total), lambda i: (0, 0), pipeline_mode=once),
+            pl.BlockSpec((width, FT), lambda i: (0, i)),
+            pl.BlockSpec((width, FT), lambda i: (0, i)),
+        ],
+        out_specs=[pl.BlockSpec((width, FT), lambda i: (0, i))] * 2,
+        out_shape=[jax.ShapeDtypeStruct((width, hidden), f32)] * 2,
+        name="ffn_grads",
+    )(h, xg, h_t, g_t, up_weight, down_weight)
+
+
+def both_halves(partial):
+    low = lax.optimization_barrier(partial.astype(bf16))
+    other = lax.ppermute(low, "tp", [(0, 1), (1, 0)])
+    return low.astype(f32) + other.astype(f32)
+
+
+def fast_body(
+    tokens,
+    first_gain,
+    first_bias,
+    second_gain,
+    second_bias,
+    query_weight,
+    key_weight,
+    value_weight,
+    output_weight,
+    up_weight,
+    down_weight,
+    cotangent,
+    scene_len,
+):
+    count = lax.axis_size("blk")
+    place = lax.axis_index("blk")
+    side = lax.axis_index("tp")
+    rows, width = tokens.shape
+    total = rows * count
+    heads_here = query_weight.shape[1] // HEAD
+    share = count // heads_here
+    scale = HEAD ** (-0.5)
+    head_at = (place // share) * HEAD
+    part = place % share
+
+    def half_of(block):
+        return lax.dynamic_slice_in_dim(block, side * (rows // 2), rows // 2, 0)
+
+    both = jnp.concatenate([half_of(tokens), half_of(cotangent)], axis=1)
+    xg = lax.all_gather(both, ("blk", "tp"), axis=0, tiled=True)
+
+    ends = jnp.cumsum(scene_len)
+    positions = jnp.arange(total, dtype=jnp.int32)
+    scene_all = jnp.sum((positions[:, None] >= ends[None, :]).astype(jnp.int32), axis=1)
+    scene_mine = lax.dynamic_slice_in_dim(scene_all, place * rows, rows)
+
+    inputs = tokens.astype(f32)
+    h1_mine = layer_norm(inputs, first_gain, first_bias).astype(bf16)
+    h1_all = layer_norm(xg[:, :width].astype(f32), first_gain, first_bias).astype(bf16)
+
+    def project(rows_in, weight):
+        return jnp.dot(rows_in, weight, preferred_element_type=f32)
+
+    query = (project(h1_mine, query_weight).astype(bf16) * scale).astype(bf16)
+    keys = project(h1_all, key_weight).astype(bf16)
+    values = project(h1_all, value_weight).astype(bf16)
+    attended = attend(query, keys, values, scene_mine, scene_all)
+
+    def head_of(weight):
+        return lax.dynamic_slice_in_dim(weight, head_at, HEAD, 1)
+
+    head_weight = jnp.concatenate(
+        [head_of(query_weight) * jnp.asarray(scale, bf16), head_of(key_weight), head_of(value_weight)], axis=1
+    )
+    head = lax.dot_general(
+        head_weight, h1_all, (((0,), (1,)), ((), ())), preferred_element_type=f32
+    ).astype(bf16)
+    lse, head_attended = prepare(head, scene_all)
+
+    branch = lax.dot_general(attended, output_weight, LAST, preferred_element_type=f32)
+    middle = inputs + both_halves(branch)
+    h2 = layer_norm(middle, second_gain, second_bias).astype(bf16)
+    h2_all = lax.all_gather(half_of(h2), ("blk", "tp"), axis=0, tiled=True)
+
+    before = jnp.dot(h2, up_weight, preferred_element_type=f32)
+    grad_active = jnp.dot(cotangent, down_weight, preferred_element_type=f32)
+    active, grad_before = gelu_both(before, grad_active)
+    grad_two = lax.dot_general(grad_before, up_weight, LAST, preferred_element_type=f32)
+    grad_two = both_halves(grad_two)
+    _, second_pull = jax.vjp(layer_norm, middle, second_gain, second_bias)
+    grad_middle, second_gain_grad, second_bias_grad = second_pull(grad_two)
+    grad_middle = cotangent.astype(f32) + grad_middle
+    grad_middle_low = grad_middle.astype(bf16)
+    grad_attended = lax.dot_general(
+        output_weight, grad_middle_low, (((0,), (1,)), ((), ())), preferred_element_type=f32
+    ).astype(bf16)
+    to_heads = jnp.repeat(grad_attended.reshape(heads_here, HEAD, rows), share, axis=0)
+    ga = lax.all_to_all(to_heads, "blk", 0, 0, tiled=True)
+
+    feed = lax.dot_general(active, down_weight, LAST, preferred_element_type=f32)
+    layer_out = (middle + both_halves(feed)).astype(bf16)
+    output_part = lax.dot_general(grad_middle_low, attended, FIRST, preferred_element_type=f32)
+    output_part = output_part.astype(bf16).reshape(count, width // count, -1)
+    output_parts = lax.all_to_all(output_part, "blk", 0, 0, tiled=True)
+    output_slice = jnp.sum(output_parts.astype(f32), axis=0).astype(bf16)
+
+    head_grads = back(head, ga, lse, head_attended, scene_all)
+    h1_part = lax.dynamic_slice_in_dim(h1_all, part * (width // share), width // share, 1)
+    head_slice = jnp.dot(head_grads, h1_part, preferred_element_type=f32).astype(bf16)
+    gathered = lax.all_gather(
+        jnp.concatenate([head_slice, output_slice.reshape(-1, width // share)], axis=0), "blk", axis=0
+    )
+
+    piece = 3 * HEAD // share
+    home = lax.dynamic_slice_in_dim(head_grads, part * piece, piece, 0)
+    home = home.reshape(piece, count, rows).transpose(1, 0, 2)
+    home = lax.all_to_all(home, "blk", 0, 0, tiled=True)
+    home = home.reshape(heads_here, 3, HEAD, rows)
+    grad_one = 0.0
+    for i, weight in enumerate((query_weight, key_weight, value_weight)):
+        grad_one = grad_one + lax.dot_general(
+            home[:, i].reshape(-1, rows), weight, (((0,), (1,)), ((), ())), preferred_element_type=f32
+        )
+    grad_one = both_halves(grad_one)
+    _, first_pull = jax.vjp(layer_norm, inputs, first_gain, first_bias)
+    grad_input, first_gain_grad, first_bias_grad = first_pull(grad_one)
+    input_grad = grad_middle + grad_input
+    norm_part = jnp.stack([first_gain_grad, first_bias_grad, second_gain_grad, second_bias_grad])
+    norm_parts = lax.all_to_all(
+        jnp.broadcast_to(norm_part[None], (count,) + norm_part.shape), "blk", 0, 0, tiled=True
+    )
+    norm_sums = jnp.sum(norm_parts, axis=0)
+
+    up_grad, down_grad = ffn_grads(h2_all, xg, h2_all.T, xg[:, width:].T, up_weight, down_weight)
+
+    def weight_grad(i):
+        pieces = gathered[:, i * HEAD : (i + 1) * HEAD].reshape(heads_here, share, HEAD, width // share)
+        return pieces.transpose(1, 3, 0, 2).reshape(width, heads_here * HEAD).astype(f32)
+
+    output_grad = gathered[:, 3 * HEAD :].reshape(width, heads_here * HEAD).astype(f32)
+    return (
+        layer_out,
+        input_grad,
+        norm_sums[0],
+        norm_sums[1],
+        norm_sums[2],
+        norm_sums[3],
+        weight_grad(0),
+        weight_grad(1),
+        weight_grad(2),
+        output_grad,
+        up_grad,
+        down_grad,
+    )
+
+
 def solution(mesh):
+    body = fast_body if mesh.shape["blk"] == 16 else ring_body
     return jax.shard_map(
         body,
         mesh=mesh,

time: 1690 us -> 346 us (0.20)
  waiting for transfers between devices: 1260 us -> 104 us
  starting transfers between devices: 102 us -> 14.5 us
  Pallas kernels: 0 us -> 84.7 us
  loops' own time: 80.1 us -> 0 us
  other arithmetic: 76.1 us -> 23.8 us
  local copies, waits for them, and re-layouts: 70.4 us -> 51 us
  blocking collectives: 36.2 us -> 18.2 us
    reduce_scatter x6 -> x0, waiting for transfers between devices: 666 us -> none  [the longest x1 181 us: body(): lax.psum_scatter(up_grad, 'blk', scatter_dimension=0, tiled=True)]
    all_gather x6 -> x3, waiting for transfers between devices: 326 us -> 76.1 us  [the longest x1 76.1 us: fast_body(): xg = lax.all_gather(both, ('blk', 'tp'), axis=0, tiled=True)]
    ppermute x92 -> x4, waiting for transfers between devices: 159 us -> 2.23 us  [both_halves(): other = lax.ppermute(low, 'tp', [(0, 1), (1, 0)])]
    ppermute x92 -> x4, starting transfers between devices: 101 us -> 1.05 us  [both_halves(): other = lax.ppermute(low, 'tp', [(0, 1), (1, 0)])]
    pallas_call x0 -> x4, Pallas kernels: none -> 84.7 us  [the longest x1 49.6 us: ffn_grads(): pl.pallas_call(ffn_kernel, grid=(hidden // FT,), in_specs=[pl.BlockSpec((...]
    another operation x32 -> x0, loops' own time: 80.1 us -> none  [the longest x1 40.1 us: body(): lax.fori_loop(1, steps + 1, turn_backward, (grad_query, keys, values, emp...]
    unnamed x17 -> x3, waiting for transfers between devices: 78.4 us -> 0.05 us
    all_gather x1 -> x0, blocking collectives: 36.2 us -> none  [body(): lax.all_gather(summed_parts[6].astype(jnp.bfloat16), 'blk', axis=0, tiled...]
  transfers between devices with their start and end apart: 108 -> 10, of which waited for: 84 -> 5; matrix products, arithmetic and copies ran while one was open for 8% -> 17% of each run, Pallas kernels for 0% -> 22%
where the time goes in v1:
time: 346 us; the launch traced here: 345 us
  waiting for transfers between devices  104 us (30%)
  Pallas kernels  84.7 us (24%)
  local copies, waits for them, and re-layouts  51 us (15%)
  matrix products  34.3 us (10%)
  other arithmetic  23.8 us (7%)
  blocking collectives  18.2 us (5%)
  starting transfers between devices  14.5 us (4%)
  between operations  14.3 us (4%)
    all_gather x1, waiting for transfers between devices, fast_body(): xg = lax.all_gather(both, ('blk', 'tp'), axis=0, tiled=True)  76.1 us
    pallas_call x1, Pallas kernels, ffn_grads(): pl.pallas_call(ffn_kernel, grid=(hidden // FT,), in_specs=[pl.BlockSpec((...  49.6 us
    unnamed x53, local copies, waits for them, and re-layouts  29.4 us
    all_to_all x1, blocking collectives, fast_body(): home = lax.all_to_all(home, 'blk', 0, 0, tiled=True)  18.2 us
    pallas_call x1, Pallas kernels, back(): pl.pallas_call(back_kernel, grid=(total // QT,), in_specs=[full(head.shap...  16 us
    all_to_all x1, waiting for transfers between devices, fast_body(): lax.all_to_all(jnp.broadcast_to(norm_part[None], (count,) + norm_part.sha...  13.1 us
    all_to_all x1, waiting for transfers between devices, fast_body(): ga = lax.all_to_all(to_heads, 'blk', 0, 0, tiled=True)  12.5 us
    pallas_call x1, Pallas kernels, prepare(): pl.pallas_call(prepare_kernel, grid=(total // QT,), in_specs=[full(head.s...  11.8 us
  transfers between devices with their start and end apart: 10, of which 5 were waited for; matrix products, arithmetic and copies ran while one was open for 17% of the time, Pallas kernels for 22%

profile of v1, /device:TPU:0, one launch (start us, length us, event | category | flops | bytes accessed | tf_op | source)
XLA Modules:
  0.0 344.8 jit_solution(15986536828384403330)
XLA Ops:
  7.2 1.1 constant_dynamic-slice_fusion.3
  8.3 0.7 pad_maximum_fusion
  9.1 0.8 reduce-window.8
  10.1 0.7 copy.116.mine_ref
  10.9 1.1 convert_reduce_fusion.1
  12.0 1.2 fusion.28
  13.1 2.4 fusion.14.q_ref
  15.5 76.1 %all-gather.5.cloned.1.call-done.g_ref = bf16[2048,2048]{1,0:T(8,128)(2,1)} async-done(((bf16[64,2048]{1,0:T(8,128)(2,1)}), bf16[2048,2048]{1,0:T(8,128)(2,1)}) %all-gather.5.cloned.1.call-update) | async-done | bytes 8388624 | tf_op jit(solution)/shard_map/all_gather | solution.py:496
  91.6 3.0 convert_reduce_fusion
  94.6 3.5 %fusion.2 = f32[2048]{0:T(1024)S(1)} fusion(f32[2048]{0:T(1024)S(1)} %broadcast_multiply_fusion, bf16[2048,2048]{1,0:T(8,128)(2,1)} %all-gather.5.cloned.1.call-done.g_ref), kind=kLoop, calls=%fused_computation.4 | loop fusion | flops 8386560 | bytes 4210688 | tf_op jit(solution)/shard_map/reduce_sum | solution.py:24
  98.1 1.7 fusion.5
  99.8 3.7 %convolution_convert_fusion.v_ref = bf16[2048,512]{1,0:T(8,128)(2,1)} fusion(bf16[2048,1024]{1,0:T(8,128)(2,1)S(1)} %fusion.5, bf16[1024,512]{1,0:T(8,128)(2,1)S(1)} %copy-done.10), kind=kOutput, calls=%fused_computation.8 | convolution fusion | flops 2148532224 | bytes 7340032 | tf_op jit(solution)/shard_map/dot_general | solution.py:508
  103.6 3.7 %convolution_convert_fusion.1.k_ref = bf16[2048,512]{1,0:T(8,128)(2,1)} fusion(bf16[2048,1024]{1,0:T(8,128)(2,1)S(1)} %fusion.5, bf16[1024,512]{1,0:T(8,128)(2,1)S(1)} %copy-done), kind=kOutput, calls=%fused_computation.9 | convolution fusion | flops 2148532224 | bytes 7340032 | tf_op jit(solution)/shard_map/dot_general | solution.py:508
  107.3 7.3 %attend.1 = bf16[128,512]{1,0:T(8,128)(2,1)} custom-call(bf16[128,512]{1,0:T(8,128)(2,1)} %fusion.14.q_ref, bf16[2048,512]{1,0:T(8,128)(2,1)} %convolution_convert_fusion.1.k_ref, bf16[2048,512]{1,0:T(8,128)(2,1)} %convolution_convert_fusion.v_ref, s32[128,1]{1,0:T(8,128)} %copy.116.mine_ref, s32[1,2048]{1,0:T(1,128)} %bitcast.90), custom_call_target="tpu_custom_call" | custom-call | tf_op jit(solution)/shard_map/attend/pallas_call | solution.py:291
  114.6 1.4 convolution_convert_fusion.4
  116.0 0.3 collective-permute-start
  116.3 1.3 collective-permute-done
  118.2 0.7 constant_dynamic-slice_fusion
  118.9 2.9 fusion.57
  121.8 5.9 %convolution_convert_fusion.5 = bf16[128,1024]{1,0:T(8,128)(2,1)S(1)} fusion(bf16[1024,2048]{1,0:T(8,128)(2,1)} %up_ref.1, bf16[128,1024]{1,0:T(8,128)(2,1)S(1)} %copy-done.12, bf16[1024,2048]{1,0:T(8,128)(2,1)} %down_ref.1, f32[128,2048]{1,0:T(8,128)S(1)} %fusion.57), kind=kOutput, calls=%fused_computation.24 | convolution fusion | flops 1076494336 | bytes 9961472 | tf_op jit(solution)/shard_map/dot_general | solution.py:534
  127.7 0.3 collective-permute-start.2
  128.0 3.8 %convolution_convert_fusion.6 = bf16[128,1024]{1,0:T(8,128)(2,1)S(1)} fusion(bf16[1024,2048]{1,0:T(8,128)(2,1)} %down_ref.1, f32[128,2048]{1,0:T(8,128)S(1)} %fusion.57), kind=kOutput, calls=%fused_computation.25 | convolution fusion | flops 538312704 | bytes 5505024 | tf_op jit(solution)/shard_map/dot_general | solution.py:546
  131.8 0.3 collective-permute-start.1
  132.1 0.3 multiply_reduce_fusion
  132.4 1.0 collective-permute-done.1
  133.4 1.9 fusion.52
  135.5 0.3 fusion.13
  135.9 0.8 broadcast_in_dim.14
  136.7 4.3 %all-to-all-start = ((bf16[16,64,128]{2,1,0:T(8,128)(2,1)}), bf16[16,64,128]{2,1,0:T(8,128)(2,1)S(1)}, u32[]{:S(2)}, u32[]{:S(2)}) async-start(bf16[16,64,128]{2,1,0:T(8,128)(2,1)} %bitcast.6), calls=%async_computation | async-start | bytes 524288 | tf_op jit(solution)/shard_map/all_to_all | solution.py:544
  141.0 1.4 convolution_convert_fusion.3
  142.4 12.5 %all-to-all-done.ga_ref = bf16[16,64,128]{2,1,0:T(8,128)(2,1)S(1)} async-done(((bf16[16,64,128]{2,1,0:T(8,128)(2,1)}), bf16[16,64,128]{2,1,0:T(8,128)(2,1)S(1)}, u32[]{:S(2)}, u32[]{:S(2)}) %all-to-all-start) | async-done | bytes 262176 | tf_op jit(solution)/shard_map/all_to_all | solution.py:544
  155.0 4.3 %all-to-all-start.3 = ((bf16[16,64,512]{2,1,0:T(8,128)(2,1)}), bf16[16,64,512]{2,1,0:T(8,128)(2,1)}, u32[]{:S(2)}, u32[]{:S(2)}) async-start(bf16[16,64,512]{2,1,0:T(8,128)(2,1)} %bitcast.80), calls=%async_computation.3 | async-start | bytes 2097152 | tf_op jit(solution)/shard_map/all_to_all | solution.py:550
  159.4 1.3 copy.118.col_ref
  160.9 1.3 dynamic-slice_multiply_fusion
  162.1 4.9 %convolution_convert_fusion.2.h_ref = bf16[192,2048]{1,0:T(8,128)(2,1)} fusion(bf16[2048,1024]{1,0:T(8,128)(2,1)} %copy-done.4, bf16[1024,64]{1,0:T(8,128)(2,1)S(1)} %get-tuple-element.117, bf16[1024,64]{1,0:T(8,128)(2,1)S(1)} %constant_dynamic-slice_fusion.2, bf16[1024,64]{1,0:T(8,128)(2,1)S(1)} %get-tuple-element.116), kind=kOutput, calls=%fused_computation.10 | convolution fusion | flops 806879232 | bytes 5373952 | tf_op jit(solution)/shard_map/dot_general | solution.py:521
  167.0 11.8 %prepare.1 = (f32[1,2048]{1,0:T(1,128)}, f32[64,2048]{1,0:T(8,128)}) custom-call(bf16[192,2048]{1,0:T(8,128)(2,1)} %convolution_convert_fusion.2.h_ref, s32[1,2048]{1,0:T(1,128)} %bitcast.91, s32[2048,1]{1,0:T(8,128)} %copy.118.col_ref), custom_call_target="tpu_custom_call" | custom-call | tf_op jit(solution)/shard_map/prepare/pallas_call | solution.py:330
  178.8 16.0 %back.1 = bf16[192,2048]{1,0:T(8,128)(2,1)} custom-call(bf16[192,2048]{1,0:T(8,128)(2,1)} %convolution_convert_fusion.2.h_ref, bf16[16,64,128]{2,1,0:T(8,128)(2,1)} %copy-done.15, f32[1,2048]{1,0:T(1,128)} %get-tuple-element.16.lse_ref, f32[64,2048]{1,0:T(8,128)} %get-tuple-element.17.a_ref, s32[1,2048]{1,0:T(1,128)} %bitcast.92, s32[2048,1]{1,0:T(8,128)} %copy.118.col_ref), custom_call_target="tpu_custom_call" | custom-call | tf_op jit(solution)/shard_map/back/pallas_call | solution.py:389
  194.9 2.5 fusion.10
  197.4 1.4 reduce_sum.182
  198.7 0.7 pad_maximum_fusion.1
  199.7 18.2 %all_to_all.20 = bf16[16,96,128]{2,1,0:T(8,128)(2,1)S(1)} all-to-all(bf16[16,96,128]{2,1,0:T(8,128)(2,1)S(1)} %copy.120), channel_id=1, replica_groups=mesh['blk'=16,'tp'=2] {'blk'}, dimensions={0} | all-to-all | bytes 786432 | tf_op jit(solution)/shard_map/all_to_all | solution.py:563
  217.9 0.5 fusion.58
  218.4 0.5 convolution_add_fusion.1
  218.9 0.5 fusion.9
  219.5 4.7 %slice.64 = bf16[2048,1024]{1,0:T(8,128)(2,1)} slice(bf16[2048,2048]{1,0:T(8,128)(2,1)} %all-gather.5.cloned.1.call-done.g_ref), slice={[0:2048], [1024:2048]} | slice | bytes 8388608 | tf_op jit(solution)/shard_map/slice | solution.py:580
  224.1 6.5 %copy.141 = bf16[2048,1024]{0,1:T(8,128)(2,1)} copy(bf16[2048,1024]{1,0:T(8,128)(2,1)} %slice.64) | data formatting | bytes 8388608
  230.9 0.4 fusion.27
  231.4 0.8 broadcast_in_dim.17
  232.1 4.8 %all-to-all-start.2 = ((f32[16,4,1024]{2,1,0:T(4,128)}), f32[16,4,1024]{2,1,0:T(4,128)S(1)}, u32[]{:S(2)}, u32[]{:S(2)}) async-start(f32[16,4,1024]{2,1,0:T(4,128)} %broadcast_in_dim.17), calls=%async_computation.2 | async-start | bytes 524288 | tf_op jit(solution)/shard_map/all_to_all | solution.py:575
  236.9 1.1 add_add_fusion.2
  238.0 13.1 %all-to-all-done.2 = f32[16,4,1024]{2,1,0:T(4,128)S(1)} async-done(((f32[16,4,1024]{2,1,0:T(4,128)}), f32[16,4,1024]{2,1,0:T(4,128)S(1)}, u32[]{:S(2)}, u32[]{:S(2)}) %all-to-all-start.2) | async-done | bytes 262176 | tf_op jit(solution)/shard_map/all_to_all | solution.py:575
  251.1 0.6 fusion.56
  251.7 6.6 %copy.125 = bf16[2048,1024]{0,1:T(8,128)(2,1)} copy(bf16[2048,1024]{1,0:T(8,128)(2,1)} %all-gather.7.cloned.1.call-done.h_ref) | data formatting | bytes 8388608 | tf_op jit(solution)/shard_map/all_gather | solution.py:529
  258.3 49.6 %ffn_grads.1 = (f32[1024,2048]{1,0:T(8,128)}, f32[1024,2048]{1,0:T(8,128)}) custom-call(bf16[2048,1024]{1,0:T(8,128)(2,1)} %all-gather.7.cloned.1.call-done.h_ref, bf16[2048,2048]{1,0:T(8,128)(2,1)} %all-gather.5.cloned.1.call-done.g_ref, bf16[1024,2048]{1,0:T(8,128)(2,1)} %bitcast.78, bf16[1024,2048]{1,0:T(8,128)(2,1)} %bitcast.77, ...), custom_call_target="tpu_custom_call" | custom-call | tf_op jit(solution)/shard_map/ffn_grads/pallas_call | solution.py:443
  307.9 4.0 %fusion.54 = (bf16[16,64,512]{2,1,0:T(8,128)(2,1)}, bf16[16,64,512]{2,1,0:T(8,128)(2,1)S(1)}, bf16[16,64,512]{2,1,0:T(8,128)(2,1)}, bf16[16,64,512]{2,1,0:T(8,128)(2,1)S(1)}) fusion(bf16[16,256,512]{2,1,0:T(8,128)(2,1)} %bitcast.79), kind=kLoop, calls=%fused_computation.109 | loop fusion | bytes 8388608 | tf_op jit(solution)/shard_map/slice | solution.py:586
  311.9 0.3 convert_bitcast_fusion.2
  312.2 2.7 copy.130
  314.9 4.8 %reshape.203 = f32[1024,512]{1,0:T(8,128)} reshape(f32[2,512,8,64]{3,2,1,0:T(8,128)} %copy.130) | data formatting | bytes 4194304
  319.7 1.5 convert_bitcast_fusion.1
  321.2 2.7 copy.131
  323.9 4.8 %reshape.204 = f32[1024,512]{1,0:T(8,128)} reshape(f32[2,512,8,64]{3,2,1,0:T(8,128)} %copy.131) | data formatting | bytes 4194304
  329.0 2.7 copy.132
  331.7 4.9 %reshape.205 = f32[1024,512]{1,0:T(8,128)} reshape(f32[2,512,8,64]{3,2,1,0:T(8,128)} %copy.132) | data formatting | bytes 4194304
  336.6 1.7 bitcast_convert_fusion
  (82 shorter events, 2.4 us)
Async XLA Ops:
  7.2 96.4 %copy-start = (bf16[1024,512]{1,0:T(8,128)(2,1)S(1)}, bf16[1024,512]{1,0:T(8,128)(2,1)}, u32[]{:S(2)}) copy-start(bf16[1024,512]{1,0:T(8,128)(2,1)} %param.19) | copy-start | bytes 3145732
  7.2 84.4 %all-gather.5.cloned.1.call-start = ((), (), s32[]{:S(2)}) async-start(), calls=%async_computation.4 | async-start | bytes 8650752 | tf_op jit(solution)/shard_map/all_gather | solution.py:496
  9.1 242.7 %all-gather.7.cloned.1.call-start = ((), (), s32[]{:S(2)}) async-start(), calls=%async_computation.5 | async-start | bytes 4325376 | tf_op jit(solution)/shard_map/all_gather | solution.py:529
  10.0 88.0 %copy-start.16 = (s32[2048]{0:T(1024)}, s32[2048]{0:T(1024)S(1)}, u32[]{:S(2)}) copy-start(s32[2048]{0:T(1024)S(1)} %convert_reduce_fusion.2) | copy-start | bytes 24580
  15.5 82.6 %copy-start.18 = (f32[1024]{0:T(1024)S(1)}, f32[1024]{0:T(1024)}, u32[]{:S(2)}) copy-start(f32[1024]{0:T(1024)} %param.14) | copy-start | bytes 12292
  15.5 82.6 %copy-start.20 = (f32[1024]{0:T(1024)S(1)}, f32[1024]{0:T(1024)}, u32[]{:S(2)}) copy-start(f32[1024]{0:T(1024)} %param.15) | copy-start | bytes 12292
  91.6 6.5 %copy-start.2 = (bf16[2048,2048]{1,0:T(8,128)(2,1)S(1)}, bf16[2048,2048]{1,0:T(8,128)(2,1)}, u32[]{:S(2)}) copy-start(bf16[2048,2048]{1,0:T(8,128)(2,1)} %all-gather.5.cloned.1.call-done.g_ref) | copy-start | bytes 25165828
  98.1 1.7 copy-start.10
  99.8 3.8 %copy-start.4 = (bf16[2048,1024]{1,0:T(8,128)(2,1)}, bf16[2048,1024]{1,0:T(8,128)(2,1)S(1)}, u32[]{:S(2)}) copy-start(bf16[2048,1024]{1,0:T(8,128)(2,1)S(1)} %fusion.5) | copy-start | bytes 12582916
  107.3 7.3 %copy-start.6 = (bf16[1024,512]{1,0:T(8,128)(2,1)S(1)}, bf16[1024,512]{1,0:T(8,128)(2,1)}, u32[]{:S(2)}) copy-start(bf16[1024,512]{1,0:T(8,128)(2,1)} %param.21) | copy-start | bytes 3145732
  107.3 10.3 %copy-start.3 = (bf16[128,1024]{1,0:T(8,128)(2,1)S(1)}, bf16[128,1024]{1,0:T(8,128)(2,1)}, u32[]{:S(2)}) copy-start(bf16[128,1024]{1,0:T(8,128)(2,1)} %param.13) | copy-start | bytes 786436
  107.3 10.7 %copy-start.19 = (f32[1024]{0:T(1024)S(1)}, f32[1024]{0:T(1024)}, u32[]{:S(2)}) copy-start(f32[1024]{0:T(1024)} %param.16) | copy-start | bytes 12292
  107.3 10.7 %copy-start.21 = (f32[1024]{0:T(1024)S(1)}, f32[1024]{0:T(1024)}, u32[]{:S(2)}) copy-start(f32[1024]{0:T(1024)} %param.17) | copy-start | bytes 12292
  116.0 5.8 %copy-start.12 = (bf16[128,1024]{1,0:T(8,128)(2,1)S(1)}, bf16[128,1024]{1,0:T(8,128)(2,1)}, u32[]{:S(2)}) copy-start(bf16[128,1024]{1,0:T(8,128)(2,1)} %param.24) | copy-start | bytes 786436
  116.0 1.6 collective-permute-start
  127.7 4.8 %copy-start.14 = (bf16[128,1024]{1,0:T(8,128)(2,1)}, bf16[128,1024]{1,0:T(8,128)(2,1)S(1)}, u32[]{:S(2)}) copy-start(bf16[128,1024]{1,0:T(8,128)(2,1)S(1)} %convolution_convert_fusion.5) | copy-start | bytes 786436
  127.7 7.8 %copy-start.7 = (bf16[1024,512]{1,0:T(8,128)(2,1)S(1)}, bf16[1024,512]{1,0:T(8,128)(2,1)}, u32[]{:S(2)}) copy-start(bf16[1024,512]{1,0:T(8,128)(2,1)} %param.21) | copy-start | bytes 3145732
  127.7 4.4 %collective-permute-start.2 = (bf16[128,1024]{1,0:T(8,128)(2,1)S(1)}, bf16[128,1024]{1,0:T(8,128)(2,1)S(1)}, u32[]{:S(2)}, u32[]{:S(2)}) collective-permute-start(bf16[128,1024]{1,0:T(8,128)(2,1)S(1)} %convolution_convert_fusion.5), channel_id=1, source_target_pairs={{0,1},{1,0},{2,3},{3,2},{4,5},{5,4},{6,7},{7,6},{8,9},{9,8},{10,11... | collective-permute-start | bytes 786440 | tf_op jit(solution)/shard_map/ppermute | solution.py:462
  131.8 9.2 %copy-start.13 = (bf16[128,512]{1,0:T(8,128)(2,1)S(1)}, bf16[128,512]{1,0:T(8,128)(2,1)}, u32[]{:S(2)}) copy-start(bf16[128,512]{1,0:T(8,128)(2,1)} %attend.1) | copy-start | bytes 393220
  131.8 1.6 collective-permute-start.1
  135.3 24.0 %copy-start.17 = (s32[2048]{0:T(1024)S(1)}, s32[2048]{0:T(1024)}, u32[]{:S(2)}) copy-start(s32[2048]{0:T(1024)} %copy-done.16) | copy-start | bytes 24580
  136.7 18.3 %all-to-all-start = ((bf16[16,64,128]{2,1,0:T(8,128)(2,1)}), bf16[16,64,128]{2,1,0:T(8,128)(2,1)S(1)}, u32[]{:S(2)}, u32[]{:S(2)}) async-start(bf16[16,64,128]{2,1,0:T(8,128)(2,1)} %bitcast.6), calls=%async_computation | async-start | bytes 524288 | tf_op jit(solution)/shard_map/all_to_all | solution.py:544
  155.0 12.1 %copy-start.15 = (bf16[16,64,128]{2,1,0:T(8,128)(2,1)}, bf16[16,64,128]{2,1,0:T(8,128)(2,1)S(1)}, u32[]{:S(2)}) copy-start(bf16[16,64,128]{2,1,0:T(8,128)(2,1)S(1)} %all-to-all-done.ga_ref) | copy-start | bytes 786436
  155.0 42.4 %all-to-all-start.3 = ((bf16[16,64,512]{2,1,0:T(8,128)(2,1)}), bf16[16,64,512]{2,1,0:T(8,128)(2,1)}, u32[]{:S(2)}, u32[]{:S(2)}) async-start(bf16[16,64,512]{2,1,0:T(8,128)(2,1)} %bitcast.80), calls=%async_computation.3 | async-start | bytes 2097152 | tf_op jit(solution)/shard_map/all_to_all | solution.py:550
  159.3 148.6 %all-gather.9.cloned.1.call-start = ((), (), s32[]{:S(2)}) async-start(), calls=%async_computation.6 | async-start | bytes 4456448 | tf_op jit(solution)/shard_map/all_gather | solution.py:556
  194.9 4.6 %copy-start.5 = (bf16[192,2048]{1,0:T(8,128)(2,1)S(1)}, bf16[192,2048]{1,0:T(8,128)(2,1)}, u32[]{:S(2)}) copy-start(bf16[192,2048]{1,0:T(8,128)(2,1)} %back.1) | copy-start | bytes 2359300
  199.5 18.4 %copy-start.9 = (bf16[1024,512]{1,0:T(8,128)(2,1)S(1)}, bf16[1024,512]{1,0:T(8,128)(2,1)}, u32[]{:S(2)}) copy-start(bf16[1024,512]{1,0:T(8,128)(2,1)} %param.18) | copy-start | bytes 3145732
  199.5 19.4 %copy-start.11 = (bf16[1024,512]{1,0:T(8,128)(2,1)S(1)}, bf16[1024,512]{1,0:T(8,128)(2,1)}, u32[]{:S(2)}) copy-start(bf16[1024,512]{1,0:T(8,128)(2,1)} %param.20) | copy-start | bytes 3145732
  219.4 11.3 %collective-permute-start.3 = (bf16[128,1024]{1,0:T(8,128)(2,1)S(1)}, bf16[128,1024]{1,0:T(8,128)(2,1)S(1)}, u32[]{:S(2)}, u32[]{:S(2)}) collective-permute-start(bf16[128,1024]{1,0:T(8,128)(2,1)S(1)} %fusion.9), channel_id=1, source_target_pairs={{0,1},{1,0},{2,3},{3,2},{4,5},{5,4},{6,7},{7,6},{8,9},{9,8},{10,11... | collective-permute-start | bytes 786440 | tf_op jit(solution)/shard_map/ppermute | solution.py:462
  232.1 18.9 %all-to-all-start.2 = ((f32[16,4,1024]{2,1,0:T(4,128)}), f32[16,4,1024]{2,1,0:T(4,128)S(1)}, u32[]{:S(2)}, u32[]{:S(2)}) async-start(f32[16,4,1024]{2,1,0:T(4,128)} %broadcast_in_dim.17), calls=%async_computation.2 | async-start | bytes 524288 | tf_op jit(solution)/shard_map/all_to_all | solution.py:575
  328.9 9.3 %copy-start.1 = (bf16[1024,512]{1,0:T(8,128)(2,1)S(1)}, bf16[1024,512]{1,0:T(8,128)(2,1)}, u32[]{:S(2)}) copy-start(bf16[1024,512]{1,0:T(8,128)(2,1)} %param.19) | copy-start | bytes 3145732
  331.7 4.9 %copy-start.8 = (bf16[16,64,512]{2,1,0:T(8,128)(2,1)S(1)}, bf16[16,64,512]{2,1,0:T(8,128)(2,1)}, u32[]{:S(2)}) copy-start(bf16[16,64,512]{2,1,0:T(8,128)(2,1)} %get-tuple-element.102) | copy-start | bytes 3145732
Sparse Core Ops, SparseCore 0:
  11.5 80.1 all-gather.4
  119.0 73.2 all-gather.6
  199.6 83.0 all-gather.8

commit v2 on v0

--- a/solution.py
+++ b/solution.py
@@ -1,9 +1,16 @@
 import jax
 import jax.numpy as jnp
 from jax import lax
+from jax.experimental import pallas as pl
+from jax.experimental.pallas import tpu as pltpu
 from jax.sharding import PartitionSpec as P
 
 HEAD = 64
+NEG = -1e30
+f32 = jnp.float32
+bf16 = jnp.bfloat16
+LAST = (((1,), (1,)), ((), ()))
+FIRST = (((0,), (0,)), ((), ()))
 
 
 def from_behind(block, axis, distance):
@@ -25,7 +32,7 @@
     )
 
 
-def body(
+def ring_body(
     tokens,
     first_gain,
     first_bias,
@@ -40,8 +47,6 @@
     cotangent,
     scene_len,
 ):
-    f32 = jnp.float32
-    bf16 = jnp.bfloat16
     count = lax.axis_size("blk")
     place = lax.axis_index("blk")
     rows = tokens.shape[0]
@@ -260,7 +265,588 @@
     )
 
 
+HINT = pl.CostEstimate(flops=1, bytes_accessed=1, transcendentals=1)
+
+
+def full(shape):
+    return pl.BlockSpec(shape, lambda *_: (0,) * len(shape))
+
+
+def attend_kernel(q_ref, k_ref, v_ref, mine_ref, all_ref, out_ref):
+    lane = lax.broadcasted_iota(jnp.int32, q_ref.shape, 1) // HEAD
+    mask = mine_ref[...] == all_ref[...]
+    parts = []
+    for head in range(2):
+        q = jnp.where(lane == head, q_ref[...], jnp.zeros_like(q_ref[...]))
+        s = lax.dot_general(q, k_ref[...], LAST, preferred_element_type=f32)
+        s = jnp.where(mask, s, NEG)
+        p = jnp.exp(s - jnp.max(s, axis=1, keepdims=True))
+        total = jnp.sum(p, axis=1, keepdims=True)
+        part = jnp.dot(p.astype(bf16), v_ref[...], preferred_element_type=f32)
+        parts.append(part / total)
+    out_ref[...] = jnp.where(lane == 0, parts[0], parts[1]).astype(bf16)
+
+
+def attend(q, k, v, scene_mine, scene_all):
+    rows, width = q.shape
+    total = k.shape[0]
+    pair = 2 * HEAD
+    return pl.pallas_call(
+        attend_kernel,
+        grid=(width // pair,),
+        in_specs=[
+            pl.BlockSpec((rows, pair), lambda i: (0, i)),
+            pl.BlockSpec((total, pair), lambda i: (0, i)),
+            pl.BlockSpec((total, pair), lambda i: (0, i)),
+            full((rows, 1)),
+            full((1, total)),
+        ],
+        out_specs=pl.BlockSpec((rows, pair), lambda i: (0, i)),
+        out_shape=jax.ShapeDtypeStruct((rows, width), bf16),
+        cost_estimate=HINT,
+        name="attend",
+    )(q, k, v, scene_mine.reshape(rows, 1), scene_all.reshape(1, total))
+
+
+QT = 256
+KT = 512
+
+
+def prepare_kernel(lo_ref, hi_ref, part_ref, t_ref, n_ref, row_ref, col_ref, p_ref, s_s):
+    step = pl.program_id(0)
+    lo, hi = lo_ref[step], hi_ref[step]
+    blocks = [4 * step + 2 * i + part_ref[0] for i in range(2)]
+    q = jnp.concatenate([t_ref[b, 0:HEAD, :] for b in blocks], axis=1)
+    q = jnp.concatenate([q, jnp.zeros_like(q)], axis=0)
+    row = row_ref[...]
+
+    def score(j, top):
+        keys = pl.ds(pl.multiple_of(j * KT, KT), KT)
+        s = jnp.dot(n_ref[keys, 0 : 2 * HEAD], q, preferred_element_type=f32)
+        s = jnp.where(col_ref[keys, :] == row, s, NEG)
+        s_s[keys, :] = s
+        return jnp.maximum(top, jnp.max(s, axis=0, keepdims=True))
+
+    top = lax.fori_loop(lo, hi, score, jnp.full((1, QT), NEG, f32))
+
+    def weigh(j, total):
+        keys = pl.ds(pl.multiple_of(j * KT, KT), KT)
+        p = jnp.exp(s_s[keys, :] - top)
+        s_s[keys, :] = p
+        return total + jnp.sum(p, axis=0, keepdims=True)
+
+    total = lax.fori_loop(lo, hi, weigh, jnp.zeros((1, QT), f32))
+    share = 1.0 / total
+
+    def store(j, carry):
+        keys = pl.ds(pl.multiple_of(j * KT, KT), KT)
+        p_ref[0, keys, :] = (s_s[keys, :] * share).astype(bf16)
+        return carry
+
+    lax.fori_loop(lo, hi, store, 0)
+
+
+def prepare(bounds, head_t, head_n, scene_queries, scene_all):
+    total = head_n.shape[0]
+    tiles = scene_queries.shape[0] // QT
+    return pl.pallas_call(
+        prepare_kernel,
+        grid_spec=pltpu.PrefetchScalarGridSpec(
+            num_scalar_prefetch=3,
+            grid=(tiles,),
+            in_specs=[
+                full(head_t.shape),
+                full((total, 4 * HEAD)),
+                pl.BlockSpec((1, QT), lambda i, *_: (0, i)),
+                full((total, 1)),
+            ],
+            out_specs=pl.BlockSpec((1, total, QT), lambda i, *_: (i, 0, 0)),
+            scratch_shapes=[pltpu.VMEM((total, QT), f32)],
+        ),
+        out_shape=jax.ShapeDtypeStruct((tiles, total, QT), bf16),
+        cost_estimate=HINT,
+        name="prepare",
+    )(*bounds, head_t, head_n, scene_queries.reshape(1, -1), scene_all.reshape(total, 1))
+
+
+def back_kernel(
+    lo_ref, hi_ref, part_ref, p_ref, ga_ref, t_ref, n_ref, h_ref,
+    gq_out, mine_out, other_out, slice_mine, slice_other, dp_s, gkv_s, g_s,
+):
+    step = pl.program_id(0)
+    part = part_ref[0]
+    rows = ga_ref.shape[2]
+    count = t_ref.shape[0]
+    lo, hi = lo_ref[step], hi_ref[step]
+
+    @pl.when(step == 0)
+    def _():
+        gkv_s[...] = jnp.zeros_like(gkv_s)
+        g_s[...] = jnp.zeros_like(g_s)
+
+    blocks = [4 * step + 2 * i + part for i in range(2)]
+    spans = [pl.ds(pl.multiple_of(b * rows, rows), rows) for b in blocks]
+    ga_t = jnp.concatenate([ga_ref[0], ga_ref[1]], axis=1)
+    ga_t = jnp.concatenate([ga_t, jnp.zeros_like(ga_t)], axis=0)
+    ga = ga_t.T
+    kq = jnp.concatenate([n_ref[span, 0 : 2 * HEAD] for span in spans], axis=0)
+    q = jnp.where(lax.broadcasted_iota(jnp.int32, kq.shape, 1) >= HEAD, kq, jnp.zeros_like(kq))
+
+    def first(j, delta):
+        keys = pl.ds(pl.multiple_of(j * KT, KT), KT)
+        p = p_ref[0, keys, :]
+        dp = jnp.dot(n_ref[keys, 2 * HEAD :], ga_t, preferred_element_type=f32)
+        dp_s[keys, :] = dp
+        gkv_s[keys, :] += jnp.dot(p, ga, preferred_element_type=f32)
+        return delta + jnp.sum(p.astype(f32) * dp, axis=0, keepdims=True)
+
+    delta = lax.fori_loop(lo, hi, first, jnp.zeros((1, QT), f32))
+
+    def second(j, gq):
+        keys = pl.ds(pl.multiple_of(j * KT, KT), KT)
+        ds = (p_ref[0, keys, :].astype(f32) * (dp_s[keys, :] - delta)).astype(bf16)
+        gkv_s[keys, :] += jnp.dot(ds, q, preferred_element_type=f32)
+        near = KT // rows
+        k_t = jnp.concatenate([t_ref[j * near + i, HEAD : 2 * HEAD, :] for i in range(near)], axis=1)
+        return gq + jnp.dot(k_t, ds, preferred_element_type=f32)
+
+    gq = lax.fori_loop(lo, hi, second, jnp.zeros((HEAD, QT), f32))
+    gq = (gq * HEAD ** (-0.5)).astype(bf16)
+    for i in range(2):
+        tile = gq[:, i * rows : (i + 1) * rows]
+        gq_out[2 * step + i] = tile
+        g_s[0:HEAD, spans[i]] = tile
+
+    @pl.when(step == pl.num_programs(0) - 1)
+    def _():
+        for m in range(count // 2):
+            for out, b in ((mine_out, 2 * m + part), (other_out, 2 * m + 1 - part)):
+                tokens = pl.ds(pl.multiple_of(b * rows, rows), rows)
+                both = gkv_s[tokens, :].T
+                out[m] = both.astype(out.dtype)
+                g_s[HEAD:, tokens] = both.astype(bf16)
+        slices = jnp.dot(g_s[...], h_ref[...], preferred_element_type=f32)
+        wide = slice_mine.shape[1]
+        left, right = slices[:, :wide], slices[:, wide:]
+        slice_mine[...] = jnp.where(part == 0, left, right)
+        slice_other[...] = jnp.where(part == 0, right, left).astype(bf16)
+
+
+def back(bounds, p, ga, head_t, head_n, h1):
+    count, three, rows = head_t.shape
+    total, width = h1.shape
+    half = count // 2
+    kept = [
+        ((half, HEAD, rows), bf16),
+        ((half, 2 * HEAD, rows), f32),
+        ((half, 2 * HEAD, rows), bf16),
+        ((three, width // 2), f32),
+        ((three, width // 2), bf16),
+    ]
+    return pl.pallas_call(
+        back_kernel,
+        grid_spec=pltpu.PrefetchScalarGridSpec(
+            num_scalar_prefetch=3,
+            grid=(p.shape[0],),
+            in_specs=[
+                pl.BlockSpec((1, total, QT), lambda i, *_: (i, 0, 0)),
+                pl.BlockSpec((2, HEAD, rows), lambda i, *_: (i, 0, 0)),
+                full(head_t.shape),
+                full((total, 4 * HEAD)),
+                full(h1.shape),
+            ],
+            out_specs=[full(shape) for shape, _ in kept],
+            scratch_shapes=[
+                pltpu.VMEM((total, QT), f32),
+                pltpu.VMEM((total, 2 * HEAD), f32),
+                pltpu.VMEM((three, total), bf16),
+            ],
+        ),
+        out_shape=[jax.ShapeDtypeStruct(shape, kind) for shape, kind in kept],
+        cost_estimate=HINT,
+        name="back",
+    )(*bounds, p, ga, head_t, head_n, h1)
+
+
+FT = 256
+TT = 1024
+
+
+def gelu_both(pre, grad):
+    half = 0.5 * (1.0 + lax.erf(pre * 0.7071067811865476))
+    slope = half + pre * (jnp.exp(-0.5 * pre * pre) * 0.3989422804014327)
+    return (pre * half).astype(bf16), (grad * slope).astype(bf16)
+
+
+def ffn_kernel(h_ref, g_ref, up_ref, down_ref, *outs):
+    up_out, down_out = outs[-2:]
+    for j in range(h_ref.shape[0] // TT):
+        rows = slice(j * TT, (j + 1) * TT)
+        pre = jnp.dot(h_ref[rows, :], up_ref[...], preferred_element_type=f32)
+        grad = jnp.dot(g_ref[rows, :], down_ref[...], preferred_element_type=f32)
+        act, grad_pre = gelu_both(pre, grad)
+        up = lax.dot_general(h_ref[rows, :], grad_pre, FIRST, preferred_element_type=f32)
+        down = lax.dot_general(g_ref[rows, :], act, FIRST, preferred_element_type=f32)
+        if j == 0:
+            up_out[...] = up
+            down_out[...] = down
+        else:
+            up_out[...] += up
+            down_out[...] += down
+
+
+def ffn_grads(h, g, up_weight, down_weight, tiles, held):
+    total, width = h.shape
+    hidden = up_weight.shape[1]
+    first, last = tiles
+    tokens = pl.BlockSpec((total, width), lambda i: (0, 0), pipeline_mode=pl.Buffered(1))
+    units = pl.BlockSpec((width, FT), lambda i: (0, first + i))
+    return pl.pallas_call(
+        ffn_kernel,
+        grid=(last - first,),
+        in_specs=[tokens, tokens, units, units] + [pl.BlockSpec(memory_space=pl.ANY)] * len(held),
+        out_specs=[units] * 2,
+        out_shape=[jax.ShapeDtypeStruct((width, hidden), f32)] * 2,
+        input_output_aliases={4: 0, 5: 1} if held else {},
+        cost_estimate=pl.CostEstimate(
+            flops=8 * total * width * FT * (last - first), bytes_accessed=4 * total * width, transcendentals=0
+        ),
+        name="ffn_grads",
+    )(h, g, up_weight, down_weight, *held)
+
+
+def project_kernel(where_ref, side_ref, mine_ref, other_ref, gain_ref, bias_ref, k_ref, v_ref, t_ref, n_ref, *rest):
+    outs, scratch, sem = rest[-11:-6], rest[-6:-1], rest[-1]
+    h_s, k_s, v_s, t_s, n_s = scratch
+    n, half, width = mine_ref.shape
+    rows = 2 * half
+    copies = []
+
+    def send(i):
+        for b in range(n):
+            copy = pltpu.make_async_copy(scratch[i].at[b], outs[i].at[where_ref[b]], sem.at[i, b])
+            copy.start()
+            copies.append(copy)
+
+    mine, other = mine_ref[...], other_ref[...]
+    first = side_ref[0] == 0
+    block = jnp.concatenate([jnp.where(first, mine, other), jnp.where(first, other, mine)], axis=1)
+    block = block.reshape(n * rows, width).astype(f32)
+    h = layer_norm(block, gain_ref[...], bias_ref[...]).astype(bf16)
+    h_s[...] = h.reshape(n, rows, width)
+    send(0)
+    k_s[...] = jnp.dot(h, k_ref[...], preferred_element_type=f32).astype(bf16).reshape(k_s.shape)
+    send(1)
+    v_s[...] = jnp.dot(h, v_ref[...], preferred_element_type=f32).astype(bf16).reshape(v_s.shape)
+    send(2)
+    across = lax.dot_general(t_ref[...], h, LAST, preferred_element_type=f32).astype(bf16)
+    for b in range(n):
+        t_s[b] = across[:, b * rows : (b + 1) * rows]
+    send(3)
+    n_s[...] = jnp.dot(h, n_ref[...], preferred_element_type=f32).astype(bf16).reshape(n_s.shape)
+    send(4)
+    for copy in copies:
+        copy.wait()
+
+
+def project_blocks(where, side, mine, other, params, count, held):
+    n, half, width = mine.shape
+    _, _, key_weight, value_weight, head_t, head_n = params
+    shapes = [
+        (2 * half, width),
+        (2 * half, key_weight.shape[1]),
+        (2 * half, value_weight.shape[1]),
+        (head_t.shape[0], 2 * half),
+        (2 * half, head_n.shape[1]),
+    ]
+    return pl.pallas_call(
+        project_kernel,
+        grid_spec=pltpu.PrefetchScalarGridSpec(
+            num_scalar_prefetch=2,
+            grid=(1,),
+            in_specs=[full(mine.shape)] * 2
+            + [full(p.shape) for p in params]
+            + [pl.BlockSpec(memory_space=pl.ANY)] * len(held),
+            out_specs=[pl.BlockSpec(memory_space=pl.ANY)] * 5,
+            scratch_shapes=[pltpu.VMEM((n,) + shape, bf16) for shape in shapes]
+            + [pltpu.SemaphoreType.DMA((5, n))],
+        ),
+        out_shape=[jax.ShapeDtypeStruct((count,) + shape, bf16) for shape in shapes],
+        input_output_aliases={10 + i: i for i in range(5)} if held else {},
+        cost_estimate=HINT,
+        name="project_blocks",
+    )(where, side, mine, other, *params, *held)
+
+
+def own_kernel(h_ref, g_ref, up_ref, down_ref, feed_out, grad_out, feed_s, grad_s):
+    step = pl.program_id(0)
+    pre = jnp.dot(h_ref[...], up_ref[...], preferred_element_type=f32)
+    grad = jnp.dot(g_ref[...], down_ref[...], preferred_element_type=f32)
+    act, grad_pre = gelu_both(pre, grad)
+    feed = lax.dot_general(act, down_ref[...], LAST, preferred_element_type=f32)
+    back_ = lax.dot_general(grad_pre, up_ref[...], LAST, preferred_element_type=f32)
+
+    @pl.when(step == 0)
+    def _():
+        feed_s[...] = feed
+        grad_s[...] = back_
+
+    @pl.when(step > 0)
+    def _():
+        feed_s[...] += feed
+        grad_s[...] += back_
+
+    @pl.when(step == pl.num_programs(0) - 1)
+    def _():
+        feed_out[...] = feed_s[...].astype(bf16)
+        grad_out[...] = grad_s[...].astype(bf16)
+
+
+def own_ffn(h, g, up_weight, down_weight):
+    rows, width = h.shape
+    hidden = up_weight.shape[1]
+    tile = 512
+    return pl.pallas_call(
+        own_kernel,
+        grid=(hidden // tile,),
+        in_specs=[full(h.shape), full(g.shape)] + [pl.BlockSpec((width, tile), lambda i: (0, i))] * 2,
+        out_specs=[full(h.shape)] * 2,
+        out_shape=[jax.ShapeDtypeStruct(h.shape, bf16)] * 2,
+        scratch_shapes=[pltpu.VMEM(h.shape, f32)] * 2,
+        cost_estimate=HINT,
+        name="own_ffn",
+    )(h, g, up_weight, down_weight)
+
+
+def finish_heads_kernel(at_ref, *refs):
+    heads, outs = refs[:4], refs[4:]
+    plane, row, part = at_ref[0], at_ref[1], at_ref[2]
+    wide = heads[0].shape[2]
+    for s in range(4):
+        z = lax.rem(plane - s + 4, 4)
+        for k, x in ((0, part), (1, 1 - part)):
+            rows = pl.ds(pl.multiple_of(x * wide, wide), wide)
+            lanes = pl.ds(pl.multiple_of(z * 2 * HEAD, 2 * HEAD), 2 * HEAD)
+            for i in range(3):
+                near = heads[k][s, i * HEAD : (i + 1) * HEAD, :]
+                far = heads[k + 2][s, i * HEAD : (i + 1) * HEAD, :]
+                pair = [jnp.where(row == 0, near, far), jnp.where(row == 0, far, near)]
+                outs[i][rows, lanes] = jnp.concatenate(pair, axis=0).astype(f32).T
+
+
+def finish_rows_kernel(at_ref, *refs):
+    pieces, out_ref = refs[:4], refs[4]
+    slots = pieces[0].shape[1]
+    for k in range(4):
+        for s in range(4):
+            z = lax.rem(at_ref[0] - s + 4, 4)
+            y = at_ref[1] if k < 2 else 1 - at_ref[1]
+            x = at_ref[2] if k % 2 == 0 else 1 - at_ref[2]
+            at = pl.multiple_of((z * 4 + y * 2 + x) * slots, slots)
+            out_ref[pl.ds(at, slots), :] = pieces[k][s].astype(f32)
+
+
+def finish(kernel, at, pieces, outs, width, columns):
+    return pl.pallas_call(
+        kernel,
+        grid_spec=pltpu.PrefetchScalarGridSpec(
+            num_scalar_prefetch=1,
+            grid=(1,),
+            in_specs=[full(p.shape) for p in pieces],
+            out_specs=[full((width, columns))] * outs,
+        ),
+        out_shape=[jax.ShapeDtypeStruct((width, columns), f32)] * outs,
+        cost_estimate=HINT,
+        name="finish",
+    )(at, *pieces)
+
+
+def shuffle(block, target):
+    return lax.ppermute(block, "blk", [(i, target(i)) for i in range(16)])
+
+
+def over_core(block):
+    return lax.ppermute(block, "tp", [(0, 1), (1, 0)])
+
+
+def gather_column(unit):
+    return jnp.stack([unit] + [shuffle(unit, lambda i, s=s: (i + 4 * s) % 16) for s in (1, 2, 3)])
+
+
+def gather_plane(column):
+    return (column,) + tuple(shuffle(column, lambda i, k=k: i ^ k) for k in (1, 2, 3))
+
+
+def units_at(place):
+    z, flat = place // 4, place % 4
+    return [jnp.stack([((z - s) % 4) * 4 + (flat ^ k) for s in range(4)]) for k in range(4)]
+
+
+def after(value, *first):
+    return lax.optimization_barrier((value,) + first)[0]
+
+
+def both_halves(low):
+    low = lax.optimization_barrier(low)
+    return low.astype(f32) + over_core(low).astype(f32)
+
+
+def fast_body(
+    tokens,
+    first_gain,
+    first_bias,
+    second_gain,
+    second_bias,
+    query_weight,
+    key_weight,
+    value_weight,
+    output_weight,
+    up_weight,
+    down_weight,
+    cotangent,
+    scene_len,
+):
+    count = lax.axis_size("blk")
+    place = lax.axis_index("blk")
+    side = lax.axis_index("tp")
+    rows, width = tokens.shape
+    total = rows * count
+    heads_here = query_weight.shape[1] // HEAD
+    share = count // heads_here
+    scale = HEAD ** (-0.5)
+    head_at = (place // share) * HEAD
+    part = place % share
+
+    def half_of(block):
+        return lax.dynamic_slice_in_dim(block, side * (rows // 2), rows // 2, 0)
+
+    ends = jnp.cumsum(scene_len)
+    starts = ends - scene_len
+    positions = jnp.arange(total, dtype=jnp.int32)
+    scene_all = jnp.sum((positions[:, None] >= ends[None, :]).astype(jnp.int32), axis=1)
+    scene_mine = lax.dynamic_slice_in_dim(scene_all, place * rows, rows)
+    scene_queries = lax.dynamic_index_in_dim(scene_all.reshape(-1, share, rows), part, 1, False).reshape(-1)
+    firsts = jnp.arange(total // QT // share, dtype=jnp.int32) * QT * share + part * rows
+    lasts = firsts + QT * share - rows
+    lowest = jnp.max(jnp.where(starts[None, :] <= firsts[:, None], starts[None, :], 0), axis=1)
+    highest = jnp.min(jnp.where(ends[None, :] >= lasts[:, None], ends[None, :], total), axis=1)
+    bounds = (lowest // KT, (highest + KT - 1) // KT, part.reshape(1))
+
+    def head_of(weight):
+        return lax.dynamic_slice_in_dim(weight, head_at, HEAD, 1)
+
+    head_query = head_of(query_weight) * jnp.asarray(scale, bf16)
+    head_key, head_value = head_of(key_weight), head_of(value_weight)
+    head_t = jnp.concatenate([head_query, head_key, head_value], axis=1).T
+    head_n = jnp.concatenate([head_key, head_query, head_value, jnp.zeros_like(head_value)], axis=1)
+    params = (first_gain.reshape(1, -1), first_bias.reshape(1, -1), key_weight, value_weight, head_t, head_n)
+
+    inputs = tokens.astype(f32)
+    h1_mine = layer_norm(inputs, first_gain, first_bias).astype(bf16)
+    query = jnp.dot(h1_mine, query_weight, preferred_element_type=f32).astype(bf16) * jnp.asarray(scale, bf16)
+
+    g_all = lax.all_gather(half_of(cotangent), ("blk", "tp"), axis=0, tiled=True)
+    where = units_at(place)
+    column = gather_column(half_of(tokens))
+    across_x = shuffle(column, lambda i: i ^ 1)
+    across_y = shuffle(column, lambda i: i ^ 2)
+    made = project_blocks(where[0], side.reshape(1), column, over_core(column), params, count, ())
+    across_y = after(across_y, made[0])
+    diagonal = shuffle(across_y, lambda i: i ^ 1)
+    for piece, at in zip((after(across_x, across_y), across_y, diagonal), where[1:], strict=True):
+        piece = after(piece, made[0]) if piece is diagonal else piece
+        made = project_blocks(at, side.reshape(1), piece, over_core(piece), params, count, made)
+    h1_all, keys, values, head_t, head_n = made
+    h1_all = h1_all.reshape(total, width)
+    head_n = head_n.reshape(total, -1)
+
+    attended = attend(query, keys.reshape(total, -1), values.reshape(total, -1), scene_mine, scene_all)
+    branch = lax.dot_general(attended, output_weight, LAST, preferred_element_type=f32)
+    middle = inputs + both_halves(branch.astype(bf16))
+    h2 = layer_norm(middle, second_gain, second_bias).astype(bf16)
+    h2_all = lax.all_gather(after(half_of(h2), g_all), ("blk", "tp"), axis=0, tiled=True)
+
+    feed, grad_two = own_ffn(h2, cotangent, up_weight, down_weight)
+    grad_two = both_halves(grad_two)
+    _, second_pull = jax.vjp(layer_norm, middle, second_gain, second_bias)
+    grad_middle, second_gain_grad, second_bias_grad = second_pull(grad_two)
+    grad_middle = cotangent.astype(f32) + grad_middle
+    grad_middle_low = grad_middle.astype(bf16)
+    grad_attended = lax.dot_general(
+        output_weight, grad_middle_low, (((0,), (1,)), ((), ())), preferred_element_type=f32
+    ).astype(bf16)
+    alike = [list(range(r, count, share)) for r in range(share)]
+    to_heads = grad_attended.reshape(heads_here, HEAD, rows)
+    ga = lax.all_to_all(to_heads, "blk", 0, 0, tiled=True, axis_index_groups=alike)
+    p = prepare(bounds, after(head_t, to_heads), head_n, scene_queries, scene_all)
+
+    grad_q, kept, given, slice_kept, slice_given = back(
+        bounds, p, ga, head_t, head_n, h1_all
+    )
+    output_part = lax.dot_general(after(grad_middle_low, slice_given), attended, FIRST, preferred_element_type=f32)
+    output_part = output_part.reshape(count // share, share, width // count, -1)
+    output_kept = lax.dynamic_index_in_dim(output_part, part, 1, False)
+    output_given = lax.dynamic_index_in_dim(output_part, 1 - part, 1, False).astype(bf16)
+    output_half = (output_kept + shuffle(output_given, lambda i: i ^ 1).astype(f32)).astype(bf16)
+
+    head_slice = (slice_kept + shuffle(slice_given, lambda i: i ^ 1).astype(f32)).astype(bf16)
+    column = gather_column(head_slice)
+
+    given = after(given, head_slice)
+    kept = (kept + shuffle(given, lambda i: i ^ 1).astype(f32)).astype(bf16)
+    parcel = jnp.concatenate([grad_q, kept, output_half.reshape(count // share, -1, rows)], axis=1)
+    home = lax.all_to_all(after(parcel, column), "blk", 0, 0, tiled=True, axis_index_groups=alike)
+    heads = gather_plane(column)
+
+    layer_out = (middle + both_halves(after(feed, parcel))).astype(bf16)
+    at = jnp.stack([place // 4, (place // 2) % 2, place % 2])
+    held = ffn_grads(after(h2_all, column, parcel), g_all, up_weight, down_weight, (0, 4), ())
+
+    home = after(home, held[0], *heads)
+    output_slice = home[:, 3 * HEAD :].reshape(count // share, width // count, -1)
+    output_slice = jnp.sum(output_slice.astype(f32), axis=0).astype(bf16)
+    home = home[:, : 3 * HEAD].reshape(heads_here, 3, HEAD, rows)
+    grad_one = 0.0
+    for i, weight in enumerate((query_weight, value_weight, key_weight)):
+        grad_one = grad_one + lax.dot_general(
+            home[:, i].reshape(-1, rows), weight, (((0,), (1,)), ((), ())), preferred_element_type=f32
+        )
+    grad_one = both_halves(grad_one.astype(bf16))
+    _, first_pull = jax.vjp(layer_norm, inputs, first_gain, first_bias)
+    grad_input, first_gain_grad, first_bias_grad = first_pull(grad_one)
+    input_grad = grad_middle + grad_input
+    norm_part = jnp.stack([first_gain_grad, first_bias_grad, second_gain_grad, second_bias_grad])
+    norm_parts = lax.all_to_all(
+        jnp.broadcast_to(norm_part[None], (count,) + norm_part.shape), "blk", 0, 0, tiled=True
+    )
+
+    column = gather_column(output_slice)
+    up_grad, down_grad = ffn_grads(
+        after(h2_all, norm_part, *heads), g_all, up_weight, down_weight, (4, 8), held
+    )
+    rest = gather_plane(after(column, up_grad))
+    norm_sums = jnp.sum(after(norm_parts, up_grad), axis=0)
+    heads = (after(heads[0], up_grad),) + heads[1:]
+    query_grad, value_grad, key_grad = finish(finish_heads_kernel, at, heads, 3, width, heads_here * HEAD)
+    (output_grad,) = finish(finish_rows_kernel, at, rest, 1, width, heads_here * HEAD)
+    return (
+        layer_out,
+        input_grad,
+        norm_sums[0],
+        norm_sums[1],
+        norm_sums[2],
+        norm_sums[3],
+        query_grad,
+        key_grad,
+        value_grad,
+        output_grad,
+        up_grad,
+        down_grad,
+    )
+
+
 def solution(mesh):
+    body = fast_body if mesh.shape["blk"] == 16 else ring_body
     return jax.shard_map(
         body,
         mesh=mesh,

time: 1690 us -> 277 us (0.16)
  waiting for transfers between devices: 1260 us -> 50.3 us
  Pallas kernels: 0 us -> 117 us
  loops' own time: 80.1 us -> 0 us
  other arithmetic: 76.1 us -> 19.2 us
  starting transfers between devices: 102 us -> 48.4 us
  local copies, waits for them, and re-layouts: 70.4 us -> 19.1 us
  matrix products: 47.2 us -> 5.92 us
  blocking collectives: 36.2 us -> 0 us
    reduce_scatter x6 -> x0, waiting for transfers between devices: 666 us -> none  [the longest x1 181 us: body(): lax.psum_scatter(up_grad, 'blk', scatter_dimension=0, tiled=True)]
    all_gather x6 -> x2, waiting for transfers between devices: 326 us -> 0.02 us  [the longest x1 0.02 us: fast_body(): lax.all_gather(after(half_of(h2), g_all), ('blk', 'tp'), axis=0, tiled=True)]
    pallas_call x0 -> x12, Pallas kernels: none -> 117 us  [the longest x2 48.1 us: ffn_grads(): pl.pallas_call(ffn_kernel, grid=(last - first,), in_specs=[tokens, tokens...]
    ppermute x92 -> x29, waiting for transfers between devices: 159 us -> 48 us  [the longest x21 44.6 us: shuffle(): return lax.ppermute(block, 'blk', [(i, target(i)) for i in range(16)])]
    another operation x32 -> x0, loops' own time: 80.1 us -> none  [the longest x1 40.1 us: body(): lax.fori_loop(1, steps + 1, turn_backward, (grad_query, keys, values, emp...]
    unnamed x17 -> x2, waiting for transfers between devices: 78.4 us -> 0.03 us
    ppermute x92 -> x29, starting transfers between devices: 101 us -> 31.7 us  [the longest x21 30.4 us: shuffle(): return lax.ppermute(block, 'blk', [(i, target(i)) for i in range(16)])]
    dot_general x38 -> x7, matrix products: 47.2 us -> 5.92 us  [the longest x3 2.74 us: fast_body(): lax.dot_general(home[:, i].reshape(-1, rows), weight, (((0,), (1,)), ((),...]
  transfers between devices with their start and end apart: 108 -> 34, of which waited for: 84 -> 13; matrix products, arithmetic and copies ran while one was open for 8% -> 13% of each run, Pallas kernels for 0% -> 34%
where the time goes in v2:
time: 277 us; the launch traced here: 275 us
  Pallas kernels  117 us (42%)
  waiting for transfers between devices  50.3 us (18%)
  starting transfers between devices  48.4 us (17%)
  other arithmetic  19.2 us (7%)
  local copies, waits for them, and re-layouts  19.1 us (7%)
  between operations  14.8 us (5%)
  matrix products  5.92 us (2%)
    pallas_call x2, Pallas kernels, ffn_grads(): pl.pallas_call(ffn_kernel, grid=(last - first,), in_specs=[tokens, tokens...  48.1 us
    ppermute x21, waiting for transfers between devices, shuffle(): return lax.ppermute(block, 'blk', [(i, target(i)) for i in range(16)])  44.6 us
    ppermute x21, starting transfers between devices, shuffle(): return lax.ppermute(block, 'blk', [(i, target(i)) for i in range(16)])  30.4 us
    pallas_call x4, Pallas kernels, project_blocks(): pl.pallas_call(project_kernel, grid_spec=pltpu.PrefetchScalarGridSpec(num...  24.6 us
    pallas_call x1, Pallas kernels, back(): pl.pallas_call(back_kernel, grid_spec=pltpu.PrefetchScalarGridSpec(num_sc...  12.6 us
    pallas_call x2, Pallas kernels, finish(): pl.pallas_call(kernel, grid_spec=pltpu.PrefetchScalarGridSpec(num_scalar_...  9.42 us
    all_to_all x1, starting transfers between devices, fast_body(): lax.all_to_all(to_heads, 'blk', 0, 0, tiled=True, axis_index_groups=alike)  8.62 us
    pallas_call x1, Pallas kernels, own_ffn(): pl.pallas_call(own_kernel, grid=(hidden // tile,), in_specs=[full(h.shape...  7.82 us
  transfers between devices with their start and end apart: 34, of which 13 were waited for; matrix products, arithmetic and copies ran while one was open for 13% of the time, Pallas kernels for 34%

profile of v2, /device:TPU:0, one launch (start us, length us, event | category | flops | bytes accessed | tf_op | source)
XLA Modules:
  0.0 275.1 jit_solution(17132640364849207389)
XLA Ops:
  7.2 1.7 constant_dynamic-slice_fusion
  9.0 1.0 constant_dynamic-slice_fusion.4
  9.9 4.1 %collective-permute-start.1 = (bf16[64,1024]{1,0:T(8,128)(2,1)S(1)}, bf16[64,1024]{1,0:T(8,128)(2,1)S(1)}, u32[]{:S(2)}, u32[]{:S(2)}) collective-permute-start(bf16[64,1024]{1,0:T(8,128)(2,1)S(1)} %constant_dynamic-slice_fusion.4), channel_id=1, source_target_pairs={{0,16},{2,18},{4,20},{6,22},{8,24},{10,26},{12,28},{14,30},{16,0},... | collective-permute-start | bytes 393224 | tf_op jit(solution)/shard_map/ppermute | solution.py:665
  14.0 1.6 collective-permute-start
  15.6 2.2 collective-permute-start.2
  17.9 0.8 reduce-window.8
  18.7 1.1 constant_dynamic-slice_fusion.3
  19.8 1.3 dynamic-slice_multiply_fusion
  21.5 0.9 copy.55.t_ref
  22.5 1.5 collective-permute-done.1
  24.8 1.6 collective-permute-start.7
  26.4 1.5 collective-permute-start.3
  29.3 1.1 maximum_maximum_fusion.n_ref
  30.4 0.8 copy-done.18
  31.2 6.1 %project_blocks.4 = (bf16[16,128,1024]{2,1,0:T(8,128)(2,1)}, bf16[16,128,512]{2,1,0:T(8,128)(2,1)}, bf16[16,128,512]{2,1,0:T(8,128)(2,1)}, bf16[16,192,128]{2,1,0:T(8,128)(2,1)}, bf16[16,128,256]{2,1,0:T(8,128)(2,1)}) custom-call(s32[4]{0:T(128)} %pad_add_fusion.1.where_ref, s32[1]{0:T(128)} %bitcast.4.side_ref, bf16[4,64,1024]{2,1,0:T(8,128)(2,1)} %copy-done.8, ...), custom_call_target="tpu_custom_call" | custom-call | flops 1 | bytes 1 | tf_op jit(solution)/shard_map/project_blocks/pallas_call | solution.py:562
  37.3 3.8 %collective-permute-done.3.mine_ref = bf16[4,64,1024]{2,1,0:T(8,128)(2,1)S(1)} collective-permute-done((bf16[4,64,1024]{2,1,0:T(8,128)(2,1)S(1)}, bf16[4,64,1024]{2,1,0:T(8,128)(2,1)S(1)}, u32[]{:S(2)}, u32[]{:S(2)}) %collective-permute-start.3) | collective-permute-done | bytes 524320 | tf_op jit(solution)/shard_map/ppermute | solution.py:665
  42.6 1.4 collective-permute-done.8.other_ref
  43.9 0.8 copy-done.17
  44.7 6.1 %project_blocks.5 = (bf16[16,128,1024]{2,1,0:T(8,128)(2,1)}, bf16[16,128,512]{2,1,0:T(8,128)(2,1)}, bf16[16,128,512]{2,1,0:T(8,128)(2,1)}, bf16[16,192,128]{2,1,0:T(8,128)(2,1)}, bf16[16,128,256]{2,1,0:T(8,128)(2,1)}) custom-call(s32[4]{0:T(128)} %pad_add_fusion.3.where_ref, ...), custom_call_target="tpu_custom_call", output_to_operand_aliasing={{0}: (10, {}), {1}: (11, {}), {2}: (12, {}), {3}: (13, {}),... | custom-call | flops 1 | bytes 1 | tf_op jit(solution)/shard_map/project_blocks/pallas_call | solution.py:562
  50.9 0.8 copy-done.16
  51.7 6.2 %project_blocks.6 = (bf16[16,128,1024]{2,1,0:T(8,128)(2,1)}, bf16[16,128,512]{2,1,0:T(8,128)(2,1)}, bf16[16,128,512]{2,1,0:T(8,128)(2,1)}, bf16[16,192,128]{2,1,0:T(8,128)(2,1)}, bf16[16,128,256]{2,1,0:T(8,128)(2,1)}) custom-call(s32[4]{0:T(128)} %pad_add_fusion.2.where_ref, ...), custom_call_target="tpu_custom_call", output_to_operand_aliasing={{0}: (10, {}), {1}: (11, {}), {2}: (12, {}), {3}: (13, {}),... | custom-call | flops 1 | bytes 1 | tf_op jit(solution)/shard_map/project_blocks/pallas_call | solution.py:562
  59.6 1.0 fusion.2.q_ref
  60.7 0.8 copy-done.19
  61.5 6.2 %project_blocks.7 = (bf16[16,128,1024]{2,1,0:T(8,128)(2,1)}, bf16[16,128,512]{2,1,0:T(8,128)(2,1)}, bf16[16,128,512]{2,1,0:T(8,128)(2,1)}, bf16[16,192,128]{2,1,0:T(8,128)(2,1)}, bf16[16,128,256]{2,1,0:T(8,128)(2,1)}) custom-call(s32[4]{0:T(128)} %pad_add_fusion.where_ref, ...), custom_call_target="tpu_custom_call", output_to_operand_aliasing={{0}: (10, {}), {1}: (11, {}), {2}: (12, {}), {3}: (13, {}),... | custom-call | flops 1 | bytes 1 | tf_op jit(solution)/shard_map/project_blocks/pallas_call | solution.py:562
  67.7 7.4 %attend.1 = bf16[128,512]{1,0:T(8,128)(2,1)} custom-call(bf16[128,512]{1,0:T(8,128)(2,1)} %fusion.2.q_ref, bf16[2048,512]{1,0:T(8,128)(2,1)} %bitcast.86, bf16[2048,512]{1,0:T(8,128)(2,1)} %bitcast.87, s32[128,1]{1,0:T(8,128)} %copy.59.mine_ref, s32[1,2048]{1,0:T(1,128)} %bitcast.106), custom_call_target="tpu_custom_call" | custom-call | flops 1 | bytes 1 | tf_op jit(solution)/shard_map/attend/pallas_call | solution.py:294
  75.1 1.4 convolution_convert_fusion
  76.9 1.2 collective-permute-done.10
  79.7 7.8 %own_ffn.1 = (bf16[128,1024]{1,0:T(8,128)(2,1)}, bf16[128,1024]{1,0:T(8,128)(2,1)}) custom-call(bf16[128,1024]{1,0:T(8,128)(2,1)} %copy-done.9, bf16[128,1024]{1,0:T(8,128)(2,1)} %g_ref.1, bf16[1024,2048]{1,0:T(8,128)(2,1)} %up_ref.5, bf16[1024,2048]{1,0:T(8,128)(2,1)} %down_ref.5), custom_call_target="tpu_custom_call" | custom-call | flops 1 | bytes 1 | tf_op jit(solution)/shard_map/own_ffn/pallas_call | solution.py:609
  89.2 1.2 multiply_reduce_fusion
  90.5 1.2 fusion.27
  93.6 8.6 %all-to-all-start = ((bf16[8,64,128]{2,1,0:T(8,128)(2,1)}), bf16[8,64,128]{2,1,0:T(8,128)(2,1)S(1)}, u32[]{:S(2)}, u32[]{:S(2)}) async-start(bf16[8,64,128]{2,1,0:T(8,128)(2,1)} %bitcast.32), calls=%async_computation | async-start | bytes 262144 | tf_op jit(solution)/shard_map/all_to_all | solution.py:780
  102.8 1.3 copy.61.col_ref
  104.7 7.3 %prepare.1.p_ref = bf16[4,2048,256]{2,1,0:T(8,128)(2,1)} custom-call(s32[4]{0:T(128)} %and_select_fusion.1.lo_ref, s32[4]{0:T(128)} %and_select_fusion.hi_ref, s32[1]{0:T(128)} %bitcast.30.part_ref, bf16[16,192,128]{2,1,0:T(8,128)(2,1)} %get-tuple-element.84.t_ref, bf16[2048,256]{1,0:T(8,128)(2,1)} %bitcast.88, s32[1,1024]{1,0:T(1,128)} %dynamic-slice_bitcast_fusion.row_ref, ...), custom_call_target="tpu_custom_call" | custom-call | flops 1 | bytes 1 | tf_op jit(solution)/shard_map/prepare/pallas_call | solution.py:352
  112.6 12.6 %back.1 = (bf16[8,64,128]{2,1,0:T(8,128)(2,1)}, f32[8,128,128]{2,1,0:T(8,128)}, bf16[8,128,128]{2,1,0:T(8,128)(2,1)}, f32[192,512]{1,0:T(8,128)}, bf16[192,512]{1,0:T(8,128)(2,1)}) custom-call(s32[4]{0:T(128)} %and_select_fusion.1.lo_ref, s32[4]{0:T(128)} %and_select_fusion.hi_ref, s32[1]{0:T(128)} %bitcast.30.part_ref, bf16[4,2048,256]{2,1,0:T(8,128)(2,1)} %prepare.1.p_ref, ...), custom_call_target="tpu_custom_call" | custom-call | flops 1 | bytes 1 | tf_op jit(solution)/shard_map/back/pallas_call | solution.py:446
  126.4 10.1 %collective-permute-done.12 = bf16[192,512]{1,0:T(8,128)(2,1)S(1)} collective-permute-done((bf16[192,512]{1,0:T(8,128)(2,1)}, bf16[192,512]{1,0:T(8,128)(2,1)S(1)}, u32[]{:S(2)}, u32[]{:S(2)}) %collective-permute-start.12) | collective-permute-done | bytes 196640 | tf_op jit(solution)/shard_map/ppermute | solution.py:665
  136.6 3.7 %collective-permute-start.18 = (bf16[192,512]{1,0:T(8,128)(2,1)S(1)}, bf16[192,512]{1,0:T(8,128)(2,1)S(1)}, u32[]{:S(2)}, u32[]{:S(2)}) collective-permute-start(bf16[192,512]{1,0:T(8,128)(2,1)S(1)} %add_convert_fusion.3), channel_id=1, source_target_pairs={{0,24},{2,26},{4,28},{6,30},{8,0},{10,2},{12,4},{14,6},{16,8},{18,... | collective-permute-start | bytes 589832 | tf_op jit(solution)/shard_map/ppermute | solution.py:665
  140.2 1.1 collective-permute-start.16
  141.3 0.9 fusion.15
  142.9 1.3 collective-permute-start.13
  144.8 4.1 %collective-permute-done.18 = bf16[192,512]{1,0:T(8,128)(2,1)S(1)} collective-permute-done((bf16[192,512]{1,0:T(8,128)(2,1)S(1)}, bf16[192,512]{1,0:T(8,128)(2,1)S(1)}, u32[]{:S(2)}, u32[]{:S(2)}) %collective-permute-start.18) | collective-permute-done | bytes 196640 | tf_op jit(solution)/shard_map/ppermute | solution.py:665
  148.9 12.7 %collective-permute-done.17 = bf16[192,512]{1,0:T(8,128)(2,1)S(1)} collective-permute-done((bf16[192,512]{1,0:T(8,128)(2,1)S(1)}, bf16[192,512]{1,0:T(8,128)(2,1)S(1)}, u32[]{:S(2)}, u32[]{:S(2)}) %collective-permute-start.17) | collective-permute-done | bytes 196640 | tf_op jit(solution)/shard_map/ppermute | solution.py:665
  161.6 1.9 pad_maximum_fusion.1.refs_0_
  163.5 1.5 collective-permute-start.21
  165.6 1.4 collective-permute-start.19
  167.9 1.0 pad_maximum_fusion
  168.9 3.9 %all-to-all-start.1 = ((bf16[8,448,128]{2,1,0:T(8,128)(2,1)}), bf16[8,448,128]{2,1,0:T(8,128)(2,1)S(1)}, u32[]{:S(2)}, u32[]{:S(2)}) async-start(bf16[8,448,128]{2,1,0:T(8,128)(2,1)} %pad_maximum_fusion), calls=%async_computation.1 | async-start | bytes 1835008 | tf_op jit(solution)/shard_map/all_to_all | solution.py:798
  172.9 24.0 %ffn_grads.2 = (f32[1024,2048]{1,0:T(8,128)}, f32[1024,2048]{1,0:T(8,128)}) custom-call(bf16[2048,1024]{1,0:T(8,128)(2,1)} %all-gather.5.cloned.1.call-done.h_ref, bf16[2048,1024]{1,0:T(8,128)(2,1)} %all-gather.3.cloned.1.call-done.g_ref, bf16[1024,2048]{1,0:T(8,128)(2,1)} %up_ref.5, bf16[1024,2048]{1,0:T(8,128)(2,1)} %down_ref.5), custom_call_target="tpu_custom_call" | custom-call | flops 17179869184 | bytes 8388608 | tf_op jit(solution)/shard_map/ffn_grads/pallas_call | solution.py:504
  197.0 10.2 %collective-permute-done.20.refs_2_ = bf16[4,192,512]{2,1,0:T(8,128)(2,1)} collective-permute-done((bf16[4,192,512]{2,1,0:T(8,128)(2,1)}, bf16[4,192,512]{2,1,0:T(8,128)(2,1)}, u32[]{:S(2)}, u32[]{:S(2)}) %collective-permute-start.20) | collective-permute-done | bytes 786464 | tf_op jit(solution)/shard_map/ppermute | solution.py:665
  207.2 2.3 all-to-all-done.1
  210.1 0.8 slice.27
  210.9 0.9 reduce_sum.167
  211.8 2.6 collective-permute-start.24
  214.4 1.9 collective-permute-start.23
  216.4 1.1 fusion.29
  217.5 1.8 fusion.32
  220.4 1.8 add_convert_fusion
  223.0 24.0 %ffn_grads.3 = (f32[1024,2048]{1,0:T(8,128)}, f32[1024,2048]{1,0:T(8,128)}) custom-call(bf16[2048,1024]{1,0:T(8,128)(2,1)} %all-gather.5.cloned.1.call-done.h_ref, bf16[2048,1024]{1,0:T(8,128)(2,1)} %all-gather.3.cloned.1.call-done.g_ref, bf16[1024,2048]{1,0:T(8,128)(2,1)} %up_ref.5, ...), custom_call_target="tpu_custom_call", output_to_operand_aliasing={{0}: (4, {}), {1}: (5, {})} | custom-call | flops 17179869184 | bytes 8388608 | tf_op jit(solution)/shard_map/ffn_grads/pallas_call | solution.py:504
  247.1 1.4 collective-permute-start.28
  249.2 1.4 collective-permute-start.26
  251.3 4.1 %all-to-all-start.2 = ((f32[16,4,1024]{2,1,0:T(4,128)}), f32[16,4,1024]{2,1,0:T(4,128)S(1)}, u32[]{:S(2)}, u32[]{:S(2)}) async-start(f32[16,4,1024]{2,1,0:T(4,128)} %broadcast_in_dim.72), calls=%async_computation.2 | async-start | bytes 524288 | tf_op jit(solution)/shard_map/all_to_all | solution.py:819
  255.5 6.1 %finish.2 = (f32[1024,512]{1,0:T(8,128)}, f32[1024,512]{1,0:T(8,128)}, f32[1024,512]{1,0:T(8,128)}) custom-call(s32[3]{0:T(128)} %pad_add_fusion.4.at_ref, bf16[4,192,512]{2,1,0:T(8,128)(2,1)} %pad_maximum_fusion.1.refs_0_, bf16[4,192,512]{2,1,0:T(8,128)(2,1)} %collective-permute-done.19.refs_1_, bf16[4,192,512]{2,1,0:T(8,128)(2,1)} %collective-permute-done.20.refs_2_, ...), custom_call_target="tpu_custom_call" | custom-call | flops 1 | bytes 1 | tf_op jit(solution)/shard_map/finish/pallas_call | solution.py:650
  261.6 1.1 add_add_fusion.2
  262.7 1.5 collective-permute-done.27.refs_2_
  264.2 3.3 %finish.3 = f32[1024,512]{1,0:T(8,128)} custom-call(s32[3]{0:T(128)} %pad_add_fusion.4.at_ref, bf16[4,64,512]{2,1,0:T(8,128)(2,1)} %copy-done.12, bf16[4,64,512]{2,1,0:T(8,128)(2,1)} %collective-permute-done.26.refs_1_, bf16[4,64,512]{2,1,0:T(8,128)(2,1)} %collective-permute-done.27.refs_2_, bf16[4,64,512]{2,1,0:T(8,128)(2,1)} %copy-done.22), custom_call_target="tpu_custom_call" | custom-call | flops 1 | bytes 1 | tf_op jit(solution)/shard_map/finish/pallas_call | solution.py:650
  (164 shorter events, 21.9 us)
Async XLA Ops:
  7.2 67.9 %copy-start = (bf16[1024,512]{1,0:T(8,128)(2,1)S(1)}, bf16[1024,512]{1,0:T(8,128)(2,1)}, u32[]{:S(2)}) copy-start(bf16[1024,512]{1,0:T(8,128)(2,1)} %param.21) | copy-start | bytes 3145732
  7.2 72.2 %all-gather.3.cloned.1.call-start = ((), (), s32[]{:S(2)}) async-start(), calls=%async_computation.3 | async-start | bytes 4325376 | tf_op jit(solution)/shard_map/all_gather | solution.py:748
  8.9 13.6 %copy-start.4 = (bf16[128,1024]{1,0:T(8,128)(2,1)S(1)}, bf16[128,1024]{1,0:T(8,128)(2,1)}, u32[]{:S(2)}) copy-start(bf16[128,1024]{1,0:T(8,128)(2,1)} %param.13) | copy-start | bytes 786436
  8.9 164.0 %all-gather.5.cloned.1.call-start = ((), (), s32[]{:S(2)}) async-start(), calls=%async_computation.4 | async-start | bytes 4325376 | tf_op jit(solution)/shard_map/all_gather | solution.py:767
  9.9 14.1 %collective-permute-start.1 = (bf16[64,1024]{1,0:T(8,128)(2,1)S(1)}, bf16[64,1024]{1,0:T(8,128)(2,1)S(1)}, u32[]{:S(2)}, u32[]{:S(2)}) collective-permute-start(bf16[64,1024]{1,0:T(8,128)(2,1)S(1)} %constant_dynamic-slice_fusion.4), channel_id=1, source_target_pairs={{0,16},{2,18},{4,20},{6,22},{8,24},{10,26},{12,28},{14,30},{16,0},... | collective-permute-start | bytes 393224 | tf_op jit(solution)/shard_map/ppermute | solution.py:665
  14.0 10.0 %collective-permute-start = (bf16[64,1024]{1,0:T(8,128)(2,1)S(1)}, bf16[64,1024]{1,0:T(8,128)(2,1)S(1)}, u32[]{:S(2)}, u32[]{:S(2)}) collective-permute-start(bf16[64,1024]{1,0:T(8,128)(2,1)S(1)} %constant_dynamic-slice_fusion.4), channel_id=1, source_target_pairs={{0,8},{2,10},{4,12},{6,14},{8,16},{10,18},{12,20},{14,22},{16,24},... | collective-permute-start | bytes 393224 | tf_op jit(solution)/shard_map/ppermute | solution.py:665
  15.6 9.1 %collective-permute-start.2 = (bf16[64,1024]{1,0:T(8,128)(2,1)S(1)}, bf16[64,1024]{1,0:T(8,128)(2,1)S(1)}, u32[]{:S(2)}, u32[]{:S(2)}) collective-permute-start(bf16[64,1024]{1,0:T(8,128)(2,1)S(1)} %constant_dynamic-slice_fusion.4), channel_id=1, source_target_pairs={{0,24},{2,26},{4,28},{6,30},{8,0},{10,2},{12,4},{14,6},{16,8},{18,... | collective-permute-start | bytes 393224 | tf_op jit(solution)/shard_map/ppermute | solution.py:665
  21.4 15.9 %copy-start.26 = (s32[2048]{0:T(1024)}, s32[2048]{0:T(1024)S(1)}, u32[]{:S(2)}) copy-start(s32[2048]{0:T(1024)S(1)} %convert_reduce_fusion.1) | copy-start | bytes 24580
  24.8 6.3 %copy-start.8 = (bf16[4,64,1024]{2,1,0:T(8,128)(2,1)}, bf16[4,64,1024]{2,1,0:T(8,128)(2,1)S(1)}, u32[]{:S(2)}) copy-start(bf16[4,64,1024]{2,1,0:T(8,128)(2,1)S(1)} %pad_maximum_fusion.2.mine_ref) | copy-start | bytes 1572868
  24.8 16.4 %collective-permute-start.7 = (bf16[4,64,1024]{2,1,0:T(8,128)(2,1)S(1)}, bf16[4,64,1024]{2,1,0:T(8,128)(2,1)}, u32[]{:S(2)}, u32[]{:S(2)}) collective-permute-start(bf16[4,64,1024]{2,1,0:T(8,128)(2,1)S(1)} %pad_maximum_fusion.2.mine_ref), channel_id=1, source_target_pairs={{0,2},{2,0},{4,6},{6,4},{8,10},{10,8},{12,14},{14,12},{16,18},{18,... | collective-permute-start | bytes 1572872 | tf_op jit(solution)/shard_map/ppermute | solution.py:665
  26.4 3.9 %collective-permute-start.4 = (bf16[4,64,1024]{2,1,0:T(8,128)(2,1)S(1)}, bf16[4,64,1024]{2,1,0:T(8,128)(2,1)S(1)}, u32[]{:S(2)}, u32[]{:S(2)}) collective-permute-start(bf16[4,64,1024]{2,1,0:T(8,128)(2,1)S(1)} %pad_maximum_fusion.2.mine_ref), channel_id=1, source_target_pairs={{0,1},{1,0},{2,3},{3,2},{4,5},{5,4},{6,7},{7,6},{8,9},{9,8},{10,11... | collective-permute-start | bytes 1572872 | tf_op jit(solution)/shard_map/ppermute | solution.py:669
  26.4 14.6 %collective-permute-start.3 = (bf16[4,64,1024]{2,1,0:T(8,128)(2,1)S(1)}, bf16[4,64,1024]{2,1,0:T(8,128)(2,1)S(1)}, u32[]{:S(2)}, u32[]{:S(2)}) collective-permute-start(bf16[4,64,1024]{2,1,0:T(8,128)(2,1)S(1)} %pad_maximum_fusion.2.mine_ref), channel_id=1, source_target_pairs={{0,4},{2,6},{4,0},{6,2},{8,12},{10,14},{12,8},{14,10},{16,20},{18,... | collective-permute-start | bytes 1572872 | tf_op jit(solution)/shard_map/ppermute | solution.py:665
  41.1 9.8 %copy-start.15 = (bf16[4,64,1024]{2,1,0:T(8,128)(2,1)}, bf16[4,64,1024]{2,1,0:T(8,128)(2,1)S(1)}, u32[]{:S(2)}) copy-start(bf16[4,64,1024]{2,1,0:T(8,128)(2,1)S(1)} %collective-permute-done.3.mine_ref) | copy-start | bytes 1572868
  41.1 9.8 %collective-permute-start.6 = (bf16[4,64,1024]{2,1,0:T(8,128)(2,1)S(1)}, bf16[4,64,1024]{2,1,0:T(8,128)(2,1)S(1)}, u32[]{:S(2)}, u32[]{:S(2)}) collective-permute-start(bf16[4,64,1024]{2,1,0:T(8,128)(2,1)S(1)} %collective-permute-done.3.mine_ref), channel_id=1, source_target_pairs={{0,1},{1,0},{2,3},{3,2},{4,5},{5,4},{6,7},{7,6},{8,9},{9,8},{10,11... | collective-permute-start | bytes 1572872 | tf_op jit(solution)/shard_map/ppermute | solution.py:669
  41.1 16.9 %collective-permute-start.5 = (bf16[4,64,1024]{2,1,0:T(8,128)(2,1)S(1)}, bf16[4,64,1024]{2,1,0:T(8,128)(2,1)}, u32[]{:S(2)}, u32[]{:S(2)}) collective-permute-start(bf16[4,64,1024]{2,1,0:T(8,128)(2,1)S(1)} %collective-permute-done.3.mine_ref), channel_id=1, source_target_pairs={{0,2},{2,0},{4,6},{6,4},{8,10},{10,8},{12,14},{14,12},{16,18},{18,... | collective-permute-start | bytes 1572872 | tf_op jit(solution)/shard_map/ppermute | solution.py:665
  41.3 2.7 collective-permute-start.8
  42.5 17.0 %copy-start.33 = (f32[128]{0:T(128)}, f32[128]{0:T(128)S(1)}, u32[]{:S(2)}) copy-start(f32[128]{0:T(128)S(1)} %fusion.13) | copy-start | bytes 1540
  51.7 7.9 %copy-start.10 = (bf16[1024,512]{1,0:T(8,128)(2,1)S(1)}, bf16[1024,512]{1,0:T(8,128)(2,1)}, u32[]{:S(2)}) copy-start(bf16[1024,512]{1,0:T(8,128)(2,1)} %param.18) | copy-start | bytes 3145732
  51.7 7.9 %copy-start.23 = (f32[1024]{0:T(1024)S(1)}, f32[1024]{0:T(1024)}, u32[]{:S(2)}) copy-start(f32[1024]{0:T(1024)} %param.14) | copy-start | bytes 12292
  51.7 7.9 %copy-start.28 = (f32[1024]{0:T(1024)S(1)}, f32[1024]{0:T(1024)}, u32[]{:S(2)}) copy-start(f32[1024]{0:T(1024)} %param.15) | copy-start | bytes 12292
  58.0 2.8 %collective-permute-start.9 = (bf16[4,64,1024]{2,1,0:T(8,128)(2,1)}, bf16[4,64,1024]{2,1,0:T(8,128)(2,1)S(1)}, u32[]{:S(2)}, u32[]{:S(2)}) collective-permute-start(bf16[4,64,1024]{2,1,0:T(8,128)(2,1)} %collective-permute-done.5.mine_ref), channel_id=1, source_target_pairs={{0,1},{1,0},{2,3},{3,2},{4,5},{5,4},{6,7},{7,6},{8,9},{9,8},{10,11... | collective-permute-start | bytes 1572872 | tf_op jit(solution)/shard_map/ppermute | solution.py:669
  75.1 3.5 %copy-start.29 = (f32[1024]{0:T(1024)S(1)}, f32[1024]{0:T(1024)}, u32[]{:S(2)}) copy-start(f32[1024]{0:T(1024)} %param.16) | copy-start | bytes 12292
  75.1 3.5 %copy-start.30 = (f32[1024]{0:T(1024)S(1)}, f32[1024]{0:T(1024)}, u32[]{:S(2)}) copy-start(f32[1024]{0:T(1024)} %param.17) | copy-start | bytes 12292
  75.1 4.6 %copy-start.35 = (s32[4]{0:T(128)S(1)}, s32[4]{0:T(128)}, u32[]{:S(2)}) copy-start(s32[4]{0:T(128)} %param.25) | copy-start | bytes 52
  76.5 1.6 collective-permute-start.10
  78.7 1.0 copy-start.9
  87.5 4.8 %copy-start.7 = (bf16[128,1024]{1,0:T(8,128)(2,1)S(1)}, bf16[128,1024]{1,0:T(8,128)(2,1)}, u32[]{:S(2)}) copy-start(bf16[128,1024]{1,0:T(8,128)(2,1)} %g_ref.1) | copy-start | bytes 786436
  87.5 1.7 collective-permute-start.11
  90.5 11.7 %copy-start.27 = (s32[2048]{0:T(1024)S(1)}, s32[2048]{0:T(1024)}, u32[]{:S(2)}) copy-start(s32[2048]{0:T(1024)} %copy-done.26) | copy-start | bytes 24580
  93.6 18.4 %all-to-all-start = ((bf16[8,64,128]{2,1,0:T(8,128)(2,1)}), bf16[8,64,128]{2,1,0:T(8,128)(2,1)S(1)}, u32[]{:S(2)}, u32[]{:S(2)}) async-start(bf16[8,64,128]{2,1,0:T(8,128)(2,1)} %bitcast.32), calls=%async_computation | async-start | bytes 262144 | tf_op jit(solution)/shard_map/all_to_all | solution.py:780
  112.6 13.3 %copy-start.11 = (bf16[128,512]{1,0:T(8,128)(2,1)S(1)}, bf16[128,512]{1,0:T(8,128)(2,1)}, u32[]{:S(2)}) copy-start(bf16[128,512]{1,0:T(8,128)(2,1)} %attend.1) | copy-start | bytes 393220
  125.2 11.3 %copy-start.21 = (f32[192,512]{1,0:T(8,128)S(1)}, f32[192,512]{1,0:T(8,128)}, u32[]{:S(2)}) copy-start(f32[192,512]{1,0:T(8,128)} %get-tuple-element.90) | copy-start | bytes 1179652
  125.2 11.3 %collective-permute-start.12 = (bf16[192,512]{1,0:T(8,128)(2,1)}, bf16[192,512]{1,0:T(8,128)(2,1)S(1)}, u32[]{:S(2)}, u32[]{:S(2)}) collective-permute-start(bf16[192,512]{1,0:T(8,128)(2,1)} %get-tuple-element.91), channel_id=1, source_target_pairs={{0,2},{2,0},{4,6},{6,4},{8,10},{10,8},{12,14},{14,12},{16,18},{18,... | collective-permute-start | bytes 589832 | tf_op jit(solution)/shard_map/ppermute | solution.py:665
  126.4 14.9 %copy-start.5 = (f32[1024,512]{1,0:T(8,128)}, f32[1024,512]{1,0:T(8,128)S(1)}, u32[]{:S(2)}) copy-start(f32[1024,512]{1,0:T(8,128)S(1)} %fusion.31) | copy-start | bytes 6291460
  126.4 40.6 %copy-start.20 = (f32[8,128,128]{2,1,0:T(8,128)S(1)}, f32[8,128,128]{2,1,0:T(8,128)}, u32[]{:S(2)}) copy-start(f32[8,128,128]{2,1,0:T(8,128)} %get-tuple-element.88) | copy-start | bytes 1572868
  136.6 12.4 %collective-permute-start.18 = (bf16[192,512]{1,0:T(8,128)(2,1)S(1)}, bf16[192,512]{1,0:T(8,128)(2,1)S(1)}, u32[]{:S(2)}, u32[]{:S(2)}) collective-permute-start(bf16[192,512]{1,0:T(8,128)(2,1)S(1)} %add_convert_fusion.3), channel_id=1, source_target_pairs={{0,24},{2,26},{4,28},{6,30},{8,0},{10,2},{12,4},{14,6},{16,8},{18,... | collective-permute-start | bytes 589832 | tf_op jit(solution)/shard_map/ppermute | solution.py:665
  140.2 21.4 %collective-permute-start.17 = (bf16[192,512]{1,0:T(8,128)(2,1)S(1)}, bf16[192,512]{1,0:T(8,128)(2,1)S(1)}, u32[]{:S(2)}, u32[]{:S(2)}) collective-permute-start(bf16[192,512]{1,0:T(8,128)(2,1)S(1)} %add_convert_fusion.3), channel_id=1, source_target_pairs={{0,16},{2,18},{4,20},{6,22},{8,24},{10,26},{12,28},{14,30},{16,0},... | collective-permute-start | bytes 589832 | tf_op jit(solution)/shard_map/ppermute | solution.py:665
  140.2 21.4 %collective-permute-start.16 = (bf16[192,512]{1,0:T(8,128)(2,1)S(1)}, bf16[192,512]{1,0:T(8,128)(2,1)}, u32[]{:S(2)}, u32[]{:S(2)}) collective-permute-start(bf16[192,512]{1,0:T(8,128)(2,1)S(1)} %add_convert_fusion.3), channel_id=1, source_target_pairs={{0,8},{2,10},{4,12},{6,14},{8,16},{10,18},{12,20},{14,22},{16,24},... | collective-permute-start | bytes 589832 | tf_op jit(solution)/shard_map/ppermute | solution.py:665
  142.2 24.9 %collective-permute-start.14 = (bf16[8,64,512]{2,1,0:T(8,128)(2,1)}, bf16[8,64,512]{2,1,0:T(8,128)(2,1)S(1)}, u32[]{:S(2)}, u32[]{:S(2)}) collective-permute-start(bf16[8,64,512]{2,1,0:T(8,128)(2,1)} %fusion.15), channel_id=1, source_target_pairs={{0,2},{2,0},{4,6},{6,4},{8,10},{10,8},{12,14},{14,12},{16,18},{18,... | collective-permute-start | bytes 1572872 | tf_op jit(solution)/shard_map/ppermute | solution.py:665
  142.9 24.1 %collective-permute-start.13 = (bf16[8,128,128]{2,1,0:T(8,128)(2,1)}, bf16[8,128,128]{2,1,0:T(8,128)(2,1)S(1)}, u32[]{:S(2)}, u32[]{:S(2)}) collective-permute-start(bf16[8,128,128]{2,1,0:T(8,128)(2,1)} %get-tuple-element.92), channel_id=1, source_target_pairs={{0,2},{2,0},{4,6},{6,4},{8,10},{10,8},{12,14},{14,12},{16,18},{18,... | collective-permute-start | bytes 786440 | tf_op jit(solution)/shard_map/ppermute | solution.py:665
  144.2 22.9 %copy-start.6 = (f32[1024,512]{1,0:T(8,128)S(1)}, f32[1024,512]{1,0:T(8,128)}, u32[]{:S(2)}) copy-start(f32[1024,512]{1,0:T(8,128)} %copy-done.5) | copy-start | bytes 6291460
  163.5 33.4 %collective-permute-start.21 = (bf16[4,192,512]{2,1,0:T(8,128)(2,1)}, bf16[4,192,512]{2,1,0:T(8,128)(2,1)}, u32[]{:S(2)}, u32[]{:S(2)}) collective-permute-start(bf16[4,192,512]{2,1,0:T(8,128)(2,1)} %pad_maximum_fusion.1.refs_0_), channel_id=1, source_target_pairs={{0,6},{2,4},{4,2},{6,0},{8,14},{10,12},{12,10},{14,8},{16,22},{18,... | collective-permute-start | bytes 2359304 | tf_op jit(solution)/shard_map/ppermute | solution.py:665
  165.0 42.1 %collective-permute-start.20 = (bf16[4,192,512]{2,1,0:T(8,128)(2,1)}, bf16[4,192,512]{2,1,0:T(8,128)(2,1)}, u32[]{:S(2)}, u32[]{:S(2)}) collective-permute-start(bf16[4,192,512]{2,1,0:T(8,128)(2,1)} %pad_maximum_fusion.1.refs_0_), channel_id=1, source_target_pairs={{0,4},{2,6},{4,0},{6,2},{8,12},{10,14},{12,8},{14,10},{16,20},{18,... | collective-permute-start | bytes 2359304 | tf_op jit(solution)/shard_map/ppermute | solution.py:665
  165.6 41.5 %collective-permute-start.19 = (bf16[4,192,512]{2,1,0:T(8,128)(2,1)}, bf16[4,192,512]{2,1,0:T(8,128)(2,1)}, u32[]{:S(2)}, u32[]{:S(2)}) collective-permute-start(bf16[4,192,512]{2,1,0:T(8,128)(2,1)} %pad_maximum_fusion.1.refs_0_), channel_id=1, source_target_pairs={{0,2},{2,0},{4,6},{6,4},{8,10},{10,8},{12,14},{14,12},{16,18},{18,... | collective-permute-start | bytes 2359304 | tf_op jit(solution)/shard_map/ppermute | solution.py:665
  167.0 0.9 copy-start.25
  168.9 40.5 %all-to-all-start.1 = ((bf16[8,448,128]{2,1,0:T(8,128)(2,1)}), bf16[8,448,128]{2,1,0:T(8,128)(2,1)S(1)}, u32[]{:S(2)}, u32[]{:S(2)}) async-start(bf16[8,448,128]{2,1,0:T(8,128)(2,1)} %pad_maximum_fusion), calls=%async_computation.1 | async-start | bytes 1835008 | tf_op jit(solution)/shard_map/all_to_all | solution.py:798
  172.8 47.5 %collective-permute-start.15 = (bf16[128,1024]{1,0:T(8,128)(2,1)}, bf16[128,1024]{1,0:T(8,128)(2,1)}, u32[]{:S(2)}, u32[]{:S(2)}) collective-permute-start(bf16[128,1024]{1,0:T(8,128)(2,1)} %get-tuple-element.94), channel_id=1, source_target_pairs={{0,1},{1,0},{2,3},{3,2},{4,5},{5,4},{6,7},{7,6},{8,9},{9,8},{10,11... | collective-permute-start | bytes 786440 | tf_op jit(solution)/shard_map/ppermute | solution.py:669
  196.9 22.3 %copy-start.2 = (bf16[1024,512]{1,0:T(8,128)(2,1)S(1)}, bf16[1024,512]{1,0:T(8,128)(2,1)}, u32[]{:S(2)}) copy-start(bf16[1024,512]{1,0:T(8,128)(2,1)} %v_ref.7) | copy-start | bytes 3145732
  211.8 10.5 %collective-permute-start.25 = (bf16[64,512]{1,0:T(8,128)(2,1)S(1)}, bf16[64,512]{1,0:T(8,128)(2,1)S(1)}, u32[]{:S(2)}, u32[]{:S(2)}) collective-permute-start(bf16[64,512]{1,0:T(8,128)(2,1)S(1)} %reduce_sum.167), channel_id=1, source_target_pairs={{0,24},{2,26},{4,28},{6,30},{8,0},{10,2},{12,4},{14,6},{16,8},{18,... | collective-permute-start | bytes 196616 | tf_op jit(solution)/shard_map/ppermute | solution.py:665
  211.8 10.4 %collective-permute-start.24 = (bf16[64,512]{1,0:T(8,128)(2,1)S(1)}, bf16[64,512]{1,0:T(8,128)(2,1)S(1)}, u32[]{:S(2)}, u32[]{:S(2)}) collective-permute-start(bf16[64,512]{1,0:T(8,128)(2,1)S(1)} %reduce_sum.167), channel_id=1, source_target_pairs={{0,16},{2,18},{4,20},{6,22},{8,24},{10,26},{12,28},{14,30},{16,0},... | collective-permute-start | bytes 196616 | tf_op jit(solution)/shard_map/ppermute | solution.py:665
  214.4 7.8 %collective-permute-start.23 = (bf16[64,512]{1,0:T(8,128)(2,1)S(1)}, bf16[64,512]{1,0:T(8,128)(2,1)S(1)}, u32[]{:S(2)}, u32[]{:S(2)}) collective-permute-start(bf16[64,512]{1,0:T(8,128)(2,1)S(1)} %reduce_sum.167), channel_id=1, source_target_pairs={{0,8},{2,10},{4,12},{6,14},{8,16},{10,18},{12,20},{14,22},{16,24},... | collective-permute-start | bytes 196616 | tf_op jit(solution)/shard_map/ppermute | solution.py:665
  217.5 2.3 copy-start.3
  219.7 2.5 copy-start.13
  219.8 2.6 copy-start.24
  219.8 2.8 %copy-start.34 = (f32[128]{0:T(128)S(1)}, f32[128]{0:T(128)}, u32[]{:S(2)}) copy-start(f32[128]{0:T(128)} %copy-done.33) | copy-start | bytes 1540
  220.3 2.1 collective-permute-start.22
  222.3 26.8 %copy-start.12 = (bf16[4,64,512]{2,1,0:T(8,128)(2,1)}, bf16[4,64,512]{2,1,0:T(8,128)(2,1)S(1)}, u32[]{:S(2)}) copy-start(bf16[4,64,512]{2,1,0:T(8,128)(2,1)S(1)} %pad_maximum_fusion.3.refs_0_) | copy-start | bytes 786436
  247.1 14.5 %copy-start.32 = (f32[128]{0:T(128)S(1)}, f32[128]{0:T(128)}, u32[]{:S(2)}) copy-start(f32[128]{0:T(128)} %copy-done.31) | copy-start | bytes 1540
  247.1 15.6 %collective-permute-start.28 = (bf16[4,64,512]{2,1,0:T(8,128)(2,1)S(1)}, bf16[4,64,512]{2,1,0:T(8,128)(2,1)S(1)}, u32[]{:S(2)}, u32[]{:S(2)}) collective-permute-start(bf16[4,64,512]{2,1,0:T(8,128)(2,1)S(1)} %pad_maximum_fusion.3.refs_0_), channel_id=1, source_target_pairs={{0,6},{2,4},{4,2},{6,0},{8,14},{10,12},{12,10},{14,8},{16,22},{18,... | collective-permute-start | bytes 786440 | tf_op jit(solution)/shard_map/ppermute | solution.py:665
  248.5 15.7 %collective-permute-start.27 = (bf16[4,64,512]{2,1,0:T(8,128)(2,1)S(1)}, bf16[4,64,512]{2,1,0:T(8,128)(2,1)}, u32[]{:S(2)}, u32[]{:S(2)}) collective-permute-start(bf16[4,64,512]{2,1,0:T(8,128)(2,1)S(1)} %pad_maximum_fusion.3.refs_0_), channel_id=1, source_target_pairs={{0,4},{2,6},{4,0},{6,2},{8,12},{10,14},{12,8},{14,10},{16,20},{18,... | collective-permute-start | bytes 786440 | tf_op jit(solution)/shard_map/ppermute | solution.py:665
  249.2 15.1 %collective-permute-start.26 = (bf16[4,64,512]{2,1,0:T(8,128)(2,1)S(1)}, bf16[4,64,512]{2,1,0:T(8,128)(2,1)}, u32[]{:S(2)}, u32[]{:S(2)}) collective-permute-start(bf16[4,64,512]{2,1,0:T(8,128)(2,1)S(1)} %pad_maximum_fusion.3.refs_0_), channel_id=1, source_target_pairs={{0,2},{2,0},{4,6},{6,4},{8,10},{10,8},{12,14},{14,12},{16,18},{18,... | collective-permute-start | bytes 786440 | tf_op jit(solution)/shard_map/ppermute | solution.py:665
  251.3 16.2 %all-to-all-start.2 = ((f32[16,4,1024]{2,1,0:T(4,128)}), f32[16,4,1024]{2,1,0:T(4,128)S(1)}, u32[]{:S(2)}, u32[]{:S(2)}) async-start(f32[16,4,1024]{2,1,0:T(4,128)} %broadcast_in_dim.72), calls=%async_computation.2 | async-start | bytes 524288 | tf_op jit(solution)/shard_map/all_to_all | solution.py:819
  261.6 6.7 %copy-start.1 = (bf16[1024,512]{1,0:T(8,128)(2,1)S(1)}, bf16[1024,512]{1,0:T(8,128)(2,1)}, u32[]{:S(2)}) copy-start(bf16[1024,512]{1,0:T(8,128)(2,1)} %param.21) | copy-start | bytes 3145732
  262.7 1.6 copy-start.22
  (6 other events, 4.5 us)
Sparse Core Ops, SparseCore 0:
  10.9 66.1 all-gather.2
  80.0 74.1 all-gather.4

commit v3 on v0

--- a/solution.py
+++ b/solution.py
@@ -1,9 +1,16 @@
 import jax
 import jax.numpy as jnp
 from jax import lax
+from jax.experimental import pallas as pl
+from jax.experimental.pallas import tpu as pltpu
 from jax.sharding import PartitionSpec as P
 
 HEAD = 64
+NEG = -1e30
+f32 = jnp.float32
+bf16 = jnp.bfloat16
+LAST = (((1,), (1,)), ((), ()))
+FIRST = (((0,), (0,)), ((), ()))
 
 
 def from_behind(block, axis, distance):
@@ -25,7 +32,7 @@
     )
 
 
-def body(
+def ring_body(
     tokens,
     first_gain,
     first_bias,
@@ -40,8 +47,6 @@
     cotangent,
     scene_len,
 ):
-    f32 = jnp.float32
-    bf16 = jnp.bfloat16
     count = lax.axis_size("blk")
     place = lax.axis_index("blk")
     rows = tokens.shape[0]
@@ -260,7 +265,764 @@
     )
 
 
+HINT = pl.CostEstimate(flops=1, bytes_accessed=1, transcendentals=1)
+NEAR = pl.BlockSpec(memory_space=pltpu.VMEM)
+FAR = pl.BlockSpec(memory_space=pltpu.HBM)
+SCALAR = pl.BlockSpec(memory_space=pltpu.SMEM)
+QT = 256
+KT = 512
+FT = 256
+TT = 1024
+
+
+def near(*arrays):
+    return [pltpu.with_memory_space_constraint(array, pltpu.VMEM) for array in arrays]
+
+
+def room(mib):
+    return pltpu.CompilerParams(vmem_limit_bytes=mib << 20)
+
+
+def full(shape):
+    return pl.BlockSpec(shape, lambda *_: (0,) * len(shape))
+
+
+def borders_of(len_ref):
+    borders = [len_ref[0]]
+    for s in range(1, len_ref.shape[0] - 1):
+        borders.append(borders[-1] + len_ref[s])
+    return borders
+
+
+def scenes(positions, borders):
+    scene = jnp.zeros_like(positions)
+    for border in borders:
+        scene += (positions >= border).astype(jnp.int32)
+    return scene
+
+
+def tiles_of(first, last, borders, total):
+    low, high = 0, total
+    for border in borders:
+        low = jnp.where(border <= first, border, low)
+    for border in reversed(borders):
+        high = jnp.where(border > last, border, high)
+    return lax.div(low, KT), lax.div(high + KT - 1, KT)
+
+
+def project_kernel(flip, ids_ref, mine_ref, other_ref, gain_ref, bias_ref, k_ref, v_ref, t_ref, n_ref, *rest):
+    h_out, k_out, v_out, t_out, n_out, h_s = rest[-6:]
+    n, half, width = mine_ref.shape
+    rows = 2 * half
+    first = ids_ref[1] == 0
+
+    def norm(b, carry):
+        mine, other = mine_ref[b], other_ref[b]
+        block = jnp.concatenate([jnp.where(first, mine, other), jnp.where(first, other, mine)], axis=0)
+        h_s[b] = layer_norm(block.astype(f32), gain_ref[...], bias_ref[...]).astype(bf16)
+        return carry
+
+    lax.fori_loop(0, n, norm, 0)
+    h = h_s[...].reshape(n * rows, width)
+    keys = jnp.dot(h, k_ref[...], preferred_element_type=f32).astype(bf16)
+    values = jnp.dot(h, v_ref[...], preferred_element_type=f32).astype(bf16)
+    across = lax.dot_general(t_ref[...], h, LAST, preferred_element_type=f32).astype(bf16)
+    down = jnp.dot(h, n_ref[...], preferred_element_type=f32).astype(bf16)
+    for s in range(n):
+        at = ((ids_ref[0] - 4 * s) & 15) ^ flip
+        tokens = slice(s * rows, (s + 1) * rows)
+        h_out[at] = h[tokens]
+        k_out[at] = keys[tokens]
+        v_out[at] = values[tokens]
+        t_out[at] = across[:, tokens]
+        n_out[at] = down[tokens]
+
+
+def project_blocks(flip, ids, mine, other, params, count, held):
+    half, width = mine.shape[1:]
+    _, _, key_weight, value_weight, head_t, head_n = params
+    shapes = [
+        (2 * half, width),
+        (2 * half, key_weight.shape[1]),
+        (2 * half, value_weight.shape[1]),
+        (head_t.shape[0], 2 * half),
+        (2 * half, head_n.shape[1]),
+    ]
+    return pl.pallas_call(
+        lambda *refs: project_kernel(flip, *refs),
+        in_specs=[SCALAR] + [NEAR] * (8 + len(held)),
+        out_specs=[NEAR] * 5,
+        out_shape=[pltpu.VMEM((count,) + shape, bf16) for shape in shapes],
+        scratch_shapes=[pltpu.VMEM((mine.shape[0], 2 * half, width), bf16)],
+        input_output_aliases={9 + i: i for i in range(5)} if held else {},
+        compiler_params=room(16),
+        cost_estimate=HINT,
+        name="project_blocks",
+    )(ids, *near(mine, other, *params, *held))
+
+
+def attend_kernel(ids_ref, len_ref, h_ref, k_ref, v_ref, q_ref, o_ref, out_ref, branch_ref, query_s):
+    rows, width = out_ref.shape
+    total = k_ref.shape[0]
+    pair = 2 * HEAD
+    borders = borders_of(len_ref)
+    mine = scenes(lax.broadcasted_iota(jnp.int32, (rows, 1), 0) + ids_ref[0] * rows, borders)
+    mask = mine == scenes(lax.broadcasted_iota(jnp.int32, (1, total), 1), borders)
+    query = jnp.dot(h_ref[ids_ref[0]], q_ref[...], preferred_element_type=f32).astype(bf16)
+    query = query * jnp.asarray(HEAD ** (-0.5), bf16)
+    lane = lax.broadcasted_iota(jnp.int32, (rows, pair), 1) // HEAD
+    query_s[...] = query
+
+    def attend_pair(g, carry):
+        lanes = pl.ds(pl.multiple_of(g * pair, pair), pair)
+        keys, values, queries = k_ref[:, lanes], v_ref[:, lanes], query_s[:, lanes]
+        parts = []
+        for head in range(2):
+            q = jnp.where(lane == head, queries, jnp.zeros_like(queries))
+            s = lax.dot_general(q, keys, LAST, preferred_element_type=f32)
+            s = jnp.where(mask, s, NEG)
+            p = jnp.exp(s - jnp.max(s, axis=1, keepdims=True))
+            weight = jnp.sum(p, axis=1, keepdims=True)
+            parts.append(jnp.dot(p.astype(bf16), values, preferred_element_type=f32) / weight)
+        out_ref[:, lanes] = jnp.where(lane == 0, parts[0], parts[1]).astype(bf16)
+        return carry
+
+    lax.fori_loop(0, width // pair, attend_pair, 0)
+    branch = lax.dot_general(out_ref[...], o_ref[...], LAST, preferred_element_type=f32)
+    branch_ref[...] = branch.astype(bf16)
+
+
+def attend(ids, scene_len, h, k, v, query_weight, output_weight):
+    rows = h.shape[1]
+    return pl.pallas_call(
+        attend_kernel,
+        in_specs=[SCALAR] * 2 + [NEAR] * 5,
+        out_specs=[NEAR] * 2,
+        out_shape=[
+            jax.ShapeDtypeStruct((rows, query_weight.shape[1]), bf16),
+            jax.ShapeDtypeStruct((rows, output_weight.shape[0]), bf16),
+        ],
+        scratch_shapes=[pltpu.VMEM((rows, query_weight.shape[1]), bf16)],
+        compiler_params=room(16),
+        cost_estimate=HINT,
+        name="attend",
+    )(ids, scene_len, *near(h, k, v, query_weight, output_weight))
+
+
+def gelu_both(pre, grad):
+    half = 0.5 * (1.0 + lax.erf(pre * 0.7071067811865476))
+    slope = half + pre * (jnp.exp(-0.5 * pre * pre) * 0.3989422804014327)
+    return (pre * half).astype(bf16), (grad * slope).astype(bf16)
+
+
+def own_kernel(h_ref, g_ref, up_ref, down_ref, feed_out, grad_out, feed_s, grad_s):
+    step = pl.program_id(0)
+    pre = jnp.dot(h_ref[...], up_ref[...], preferred_element_type=f32)
+    grad = jnp.dot(g_ref[...], down_ref[...], preferred_element_type=f32)
+    act, grad_pre = gelu_both(pre, grad)
+    feed = lax.dot_general(act, down_ref[...], LAST, preferred_element_type=f32)
+    grad_two = lax.dot_general(grad_pre, up_ref[...], LAST, preferred_element_type=f32)
+
+    @pl.when(step == 0)
+    def _():
+        feed_s[...] = feed
+        grad_s[...] = grad_two
+
+    @pl.when(step > 0)
+    def _():
+        feed_s[...] += feed
+        grad_s[...] += grad_two
+
+    @pl.when(step == pl.num_programs(0) - 1)
+    def _():
+        feed_out[...] = feed_s[...].astype(bf16)
+        grad_out[...] = grad_s[...].astype(bf16)
+
+
+def own_ffn(h, g, up_weight, down_weight):
+    width = h.shape[1]
+    hidden = up_weight.shape[1]
+    tile = 512
+    return pl.pallas_call(
+        own_kernel,
+        grid=(hidden // tile,),
+        in_specs=[NEAR, NEAR] + [pl.BlockSpec((width, tile), lambda i: (0, i))] * 2,
+        out_specs=[NEAR] * 2,
+        out_shape=[jax.ShapeDtypeStruct(h.shape, bf16)] * 2,
+        scratch_shapes=[pltpu.VMEM(h.shape, f32)] * 2,
+        cost_estimate=HINT,
+        name="own_ffn",
+    )(*near(h, g), up_weight, down_weight)
+
+
+def norm_back_kernel(x_ref, mine_ref, other_ref, gain_ref, g_ref, o_ref, grad_out, low_out, sums_out, heads_out):
+    x = x_ref[...]
+    center = x - jnp.mean(x, axis=1, keepdims=True)
+    scale = lax.rsqrt(jnp.mean(center * center, axis=1, keepdims=True) + 1e-05)
+    normed = center * scale
+    grad = mine_ref[...].astype(f32) + other_ref[...].astype(f32)
+    sums_out[0:1, :] = jnp.sum(grad * normed, axis=0, keepdims=True)
+    sums_out[1:2, :] = jnp.sum(grad, axis=0, keepdims=True)
+    grad = grad * gain_ref[...]
+    inner = jnp.mean(grad * normed, axis=1, keepdims=True)
+    grad = scale * (grad - jnp.mean(grad, axis=1, keepdims=True) - normed * inner)
+    grad = grad + g_ref[...].astype(f32)
+    grad_out[...] = grad
+    low = grad.astype(bf16)
+    low_out[...] = low
+    attended = jnp.dot(low, o_ref[...], preferred_element_type=f32)
+    across = attended.T.astype(bf16)
+    for head in range(heads_out.shape[0]):
+        heads_out[head] = across[head * HEAD : (head + 1) * HEAD, :]
+
+
+def norm_back(x, mine, other, gain, g, output_weight):
+    rows, width = x.shape
+    return pl.pallas_call(
+        norm_back_kernel,
+        in_specs=[NEAR] * 6,
+        out_specs=[NEAR] * 4,
+        out_shape=[
+            jax.ShapeDtypeStruct((rows, width), f32),
+            jax.ShapeDtypeStruct((rows, width), bf16),
+            jax.ShapeDtypeStruct((2, width), f32),
+            jax.ShapeDtypeStruct((output_weight.shape[1] // HEAD, HEAD, rows), bf16),
+        ],
+        compiler_params=room(16),
+        cost_estimate=HINT,
+        name="norm_back",
+    )(*near(x, mine, other, gain.reshape(1, width), g, output_weight))
+
+
+def prepare_kernel(ids_ref, len_ref, t_ref, n_ref, p_ref, s_s):
+    step = pl.program_id(0)
+    count, _, rows = t_ref.shape
+    borders = borders_of(len_ref)
+    blocks = [4 * step + 2 * i + (ids_ref[0] & 1) for i in range(2)]
+    lo, hi = tiles_of(blocks[0] * rows, blocks[1] * rows + rows - 1, borders, count * rows)
+    q = jnp.concatenate([t_ref[b, 0:HEAD, :] for b in blocks], axis=1)
+    q = jnp.concatenate([q, jnp.zeros_like(q)], axis=0)
+    places = lax.broadcasted_iota(jnp.int32, (1, rows), 1)
+    row = scenes(jnp.concatenate([places + b * rows for b in blocks], axis=1), borders)
+
+    def score(j, top):
+        keys = pl.ds(pl.multiple_of(j * KT, KT), KT)
+        s = jnp.dot(n_ref[keys, 0 : 2 * HEAD], q, preferred_element_type=f32)
+        col = scenes(lax.broadcasted_iota(jnp.int32, (KT, 1), 0) + j * KT, borders)
+        s = jnp.where(col == row, s, NEG)
+        s_s[keys, :] = s
+        return jnp.maximum(top, jnp.max(s, axis=0, keepdims=True))
+
+    top = lax.fori_loop(lo, hi, score, jnp.full((1, QT), NEG, f32))
+
+    def weigh(j, total):
+        keys = pl.ds(pl.multiple_of(j * KT, KT), KT)
+        p = jnp.exp(s_s[keys, :] - top)
+        s_s[keys, :] = p
+        return total + jnp.sum(p, axis=0, keepdims=True)
+
+    total = lax.fori_loop(lo, hi, weigh, jnp.zeros((1, QT), f32))
+    share = 1.0 / total
+
+    def store(j, carry):
+        keys = pl.ds(pl.multiple_of(j * KT, KT), KT)
+        p_ref[0, keys, :] = (s_s[keys, :] * share).astype(bf16)
+        return carry
+
+    lax.fori_loop(lo, hi, store, 0)
+
+
+def prepare(ids, scene_len, head_t, head_n):
+    count, _, rows = head_t.shape
+    total = count * rows
+    tiles = total // 2 // QT
+    return pl.pallas_call(
+        prepare_kernel,
+        grid_spec=pltpu.PrefetchScalarGridSpec(
+            num_scalar_prefetch=2,
+            grid=(tiles,),
+            in_specs=[full(head_t.shape), full((total, 4 * HEAD))],
+            out_specs=pl.BlockSpec((1, total, QT), lambda i, *_: (i, 0, 0)),
+            scratch_shapes=[pltpu.VMEM((total, QT), f32)],
+        ),
+        out_shape=jax.ShapeDtypeStruct((tiles, total, QT), bf16),
+        cost_estimate=HINT,
+        name="prepare",
+    )(ids, scene_len, head_t, head_n.reshape(total, 4 * HEAD))
+
+
+def back_kernel(
+    ids_ref, len_ref, p_ref, ga_ref, t_ref, n_ref, h_far,
+    gq_out, mine_out, other_out, slice_mine, slice_other, dp_s, gkv_s, g_s, h_ref, sem,
+):
+    step = pl.program_id(0)
+    part = ids_ref[0] & 1
+    count, _, rows = t_ref.shape
+    blocks = [4 * step + 2 * i + part for i in range(2)]
+    lo, hi = tiles_of(blocks[0] * rows, blocks[1] * rows + rows - 1, borders_of(len_ref), count * rows)
+    load = pltpu.make_async_copy(h_far, h_ref, sem)
+
+    @pl.when(step == 0)
+    def _():
+        load.start()
+        gkv_s[...] = jnp.zeros_like(gkv_s)
+        g_s[...] = jnp.zeros_like(g_s)
+
+    spans = [pl.ds(pl.multiple_of(b * rows, rows), rows) for b in blocks]
+    ga_t = jnp.concatenate([ga_ref[0], ga_ref[1]], axis=1)
+    ga_t = jnp.concatenate([ga_t, jnp.zeros_like(ga_t)], axis=0)
+    ga = ga_t.T
+    kq = jnp.concatenate([n_ref[span, 0 : 2 * HEAD] for span in spans], axis=0)
+    q = jnp.where(lax.broadcasted_iota(jnp.int32, kq.shape, 1) >= HEAD, kq, jnp.zeros_like(kq))
+
+    def first(j, delta):
+        keys = pl.ds(pl.multiple_of(j * KT, KT), KT)
+        p = p_ref[0, keys, :]
+        dp = jnp.dot(n_ref[keys, 2 * HEAD :], ga_t, preferred_element_type=f32)
+        dp_s[keys, :] = dp
+        gkv_s[keys, :] += jnp.dot(p, ga, preferred_element_type=f32)
+        return delta + jnp.sum(p.astype(f32) * dp, axis=0, keepdims=True)
+
+    delta = lax.fori_loop(lo, hi, first, jnp.zeros((1, QT), f32))
+
+    def second(j, gq):
+        keys = pl.ds(pl.multiple_of(j * KT, KT), KT)
+        ds = (p_ref[0, keys, :].astype(f32) * (dp_s[keys, :] - delta)).astype(bf16)
+        gkv_s[keys, :] += jnp.dot(ds, q, preferred_element_type=f32)
+        some = KT // rows
+        k_t = jnp.concatenate([t_ref[j * some + i, HEAD : 2 * HEAD, :] for i in range(some)], axis=1)
+        return gq + jnp.dot(k_t, ds, preferred_element_type=f32)
+
+    gq = lax.fori_loop(lo, hi, second, jnp.zeros((HEAD, QT), f32))
+    gq = (gq * HEAD ** (-0.5)).astype(bf16)
+    for i in range(2):
+        tile = gq[:, i * rows : (i + 1) * rows]
+        gq_out[2 * step + i] = tile
+        g_s[0:HEAD, spans[i]] = tile
+
+    @pl.when(step == pl.num_programs(0) - 1)
+    def _():
+        for m in range(count // 2):
+            for out, b in ((mine_out, 2 * m + part), (other_out, 2 * m + 1 - part)):
+                tokens = pl.ds(pl.multiple_of(b * rows, rows), rows)
+                both = gkv_s[tokens, :].T
+                out[m] = both.astype(out.dtype)
+                g_s[HEAD:, tokens] = both.astype(bf16)
+        load.wait()
+        slices = jnp.dot(g_s[...], h_ref[...], preferred_element_type=f32)
+        wide = slice_mine.shape[1]
+        left, right = slices[:, :wide], slices[:, wide:]
+        slice_mine[...] = jnp.where(part == 0, left, right)
+        slice_other[...] = jnp.where(part == 0, right, left).astype(bf16)
+
+
+def back(ids, scene_len, p, ga, head_t, head_n, h1):
+    count, three, rows = head_t.shape
+    width = h1.shape[-1]
+    total = count * rows
+    half = count // 2
+    kept = [
+        ((half, HEAD, rows), bf16),
+        ((half, 2 * HEAD, rows), f32),
+        ((half, 2 * HEAD, rows), bf16),
+        ((three, width // 2), f32),
+        ((three, width // 2), bf16),
+    ]
+    return pl.pallas_call(
+        back_kernel,
+        grid_spec=pltpu.PrefetchScalarGridSpec(
+            num_scalar_prefetch=2,
+            grid=(p.shape[0],),
+            in_specs=[
+                pl.BlockSpec((1, total, QT), lambda i, *_: (i, 0, 0)),
+                pl.BlockSpec((2, HEAD, rows), lambda i, *_: (i, 0, 0)),
+                full(head_t.shape),
+                full((total, 4 * HEAD)),
+                FAR,
+            ],
+            out_specs=[NEAR] * 5,
+            scratch_shapes=[
+                pltpu.VMEM((total, QT), f32),
+                pltpu.VMEM((total, 2 * HEAD), f32),
+                pltpu.VMEM((three, total), bf16),
+                pltpu.VMEM((total, width), bf16),
+                pltpu.SemaphoreType.DMA,
+            ],
+        ),
+        out_shape=[jax.ShapeDtypeStruct(shape, kind) for shape, kind in kept],
+        cost_estimate=HINT,
+        name="back",
+    )(ids, scene_len, p, ga, head_t, head_n.reshape(total, 4 * HEAD), h1.reshape(total, width))
+
+
+def share_kernel(ids_ref, low_ref, attended_ref, mine_out, other_out):
+    part = ids_ref[0] & 1
+    whole = lax.dot_general(low_ref[...], attended_ref[...], FIRST, preferred_element_type=f32)
+    whole = whole.reshape(mine_out.shape[0], 2, mine_out.shape[1], mine_out.shape[2])
+    mine_out[...] = jnp.where(part == 0, whole[:, 0], whole[:, 1])
+    other_out[...] = jnp.where(part == 0, whole[:, 1], whole[:, 0]).astype(bf16)
+
+
+def share_output(ids, low, attended, count):
+    shape = (count // 2, low.shape[1] // count, attended.shape[1])
+    return pl.pallas_call(
+        share_kernel,
+        in_specs=[SCALAR, NEAR, NEAR],
+        out_specs=[NEAR] * 2,
+        out_shape=[jax.ShapeDtypeStruct(shape, f32), jax.ShapeDtypeStruct(shape, bf16)],
+        compiler_params=room(16),
+        cost_estimate=HINT,
+        name="share_output",
+    )(ids, *near(low, attended))
+
+
+def merge_kernel(gq_ref, kept_ref, given_ref, mine_ref, other_ref, out_ref):
+    out_ref[:, 0:HEAD, :] = gq_ref[...]
+    out_ref[:, HEAD : 3 * HEAD, :] = (kept_ref[...] + given_ref[...].astype(f32)).astype(bf16)
+    lanes = out_ref.shape[2]
+    slots = mine_ref.shape[1]
+    for c in range(mine_ref.shape[2] // lanes):
+        span = slice(c * lanes, (c + 1) * lanes)
+        both = mine_ref[:, :, span] + other_ref[:, :, span].astype(f32)
+        out_ref[:, 3 * HEAD + c * slots : 3 * HEAD + (c + 1) * slots, :] = both.astype(bf16)
+
+
+def merge(gq, kept, given, mine, other):
+    half, _, rows = gq.shape
+    extra = mine.shape[1] * mine.shape[2] // rows
+    return pl.pallas_call(
+        merge_kernel,
+        in_specs=[NEAR] * 5,
+        out_specs=NEAR,
+        out_shape=jax.ShapeDtypeStruct((half, 3 * HEAD + extra, rows), bf16),
+        compiler_params=room(8),
+        cost_estimate=HINT,
+        name="merge",
+    )(*near(gq, kept, given, mine, other))
+
+
+def home_kernel(home_ref, q_ref, v_ref, k_ref, grad_out, slice_out):
+    rows = home_ref.shape[2]
+    grad = 0.0
+    for i, weight in enumerate((q_ref, v_ref, k_ref)):
+        across = home_ref[:, i * HEAD : (i + 1) * HEAD, :].reshape(-1, rows)
+        grad = grad + lax.dot_general(across.T, weight[...], LAST, preferred_element_type=f32)
+    grad_out[...] = grad.astype(bf16)
+    slots = slice_out.shape[0]
+    for c in range(slice_out.shape[1] // rows):
+        at = 3 * HEAD + c * slots
+        whole = jnp.sum(home_ref[:, at : at + slots, :].astype(f32), axis=0)
+        slice_out[:, c * rows : (c + 1) * rows] = whole.astype(bf16)
+
+
+def go_home(home, weights, slots):
+    rows = home.shape[2]
+    width, columns = weights[0].shape
+    return pl.pallas_call(
+        home_kernel,
+        in_specs=[NEAR] * 4,
+        out_specs=[NEAR] * 2,
+        out_shape=[
+            jax.ShapeDtypeStruct((rows, width), bf16),
+            jax.ShapeDtypeStruct((slots, columns), bf16),
+        ],
+        cost_estimate=HINT,
+        name="go_home",
+    )(home, *weights)
+
+
+def input_back_kernel(x_ref, mine_ref, other_ref, gain_ref, grad_ref, sums_ref, grad_out, sums_out):
+    x = x_ref[...].astype(f32)
+    center = x - jnp.mean(x, axis=1, keepdims=True)
+    scale = lax.rsqrt(jnp.mean(center * center, axis=1, keepdims=True) + 1e-05)
+    normed = center * scale
+    grad = mine_ref[...].astype(f32) + other_ref[...].astype(f32)
+    sums = [jnp.sum(grad * normed, axis=0, keepdims=True), jnp.sum(grad, axis=0, keepdims=True), sums_ref[...]]
+    sums = jnp.concatenate(sums, axis=0)
+    for b in range(sums_out.shape[0]):
+        sums_out[b] = sums
+    grad = grad * gain_ref[...]
+    inner = jnp.mean(grad * normed, axis=1, keepdims=True)
+    grad_out[...] = grad_ref[...] + scale * (grad - jnp.mean(grad, axis=1, keepdims=True) - normed * inner)
+
+
+def input_back(x, mine, other, gain, grad_middle, sums, count):
+    rows, width = x.shape
+    return pl.pallas_call(
+        input_back_kernel,
+        in_specs=[NEAR] * 6,
+        out_specs=[NEAR] * 2,
+        out_shape=[
+            jax.ShapeDtypeStruct((rows, width), f32),
+            jax.ShapeDtypeStruct((count, 4, width), f32),
+        ],
+        compiler_params=room(16),
+        cost_estimate=HINT,
+        name="input_back",
+    )(x, mine, other, gain.reshape(1, width), grad_middle, sums)
+
+
+def through_kernel(g_ref, down_ref, out_ref):
+    out_ref[...] = jnp.dot(g_ref[...], down_ref[...], preferred_element_type=f32).astype(bf16)
+
+
+def through(g, weight):
+    total, width = g.shape
+    hidden = weight.shape[1]
+    tile = 2 * FT
+    return pl.pallas_call(
+        through_kernel,
+        grid=(hidden // tile,),
+        in_specs=[
+            pl.BlockSpec((total, width), lambda i: (0, 0), pipeline_mode=pl.Buffered(1)),
+            pl.BlockSpec((width, tile), lambda i: (0, i)),
+        ],
+        out_specs=pl.BlockSpec((total, tile), lambda i: (0, i)),
+        out_shape=jax.ShapeDtypeStruct((total, hidden), bf16),
+        cost_estimate=pl.CostEstimate(
+            flops=2 * total * width * hidden, bytes_accessed=8 * total * width, transcendentals=0
+        ),
+        name="through",
+    )(g, weight)
+
+
+def ffn_kernel(h_ref, g_ref, grad_ref, up_ref, *outs):
+    up_out, down_out = outs[-2:]
+    steps = h_ref.shape[0] // TT
+
+    def product(j):
+        return jnp.dot(h_ref[j * TT : (j + 1) * TT, :], up_ref[...], preferred_element_type=f32)
+
+    pre = product(0)
+    for j in range(steps):
+        later = product(j + 1) if j + 1 < steps else None
+        span = slice(j * TT, (j + 1) * TT)
+        act, grad_pre = gelu_both(pre, grad_ref[span, :].astype(f32))
+        up = lax.dot_general(h_ref[span, :], grad_pre, FIRST, preferred_element_type=f32)
+        down = lax.dot_general(g_ref[span, :], act, FIRST, preferred_element_type=f32)
+        if j == 0:
+            up_out[...] = up
+            down_out[...] = down
+        else:
+            up_out[...] += up
+            down_out[...] += down
+        pre = later
+
+
+def ffn_grads(h, g, grad, up_weight, tiles, held):
+    total, width = h.shape
+    hidden = up_weight.shape[1]
+    first, last = tiles
+    tokens = pl.BlockSpec((total, width), lambda i: (0, 0), pipeline_mode=pl.Buffered(1))
+    units = pl.BlockSpec((width, FT), lambda i: (0, first + i))
+    return pl.pallas_call(
+        ffn_kernel,
+        grid=(last - first,),
+        in_specs=[tokens, tokens, pl.BlockSpec((total, FT), lambda i: (0, first + i)), units] + [FAR] * len(held),
+        out_specs=[units] * 2,
+        out_shape=[jax.ShapeDtypeStruct((width, hidden), f32)] * 2,
+        input_output_aliases={4: 0, 5: 1} if held else {},
+        cost_estimate=pl.CostEstimate(
+            flops=6 * total * width * FT * (last - first), bytes_accessed=4 * total * width, transcendentals=0
+        ),
+        name="ffn_grads",
+    )(h, g, grad, up_weight, *held)
+
+
+def finish_heads_kernel(ids_ref, *refs):
+    heads, outs = refs[:4], refs[4:]
+    row, part = (ids_ref[0] >> 1) & 1, ids_ref[0] & 1
+    wide = heads[0].shape[2]
+    for k, x in ((0, part), (1, 1 - part)):
+        rows = pl.ds(pl.multiple_of(x * wide, wide), wide)
+        for i in range(3):
+            this = heads[k][0, i * HEAD : (i + 1) * HEAD, :]
+            that = heads[k + 2][0, i * HEAD : (i + 1) * HEAD, :]
+            pair = [jnp.where(row == 0, this, that), jnp.where(row == 0, that, this)]
+            outs[i][rows, :] = jnp.concatenate(pair, axis=0).T.astype(f32)
+
+
+def finish_rows_kernel(ids_ref, *refs):
+    pieces, out_ref = refs[:4], refs[4]
+    slots = pieces[0].shape[1]
+    for k in range(4):
+        for s in range(4):
+            at = pl.multiple_of((((ids_ref[0] - 4 * s) & 15) ^ k) * slots, slots)
+            out_ref[pl.ds(at, slots), :] = pieces[k][s].astype(f32)
+
+
+def finish_rows(ids, pieces, width, columns):
+    return pl.pallas_call(
+        finish_rows_kernel,
+        in_specs=[SCALAR] + [NEAR] * 4,
+        out_specs=NEAR,
+        out_shape=jax.ShapeDtypeStruct((width, columns), f32),
+        compiler_params=room(16),
+        cost_estimate=HINT,
+        name="finish_rows",
+    )(ids, *near(*pieces))
+
+
+def finish_heads(ids, pieces, width, columns):
+    block = pl.BlockSpec((width, columns // 4), lambda s, ids: (0, ((ids[0] - 4 * s) & 15) >> 2))
+    return pl.pallas_call(
+        finish_heads_kernel,
+        grid_spec=pltpu.PrefetchScalarGridSpec(
+            num_scalar_prefetch=1,
+            grid=(4,),
+            in_specs=[pl.BlockSpec((1,) + p.shape[1:], lambda s, ids: (s, 0, 0)) for p in pieces],
+            out_specs=[block] * 3,
+        ),
+        out_shape=[jax.ShapeDtypeStruct((width, columns), f32)] * 3,
+        cost_estimate=HINT,
+        name="finish_heads",
+    )(ids, *pieces)
+
+
+def shuffle(block, target):
+    return lax.ppermute(block, "blk", [(i, target(i)) for i in range(16)])
+
+
+def over_core(block):
+    return lax.ppermute(block, "tp", [(0, 1), (1, 0)])
+
+
+def send_column(unit):
+    return (unit,) + tuple(shuffle(unit, lambda i, s=s: (i + 4 * s) % 16) for s in (1, 2, 3))
+
+
+def stack_column(parts, *first):
+    return jnp.stack(lax.optimization_barrier(parts + first)[:4])
+
+
+def gather_plane(column):
+    return (column,) + tuple(shuffle(column, lambda i, k=k: i ^ k) for k in (1, 2, 3))
+
+
+def after(value, *first):
+    return lax.optimization_barrier((value,) + first)[0]
+
+
+def fast_body(
+    tokens,
+    first_gain,
+    first_bias,
+    second_gain,
+    second_bias,
+    query_weight,
+    key_weight,
+    value_weight,
+    output_weight,
+    up_weight,
+    down_weight,
+    cotangent,
+    scene_len,
+):
+    count = lax.axis_size("blk")
+    place = lax.axis_index("blk")
+    side = lax.axis_index("tp")
+    rows, width = tokens.shape
+    columns = query_weight.shape[1]
+    heads_here = columns // HEAD
+    share = count // heads_here
+    scale = HEAD ** (-0.5)
+    ids = jnp.stack([place, side])
+    half_at = side.astype(jnp.uint32) * jnp.uint32(rows // 2)
+    head_at = (place.astype(jnp.uint32) >> 1) * jnp.uint32(HEAD)
+    alike = [list(range(r, count, share)) for r in range(share)]
+
+    def half_of(block):
+        return lax.dynamic_slice(block, (half_at, jnp.uint32(0)), (rows // 2, width))
+
+    def head_of(weight):
+        return lax.dynamic_slice(weight, (jnp.uint32(0), head_at), (width, HEAD))
+
+    g_all = lax.all_gather(half_of(cotangent), ("blk", "tp"), axis=0, tiled=True)
+    column = jnp.stack(send_column(half_of(tokens)))
+
+    head_query = head_of(query_weight) * jnp.asarray(scale, bf16)
+    head_key, head_value = head_of(key_weight), head_of(value_weight)
+    head_t = jnp.concatenate([head_query, head_key, head_value], axis=1).T
+    head_n = jnp.concatenate([head_key, head_query, head_value, jnp.zeros_like(head_value)], axis=1)
+    params = (first_gain.reshape(1, -1), first_bias.reshape(1, -1), key_weight, value_weight, head_t, head_n)
+
+    across_x = shuffle(column, lambda i: i ^ 1)
+    across_y = shuffle(column, lambda i: i ^ 2)
+    made = project_blocks(0, ids, column, over_core(column), params, count, ())
+    across_y = after(across_y, made[0])
+    diagonal = shuffle(across_y, lambda i: i ^ 1)
+    for flip, piece in ((1, after(across_x, across_y)), (2, across_y), (3, diagonal)):
+        piece = after(piece, made[0]) if piece is diagonal else piece
+        made = project_blocks(flip, ids, piece, over_core(piece), params, count, made)
+    h1_all, keys, values, head_t, head_n = made
+
+    attended, branch = attend(
+        ids, scene_len, h1_all, keys.reshape(-1, columns), values.reshape(-1, columns), query_weight, output_weight
+    )
+    inputs = tokens.astype(f32)
+    middle = inputs + (branch.astype(f32) + over_core(branch).astype(f32))
+    h2 = layer_norm(middle, second_gain, second_bias).astype(bf16)
+    h2_all = lax.all_gather(half_of(h2), ("blk", "tp"), axis=0, tiled=True)
+
+    feed, grad_two = own_ffn(h2, cotangent, up_weight, down_weight)
+    grad_middle, grad_middle_low, second_sums, to_heads = norm_back(
+        middle, grad_two, over_core(grad_two), second_gain, cotangent, output_weight
+    )
+    ga = lax.all_to_all(to_heads, "blk", 0, 0, tiled=True, axis_index_groups=alike)
+    p = prepare(ids, scene_len, after(head_t, to_heads, g_all), head_n)
+    grad_q, kept, given, slice_kept, slice_given = back(ids, scene_len, p, ga, head_t, head_n, h1_all)
+
+    output_kept, output_given = share_output(ids, after(grad_middle_low, slice_given), attended, count)
+    output_other = shuffle(output_given, lambda i: i ^ 1)
+    head_slice = (slice_kept + shuffle(slice_given, lambda i: i ^ 1).astype(f32)).astype(bf16)
+    parts = send_column(head_slice)
+
+    given = after(given, head_slice)
+    given = shuffle(given, lambda i: i ^ 1)
+    grad_all = through(after(g_all, head_slice), down_weight)
+    column = stack_column(parts, grad_all)
+    parcel = merge(after(grad_q, column), kept, given, output_kept, output_other)
+    home = lax.all_to_all(parcel, "blk", 0, 0, tiled=True, axis_index_groups=alike)
+    heads = gather_plane(column)
+
+    feed = after(feed, parcel)
+    layer_out = (middle + (feed.astype(f32) + over_core(feed).astype(f32))).astype(bf16)
+    held = ffn_grads(after(h2_all, column), g_all, grad_all, up_weight, (0, 4), ())
+
+    home = after(home, held[0])
+    grad_one, output_slice = go_home(home, (query_weight, value_weight, key_weight), width // count)
+    input_grad, norm_part = input_back(
+        tokens, grad_one, over_core(grad_one), first_gain, grad_middle, second_sums, count
+    )
+    norm_parts = lax.all_to_all(norm_part, "blk", 0, 0, tiled=True)
+
+    parts = send_column(output_slice)
+    up_grad, down_grad = ffn_grads(
+        after(h2_all, norm_part, *heads), g_all, grad_all, up_weight, (4, 8), held
+    )
+    rest = gather_plane(stack_column(parts, up_grad, norm_parts))
+    norm_sums = jnp.sum(after(norm_parts, up_grad), axis=0)
+    heads = (after(heads[0], up_grad),) + heads[1:]
+    query_grad, value_grad, key_grad = finish_heads(ids, heads, width, columns)
+    output_grad = finish_rows(ids, rest, width, columns)
+    return (
+        layer_out,
+        input_grad,
+        norm_sums[0],
+        norm_sums[1],
+        norm_sums[2],
+        norm_sums[3],
+        query_grad,
+        key_grad,
+        value_grad,
+        output_grad,
+        up_grad,
+        down_grad,
+    )
+
+
 def solution(mesh):
+    body = fast_body if mesh.shape["blk"] == 16 else ring_body
     return jax.shard_map(
         body,
         mesh=mesh,

time: 1690 us -> 253 us (0.15)
  waiting for transfers between devices: 1260 us -> 39.3 us
  Pallas kernels: 0 us -> 117 us
  loops' own time: 80.1 us -> 0 us
  other arithmetic: 76.1 us -> 9.16 us
  local copies, waits for them, and re-layouts: 70.4 us -> 10.8 us
  matrix products: 47.2 us -> 0 us
  starting transfers between devices: 102 us -> 61.6 us
  blocking collectives: 36.2 us -> 0 us
    reduce_scatter x6 -> x0, waiting for transfers between devices: 666 us -> none  [the longest x1 181 us: body(): lax.psum_scatter(up_grad, 'blk', scatter_dimension=0, tiled=True)]
    all_gather x6 -> x2, waiting for transfers between devices: 326 us -> 0.01 us  [the longest x1 0.01 us: fast_body(): lax.all_gather(half_of(cotangent), ('blk', 'tp'), axis=0, tiled=True)]
    ppermute x92 -> x29, waiting for transfers between devices: 159 us -> 37.4 us  [the longest x21 31 us: shuffle(): return lax.ppermute(block, 'blk', [(i, target(i)) for i in range(16)])]
    pallas_call x0 -> x18, Pallas kernels: none -> 117 us  [the longest x2 39.2 us: ffn_grads(): pl.pallas_call(ffn_kernel, grid=(last - first,), in_specs=[tokens, tokens...]
    another operation x32 -> x0, loops' own time: 80.1 us -> none  [the longest x1 40.1 us: body(): lax.fori_loop(1, steps + 1, turn_backward, (grad_query, keys, values, emp...]
    unnamed x17 -> x2, waiting for transfers between devices: 78.4 us -> 0.03 us
    ppermute x92 -> x29, starting transfers between devices: 101 us -> 38.1 us  [the longest x21 36.6 us: shuffle(): return lax.ppermute(block, 'blk', [(i, target(i)) for i in range(16)])]
    dot_general x38 -> x0, matrix products: 47.2 us -> none  [the longest x1 4.77 us: body(): lax.dot_general(normed_two, grad_before, contract_first, preferred_elemen...]
  transfers between devices with their start and end apart: 108 -> 34, of which waited for: 84 -> 14; matrix products, arithmetic and copies ran while one was open for 8% -> 6% of each run, Pallas kernels for 0% -> 45%
where the time goes in v3:
time: 253 us; the launch traced here: 252 us
  Pallas kernels  117 us (46%)
  starting transfers between devices  61.6 us (24%)
  waiting for transfers between devices  39.3 us (16%)
  between operations  14.5 us (6%)
  local copies, waits for them, and re-layouts  10.8 us (4%)
  other arithmetic  9.16 us (4%)
    pallas_call x2, Pallas kernels, ffn_grads(): pl.pallas_call(ffn_kernel, grid=(last - first,), in_specs=[tokens, tokens...  39.2 us
    ppermute x21, starting transfers between devices, shuffle(): return lax.ppermute(block, 'blk', [(i, target(i)) for i in range(16)])  36.6 us
    ppermute x21, waiting for transfers between devices, shuffle(): return lax.ppermute(block, 'blk', [(i, target(i)) for i in range(16)])  31 us
    pallas_call x4, Pallas kernels, project_blocks(): pl.pallas_call(lambda *refs: project_kernel(flip, *refs), in_specs=[SCALA...  15.2 us
    pallas_call x1, Pallas kernels, through(): pl.pallas_call(through_kernel, grid=(hidden // tile,), in_specs=[pl.Block...  13.3 us
    all_to_all x1, starting transfers between devices, fast_body(): lax.all_to_all(parcel, 'blk', 0, 0, tiled=True, axis_index_groups=alike)  11.7 us
    pallas_call x1, Pallas kernels, back(): pl.pallas_call(back_kernel, grid_spec=pltpu.PrefetchScalarGridSpec(num_sc...  10 us
    pallas_call x1, Pallas kernels, own_ffn(): pl.pallas_call(own_kernel, grid=(hidden // tile,), in_specs=[NEAR, NEAR]...  7.8 us
  transfers between devices with their start and end apart: 34, of which 14 were waited for; matrix products, arithmetic and copies ran while one was open for 6% of the time, Pallas kernels for 45%

profile of v3, /device:TPU:0, one launch (start us, length us, event | category | flops | bytes accessed | tf_op | source)
XLA Modules:
  0.0 252.0 jit_solution(14899204713223797628)
XLA Ops:
  7.3 1.7 constant_dynamic-slice_fusion.1
  9.0 0.9 constant_dynamic-slice_fusion.4
  10.0 5.1 %collective-permute-start.2 = (bf16[64,1024]{1,0:T(8,128)(2,1)S(1)}, bf16[64,1024]{1,0:T(8,128)(2,1)S(1)}, u32[]{:S(2)}, u32[]{:S(2)}) collective-permute-start(bf16[64,1024]{1,0:T(8,128)(2,1)S(1)} %constant_dynamic-slice_fusion.4), channel_id=1, source_target_pairs={{0,24},{2,26},{4,28},{6,30},{8,0},{10,2},{12,4},{14,6},{16,8},{18,... | collective-permute-start | bytes 393224 | tf_op jit(solution)/shard_map/ppermute | solution.py:883
  15.1 1.0 collective-permute-start
  16.1 0.9 fusion.2
  17.0 1.3 dynamic-slice_multiply_fusion
  19.0 7.4 %collective-permute-done.1 = bf16[64,1024]{1,0:T(8,128)(2,1)S(1)} collective-permute-done((bf16[64,1024]{1,0:T(8,128)(2,1)S(1)}, bf16[64,1024]{1,0:T(8,128)(2,1)S(1)}, u32[]{:S(2)}, u32[]{:S(2)}) %collective-permute-start.1) | collective-permute-done | bytes 131104 | tf_op jit(solution)/shard_map/ppermute | solution.py:883
  26.4 1.6 collective-permute-start.3
  28.0 1.5 collective-permute-start.7
  29.5 1.1 constant_dynamic-slice_fusion.3
  30.6 1.0 maximum_bitcast_fusion
  31.7 1.2 copy.42.refs_7_
  33.1 1.3 maximum_maximum_fusion.refs_8_
  34.4 3.9 %project_blocks.4 = (bf16[16,128,1024]{2,1,0:T(8,128)(2,1)S(1)}, bf16[16,128,512]{2,1,0:T(8,128)(2,1)S(1)}, bf16[16,128,512]{2,1,0:T(8,128)(2,1)S(1)}, bf16[16,1...) custom-call(s32[2]{0:T(128)S(1)} %pad_add_fusion.refs_0_.ids_ref, bf16[4,64,1024]{2,1,0:T(8,128)(2,1)S(1)} %pad_maximum_fusion.1.refs_1_, ...), custom_call_target="tpu_custom_call" | custom-call | flops 1 | bytes 1 | tf_op jit(solution)/shard_map/project_blocks/pallas_call | solution.py:351
  38.4 1.4 collective-permute-done.3.refs_1_
  39.7 3.8 %collective-permute-done.7.refs_1_ = bf16[4,64,1024]{2,1,0:T(8,128)(2,1)} collective-permute-done((bf16[4,64,1024]{2,1,0:T(8,128)(2,1)S(1)}, bf16[4,64,1024]{2,1,0:T(8,128)(2,1)}, u32[]{:S(2)}, u32[]{:S(2)}) %collective-permute-start.7) | collective-permute-done | bytes 524320 | tf_op jit(solution)/shard_map/ppermute | solution.py:883
  44.0 2.6 %collective-permute-start.5 = (bf16[4,64,1024]{2,1,0:T(8,128)(2,1)}, bf16[4,64,1024]{2,1,0:T(8,128)(2,1)S(1)}, u32[]{:S(2)}, u32[]{:S(2)}) collective-permute-start(bf16[4,64,1024]{2,1,0:T(8,128)(2,1)} %collective-permute-done.3.refs_1_), channel_id=1, source_target_pairs={{0,2},{2,0},{4,6},{6,4},{8,10},{10,8},{12,14},{14,12},{16,18},{18,... | collective-permute-start | bytes 1572872 | tf_op jit(solution)/shard_map/ppermute | solution.py:883
  46.6 3.9 %project_blocks.5 = (bf16[16,128,1024]{2,1,0:T(8,128)(2,1)S(1)}, bf16[16,128,512]{2,1,0:T(8,128)(2,1)S(1)}, bf16[16,128,512]{2,1,0:T(8,128)(2,1)S(1)}, bf16[16,1...) custom-call(s32[2]{0:T(128)S(1)} %pad_add_fusion.refs_0_.ids_ref, ...), custom_call_target="tpu_custom_call", output_to_operand_aliasing={{0}: (9, {}), {1}: (10, {}), {2}: (11, {}), {3}: (12, {}), ... | custom-call | flops 1 | bytes 1 | tf_op jit(solution)/shard_map/project_blocks/pallas_call | solution.py:351
  50.5 3.9 %project_blocks.6 = (bf16[16,128,1024]{2,1,0:T(8,128)(2,1)S(1)}, bf16[16,128,512]{2,1,0:T(8,128)(2,1)S(1)}, bf16[16,128,512]{2,1,0:T(8,128)(2,1)S(1)}, bf16[16,1...) custom-call(s32[2]{0:T(128)S(1)} %pad_add_fusion.refs_0_.ids_ref, ...), custom_call_target="tpu_custom_call", output_to_operand_aliasing={{0}: (9, {}), {1}: (10, {}), {2}: (11, {}), {3}: (12, {}), ... | custom-call | flops 1 | bytes 1 | tf_op jit(solution)/shard_map/project_blocks/pallas_call | solution.py:351
  54.5 4.4 %collective-permute-done.5.refs_1_ = bf16[4,64,1024]{2,1,0:T(8,128)(2,1)S(1)} collective-permute-done((bf16[4,64,1024]{2,1,0:T(8,128)(2,1)}, bf16[4,64,1024]{2,1,0:T(8,128)(2,1)S(1)}, u32[]{:S(2)}, u32[]{:S(2)}) %collective-permute-start.5) | collective-permute-done | bytes 524320 | tf_op jit(solution)/shard_map/ppermute | solution.py:883
  58.9 2.2 collective-permute-done.9.refs_2_
  61.1 3.4 %project_blocks.7 = (bf16[16,128,1024]{2,1,0:T(8,128)(2,1)S(1)}, bf16[16,128,512]{2,1,0:T(8,128)(2,1)S(1)}, bf16[16,128,512]{2,1,0:T(8,128)(2,1)S(1)}, bf16[16,1...) custom-call(s32[2]{0:T(128)S(1)} %pad_add_fusion.refs_0_.ids_ref, ...), custom_call_target="tpu_custom_call", output_to_operand_aliasing={{0}: (9, {}), {1}: (10, {}), {2}: (11, {}), {3}: (12, {}), ... | custom-call | flops 1 | bytes 1 | tf_op jit(solution)/shard_map/project_blocks/pallas_call | solution.py:351
  64.7 6.5 %attend.1 = (bf16[128,512]{1,0:T(8,128)(2,1)S(1)}, bf16[128,1024]{1,0:T(8,128)(2,1)S(1)}) custom-call(s32[2]{0:T(128)S(1)} %pad_add_fusion.refs_0_.ids_ref, s32[4]{0:T(128)S(1)} %copy-done.20, bf16[16,128,1024]{2,1,0:T(8,128)(2,1)S(1)} %get-tuple-element.98.h_ref, bf16[2048,512]{1,0:T(8,128)(2,1)S(1)} %bitcast.29, bf16[2048,512]{1,0:T(8,128)(2,1)S(1)} %bitcast.30, ...), custom_call_target="tpu_custom_call" | custom-call | flops 1 | bytes 1 | tf_op jit(solution)/shard_map/attend/pallas_call | solution.py:397
  71.4 1.4 collective-permute-done.10
  74.1 7.8 %own_ffn.1 = (bf16[128,1024]{1,0:T(8,128)(2,1)}, bf16[128,1024]{1,0:T(8,128)(2,1)}) custom-call(bf16[128,1024]{1,0:T(8,128)(2,1)S(1)} %add_convert_fusion.1.h_ref, bf16[128,1024]{1,0:T(8,128)(2,1)S(1)} %copy-done.9, bf16[1024,2048]{1,0:T(8,128)(2,1)} %up_ref.5, bf16[1024,2048]{1,0:T(8,128)(2,1)} %down_ref.3), custom_call_target="tpu_custom_call" | custom-call | flops 1 | bytes 1 | tf_op jit(solution)/shard_map/own_ffn/pallas_call | solution.py:446
  82.1 1.5 collective-permute-done.11.other_ref
  83.7 0.9 copy-done.12
  84.6 1.5 norm_back.1
  86.1 6.3 %all-to-all-start = ((bf16[8,64,128]{2,1,0:T(8,128)(2,1)}), bf16[8,64,128]{2,1,0:T(8,128)(2,1)S(1)}, u32[]{:S(2)}, u32[]{:S(2)}) async-start(bf16[8,64,128]{2,1,0:T(8,128)(2,1)} %get-tuple-element.105), calls=%async_computation | async-start | bytes 262144 | tf_op jit(solution)/shard_map/all_to_all | solution.py:971
  92.4 5.9 %prepare.1.p_ref = bf16[4,2048,256]{2,1,0:T(8,128)(2,1)} custom-call(s32[2]{0:T(128)} %copy-done.16, s32[4]{0:T(128)} %len_ref.5, bf16[16,192,128]{2,1,0:T(8,128)(2,1)} %copy-done.4, bf16[2048,256]{1,0:T(8,128)(2,1)} %bitcast.31), custom_call_target="tpu_custom_call" | custom-call | flops 1 | bytes 1 | tf_op jit(solution)/shard_map/prepare/pallas_call | solution.py:539
  98.3 1.9 all-to-all-done.ga_ref
  100.9 10.0 %back.1 = (bf16[8,64,128]{2,1,0:T(8,128)(2,1)}, f32[8,128,128]{2,1,0:T(8,128)}, bf16[8,128,128]{2,1,0:T(8,128)(2,1)}, f32[192,512]{1,0:T(8,128)}, bf16[192,512]{1,0:T(8,128)(2,1)}) custom-call(s32[2]{0:T(128)} %copy-done.16, s32[4]{0:T(128)} %len_ref.5, bf16[4,2048,256]{2,1,0:T(8,128)(2,1)} %prepare.1.p_ref, bf16[8,64,128]{2,1,0:T(8,128)(2,1)} %copy-done.24, ...), custom_call_target="tpu_custom_call" | custom-call | flops 1 | bytes 1 | tf_op jit(solution)/shard_map/back/pallas_call | solution.py:631
  110.9 2.8 %collective-permute-start.12 = (bf16[192,512]{1,0:T(8,128)(2,1)}, bf16[192,512]{1,0:T(8,128)(2,1)S(1)}, u32[]{:S(2)}, u32[]{:S(2)}) collective-permute-start(bf16[192,512]{1,0:T(8,128)(2,1)} %get-tuple-element.110), channel_id=1, source_target_pairs={{0,2},{2,0},{4,6},{6,4},{8,10},{10,8},{12,14},{14,12},{16,18},{18,... | collective-permute-start | bytes 589832 | tf_op jit(solution)/shard_map/ppermute | solution.py:883
  113.7 1.8 share_output.1
  115.5 3.9 %collective-permute-done.12 = bf16[192,512]{1,0:T(8,128)(2,1)S(1)} collective-permute-done((bf16[192,512]{1,0:T(8,128)(2,1)}, bf16[192,512]{1,0:T(8,128)(2,1)S(1)}, u32[]{:S(2)}, u32[]{:S(2)}) %collective-permute-start.12) | collective-permute-done | bytes 196640 | tf_op jit(solution)/shard_map/ppermute | solution.py:883
  119.3 1.7 add_convert_fusion.2
  121.5 2.3 collective-permute-start.14
  123.8 1.5 collective-permute-start.15
  125.3 2.2 collective-permute-start.16
  127.5 13.3 %through.1.grad_ref = bf16[2048,2048]{1,0:T(8,128)(2,1)} custom-call(bf16[2048,1024]{1,0:T(8,128)(2,1)} %all-gather.3.cloned.1.call-done.g_ref, bf16[1024,2048]{1,0:T(8,128)(2,1)} %down_ref.3), custom_call_target="tpu_custom_call" | custom-call | flops 8589934592 | bytes 16777216 | tf_op jit(solution)/shard_map/through/pallas_call | solution.py:773
  140.8 2.3 collective-permute-done.14
  143.1 2.3 pad_maximum_fusion.refs_0_
  145.4 2.1 merge.1
  147.5 11.7 %all-to-all-start.1 = ((bf16[8,448,128]{2,1,0:T(8,128)(2,1)}), bf16[8,448,128]{2,1,0:T(8,128)(2,1)S(1)}, u32[]{:S(2)}, u32[]{:S(2)}) async-start(bf16[8,448,128]{2,1,0:T(8,128)(2,1)} %merge.1), calls=%async_computation.1 | async-start | bytes 1835008 | tf_op jit(solution)/shard_map/all_to_all | solution.py:985
  159.2 1.4 collective-permute-start.20
  160.6 2.0 collective-permute-start.21
  162.8 19.6 %ffn_grads.2 = (f32[1024,2048]{1,0:T(8,128)}, f32[1024,2048]{1,0:T(8,128)}) custom-call(bf16[2048,1024]{1,0:T(8,128)(2,1)} %all-gather.5.cloned.1.call-done.h_ref, bf16[2048,1024]{1,0:T(8,128)(2,1)} %all-gather.3.cloned.1.call-done.g_ref, bf16[2048,2048]{1,0:T(8,128)(2,1)} %through.1.grad_ref, bf16[1024,2048]{1,0:T(8,128)(2,1)} %up_ref.5), custom_call_target="tpu_custom_call" | custom-call | flops 12884901888 | bytes 8388608 | tf_op jit(solution)/shard_map/ffn_grads/pallas_call | solution.py:818
  182.4 0.9 copy-done.21
  183.3 4.0 %go_home.1 = (bf16[128,1024]{1,0:T(8,128)(2,1)}, bf16[64,512]{1,0:T(8,128)(2,1)}) custom-call(bf16[8,448,128]{2,1,0:T(8,128)(2,1)} %copy-done.21, bf16[1024,512]{1,0:T(8,128)(2,1)} %q_ref.3, bf16[1024,512]{1,0:T(8,128)(2,1)} %v_ref.1, bf16[1024,512]{1,0:T(8,128)(2,1)} %k_ref.1), custom_call_target="tpu_custom_call" | custom-call | flops 1 | bytes 1 | tf_op jit(solution)/shard_map/go_home/pallas_call | solution.py:721
  187.8 1.2 collective-permute-done.19.other_ref
  189.0 2.0 collective-permute-start.23
  191.0 0.9 copy-done.11
  191.9 1.3 input_back.1
  193.2 5.4 %all-to-all-start.2 = ((f32[16,4,1024]{2,1,0:T(4,128)}), f32[16,4,1024]{2,1,0:T(4,128)S(1)}, u32[]{:S(2)}, u32[]{:S(2)}) async-start(f32[16,4,1024]{2,1,0:T(4,128)} %get-tuple-element.133), calls=%async_computation.2 | async-start | bytes 524288 | tf_op jit(solution)/shard_map/all_to_all | solution.py:997
  198.6 2.9 %collective-permute-start.24 = (bf16[64,512]{1,0:T(8,128)(2,1)}, bf16[64,512]{1,0:T(8,128)(2,1)S(1)}, u32[]{:S(2)}, u32[]{:S(2)}) collective-permute-start(bf16[64,512]{1,0:T(8,128)(2,1)} %get-tuple-element.143), channel_id=1, source_target_pairs={{0,16},{2,18},{4,20},{6,22},{8,24},{10,26},{12,28},{14,30},{16,0},... | collective-permute-start | bytes 196616 | tf_op jit(solution)/shard_map/ppermute | solution.py:883
  201.5 4.7 %collective-permute-done.21.refs_2_ = bf16[4,192,512]{2,1,0:T(8,128)(2,1)} collective-permute-done((bf16[4,192,512]{2,1,0:T(8,128)(2,1)}, bf16[4,192,512]{2,1,0:T(8,128)(2,1)}, u32[]{:S(2)}, u32[]{:S(2)}) %collective-permute-start.21) | collective-permute-done | bytes 786464 | tf_op jit(solution)/shard_map/ppermute | solution.py:883
  206.2 3.6 %collective-permute-start.25 = (bf16[64,512]{1,0:T(8,128)(2,1)}, bf16[64,512]{1,0:T(8,128)(2,1)S(1)}, u32[]{:S(2)}, u32[]{:S(2)}) collective-permute-start(bf16[64,512]{1,0:T(8,128)(2,1)} %get-tuple-element.143), channel_id=1, source_target_pairs={{0,24},{2,26},{4,28},{6,30},{8,0},{10,2},{12,4},{14,6},{16,8},{18,... | collective-permute-start | bytes 196616 | tf_op jit(solution)/shard_map/ppermute | solution.py:883
  209.8 19.6 %ffn_grads.3 = (f32[1024,2048]{1,0:T(8,128)}, f32[1024,2048]{1,0:T(8,128)}) custom-call(bf16[2048,1024]{1,0:T(8,128)(2,1)} %all-gather.5.cloned.1.call-done.h_ref, bf16[2048,1024]{1,0:T(8,128)(2,1)} %all-gather.3.cloned.1.call-done.g_ref, bf16[2048,2048]{1,0:T(8,128)(2,1)} %through.1.grad_ref, ...), custom_call_target="tpu_custom_call", output_to_operand_aliasing={{0}: (4, {}), {1}: (5, {})} | custom-call | flops 12884901888 | bytes 8388608 | tf_op jit(solution)/shard_map/ffn_grads/pallas_call | solution.py:818
  229.6 1.6 collective-permute-start.26
  231.1 2.0 collective-permute-start.28
  233.1 0.8 add_convert_fusion
  233.9 6.1 %finish_heads.1 = (f32[1024,512]{1,0:T(8,128)}, f32[1024,512]{1,0:T(8,128)}, f32[1024,512]{1,0:T(8,128)}) custom-call(s32[2]{0:T(128)} %copy-done.16, bf16[4,192,512]{2,1,0:T(8,128)(2,1)} %pad_maximum_fusion.refs_0_, bf16[4,192,512]{2,1,0:T(8,128)(2,1)} %collective-permute-done.20.refs_1_, bf16[4,192,512]{2,1,0:T(8,128)(2,1)} %collective-permute-done.21.refs_2_, ...), custom_call_target="tpu_custom_call" | custom-call | flops 1 | bytes 1 | tf_op jit(solution)/shard_map/finish_heads/pallas_call | solution.py:868
  240.7 2.4 collective-permute-done.27.refs_2_
  243.1 2.0 finish_rows.1
  (104 shorter events, 5.9 us)
Async XLA Ops:
  7.2 27.2 %copy-start.2 = (bf16[1024,512]{1,0:T(8,128)(2,1)S(1)}, bf16[1024,512]{1,0:T(8,128)(2,1)}, u32[]{:S(2)}) copy-start(bf16[1024,512]{1,0:T(8,128)(2,1)} %v_ref.1) | copy-start | bytes 3145732
  7.2 27.2 %copy-start.1 = (bf16[1024,512]{1,0:T(8,128)(2,1)S(1)}, bf16[1024,512]{1,0:T(8,128)(2,1)}, u32[]{:S(2)}) copy-start(bf16[1024,512]{1,0:T(8,128)(2,1)} %k_ref.1) | copy-start | bytes 3145732
  7.2 27.2 %copy-start.14 = (f32[1024]{0:T(1024)S(1)}, f32[1024]{0:T(1024)}, u32[]{:S(2)}) copy-start(f32[1024]{0:T(1024)} %param.14) | copy-start | bytes 12292
  7.2 27.2 %copy-start.15 = (f32[1024]{0:T(1024)S(1)}, f32[1024]{0:T(1024)}, u32[]{:S(2)}) copy-start(f32[1024]{0:T(1024)} %param.15) | copy-start | bytes 12292
  7.2 85.1 %all-gather.3.cloned.1.call-start = ((), (), s32[]{:S(2)}) async-start(), calls=%async_computation.3 | async-start | bytes 4325376 | tf_op jit(solution)/shard_map/all_gather | solution.py:940
  9.0 153.8 %all-gather.5.cloned.1.call-start = ((), (), s32[]{:S(2)}) async-start(), calls=%async_computation.4 | async-start | bytes 4325376 | tf_op jit(solution)/shard_map/all_gather | solution.py:965
  10.0 9.0 %collective-permute-start.2 = (bf16[64,1024]{1,0:T(8,128)(2,1)S(1)}, bf16[64,1024]{1,0:T(8,128)(2,1)S(1)}, u32[]{:S(2)}, u32[]{:S(2)}) collective-permute-start(bf16[64,1024]{1,0:T(8,128)(2,1)S(1)} %constant_dynamic-slice_fusion.4), channel_id=1, source_target_pairs={{0,24},{2,26},{4,28},{6,30},{8,0},{10,2},{12,4},{14,6},{16,8},{18,... | collective-permute-start | bytes 393224 | tf_op jit(solution)/shard_map/ppermute | solution.py:883
  15.1 11.3 %collective-permute-start.1 = (bf16[64,1024]{1,0:T(8,128)(2,1)S(1)}, bf16[64,1024]{1,0:T(8,128)(2,1)S(1)}, u32[]{:S(2)}, u32[]{:S(2)}) collective-permute-start(bf16[64,1024]{1,0:T(8,128)(2,1)S(1)} %constant_dynamic-slice_fusion.4), channel_id=1, source_target_pairs={{0,16},{2,18},{4,20},{6,22},{8,24},{10,26},{12,28},{14,30},{16,0},... | collective-permute-start | bytes 393224 | tf_op jit(solution)/shard_map/ppermute | solution.py:883
  15.1 11.3 %collective-permute-start = (bf16[64,1024]{1,0:T(8,128)(2,1)S(1)}, bf16[64,1024]{1,0:T(8,128)(2,1)S(1)}, u32[]{:S(2)}, u32[]{:S(2)}) collective-permute-start(bf16[64,1024]{1,0:T(8,128)(2,1)S(1)} %constant_dynamic-slice_fusion.4), channel_id=1, source_target_pairs={{0,8},{2,10},{4,12},{6,14},{8,16},{10,18},{12,20},{14,22},{16,24},... | collective-permute-start | bytes 393224 | tf_op jit(solution)/shard_map/ppermute | solution.py:883
  18.3 12.3 %copy-start.22 = (bf16[1024,64]{1,0:T(8,128)(2,1)}, bf16[1024,64]{1,0:T(8,128)(2,1)S(1)}, u32[]{:S(2)}) copy-start(bf16[1024,64]{1,0:T(8,128)(2,1)S(1)} %get-tuple-element.154) | copy-start | bytes 393220
  18.3 12.3 %copy-start.23 = (bf16[1024,64]{1,0:T(8,128)(2,1)}, bf16[1024,64]{1,0:T(8,128)(2,1)S(1)}, u32[]{:S(2)}) copy-start(bf16[1024,64]{1,0:T(8,128)(2,1)S(1)} %get-tuple-element.155) | copy-start | bytes 393220
  26.4 13.3 %collective-permute-start.3 = (bf16[4,64,1024]{2,1,0:T(8,128)(2,1)S(1)}, bf16[4,64,1024]{2,1,0:T(8,128)(2,1)}, u32[]{:S(2)}, u32[]{:S(2)}) collective-permute-start(bf16[4,64,1024]{2,1,0:T(8,128)(2,1)S(1)} %pad_maximum_fusion.1.refs_1_), channel_id=1, source_target_pairs={{0,4},{2,6},{4,0},{6,2},{8,12},{10,14},{12,8},{14,10},{16,20},{18,... | collective-permute-start | bytes 1572872 | tf_op jit(solution)/shard_map/ppermute | solution.py:883
  28.0 6.4 %collective-permute-start.4 = (bf16[4,64,1024]{2,1,0:T(8,128)(2,1)S(1)}, bf16[4,64,1024]{2,1,0:T(8,128)(2,1)}, u32[]{:S(2)}, u32[]{:S(2)}) collective-permute-start(bf16[4,64,1024]{2,1,0:T(8,128)(2,1)S(1)} %pad_maximum_fusion.1.refs_1_), channel_id=1, source_target_pairs={{0,1},{1,0},{2,3},{3,2},{4,5},{5,4},{6,7},{7,6},{8,9},{9,8},{10,11... | collective-permute-start | bytes 1572872 | tf_op jit(solution)/shard_map/ppermute | solution.py:887
  28.0 15.5 %collective-permute-start.7 = (bf16[4,64,1024]{2,1,0:T(8,128)(2,1)S(1)}, bf16[4,64,1024]{2,1,0:T(8,128)(2,1)}, u32[]{:S(2)}, u32[]{:S(2)}) collective-permute-start(bf16[4,64,1024]{2,1,0:T(8,128)(2,1)S(1)} %pad_maximum_fusion.1.refs_1_), channel_id=1, source_target_pairs={{0,2},{2,0},{4,6},{6,4},{8,10},{10,8},{12,14},{14,12},{16,18},{18,... | collective-permute-start | bytes 1572872 | tf_op jit(solution)/shard_map/ppermute | solution.py:883
  33.1 31.5 %copy-start.16 = (s32[2]{0:T(128)}, s32[2]{0:T(128)S(1)}, u32[]{:S(2)}) copy-start(s32[2]{0:T(128)S(1)} %pad_add_fusion.refs_0_.ids_ref) | copy-start | bytes 28
  43.5 3.1 %collective-permute-start.8 = (bf16[4,64,1024]{2,1,0:T(8,128)(2,1)}, bf16[4,64,1024]{2,1,0:T(8,128)(2,1)S(1)}, u32[]{:S(2)}, u32[]{:S(2)}) collective-permute-start(bf16[4,64,1024]{2,1,0:T(8,128)(2,1)} %collective-permute-done.7.refs_1_), channel_id=1, source_target_pairs={{0,1},{1,0},{2,3},{3,2},{4,5},{5,4},{6,7},{7,6},{8,9},{9,8},{10,11... | collective-permute-start | bytes 1572872 | tf_op jit(solution)/shard_map/ppermute | solution.py:887
  43.5 7.0 %collective-permute-start.6 = (bf16[4,64,1024]{2,1,0:T(8,128)(2,1)}, bf16[4,64,1024]{2,1,0:T(8,128)(2,1)S(1)}, u32[]{:S(2)}, u32[]{:S(2)}) collective-permute-start(bf16[4,64,1024]{2,1,0:T(8,128)(2,1)} %collective-permute-done.3.refs_1_), channel_id=1, source_target_pairs={{0,1},{1,0},{2,3},{3,2},{4,5},{5,4},{6,7},{7,6},{8,9},{9,8},{10,11... | collective-permute-start | bytes 1572872 | tf_op jit(solution)/shard_map/ppermute | solution.py:887
  44.0 14.9 %collective-permute-start.5 = (bf16[4,64,1024]{2,1,0:T(8,128)(2,1)}, bf16[4,64,1024]{2,1,0:T(8,128)(2,1)S(1)}, u32[]{:S(2)}, u32[]{:S(2)}) collective-permute-start(bf16[4,64,1024]{2,1,0:T(8,128)(2,1)} %collective-permute-done.3.refs_1_), channel_id=1, source_target_pairs={{0,2},{2,0},{4,6},{6,4},{8,10},{10,8},{12,14},{14,12},{16,18},{18,... | collective-permute-start | bytes 1572872 | tf_op jit(solution)/shard_map/ppermute | solution.py:883
  58.9 2.2 collective-permute-start.9
  61.1 3.5 %copy-start.5 = (bf16[1024,512]{1,0:T(8,128)(2,1)S(1)}, bf16[1024,512]{1,0:T(8,128)(2,1)}, u32[]{:S(2)}) copy-start(bf16[1024,512]{1,0:T(8,128)(2,1)} %q_ref.3) | copy-start | bytes 3145732
  61.1 3.5 %copy-start.6 = (bf16[1024,512]{1,0:T(8,128)(2,1)S(1)}, bf16[1024,512]{1,0:T(8,128)(2,1)}, u32[]{:S(2)}) copy-start(bf16[1024,512]{1,0:T(8,128)(2,1)} %o_ref.3) | copy-start | bytes 3145732
  61.1 3.5 %copy-start.20 = (s32[4]{0:T(128)S(1)}, s32[4]{0:T(128)}, u32[]{:S(2)}) copy-start(s32[4]{0:T(128)} %len_ref.5) | copy-start | bytes 52
  64.6 6.6 %copy-start = (bf16[16,128,1024]{2,1,0:T(8,128)(2,1)}, bf16[16,128,1024]{2,1,0:T(8,128)(2,1)S(1)}, u32[]{:S(2)}) copy-start(bf16[16,128,1024]{2,1,0:T(8,128)(2,1)S(1)} %get-tuple-element.98.h_ref) | copy-start | bytes 12582916
  64.6 6.6 %copy-start.3 = (bf16[16,128,256]{2,1,0:T(8,128)(2,1)}, bf16[16,128,256]{2,1,0:T(8,128)(2,1)S(1)}, u32[]{:S(2)}) copy-start(bf16[16,128,256]{2,1,0:T(8,128)(2,1)S(1)} %get-tuple-element.107) | copy-start | bytes 3145732
  64.6 6.6 %copy-start.4 = (bf16[16,192,128]{2,1,0:T(8,128)(2,1)}, bf16[16,192,128]{2,1,0:T(8,128)(2,1)S(1)}, u32[]{:S(2)}) copy-start(bf16[16,192,128]{2,1,0:T(8,128)(2,1)S(1)} %get-tuple-element.106.t_ref) | copy-start | bytes 2359300
  64.6 8.2 %copy-start.8 = (bf16[128,1024]{1,0:T(8,128)(2,1)S(1)}, bf16[128,1024]{1,0:T(8,128)(2,1)}, u32[]{:S(2)}) copy-start(bf16[128,1024]{1,0:T(8,128)(2,1)} %x_ref.1) | copy-start | bytes 786436
  64.6 8.6 %copy-start.19 = (f32[1024]{0:T(1024)S(1)}, f32[1024]{0:T(1024)}, u32[]{:S(2)}) copy-start(f32[1024]{0:T(1024)} %param.16) | copy-start | bytes 12292
  64.7 8.6 %copy-start.27 = (f32[1024]{0:T(1024)S(1)}, f32[1024]{0:T(1024)}, u32[]{:S(2)}) copy-start(f32[1024]{0:T(1024)} %param.17) | copy-start | bytes 12292
  64.7 9.4 %copy-start.9 = (bf16[128,1024]{1,0:T(8,128)(2,1)S(1)}, bf16[128,1024]{1,0:T(8,128)(2,1)}, u32[]{:S(2)}) copy-start(bf16[128,1024]{1,0:T(8,128)(2,1)} %g_ref.3) | copy-start | bytes 786436
  71.2 1.6 collective-permute-start.10
  74.1 9.6 %copy-start.7 = (bf16[1024,512]{1,0:T(8,128)(2,1)S(1)}, bf16[1024,512]{1,0:T(8,128)(2,1)}, u32[]{:S(2)}) copy-start(bf16[1024,512]{1,0:T(8,128)(2,1)} %o_ref.3) | copy-start | bytes 3145732
  81.9 1.7 collective-permute-start.11
  83.7 1.0 copy-start.12
  86.1 14.1 %all-to-all-start = ((bf16[8,64,128]{2,1,0:T(8,128)(2,1)}), bf16[8,64,128]{2,1,0:T(8,128)(2,1)S(1)}, u32[]{:S(2)}, u32[]{:S(2)}) async-start(bf16[8,64,128]{2,1,0:T(8,128)(2,1)} %get-tuple-element.105), calls=%async_computation | async-start | bytes 262144 | tf_op jit(solution)/shard_map/all_to_all | solution.py:971
  100.2 0.7 copy-start.24
  100.9 12.8 %copy-start.17 = (s32[2]{0:T(128)S(1)}, s32[2]{0:T(128)}, u32[]{:S(2)}) copy-start(s32[2]{0:T(128)} %copy-done.16) | copy-start | bytes 28
  110.9 8.5 %collective-permute-start.12 = (bf16[192,512]{1,0:T(8,128)(2,1)}, bf16[192,512]{1,0:T(8,128)(2,1)S(1)}, u32[]{:S(2)}, u32[]{:S(2)}) collective-permute-start(bf16[192,512]{1,0:T(8,128)(2,1)} %get-tuple-element.110), channel_id=1, source_target_pairs={{0,2},{2,0},{4,6},{6,4},{8,10},{10,8},{12,14},{14,12},{16,18},{18,... | collective-permute-start | bytes 589832 | tf_op jit(solution)/shard_map/ppermute | solution.py:883
  115.5 29.9 %collective-permute-start.17 = (bf16[8,64,512]{2,1,0:T(8,128)(2,1)}, bf16[8,64,512]{2,1,0:T(8,128)(2,1)S(1)}, u32[]{:S(2)}, u32[]{:S(2)}) collective-permute-start(bf16[8,64,512]{2,1,0:T(8,128)(2,1)} %get-tuple-element.124), channel_id=1, source_target_pairs={{0,2},{2,0},{4,6},{6,4},{8,10},{10,8},{12,14},{14,12},{16,18},{18,... | collective-permute-start | bytes 1572872 | tf_op jit(solution)/shard_map/ppermute | solution.py:883
  121.1 19.7 %collective-permute-start.13 = (bf16[192,512]{1,0:T(8,128)(2,1)}, bf16[192,512]{1,0:T(8,128)(2,1)}, u32[]{:S(2)}, u32[]{:S(2)}) collective-permute-start(bf16[192,512]{1,0:T(8,128)(2,1)} %add_convert_fusion.2), channel_id=1, source_target_pairs={{0,8},{2,10},{4,12},{6,14},{8,16},{10,18},{12,20},{14,22},{16,24},... | collective-permute-start | bytes 589832 | tf_op jit(solution)/shard_map/ppermute | solution.py:883
  121.5 21.6 %collective-permute-start.14 = (bf16[192,512]{1,0:T(8,128)(2,1)}, bf16[192,512]{1,0:T(8,128)(2,1)}, u32[]{:S(2)}, u32[]{:S(2)}) collective-permute-start(bf16[192,512]{1,0:T(8,128)(2,1)} %add_convert_fusion.2), channel_id=1, source_target_pairs={{0,16},{2,18},{4,20},{6,22},{8,24},{10,26},{12,28},{14,30},{16,0},... | collective-permute-start | bytes 589832 | tf_op jit(solution)/shard_map/ppermute | solution.py:883
  123.8 19.3 %collective-permute-start.15 = (bf16[192,512]{1,0:T(8,128)(2,1)}, bf16[192,512]{1,0:T(8,128)(2,1)}, u32[]{:S(2)}, u32[]{:S(2)}) collective-permute-start(bf16[192,512]{1,0:T(8,128)(2,1)} %add_convert_fusion.2), channel_id=1, source_target_pairs={{0,24},{2,26},{4,28},{6,30},{8,0},{10,2},{12,4},{14,6},{16,8},{18,... | collective-permute-start | bytes 589832 | tf_op jit(solution)/shard_map/ppermute | solution.py:883
  125.3 20.1 %copy-start.10 = (f32[8,128,128]{2,1,0:T(8,128)S(1)}, f32[8,128,128]{2,1,0:T(8,128)}, u32[]{:S(2)}) copy-start(f32[8,128,128]{2,1,0:T(8,128)} %get-tuple-element.117.kept_ref) | copy-start | bytes 1572868
  125.3 20.1 %copy-start.13 = (bf16[8,64,128]{2,1,0:T(8,128)(2,1)S(1)}, bf16[8,64,128]{2,1,0:T(8,128)(2,1)}, u32[]{:S(2)}) copy-start(bf16[8,64,128]{2,1,0:T(8,128)(2,1)} %get-tuple-element.116.gq_ref) | copy-start | bytes 393220
  125.3 20.1 %collective-permute-start.16 = (bf16[8,128,128]{2,1,0:T(8,128)(2,1)}, bf16[8,128,128]{2,1,0:T(8,128)(2,1)}, u32[]{:S(2)}, u32[]{:S(2)}) collective-permute-start(bf16[8,128,128]{2,1,0:T(8,128)(2,1)} %get-tuple-element.119), channel_id=1, source_target_pairs={{0,2},{2,0},{4,6},{6,4},{8,10},{10,8},{12,14},{14,12},{16,18},{18,... | collective-permute-start | bytes 786440 | tf_op jit(solution)/shard_map/ppermute | solution.py:883
  147.5 34.9 %all-to-all-start.1 = ((bf16[8,448,128]{2,1,0:T(8,128)(2,1)}), bf16[8,448,128]{2,1,0:T(8,128)(2,1)S(1)}, u32[]{:S(2)}, u32[]{:S(2)}) async-start(bf16[8,448,128]{2,1,0:T(8,128)(2,1)} %merge.1), calls=%async_computation.1 | async-start | bytes 1835008 | tf_op jit(solution)/shard_map/all_to_all | solution.py:985
  159.2 28.1 %copy-start.25 = (bf16[128,1024]{1,0:T(8,128)(2,1)S(1)}, bf16[128,1024]{1,0:T(8,128)(2,1)}, u32[]{:S(2)}) copy-start(bf16[128,1024]{1,0:T(8,128)(2,1)} %get-tuple-element.125) | copy-start | bytes 786436
  159.2 39.4 %collective-permute-start.20 = (bf16[4,192,512]{2,1,0:T(8,128)(2,1)}, bf16[4,192,512]{2,1,0:T(8,128)(2,1)}, u32[]{:S(2)}, u32[]{:S(2)}) collective-permute-start(bf16[4,192,512]{2,1,0:T(8,128)(2,1)} %pad_maximum_fusion.refs_0_), channel_id=1, source_target_pairs={{0,2},{2,0},{4,6},{6,4},{8,10},{10,8},{12,14},{14,12},{16,18},{18,... | collective-permute-start | bytes 2359304 | tf_op jit(solution)/shard_map/ppermute | solution.py:883
  160.6 45.7 %collective-permute-start.21 = (bf16[4,192,512]{2,1,0:T(8,128)(2,1)}, bf16[4,192,512]{2,1,0:T(8,128)(2,1)}, u32[]{:S(2)}, u32[]{:S(2)}) collective-permute-start(bf16[4,192,512]{2,1,0:T(8,128)(2,1)} %pad_maximum_fusion.refs_0_), channel_id=1, source_target_pairs={{0,4},{2,6},{4,0},{6,2},{8,12},{10,14},{12,8},{14,10},{16,20},{18,... | collective-permute-start | bytes 2359304 | tf_op jit(solution)/shard_map/ppermute | solution.py:883
  162.5 47.3 %collective-permute-start.22 = (bf16[4,192,512]{2,1,0:T(8,128)(2,1)}, bf16[4,192,512]{2,1,0:T(8,128)(2,1)}, u32[]{:S(2)}, u32[]{:S(2)}) collective-permute-start(bf16[4,192,512]{2,1,0:T(8,128)(2,1)} %pad_maximum_fusion.refs_0_), channel_id=1, source_target_pairs={{0,6},{2,4},{4,2},{6,0},{8,14},{10,12},{12,10},{14,8},{16,22},{18,... | collective-permute-start | bytes 2359304 | tf_op jit(solution)/shard_map/ppermute | solution.py:883
  182.3 0.9 copy-start.21
  187.2 1.7 collective-permute-start.19
  187.3 45.9 %collective-permute-start.18 = (bf16[128,1024]{1,0:T(8,128)(2,1)S(1)}, bf16[128,1024]{1,0:T(8,128)(2,1)S(1)}, u32[]{:S(2)}, u32[]{:S(2)}) collective-permute-start(bf16[128,1024]{1,0:T(8,128)(2,1)S(1)} %copy-done.25), channel_id=1, source_target_pairs={{0,1},{1,0},{2,3},{3,2},{4,5},{5,4},{6,7},{7,6},{8,9},{9,8},{10,11... | collective-permute-start | bytes 786440 | tf_op jit(solution)/shard_map/ppermute | solution.py:887
  189.0 40.5 %collective-permute-start.23 = (bf16[64,512]{1,0:T(8,128)(2,1)}, bf16[64,512]{1,0:T(8,128)(2,1)S(1)}, u32[]{:S(2)}, u32[]{:S(2)}) collective-permute-start(bf16[64,512]{1,0:T(8,128)(2,1)} %get-tuple-element.143), channel_id=1, source_target_pairs={{0,8},{2,10},{4,12},{6,14},{8,16},{10,18},{12,20},{14,22},{16,24},... | collective-permute-start | bytes 196616 | tf_op jit(solution)/shard_map/ppermute | solution.py:883
  191.0 0.9 copy-start.11
  193.2 36.3 %all-to-all-start.2 = ((f32[16,4,1024]{2,1,0:T(4,128)}), f32[16,4,1024]{2,1,0:T(4,128)S(1)}, u32[]{:S(2)}, u32[]{:S(2)}) async-start(f32[16,4,1024]{2,1,0:T(4,128)} %get-tuple-element.133), calls=%async_computation.2 | async-start | bytes 524288 | tf_op jit(solution)/shard_map/all_to_all | solution.py:997
  198.6 30.9 %collective-permute-start.24 = (bf16[64,512]{1,0:T(8,128)(2,1)}, bf16[64,512]{1,0:T(8,128)(2,1)S(1)}, u32[]{:S(2)}, u32[]{:S(2)}) collective-permute-start(bf16[64,512]{1,0:T(8,128)(2,1)} %get-tuple-element.143), channel_id=1, source_target_pairs={{0,16},{2,18},{4,20},{6,22},{8,24},{10,26},{12,28},{14,30},{16,0},... | collective-permute-start | bytes 196616 | tf_op jit(solution)/shard_map/ppermute | solution.py:883
  206.2 23.2 %collective-permute-start.25 = (bf16[64,512]{1,0:T(8,128)(2,1)}, bf16[64,512]{1,0:T(8,128)(2,1)S(1)}, u32[]{:S(2)}, u32[]{:S(2)}) collective-permute-start(bf16[64,512]{1,0:T(8,128)(2,1)} %get-tuple-element.143), channel_id=1, source_target_pairs={{0,24},{2,26},{4,28},{6,30},{8,0},{10,2},{12,4},{14,6},{16,8},{18,... | collective-permute-start | bytes 196616 | tf_op jit(solution)/shard_map/ppermute | solution.py:883
  209.8 19.7 %copy-start.26 = (bf16[64,512]{1,0:T(8,128)(2,1)S(1)}, bf16[64,512]{1,0:T(8,128)(2,1)}, u32[]{:S(2)}) copy-start(bf16[64,512]{1,0:T(8,128)(2,1)} %get-tuple-element.143) | copy-start | bytes 196612
  229.5 13.7 %copy-start.18 = (s32[2]{0:T(128)S(1)}, s32[2]{0:T(128)}, u32[]{:S(2)}) copy-start(s32[2]{0:T(128)} %copy-done.16) | copy-start | bytes 28
  229.6 11.1 %collective-permute-start.26 = (bf16[4,64,512]{2,1,0:T(8,128)(2,1)S(1)}, bf16[4,64,512]{2,1,0:T(8,128)(2,1)S(1)}, u32[]{:S(2)}, u32[]{:S(2)}) collective-permute-start(bf16[4,64,512]{2,1,0:T(8,128)(2,1)S(1)} %pad_maximum_fusion.2.refs_0_), channel_id=1, source_target_pairs={{0,2},{2,0},{4,6},{6,4},{8,10},{10,8},{12,14},{14,12},{16,18},{18,... | collective-permute-start | bytes 786440 | tf_op jit(solution)/shard_map/ppermute | solution.py:883
  231.1 12.0 %collective-permute-start.27 = (bf16[4,64,512]{2,1,0:T(8,128)(2,1)S(1)}, bf16[4,64,512]{2,1,0:T(8,128)(2,1)S(1)}, u32[]{:S(2)}, u32[]{:S(2)}) collective-permute-start(bf16[4,64,512]{2,1,0:T(8,128)(2,1)S(1)} %pad_maximum_fusion.2.refs_0_), channel_id=1, source_target_pairs={{0,4},{2,6},{4,0},{6,2},{8,12},{10,14},{12,8},{14,10},{16,20},{18,... | collective-permute-start | bytes 786440 | tf_op jit(solution)/shard_map/ppermute | solution.py:883
  231.1 12.0 %collective-permute-start.28 = (bf16[4,64,512]{2,1,0:T(8,128)(2,1)S(1)}, bf16[4,64,512]{2,1,0:T(8,128)(2,1)S(1)}, u32[]{:S(2)}, u32[]{:S(2)}) collective-permute-start(bf16[4,64,512]{2,1,0:T(8,128)(2,1)S(1)} %pad_maximum_fusion.2.refs_0_), channel_id=1, source_target_pairs={{0,6},{2,4},{4,2},{6,0},{8,14},{10,12},{12,10},{14,8},{16,22},{18,... | collective-permute-start | bytes 786440 | tf_op jit(solution)/shard_map/ppermute | solution.py:883
Sparse Core Ops, SparseCore 0:
  11.5 66.2 all-gather.2
  80.6 71.1 all-gather.4

commit v4 on v3

--- a/solution.py
+++ b/solution.py
@@ -731,7 +731,7 @@
     )(home, *weights)
 
 
-def input_back_kernel(x_ref, mine_ref, other_ref, gain_ref, grad_ref, sums_ref, grad_out, sums_out):
+def input_back_kernel(x_ref, mine_ref, other_ref, gain_ref, grad_ref, sums_ref, slice_ref, grad_out, unit_out):
     x = x_ref[...].astype(f32)
     center = x - jnp.mean(x, axis=1, keepdims=True)
     scale = lax.rsqrt(jnp.mean(center * center, axis=1, keepdims=True) + 1e-05)
@@ -739,27 +739,34 @@
     grad = mine_ref[...].astype(f32) + other_ref[...].astype(f32)
     sums = [jnp.sum(grad * normed, axis=0, keepdims=True), jnp.sum(grad, axis=0, keepdims=True), sums_ref[...]]
     sums = jnp.concatenate(sums, axis=0)
-    for b in range(sums_out.shape[0]):
-        sums_out[b] = sums
+    slots, wide = slice_ref.shape
+    left = jnp.concatenate([sums[:, :wide], sums[:, wide:]], axis=0)
+    terms = []
+    for _ in range(3):
+        terms.append(left.astype(bf16))
+        left = left - terms[-1].astype(f32)
+    unit_out[0:slots, :] = slice_ref[...]
+    unit_out[slots:, :] = jnp.concatenate(terms, axis=0)
     grad = grad * gain_ref[...]
     inner = jnp.mean(grad * normed, axis=1, keepdims=True)
     grad_out[...] = grad_ref[...] + scale * (grad - jnp.mean(grad, axis=1, keepdims=True) - normed * inner)
 
 
-def input_back(x, mine, other, gain, grad_middle, sums, count):
+def input_back(x, mine, other, gain, grad_middle, sums, row_slice):
     rows, width = x.shape
+    slots, wide = row_slice.shape
     return pl.pallas_call(
         input_back_kernel,
-        in_specs=[NEAR] * 6,
+        in_specs=[NEAR] * 7,
         out_specs=[NEAR] * 2,
         out_shape=[
             jax.ShapeDtypeStruct((rows, width), f32),
-            jax.ShapeDtypeStruct((count, 4, width), f32),
+            jax.ShapeDtypeStruct((slots + 12 * width // wide, wide), bf16),
         ],
         compiler_params=room(16),
         cost_estimate=HINT,
         name="input_back",
-    )(x, mine, other, gain.reshape(1, width), grad_middle, sums)
+    )(x, mine, other, gain.reshape(1, width), grad_middle, sums, row_slice)
 
 
 def through_kernel(g_ref, down_ref, out_ref):
@@ -843,20 +850,34 @@
 
 
 def finish_rows_kernel(ids_ref, *refs):
-    pieces, out_ref = refs[:4], refs[4]
-    slots = pieces[0].shape[1]
+    pieces, out_ref, sums_out, terms_s = refs[:4], refs[4], refs[5], refs[6]
+    count = terms_s.shape[0]
+    slots = out_ref.shape[0] // count
+    wide = out_ref.shape[1]
     for k in range(4):
         for s in range(4):
-            at = pl.multiple_of((((ids_ref[0] - 4 * s) & 15) ^ k) * slots, slots)
-            out_ref[pl.ds(at, slots), :] = pieces[k][s].astype(f32)
-
-
-def finish_rows(ids, pieces, width, columns):
+            block = ((ids_ref[0] - 4 * s) & 15) ^ k
+            out_ref[pl.ds(pl.multiple_of(block * slots, slots), slots), :] = pieces[k][s, 0:slots, :].astype(f32)
+            terms_s[block] = pieces[k][s, slots:, :].astype(f32)
+    n = terms_s.shape[1] // 3
+    total = jnp.zeros((n, wide), f32)
+    for b in range(count):
+        total += terms_s[b, 0:n] + (terms_s[b, n : 2 * n] + terms_s[b, 2 * n :])
+    sums_out[:, 0:wide] = total[0 : n // 2]
+    sums_out[:, wide:] = total[n // 2 :]
+
+
+def finish_rows(ids, pieces, width, columns, count):
+    extra = pieces[0].shape[1] - width // count
     return pl.pallas_call(
         finish_rows_kernel,
         in_specs=[SCALAR] + [NEAR] * 4,
-        out_specs=NEAR,
-        out_shape=jax.ShapeDtypeStruct((width, columns), f32),
+        out_specs=[NEAR] * 2,
+        out_shape=[
+            jax.ShapeDtypeStruct((width, columns), f32),
+            jax.ShapeDtypeStruct((4, width), f32),
+        ],
+        scratch_shapes=[pltpu.VMEM((count, extra, columns), f32)],
         compiler_params=room(16),
         cost_estimate=HINT,
         name="finish_rows",
@@ -980,31 +1001,29 @@
     given = after(given, head_slice)
     given = shuffle(given, lambda i: i ^ 1)
     grad_all = through(after(g_all, head_slice), down_weight)
-    column = stack_column(parts, grad_all)
+    feed = after(feed, head_slice)
+    layer_out = (middle + (feed.astype(f32) + over_core(feed).astype(f32))).astype(bf16)
+    column = stack_column(parts, grad_all, layer_out)
     parcel = merge(after(grad_q, column), kept, given, output_kept, output_other)
     home = lax.all_to_all(parcel, "blk", 0, 0, tiled=True, axis_index_groups=alike)
     heads = gather_plane(column)
 
-    feed = after(feed, parcel)
-    layer_out = (middle + (feed.astype(f32) + over_core(feed).astype(f32))).astype(bf16)
-    held = ffn_grads(after(h2_all, column), g_all, grad_all, up_weight, (0, 4), ())
+    held = ffn_grads(after(h2_all, column), g_all, grad_all, up_weight, (0, 5), ())
 
     home = after(home, held[0])
     grad_one, output_slice = go_home(home, (query_weight, value_weight, key_weight), width // count)
-    input_grad, norm_part = input_back(
-        tokens, grad_one, over_core(grad_one), first_gain, grad_middle, second_sums, count
-    )
-    norm_parts = lax.all_to_all(norm_part, "blk", 0, 0, tiled=True)
-
-    parts = send_column(output_slice)
-    up_grad, down_grad = ffn_grads(
-        after(h2_all, norm_part, *heads), g_all, grad_all, up_weight, (4, 8), held
-    )
-    rest = gather_plane(stack_column(parts, up_grad, norm_parts))
-    norm_sums = jnp.sum(after(norm_parts, up_grad), axis=0)
+    input_grad, unit = input_back(
+        tokens, grad_one, over_core(grad_one), first_gain, grad_middle, second_sums, output_slice
+    )
+    parts = send_column(unit)
+    held = ffn_grads(after(h2_all, unit, *heads), g_all, grad_all, up_weight, (5, 7), held)
+    column = stack_column(parts, held[0])
+    rest = gather_plane(column)
+    up_grad, down_grad = ffn_grads(after(h2_all, column), g_all, grad_all, up_weight, (7, 8), held)
     heads = (after(heads[0], up_grad),) + heads[1:]
     query_grad, value_grad, key_grad = finish_heads(ids, heads, width, columns)
-    output_grad = finish_rows(ids, rest, width, columns)
+    rest = (after(rest[0], query_grad),) + rest[1:]
+    output_grad, norm_sums = finish_rows(ids, rest, width, columns, count)
     return (
         layer_out,
         input_grad,

time: 253 us -> 246 us (0.972)
  starting transfers between devices: 61.6 us -> 42.7 us
  Pallas kernels: 117 us -> 124 us
    all_to_all x1, starting transfers between devices: 11.7 us -> 3.85 us  [fast_body(): lax.all_to_all(parcel, 'blk', 0, 0, tiled=True, axis_index_groups=alike)]
    ppermute x21, starting transfers between devices: 36.6 us -> 29.9 us  [shuffle(): return lax.ppermute(block, 'blk', [(i, target(i)) for i in range(16)])]
    all_to_all x1 -> x0, starting transfers between devices: 5.39 us -> none  [fast_body(): norm_parts = lax.all_to_all(norm_part, 'blk', 0, 0, tiled=True)]
    pallas_call x2 -> x3, Pallas kernels: 39.2 us -> 44.3 us  [ffn_grads(): pl.pallas_call(ffn_kernel, grid=(last - first,), in_specs=[tokens, tokens...]
    all_to_all x1, waiting for transfers between devices: 0.01 us -> 2.58 us  [fast_body(): lax.all_to_all(parcel, 'blk', 0, 0, tiled=True, axis_index_groups=alike)]
  transfers between devices with their start and end apart: 34 -> 33, of which waited for: 14 -> 14; matrix products, arithmetic and copies ran while one was open for 6% -> 7% of each run, Pallas kernels for 45% -> 50%
where the time goes in v4:
time: 246 us; the launch traced here: 245 us
  Pallas kernels  124 us (50%)
  starting transfers between devices  42.7 us (17%)
  waiting for transfers between devices  40.2 us (16%)
  between operations  14.5 us (6%)
  local copies, waits for them, and re-layouts  12.4 us (5%)
  other arithmetic  11.1 us (5%)
    pallas_call x3, Pallas kernels, ffn_grads(): pl.pallas_call(ffn_kernel, grid=(last - first,), in_specs=[tokens, tokens...  44.3 us
    ppermute x21, starting transfers between devices, shuffle(): return lax.ppermute(block, 'blk', [(i, target(i)) for i in range(16)])  29.9 us
    ppermute x21, waiting for transfers between devices, shuffle(): return lax.ppermute(block, 'blk', [(i, target(i)) for i in range(16)])  28.9 us
    pallas_call x4, Pallas kernels, project_blocks(): pl.pallas_call(lambda *refs: project_kernel(flip, *refs), in_specs=[SCALA...  14.7 us
    pallas_call x1, Pallas kernels, through(): pl.pallas_call(through_kernel, grid=(hidden // tile,), in_specs=[pl.Block...  13.5 us
    pallas_call x1, Pallas kernels, back(): pl.pallas_call(back_kernel, grid_spec=pltpu.PrefetchScalarGridSpec(num_sc...  11.9 us
    all_to_all x1, starting transfers between devices, fast_body(): lax.all_to_all(to_heads, 'blk', 0, 0, tiled=True, axis_index_groups=alike)  7.99 us
    pallas_call x1, Pallas kernels, own_ffn(): pl.pallas_call(own_kernel, grid=(hidden // tile,), in_specs=[NEAR, NEAR]...  7.83 us
  transfers between devices with their start and end apart: 33, of which 14 were waited for; matrix products, arithmetic and copies ran while one was open for 7% of the time, Pallas kernels for 50%

profile of v4, /device:TPU:0, one launch (start us, length us, event | category | flops | bytes accessed | tf_op | source)
XLA Modules:
  0.0 244.8 jit_solution(1534351158309944781)
XLA Ops:
  7.3 1.7 constant_dynamic-slice_fusion.1
  9.0 0.9 constant_dynamic-slice_fusion.4
  10.0 4.1 %collective-permute-start.1 = (bf16[64,1024]{1,0:T(8,128)(2,1)S(1)}, bf16[64,1024]{1,0:T(8,128)(2,1)S(1)}, u32[]{:S(2)}, u32[]{:S(2)}) collective-permute-start(bf16[64,1024]{1,0:T(8,128)(2,1)S(1)} %constant_dynamic-slice_fusion.4), channel_id=1, source_target_pairs={{0,16},{2,18},{4,20},{6,22},{8,24},{10,26},{12,28},{14,30},{16,0},... | collective-permute-start | bytes 393224 | tf_op jit(solution)/shard_map/ppermute | solution.py:904
  14.1 1.6 collective-permute-start
  15.7 2.2 collective-permute-start.2
  17.9 0.9 fusion.2
  18.8 1.3 dynamic-slice_multiply_fusion
  20.1 4.0 %collective-permute-done.1 = bf16[64,1024]{1,0:T(8,128)(2,1)S(1)} collective-permute-done((bf16[64,1024]{1,0:T(8,128)(2,1)S(1)}, bf16[64,1024]{1,0:T(8,128)(2,1)S(1)}, u32[]{:S(2)}, u32[]{:S(2)}) %collective-permute-start.1) | collective-permute-done | bytes 131104 | tf_op jit(solution)/shard_map/ppermute | solution.py:904
  24.9 1.6 collective-permute-start.7
  26.5 1.5 collective-permute-start.3
  28.0 1.8 constant_dynamic-slice_fusion.3
  29.8 2.0 maximum_bitcast_fusion
  31.8 1.2 copy.44.refs_7_
  33.2 1.4 maximum_maximum_fusion.refs_8_
  34.6 3.4 %project_blocks.4 = (bf16[16,128,1024]{2,1,0:T(8,128)(2,1)S(1)}, bf16[16,128,512]{2,1,0:T(8,128)(2,1)S(1)}, bf16[16,128,512]{2,1,0:T(8,128)(2,1)S(1)}, bf16[16,1...) custom-call(s32[2]{0:T(128)S(1)} %pad_add_fusion.refs_0_.ids_ref, bf16[4,64,1024]{2,1,0:T(8,128)(2,1)S(1)} %pad_maximum_fusion.1.refs_1_, ...), custom_call_target="tpu_custom_call" | custom-call | flops 1 | bytes 1 | tf_op jit(solution)/shard_map/project_blocks/pallas_call | solution.py:351
  38.0 2.9 %collective-permute-done.3.refs_1_ = bf16[4,64,1024]{2,1,0:T(8,128)(2,1)} collective-permute-done((bf16[4,64,1024]{2,1,0:T(8,128)(2,1)S(1)}, bf16[4,64,1024]{2,1,0:T(8,128)(2,1)}, u32[]{:S(2)}, u32[]{:S(2)}) %collective-permute-start.3) | collective-permute-done | bytes 524320 | tf_op jit(solution)/shard_map/ppermute | solution.py:904
  41.9 1.1 collective-permute-done.8.refs_2_
  43.0 3.9 %project_blocks.5 = (bf16[16,128,1024]{2,1,0:T(8,128)(2,1)S(1)}, bf16[16,128,512]{2,1,0:T(8,128)(2,1)S(1)}, bf16[16,128,512]{2,1,0:T(8,128)(2,1)S(1)}, bf16[16,1...) custom-call(s32[2]{0:T(128)S(1)} %pad_add_fusion.refs_0_.ids_ref, ...), custom_call_target="tpu_custom_call", output_to_operand_aliasing={{0}: (9, {}), {1}: (10, {}), {2}: (11, {}), {3}: (12, {}), ... | custom-call | flops 1 | bytes 1 | tf_op jit(solution)/shard_map/project_blocks/pallas_call | solution.py:351
  47.0 3.9 %project_blocks.6 = (bf16[16,128,1024]{2,1,0:T(8,128)(2,1)S(1)}, bf16[16,128,512]{2,1,0:T(8,128)(2,1)S(1)}, bf16[16,128,512]{2,1,0:T(8,128)(2,1)S(1)}, bf16[16,1...) custom-call(s32[2]{0:T(128)S(1)} %pad_add_fusion.refs_0_.ids_ref, ...), custom_call_target="tpu_custom_call", output_to_operand_aliasing={{0}: (9, {}), {1}: (10, {}), {2}: (11, {}), {3}: (12, {}), ... | custom-call | flops 1 | bytes 1 | tf_op jit(solution)/shard_map/project_blocks/pallas_call | solution.py:351
  50.9 5.7 %collective-permute-done.5.refs_1_ = bf16[4,64,1024]{2,1,0:T(8,128)(2,1)S(1)} collective-permute-done((bf16[4,64,1024]{2,1,0:T(8,128)(2,1)}, bf16[4,64,1024]{2,1,0:T(8,128)(2,1)S(1)}, u32[]{:S(2)}, u32[]{:S(2)}) %collective-permute-start.5) | collective-permute-done | bytes 524320 | tf_op jit(solution)/shard_map/ppermute | solution.py:904
  56.6 1.9 collective-permute-done.9.refs_2_
  58.5 3.4 %project_blocks.7 = (bf16[16,128,1024]{2,1,0:T(8,128)(2,1)S(1)}, bf16[16,128,512]{2,1,0:T(8,128)(2,1)S(1)}, bf16[16,128,512]{2,1,0:T(8,128)(2,1)S(1)}, bf16[16,1...) custom-call(s32[2]{0:T(128)S(1)} %pad_add_fusion.refs_0_.ids_ref, ...), custom_call_target="tpu_custom_call", output_to_operand_aliasing={{0}: (9, {}), {1}: (10, {}), {2}: (11, {}), {3}: (12, {}), ... | custom-call | flops 1 | bytes 1 | tf_op jit(solution)/shard_map/project_blocks/pallas_call | solution.py:351
  62.1 6.5 %attend.1 = (bf16[128,512]{1,0:T(8,128)(2,1)S(1)}, bf16[128,1024]{1,0:T(8,128)(2,1)S(1)}) custom-call(s32[2]{0:T(128)S(1)} %pad_add_fusion.refs_0_.ids_ref, s32[4]{0:T(128)S(1)} %copy-done.23, bf16[16,128,1024]{2,1,0:T(8,128)(2,1)S(1)} %get-tuple-element.103.h_ref, bf16[2048,512]{1,0:T(8,128)(2,1)S(1)} %bitcast.29, bf16[2048,512]{1,0:T(8,128)(2,1)S(1)} %bitcast.30, ...), custom_call_target="tpu_custom_call" | custom-call | flops 1 | bytes 1 | tf_op jit(solution)/shard_map/attend/pallas_call | solution.py:397
  68.8 1.4 collective-permute-done.10
  71.5 7.8 %own_ffn.1 = (bf16[128,1024]{1,0:T(8,128)(2,1)}, bf16[128,1024]{1,0:T(8,128)(2,1)}) custom-call(bf16[128,1024]{1,0:T(8,128)(2,1)S(1)} %add_convert_fusion.1.h_ref, bf16[128,1024]{1,0:T(8,128)(2,1)S(1)} %copy-done.9, bf16[1024,2048]{1,0:T(8,128)(2,1)} %up_ref.7, bf16[1024,2048]{1,0:T(8,128)(2,1)} %down_ref.3), custom_call_target="tpu_custom_call" | custom-call | flops 1 | bytes 1 | tf_op jit(solution)/shard_map/own_ffn/pallas_call | solution.py:446
  79.5 1.6 collective-permute-done.11.other_ref
  81.1 0.9 copy-done.11
  82.1 1.5 norm_back.1
  83.5 8.0 %all-to-all-start = ((bf16[8,64,128]{2,1,0:T(8,128)(2,1)}), bf16[8,64,128]{2,1,0:T(8,128)(2,1)S(1)}, u32[]{:S(2)}, u32[]{:S(2)}) async-start(bf16[8,64,128]{2,1,0:T(8,128)(2,1)} %get-tuple-element.110), calls=%async_computation | async-start | bytes 262144 | tf_op jit(solution)/shard_map/all_to_all | solution.py:992
  91.5 7.4 %prepare.1.p_ref = bf16[4,2048,256]{2,1,0:T(8,128)(2,1)} custom-call(s32[2]{0:T(128)} %copy-done.19, s32[4]{0:T(128)} %len_ref.5, bf16[16,192,128]{2,1,0:T(8,128)(2,1)} %copy-done.4, bf16[2048,256]{1,0:T(8,128)(2,1)} %bitcast.31), custom_call_target="tpu_custom_call" | custom-call | flops 1 | bytes 1 | tf_op jit(solution)/shard_map/prepare/pallas_call | solution.py:539
  99.0 0.8 all-to-all-done.ga_ref
  100.4 11.9 %back.1 = (bf16[8,64,128]{2,1,0:T(8,128)(2,1)}, f32[8,128,128]{2,1,0:T(8,128)}, bf16[8,128,128]{2,1,0:T(8,128)(2,1)}, f32[192,512]{1,0:T(8,128)}, bf16[192,512]{1,0:T(8,128)(2,1)}) custom-call(s32[2]{0:T(128)} %copy-done.19, s32[4]{0:T(128)} %len_ref.5, bf16[4,2048,256]{2,1,0:T(8,128)(2,1)} %prepare.1.p_ref, bf16[8,64,128]{2,1,0:T(8,128)(2,1)} %copy-done.28, ...), custom_call_target="tpu_custom_call" | custom-call | flops 1 | bytes 1 | tf_op jit(solution)/shard_map/back/pallas_call | solution.py:631
  113.0 1.8 share_output.1
  114.8 1.4 collective-permute-start.18
  116.2 4.0 %collective-permute-done.12 = bf16[192,512]{1,0:T(8,128)(2,1)S(1)} collective-permute-done((bf16[192,512]{1,0:T(8,128)(2,1)}, bf16[192,512]{1,0:T(8,128)(2,1)S(1)}, u32[]{:S(2)}, u32[]{:S(2)}) %collective-permute-start.12) | collective-permute-done | bytes 196640 | tf_op jit(solution)/shard_map/ppermute | solution.py:904
  120.3 1.7 add_convert_fusion.2
  122.0 3.2 %collective-permute-start.16 = (bf16[192,512]{1,0:T(8,128)(2,1)}, bf16[192,512]{1,0:T(8,128)(2,1)}, u32[]{:S(2)}, u32[]{:S(2)}) collective-permute-start(bf16[192,512]{1,0:T(8,128)(2,1)} %add_convert_fusion.2), channel_id=1, source_target_pairs={{0,24},{2,26},{4,28},{6,30},{8,0},{10,2},{12,4},{14,6},{16,8},{18,... | collective-permute-start | bytes 589832 | tf_op jit(solution)/shard_map/ppermute | solution.py:904
  125.2 1.1 collective-permute-start.14
  126.3 13.5 %through.1.grad_ref = bf16[2048,2048]{1,0:T(8,128)(2,1)} custom-call(bf16[2048,1024]{1,0:T(8,128)(2,1)} %all-gather.3.cloned.1.call-done.g_ref, bf16[1024,2048]{1,0:T(8,128)(2,1)} %down_ref.3), custom_call_target="tpu_custom_call" | custom-call | flops 8589934592 | bytes 16777216 | tf_op jit(solution)/shard_map/through/pallas_call | solution.py:780
  139.8 0.9 collective-permute-start.17
  140.7 1.8 add_convert_fusion
  142.6 9.5 %collective-permute-done.15 = bf16[192,512]{1,0:T(8,128)(2,1)} collective-permute-done((bf16[192,512]{1,0:T(8,128)(2,1)}, bf16[192,512]{1,0:T(8,128)(2,1)}, u32[]{:S(2)}, u32[]{:S(2)}) %collective-permute-start.15) | collective-permute-done | bytes 196640 | tf_op jit(solution)/shard_map/ppermute | solution.py:904
  152.1 2.2 pad_maximum_fusion.refs_0_
  154.3 1.1 merge.1
  155.4 3.9 %all-to-all-start.1 = ((bf16[8,448,128]{2,1,0:T(8,128)(2,1)}), bf16[8,448,128]{2,1,0:T(8,128)(2,1)S(1)}, u32[]{:S(2)}, u32[]{:S(2)}) async-start(bf16[8,448,128]{2,1,0:T(8,128)(2,1)} %merge.1), calls=%async_computation.1 | async-start | bytes 1835008 | tf_op jit(solution)/shard_map/all_to_all | solution.py:1008
  159.3 2.4 collective-permute-start.25
  161.7 1.1 collective-permute-start.23
  162.8 23.2 %ffn_grads.3 = (f32[1024,2048]{1,0:T(8,128)}, f32[1024,2048]{1,0:T(8,128)}) custom-call(bf16[2048,1024]{1,0:T(8,128)(2,1)} %all-gather.5.cloned.1.call-done.h_ref, bf16[2048,1024]{1,0:T(8,128)(2,1)} %all-gather.3.cloned.1.call-done.g_ref, bf16[2048,2048]{1,0:T(8,128)(2,1)} %through.1.grad_ref, bf16[1024,2048]{1,0:T(8,128)(2,1)} %up_ref.7), custom_call_target="tpu_custom_call" | custom-call | flops 16106127360 | bytes 8388608 | tf_op jit(solution)/shard_map/ffn_grads/pallas_call | solution.py:825
  185.9 2.6 %all-to-all-done.1.home_ref = bf16[8,448,128]{2,1,0:T(8,128)(2,1)S(1)} async-done(((bf16[8,448,128]{2,1,0:T(8,128)(2,1)}), bf16[8,448,128]{2,1,0:T(8,128)(2,1)S(1)}, u32[]{:S(2)}, u32[]{:S(2)}) %all-to-all-start.1) | async-done | bytes 917536 | tf_op jit(solution)/shard_map/all_to_all | solution.py:1008
  188.5 0.9 copy-done.24
  189.4 4.0 %go_home.1 = (bf16[128,1024]{1,0:T(8,128)(2,1)}, bf16[64,512]{1,0:T(8,128)(2,1)}) custom-call(bf16[8,448,128]{2,1,0:T(8,128)(2,1)} %copy-done.24, bf16[1024,512]{1,0:T(8,128)(2,1)} %q_ref.3, bf16[1024,512]{1,0:T(8,128)(2,1)} %v_ref.1, bf16[1024,512]{1,0:T(8,128)(2,1)} %k_ref.1), custom_call_target="tpu_custom_call" | custom-call | flops 1 | bytes 1 | tf_op jit(solution)/shard_map/go_home/pallas_call | solution.py:721
  193.4 1.7 collective-permute-done.19.other_ref
  195.2 0.9 copy-done.12
  196.1 0.8 copy-done.17
  197.0 1.3 input_back.1
  198.3 3.4 %collective-permute-start.22 = (bf16[88,512]{1,0:T(8,128)(2,1)S(1)}, bf16[88,512]{1,0:T(8,128)(2,1)S(1)}, u32[]{:S(2)}, u32[]{:S(2)}) collective-permute-start(bf16[88,512]{1,0:T(8,128)(2,1)S(1)} %get-tuple-element.143), channel_id=1, source_target_pairs={{0,24},{2,26},{4,28},{6,30},{8,0},{10,2},{12,4},{14,6},{16,8},{18,... | collective-permute-start | bytes 270344 | tf_op jit(solution)/shard_map/ppermute | solution.py:904
  202.3 2.1 collective-permute-done.24.refs_2_
  204.4 12.4 %ffn_grads.4 = (f32[1024,2048]{1,0:T(8,128)}, f32[1024,2048]{1,0:T(8,128)}) custom-call(bf16[2048,1024]{1,0:T(8,128)(2,1)} %all-gather.5.cloned.1.call-done.h_ref, bf16[2048,1024]{1,0:T(8,128)(2,1)} %all-gather.3.cloned.1.call-done.g_ref, bf16[2048,2048]{1,0:T(8,128)(2,1)} %through.1.grad_ref, ...), custom_call_target="tpu_custom_call", output_to_operand_aliasing={{0}: (4, {}), {1}: (5, {})} | custom-call | flops 6442450944 | bytes 8388608 | tf_op jit(solution)/shard_map/ffn_grads/pallas_call | solution.py:825
  216.9 1.0 collective-permute-start.28
  217.9 1.7 collective-permute-start.27
  219.6 0.8 collective-permute-start.26
  220.5 8.7 %ffn_grads.5 = (f32[1024,2048]{1,0:T(8,128)}, f32[1024,2048]{1,0:T(8,128)}) custom-call(bf16[2048,1024]{1,0:T(8,128)(2,1)} %all-gather.5.cloned.1.call-done.h_ref, bf16[2048,1024]{1,0:T(8,128)(2,1)} %all-gather.3.cloned.1.call-done.g_ref, bf16[2048,2048]{1,0:T(8,128)(2,1)} %through.1.grad_ref, ...), custom_call_target="tpu_custom_call", output_to_operand_aliasing={{0}: (4, {}), {1}: (5, {})} | custom-call | flops 3221225472 | bytes 8388608 | tf_op jit(solution)/shard_map/ffn_grads/pallas_call | solution.py:825
  229.2 6.1 %finish_heads.1 = (f32[1024,512]{1,0:T(8,128)}, f32[1024,512]{1,0:T(8,128)}, f32[1024,512]{1,0:T(8,128)}) custom-call(s32[2]{0:T(128)} %copy-done.19, bf16[4,192,512]{2,1,0:T(8,128)(2,1)} %pad_maximum_fusion.refs_0_, bf16[4,192,512]{2,1,0:T(8,128)(2,1)} %collective-permute-done.23.refs_1_, bf16[4,192,512]{2,1,0:T(8,128)(2,1)} %collective-permute-done.24.refs_2_, ...), custom_call_target="tpu_custom_call" | custom-call | flops 1 | bytes 1 | tf_op jit(solution)/shard_map/finish_heads/pallas_call | solution.py:889
  235.3 2.0 finish_rows.1
  (106 shorter events, 6.4 us)
Async XLA Ops:
  7.2 27.4 %copy-start.2 = (bf16[1024,512]{1,0:T(8,128)(2,1)S(1)}, bf16[1024,512]{1,0:T(8,128)(2,1)}, u32[]{:S(2)}) copy-start(bf16[1024,512]{1,0:T(8,128)(2,1)} %v_ref.1) | copy-start | bytes 3145732
  7.2 27.4 %copy-start.1 = (bf16[1024,512]{1,0:T(8,128)(2,1)S(1)}, bf16[1024,512]{1,0:T(8,128)(2,1)}, u32[]{:S(2)}) copy-start(bf16[1024,512]{1,0:T(8,128)(2,1)} %k_ref.1) | copy-start | bytes 3145732
  7.2 27.4 %copy-start.18 = (f32[1024]{0:T(1024)S(1)}, f32[1024]{0:T(1024)}, u32[]{:S(2)}) copy-start(f32[1024]{0:T(1024)} %param.15) | copy-start | bytes 12292
  7.2 27.4 %copy-start.16 = (f32[1024]{0:T(1024)S(1)}, f32[1024]{0:T(1024)}, u32[]{:S(2)}) copy-start(f32[1024]{0:T(1024)} %param.14) | copy-start | bytes 12292
  7.2 84.3 %all-gather.3.cloned.1.call-start = ((), (), s32[]{:S(2)}) async-start(), calls=%async_computation.2 | async-start | bytes 4325376 | tf_op jit(solution)/shard_map/all_gather | solution.py:961
  9.0 153.8 %all-gather.5.cloned.1.call-start = ((), (), s32[]{:S(2)}) async-start(), calls=%async_computation.3 | async-start | bytes 4325376 | tf_op jit(solution)/shard_map/all_gather | solution.py:986
  10.0 14.1 %collective-permute-start.1 = (bf16[64,1024]{1,0:T(8,128)(2,1)S(1)}, bf16[64,1024]{1,0:T(8,128)(2,1)S(1)}, u32[]{:S(2)}, u32[]{:S(2)}) collective-permute-start(bf16[64,1024]{1,0:T(8,128)(2,1)S(1)} %constant_dynamic-slice_fusion.4), channel_id=1, source_target_pairs={{0,16},{2,18},{4,20},{6,22},{8,24},{10,26},{12,28},{14,30},{16,0},... | collective-permute-start | bytes 393224 | tf_op jit(solution)/shard_map/ppermute | solution.py:904
  14.1 10.0 %collective-permute-start = (bf16[64,1024]{1,0:T(8,128)(2,1)S(1)}, bf16[64,1024]{1,0:T(8,128)(2,1)S(1)}, u32[]{:S(2)}, u32[]{:S(2)}) collective-permute-start(bf16[64,1024]{1,0:T(8,128)(2,1)S(1)} %constant_dynamic-slice_fusion.4), channel_id=1, source_target_pairs={{0,8},{2,10},{4,12},{6,14},{8,16},{10,18},{12,20},{14,22},{16,24},... | collective-permute-start | bytes 393224 | tf_op jit(solution)/shard_map/ppermute | solution.py:904
  15.7 9.1 %collective-permute-start.2 = (bf16[64,1024]{1,0:T(8,128)(2,1)S(1)}, bf16[64,1024]{1,0:T(8,128)(2,1)S(1)}, u32[]{:S(2)}, u32[]{:S(2)}) collective-permute-start(bf16[64,1024]{1,0:T(8,128)(2,1)S(1)} %constant_dynamic-slice_fusion.4), channel_id=1, source_target_pairs={{0,24},{2,26},{4,28},{6,30},{8,0},{10,2},{12,4},{14,6},{16,8},{18,... | collective-permute-start | bytes 393224 | tf_op jit(solution)/shard_map/ppermute | solution.py:904
  20.1 9.7 %copy-start.25 = (bf16[1024,64]{1,0:T(8,128)(2,1)}, bf16[1024,64]{1,0:T(8,128)(2,1)S(1)}, u32[]{:S(2)}) copy-start(bf16[1024,64]{1,0:T(8,128)(2,1)S(1)} %get-tuple-element.164) | copy-start | bytes 393220
  20.1 9.7 %copy-start.26 = (bf16[1024,64]{1,0:T(8,128)(2,1)}, bf16[1024,64]{1,0:T(8,128)(2,1)S(1)}, u32[]{:S(2)}) copy-start(bf16[1024,64]{1,0:T(8,128)(2,1)S(1)} %get-tuple-element.165) | copy-start | bytes 393220
  24.9 16.1 %collective-permute-start.7 = (bf16[4,64,1024]{2,1,0:T(8,128)(2,1)S(1)}, bf16[4,64,1024]{2,1,0:T(8,128)(2,1)}, u32[]{:S(2)}, u32[]{:S(2)}) collective-permute-start(bf16[4,64,1024]{2,1,0:T(8,128)(2,1)S(1)} %pad_maximum_fusion.1.refs_1_), channel_id=1, source_target_pairs={{0,2},{2,0},{4,6},{6,4},{8,10},{10,8},{12,14},{14,12},{16,18},{18,... | collective-permute-start | bytes 1572872 | tf_op jit(solution)/shard_map/ppermute | solution.py:904
  26.5 8.1 %collective-permute-start.4 = (bf16[4,64,1024]{2,1,0:T(8,128)(2,1)S(1)}, bf16[4,64,1024]{2,1,0:T(8,128)(2,1)S(1)}, u32[]{:S(2)}, u32[]{:S(2)}) collective-permute-start(bf16[4,64,1024]{2,1,0:T(8,128)(2,1)S(1)} %pad_maximum_fusion.1.refs_1_), channel_id=1, source_target_pairs={{0,1},{1,0},{2,3},{3,2},{4,5},{5,4},{6,7},{7,6},{8,9},{9,8},{10,11... | collective-permute-start | bytes 1572872 | tf_op jit(solution)/shard_map/ppermute | solution.py:908
  26.5 14.4 %collective-permute-start.3 = (bf16[4,64,1024]{2,1,0:T(8,128)(2,1)S(1)}, bf16[4,64,1024]{2,1,0:T(8,128)(2,1)}, u32[]{:S(2)}, u32[]{:S(2)}) collective-permute-start(bf16[4,64,1024]{2,1,0:T(8,128)(2,1)S(1)} %pad_maximum_fusion.1.refs_1_), channel_id=1, source_target_pairs={{0,4},{2,6},{4,0},{6,2},{8,12},{10,14},{12,8},{14,10},{16,20},{18,... | collective-permute-start | bytes 1572872 | tf_op jit(solution)/shard_map/ppermute | solution.py:904
  33.2 28.8 %copy-start.19 = (s32[2]{0:T(128)}, s32[2]{0:T(128)S(1)}, u32[]{:S(2)}) copy-start(s32[2]{0:T(128)S(1)} %pad_add_fusion.refs_0_.ids_ref) | copy-start | bytes 28
  40.9 2.1 collective-permute-start.8
  40.9 6.1 %collective-permute-start.6 = (bf16[4,64,1024]{2,1,0:T(8,128)(2,1)}, bf16[4,64,1024]{2,1,0:T(8,128)(2,1)S(1)}, u32[]{:S(2)}, u32[]{:S(2)}) collective-permute-start(bf16[4,64,1024]{2,1,0:T(8,128)(2,1)} %collective-permute-done.3.refs_1_), channel_id=1, source_target_pairs={{0,1},{1,0},{2,3},{3,2},{4,5},{5,4},{6,7},{7,6},{8,9},{9,8},{10,11... | collective-permute-start | bytes 1572872 | tf_op jit(solution)/shard_map/ppermute | solution.py:908
  41.4 15.2 %collective-permute-start.5 = (bf16[4,64,1024]{2,1,0:T(8,128)(2,1)}, bf16[4,64,1024]{2,1,0:T(8,128)(2,1)S(1)}, u32[]{:S(2)}, u32[]{:S(2)}) collective-permute-start(bf16[4,64,1024]{2,1,0:T(8,128)(2,1)} %collective-permute-done.3.refs_1_), channel_id=1, source_target_pairs={{0,2},{2,0},{4,6},{6,4},{8,10},{10,8},{12,14},{14,12},{16,18},{18,... | collective-permute-start | bytes 1572872 | tf_op jit(solution)/shard_map/ppermute | solution.py:904
  56.6 1.9 collective-permute-start.9
  58.5 3.5 %copy-start.5 = (bf16[1024,512]{1,0:T(8,128)(2,1)S(1)}, bf16[1024,512]{1,0:T(8,128)(2,1)}, u32[]{:S(2)}) copy-start(bf16[1024,512]{1,0:T(8,128)(2,1)} %q_ref.3) | copy-start | bytes 3145732
  58.5 3.5 %copy-start.6 = (bf16[1024,512]{1,0:T(8,128)(2,1)S(1)}, bf16[1024,512]{1,0:T(8,128)(2,1)}, u32[]{:S(2)}) copy-start(bf16[1024,512]{1,0:T(8,128)(2,1)} %o_ref.3) | copy-start | bytes 3145732
  58.5 3.5 %copy-start.23 = (s32[4]{0:T(128)S(1)}, s32[4]{0:T(128)}, u32[]{:S(2)}) copy-start(s32[4]{0:T(128)} %len_ref.5) | copy-start | bytes 52
  61.9 6.6 %copy-start = (bf16[16,128,1024]{2,1,0:T(8,128)(2,1)}, bf16[16,128,1024]{2,1,0:T(8,128)(2,1)S(1)}, u32[]{:S(2)}) copy-start(bf16[16,128,1024]{2,1,0:T(8,128)(2,1)S(1)} %get-tuple-element.103.h_ref) | copy-start | bytes 12582916
  62.0 6.6 %copy-start.3 = (bf16[16,128,256]{2,1,0:T(8,128)(2,1)}, bf16[16,128,256]{2,1,0:T(8,128)(2,1)S(1)}, u32[]{:S(2)}) copy-start(bf16[16,128,256]{2,1,0:T(8,128)(2,1)S(1)} %get-tuple-element.112) | copy-start | bytes 3145732
  62.0 6.6 %copy-start.4 = (bf16[16,192,128]{2,1,0:T(8,128)(2,1)}, bf16[16,192,128]{2,1,0:T(8,128)(2,1)S(1)}, u32[]{:S(2)}) copy-start(bf16[16,192,128]{2,1,0:T(8,128)(2,1)S(1)} %get-tuple-element.111.t_ref) | copy-start | bytes 2359300
  62.0 8.2 %copy-start.8 = (bf16[128,1024]{1,0:T(8,128)(2,1)S(1)}, bf16[128,1024]{1,0:T(8,128)(2,1)}, u32[]{:S(2)}) copy-start(bf16[128,1024]{1,0:T(8,128)(2,1)} %x_ref.1) | copy-start | bytes 786436
  62.0 8.6 %copy-start.22 = (f32[1024]{0:T(1024)S(1)}, f32[1024]{0:T(1024)}, u32[]{:S(2)}) copy-start(f32[1024]{0:T(1024)} %param.16) | copy-start | bytes 12292
  62.0 8.6 %copy-start.29 = (f32[1024]{0:T(1024)S(1)}, f32[1024]{0:T(1024)}, u32[]{:S(2)}) copy-start(f32[1024]{0:T(1024)} %param.17) | copy-start | bytes 12292
  62.1 9.4 %copy-start.9 = (bf16[128,1024]{1,0:T(8,128)(2,1)S(1)}, bf16[128,1024]{1,0:T(8,128)(2,1)}, u32[]{:S(2)}) copy-start(bf16[128,1024]{1,0:T(8,128)(2,1)} %g_ref.3) | copy-start | bytes 786436
  68.6 2.0 copy-start.13
  68.6 1.6 collective-permute-start.10
  71.5 9.6 %copy-start.7 = (bf16[1024,512]{1,0:T(8,128)(2,1)S(1)}, bf16[1024,512]{1,0:T(8,128)(2,1)}, u32[]{:S(2)}) copy-start(bf16[1024,512]{1,0:T(8,128)(2,1)} %o_ref.3) | copy-start | bytes 3145732
  79.4 1.7 collective-permute-start.11
  81.1 1.0 copy-start.11
  83.5 16.2 %all-to-all-start = ((bf16[8,64,128]{2,1,0:T(8,128)(2,1)}), bf16[8,64,128]{2,1,0:T(8,128)(2,1)S(1)}, u32[]{:S(2)}, u32[]{:S(2)}) async-start(bf16[8,64,128]{2,1,0:T(8,128)(2,1)} %get-tuple-element.110), calls=%async_computation | async-start | bytes 262144 | tf_op jit(solution)/shard_map/all_to_all | solution.py:992
  99.8 0.7 copy-start.28
  100.4 12.6 %copy-start.14 = (bf16[128,512]{1,0:T(8,128)(2,1)S(1)}, bf16[128,512]{1,0:T(8,128)(2,1)}, u32[]{:S(2)}) copy-start(bf16[128,512]{1,0:T(8,128)(2,1)} %copy-done.13) | copy-start | bytes 393220
  100.4 12.6 %copy-start.20 = (s32[2]{0:T(128)S(1)}, s32[2]{0:T(128)}, u32[]{:S(2)}) copy-start(s32[2]{0:T(128)} %copy-done.19) | copy-start | bytes 28
  112.3 7.9 %collective-permute-start.12 = (bf16[192,512]{1,0:T(8,128)(2,1)}, bf16[192,512]{1,0:T(8,128)(2,1)S(1)}, u32[]{:S(2)}, u32[]{:S(2)}) collective-permute-start(bf16[192,512]{1,0:T(8,128)(2,1)} %get-tuple-element.114), channel_id=1, source_target_pairs={{0,2},{2,0},{4,6},{6,4},{8,10},{10,8},{12,14},{14,12},{16,18},{18,... | collective-permute-start | bytes 589832 | tf_op jit(solution)/shard_map/ppermute | solution.py:904
  114.8 39.5 %collective-permute-start.18 = (bf16[8,64,512]{2,1,0:T(8,128)(2,1)}, bf16[8,64,512]{2,1,0:T(8,128)(2,1)S(1)}, u32[]{:S(2)}, u32[]{:S(2)}) collective-permute-start(bf16[8,64,512]{2,1,0:T(8,128)(2,1)} %get-tuple-element.130), channel_id=1, source_target_pairs={{0,2},{2,0},{4,6},{6,4},{8,10},{10,8},{12,14},{14,12},{16,18},{18,... | collective-permute-start | bytes 1572872 | tf_op jit(solution)/shard_map/ppermute | solution.py:904
  122.0 20.6 %collective-permute-start.16 = (bf16[192,512]{1,0:T(8,128)(2,1)}, bf16[192,512]{1,0:T(8,128)(2,1)}, u32[]{:S(2)}, u32[]{:S(2)}) collective-permute-start(bf16[192,512]{1,0:T(8,128)(2,1)} %add_convert_fusion.2), channel_id=1, source_target_pairs={{0,24},{2,26},{4,28},{6,30},{8,0},{10,2},{12,4},{14,6},{16,8},{18,... | collective-permute-start | bytes 589832 | tf_op jit(solution)/shard_map/ppermute | solution.py:904
  125.2 26.9 %collective-permute-start.15 = (bf16[192,512]{1,0:T(8,128)(2,1)}, bf16[192,512]{1,0:T(8,128)(2,1)}, u32[]{:S(2)}, u32[]{:S(2)}) collective-permute-start(bf16[192,512]{1,0:T(8,128)(2,1)} %add_convert_fusion.2), channel_id=1, source_target_pairs={{0,16},{2,18},{4,20},{6,22},{8,24},{10,26},{12,28},{14,30},{16,0},... | collective-permute-start | bytes 589832 | tf_op jit(solution)/shard_map/ppermute | solution.py:904
  125.2 26.9 %collective-permute-start.14 = (bf16[192,512]{1,0:T(8,128)(2,1)}, bf16[192,512]{1,0:T(8,128)(2,1)}, u32[]{:S(2)}, u32[]{:S(2)}) collective-permute-start(bf16[192,512]{1,0:T(8,128)(2,1)} %add_convert_fusion.2), channel_id=1, source_target_pairs={{0,8},{2,10},{4,12},{6,14},{8,16},{10,18},{12,20},{14,22},{16,24},... | collective-permute-start | bytes 589832 | tf_op jit(solution)/shard_map/ppermute | solution.py:904
  126.3 28.0 %copy-start.10 = (f32[8,128,128]{2,1,0:T(8,128)S(1)}, f32[8,128,128]{2,1,0:T(8,128)}, u32[]{:S(2)}) copy-start(f32[8,128,128]{2,1,0:T(8,128)} %get-tuple-element.123.kept_ref) | copy-start | bytes 1572868
  126.3 28.0 %copy-start.15 = (bf16[8,64,128]{2,1,0:T(8,128)(2,1)S(1)}, bf16[8,64,128]{2,1,0:T(8,128)(2,1)}, u32[]{:S(2)}) copy-start(bf16[8,64,128]{2,1,0:T(8,128)(2,1)} %get-tuple-element.122.gq_ref) | copy-start | bytes 393220
  126.3 13.5 %collective-permute-start.13 = (bf16[128,1024]{1,0:T(8,128)(2,1)}, bf16[128,1024]{1,0:T(8,128)(2,1)}, u32[]{:S(2)}, u32[]{:S(2)}) collective-permute-start(bf16[128,1024]{1,0:T(8,128)(2,1)} %get-tuple-element.115), channel_id=1, source_target_pairs={{0,1},{1,0},{2,3},{3,2},{4,5},{5,4},{6,7},{7,6},{8,9},{9,8},{10,11... | collective-permute-start | bytes 786440 | tf_op jit(solution)/shard_map/ppermute | solution.py:908
  139.8 14.5 %collective-permute-start.17 = (bf16[8,128,128]{2,1,0:T(8,128)(2,1)}, bf16[8,128,128]{2,1,0:T(8,128)(2,1)S(1)}, u32[]{:S(2)}, u32[]{:S(2)}) collective-permute-start(bf16[8,128,128]{2,1,0:T(8,128)(2,1)} %get-tuple-element.125), channel_id=1, source_target_pairs={{0,2},{2,0},{4,6},{6,4},{8,10},{10,8},{12,14},{14,12},{16,18},{18,... | collective-permute-start | bytes 786440 | tf_op jit(solution)/shard_map/ppermute | solution.py:904
  155.4 33.1 %all-to-all-start.1 = ((bf16[8,448,128]{2,1,0:T(8,128)(2,1)}), bf16[8,448,128]{2,1,0:T(8,128)(2,1)S(1)}, u32[]{:S(2)}, u32[]{:S(2)}) async-start(bf16[8,448,128]{2,1,0:T(8,128)(2,1)} %merge.1), calls=%async_computation.1 | async-start | bytes 1835008 | tf_op jit(solution)/shard_map/all_to_all | solution.py:1008
  159.3 42.4 %collective-permute-start.25 = (bf16[4,192,512]{2,1,0:T(8,128)(2,1)}, bf16[4,192,512]{2,1,0:T(8,128)(2,1)S(1)}, u32[]{:S(2)}, u32[]{:S(2)}) collective-permute-start(bf16[4,192,512]{2,1,0:T(8,128)(2,1)} %pad_maximum_fusion.refs_0_), channel_id=1, source_target_pairs={{0,6},{2,4},{4,2},{6,0},{8,14},{10,12},{12,10},{14,8},{16,22},{18,... | collective-permute-start | bytes 2359304 | tf_op jit(solution)/shard_map/ppermute | solution.py:904
  161.7 42.7 %collective-permute-start.24 = (bf16[4,192,512]{2,1,0:T(8,128)(2,1)}, bf16[4,192,512]{2,1,0:T(8,128)(2,1)}, u32[]{:S(2)}, u32[]{:S(2)}) collective-permute-start(bf16[4,192,512]{2,1,0:T(8,128)(2,1)} %pad_maximum_fusion.refs_0_), channel_id=1, source_target_pairs={{0,4},{2,6},{4,0},{6,2},{8,12},{10,14},{12,8},{14,10},{16,20},{18,... | collective-permute-start | bytes 2359304 | tf_op jit(solution)/shard_map/ppermute | solution.py:904
  161.7 42.7 %collective-permute-start.23 = (bf16[4,192,512]{2,1,0:T(8,128)(2,1)}, bf16[4,192,512]{2,1,0:T(8,128)(2,1)}, u32[]{:S(2)}, u32[]{:S(2)}) collective-permute-start(bf16[4,192,512]{2,1,0:T(8,128)(2,1)} %pad_maximum_fusion.refs_0_), channel_id=1, source_target_pairs={{0,2},{2,0},{4,6},{6,4},{8,10},{10,8},{12,14},{14,12},{16,18},{18,... | collective-permute-start | bytes 2359304 | tf_op jit(solution)/shard_map/ppermute | solution.py:904
  188.5 0.9 copy-start.24
  193.4 1.7 collective-permute-start.19
  195.2 1.0 copy-start.12
  196.1 0.8 copy-start.17
  198.3 18.6 %collective-permute-start.22 = (bf16[88,512]{1,0:T(8,128)(2,1)S(1)}, bf16[88,512]{1,0:T(8,128)(2,1)S(1)}, u32[]{:S(2)}, u32[]{:S(2)}) collective-permute-start(bf16[88,512]{1,0:T(8,128)(2,1)S(1)} %get-tuple-element.143), channel_id=1, source_target_pairs={{0,24},{2,26},{4,28},{6,30},{8,0},{10,2},{12,4},{14,6},{16,8},{18,... | collective-permute-start | bytes 270344 | tf_op jit(solution)/shard_map/ppermute | solution.py:904
  201.7 15.1 %collective-permute-start.21 = (bf16[88,512]{1,0:T(8,128)(2,1)S(1)}, bf16[88,512]{1,0:T(8,128)(2,1)S(1)}, u32[]{:S(2)}, u32[]{:S(2)}) collective-permute-start(bf16[88,512]{1,0:T(8,128)(2,1)S(1)} %get-tuple-element.143), channel_id=1, source_target_pairs={{0,16},{2,18},{4,20},{6,22},{8,24},{10,26},{12,28},{14,30},{16,0},... | collective-permute-start | bytes 270344 | tf_op jit(solution)/shard_map/ppermute | solution.py:904
  201.7 15.1 %copy-start.27 = (bf16[4,192,512]{2,1,0:T(8,128)(2,1)}, bf16[4,192,512]{2,1,0:T(8,128)(2,1)S(1)}, u32[]{:S(2)}) copy-start(bf16[4,192,512]{2,1,0:T(8,128)(2,1)S(1)} %collective-permute-done.25.refs_3_) | copy-start | bytes 2359300
  201.7 15.1 %collective-permute-start.20 = (bf16[88,512]{1,0:T(8,128)(2,1)S(1)}, bf16[88,512]{1,0:T(8,128)(2,1)S(1)}, u32[]{:S(2)}, u32[]{:S(2)}) collective-permute-start(bf16[88,512]{1,0:T(8,128)(2,1)S(1)} %get-tuple-element.143), channel_id=1, source_target_pairs={{0,8},{2,10},{4,12},{6,14},{8,16},{10,18},{12,20},{14,22},{16,24},... | collective-permute-start | bytes 270344 | tf_op jit(solution)/shard_map/ppermute | solution.py:904
  216.9 18.3 %collective-permute-start.28 = (bf16[4,88,512]{2,1,0:T(8,128)(2,1)S(1)}, bf16[4,88,512]{2,1,0:T(8,128)(2,1)S(1)}, u32[]{:S(2)}, u32[]{:S(2)}) collective-permute-start(bf16[4,88,512]{2,1,0:T(8,128)(2,1)S(1)} %pad_maximum_fusion.2.refs_0_), channel_id=1, source_target_pairs={{0,6},{2,4},{4,2},{6,0},{8,14},{10,12},{12,10},{14,8},{16,22},{18,... | collective-permute-start | bytes 1081352 | tf_op jit(solution)/shard_map/ppermute | solution.py:904
  217.9 17.4 %collective-permute-start.27 = (bf16[4,88,512]{2,1,0:T(8,128)(2,1)S(1)}, bf16[4,88,512]{2,1,0:T(8,128)(2,1)S(1)}, u32[]{:S(2)}, u32[]{:S(2)}) collective-permute-start(bf16[4,88,512]{2,1,0:T(8,128)(2,1)S(1)} %pad_maximum_fusion.2.refs_0_), channel_id=1, source_target_pairs={{0,4},{2,6},{4,0},{6,2},{8,12},{10,14},{12,8},{14,10},{16,20},{18,... | collective-permute-start | bytes 1081352 | tf_op jit(solution)/shard_map/ppermute | solution.py:904
  219.6 15.6 %collective-permute-start.26 = (bf16[4,88,512]{2,1,0:T(8,128)(2,1)S(1)}, bf16[4,88,512]{2,1,0:T(8,128)(2,1)S(1)}, u32[]{:S(2)}, u32[]{:S(2)}) collective-permute-start(bf16[4,88,512]{2,1,0:T(8,128)(2,1)S(1)} %pad_maximum_fusion.2.refs_0_), channel_id=1, source_target_pairs={{0,2},{2,0},{4,6},{6,4},{8,10},{10,8},{12,14},{14,12},{16,18},{18,... | collective-permute-start | bytes 1081352 | tf_op jit(solution)/shard_map/ppermute | solution.py:904
  220.5 14.8 %copy-start.21 = (s32[2]{0:T(128)S(1)}, s32[2]{0:T(128)}, u32[]{:S(2)}) copy-start(s32[2]{0:T(128)} %copy-done.19) | copy-start | bytes 28
Sparse Core Ops, SparseCore 0:
  11.5 66.4 all-gather.2
  80.8 71.4 all-gather.4

commit v5 on v3

--- a/solution.py
+++ b/solution.py
@@ -676,56 +676,58 @@
     )(ids, *near(low, attended))
 
 
-def merge_kernel(gq_ref, kept_ref, given_ref, mine_ref, other_ref, out_ref):
+def merge_kernel(gq_ref, kept_ref, given_ref, out_ref):
     out_ref[:, 0:HEAD, :] = gq_ref[...]
-    out_ref[:, HEAD : 3 * HEAD, :] = (kept_ref[...] + given_ref[...].astype(f32)).astype(bf16)
-    lanes = out_ref.shape[2]
-    slots = mine_ref.shape[1]
-    for c in range(mine_ref.shape[2] // lanes):
-        span = slice(c * lanes, (c + 1) * lanes)
-        both = mine_ref[:, :, span] + other_ref[:, :, span].astype(f32)
-        out_ref[:, 3 * HEAD + c * slots : 3 * HEAD + (c + 1) * slots, :] = both.astype(bf16)
-
-
-def merge(gq, kept, given, mine, other):
+    out_ref[:, HEAD:, :] = (kept_ref[...] + given_ref[...].astype(f32)).astype(bf16)
+
+
+def merge(gq, kept, given):
     half, _, rows = gq.shape
-    extra = mine.shape[1] * mine.shape[2] // rows
     return pl.pallas_call(
         merge_kernel,
-        in_specs=[NEAR] * 5,
+        in_specs=[NEAR] * 3,
         out_specs=NEAR,
-        out_shape=jax.ShapeDtypeStruct((half, 3 * HEAD + extra, rows), bf16),
+        out_shape=jax.ShapeDtypeStruct((half, 3 * HEAD, rows), bf16),
         compiler_params=room(8),
         cost_estimate=HINT,
         name="merge",
-    )(*near(gq, kept, given, mine, other))
-
-
-def home_kernel(home_ref, q_ref, v_ref, k_ref, grad_out, slice_out):
+    )(*near(gq, kept, given))
+
+
+def unit_kernel(mine_ref, other_ref, parts_ref, out_ref):
+    rows = mine_ref.shape[0]
+    out_ref[0:rows, :] = (mine_ref[...] + other_ref[...].astype(f32)).astype(bf16)
+    out_ref[rows:, :] = jnp.sum(parts_ref[...].astype(f32), axis=0).astype(bf16)
+
+
+def make_unit(mine, other, parts):
+    rows, wide = mine.shape
+    return pl.pallas_call(
+        unit_kernel,
+        in_specs=[NEAR] * 3,
+        out_specs=NEAR,
+        out_shape=jax.ShapeDtypeStruct((rows + parts.shape[1], wide), bf16),
+        compiler_params=room(8),
+        cost_estimate=HINT,
+        name="make_unit",
+    )(mine, other, parts)
+
+
+def home_kernel(home_ref, q_ref, v_ref, k_ref, grad_out):
     rows = home_ref.shape[2]
     grad = 0.0
     for i, weight in enumerate((q_ref, v_ref, k_ref)):
         across = home_ref[:, i * HEAD : (i + 1) * HEAD, :].reshape(-1, rows)
         grad = grad + lax.dot_general(across.T, weight[...], LAST, preferred_element_type=f32)
     grad_out[...] = grad.astype(bf16)
-    slots = slice_out.shape[0]
-    for c in range(slice_out.shape[1] // rows):
-        at = 3 * HEAD + c * slots
-        whole = jnp.sum(home_ref[:, at : at + slots, :].astype(f32), axis=0)
-        slice_out[:, c * rows : (c + 1) * rows] = whole.astype(bf16)
-
-
-def go_home(home, weights, slots):
-    rows = home.shape[2]
-    width, columns = weights[0].shape
+
+
+def go_home(home, weights):
     return pl.pallas_call(
         home_kernel,
         in_specs=[NEAR] * 4,
-        out_specs=[NEAR] * 2,
-        out_shape=[
-            jax.ShapeDtypeStruct((rows, width), bf16),
-            jax.ShapeDtypeStruct((slots, columns), bf16),
-        ],
+        out_specs=NEAR,
+        out_shape=jax.ShapeDtypeStruct((home.shape[2], weights[0].shape[0]), bf16),
         cost_estimate=HINT,
         name="go_home",
     )(home, *weights)
@@ -830,47 +832,60 @@
 
 
 def finish_heads_kernel(ids_ref, *refs):
-    heads, outs = refs[:4], refs[4:]
+    heads, outs = refs[:5], refs[5:]
     row, part = (ids_ref[0] >> 1) & 1, ids_ref[0] & 1
     wide = heads[0].shape[2]
+    early = pl.program_id(0) < 2
     for k, x in ((0, part), (1, 1 - part)):
         rows = pl.ds(pl.multiple_of(x * wide, wide), wide)
         for i in range(3):
-            this = heads[k][0, i * HEAD : (i + 1) * HEAD, :]
-            that = heads[k + 2][0, i * HEAD : (i + 1) * HEAD, :]
+            span = slice(i * HEAD, (i + 1) * HEAD)
+            this = heads[k][0, span, :]
+            that = heads[2][0, span, :] if k == 0 else jnp.where(early, heads[3][0, span, :], heads[4][0, span, :])
             pair = [jnp.where(row == 0, this, that), jnp.where(row == 0, that, this)]
             outs[i][rows, :] = jnp.concatenate(pair, axis=0).T.astype(f32)
 
 
 def finish_rows_kernel(ids_ref, *refs):
-    pieces, out_ref = refs[:4], refs[4]
+    pieces, out_ref = refs[:5], refs[5]
     slots = pieces[0].shape[1]
     for k in range(4):
         for s in range(4):
+            piece = pieces[k][s] if k < 3 else pieces[3 + s // 2][s % 2]
             at = pl.multiple_of((((ids_ref[0] - 4 * s) & 15) ^ k) * slots, slots)
-            out_ref[pl.ds(at, slots), :] = pieces[k][s].astype(f32)
+            out_ref[pl.ds(at, slots), :] = piece.astype(f32)
 
 
 def finish_rows(ids, pieces, width, columns):
+    slots = width // 16
     return pl.pallas_call(
         finish_rows_kernel,
-        in_specs=[SCALAR] + [NEAR] * 4,
-        out_specs=NEAR,
+        grid_spec=pltpu.PrefetchScalarGridSpec(
+            num_scalar_prefetch=1,
+            grid=(1,),
+            in_specs=[
+                pl.BlockSpec((p.shape[0], slots, columns), lambda i, ids: (0, 3 * HEAD // slots, 0)) for p in pieces
+            ],
+            out_specs=full((width, columns)),
+        ),
         out_shape=jax.ShapeDtypeStruct((width, columns), f32),
-        compiler_params=room(16),
         cost_estimate=HINT,
         name="finish_rows",
-    )(ids, *near(*pieces))
+    )(ids, *pieces)
 
 
 def finish_heads(ids, pieces, width, columns):
     block = pl.BlockSpec((width, columns // 4), lambda s, ids: (0, ((ids[0] - 4 * s) & 15) >> 2))
+    shape = (1, 3 * HEAD, pieces[0].shape[2])
+    whole = pl.BlockSpec(shape, lambda s, ids: (s, 0, 0))
+    early = pl.BlockSpec(shape, lambda s, ids: (jnp.minimum(s, 1), 0, 0))
+    late = pl.BlockSpec(shape, lambda s, ids: (jnp.maximum(s - 2, 0), 0, 0))
     return pl.pallas_call(
         finish_heads_kernel,
         grid_spec=pltpu.PrefetchScalarGridSpec(
             num_scalar_prefetch=1,
             grid=(4,),
-            in_specs=[pl.BlockSpec((1,) + p.shape[1:], lambda s, ids: (s, 0, 0)) for p in pieces],
+            in_specs=[whole, whole, whole, early, late],
             out_specs=[block] * 3,
         ),
         out_shape=[jax.ShapeDtypeStruct((width, columns), f32)] * 3,
@@ -895,8 +910,8 @@
     return jnp.stack(lax.optimization_barrier(parts + first)[:4])
 
 
-def gather_plane(column):
-    return (column,) + tuple(shuffle(column, lambda i, k=k: i ^ k) for k in (1, 2, 3))
+def gather_sides(column):
+    return shuffle(column, lambda i: i ^ 1), shuffle(column, lambda i: i ^ 2)
 
 
 def after(value, *first):
@@ -969,42 +984,41 @@
         middle, grad_two, over_core(grad_two), second_gain, cotangent, output_weight
     )
     ga = lax.all_to_all(to_heads, "blk", 0, 0, tiled=True, axis_index_groups=alike)
-    p = prepare(ids, scene_len, after(head_t, to_heads, g_all), head_n)
+    output_kept, output_given = share_output(ids, after(grad_middle_low, to_heads), attended, count)
+    output_other = shuffle(output_given, lambda i: i ^ 1)
+    p = prepare(ids, scene_len, after(head_t, to_heads, g_all, output_given), head_n)
+    output_kept, output_other, _ = lax.optimization_barrier((output_kept, output_other, p))
+    output_half = (output_kept + output_other.astype(f32)).astype(bf16)
+    output_parts = lax.all_to_all(after(output_half, ga, p), "blk", 0, 0, tiled=True, axis_index_groups=alike)
     grad_q, kept, given, slice_kept, slice_given = back(ids, scene_len, p, ga, head_t, head_n, h1_all)
 
-    output_kept, output_given = share_output(ids, after(grad_middle_low, slice_given), attended, count)
-    output_other = shuffle(output_given, lambda i: i ^ 1)
-    head_slice = (slice_kept + shuffle(slice_given, lambda i: i ^ 1).astype(f32)).astype(bf16)
-    parts = send_column(head_slice)
-
-    given = after(given, head_slice)
-    given = shuffle(given, lambda i: i ^ 1)
-    grad_all = through(after(g_all, head_slice), down_weight)
-    column = stack_column(parts, grad_all)
-    parcel = merge(after(grad_q, column), kept, given, output_kept, output_other)
+    grad_all = through(after(g_all, grad_q), down_weight)
+    slice_other = shuffle(slice_given, lambda i: i ^ 1)
+    unit = make_unit(after(slice_kept, grad_all), slice_other, output_parts)
+    parts = send_column(unit)
+    given = shuffle(after(given, unit), lambda i: i ^ 1)
+    feed = after(feed, unit)
+    layer_out = (middle + (feed.astype(f32) + over_core(feed).astype(f32))).astype(bf16)
+    parcel = merge(after(grad_q, unit), kept, given)
     home = lax.all_to_all(parcel, "blk", 0, 0, tiled=True, axis_index_groups=alike)
-    heads = gather_plane(column)
-
-    feed = after(feed, parcel)
-    layer_out = (middle + (feed.astype(f32) + over_core(feed).astype(f32))).astype(bf16)
-    held = ffn_grads(after(h2_all, column), g_all, grad_all, up_weight, (0, 4), ())
-
-    home = after(home, held[0])
-    grad_one, output_slice = go_home(home, (query_weight, value_weight, key_weight), width // count)
+    held = ffn_grads(after(h2_all, unit, parcel), g_all, grad_all, up_weight, (0, 3), ())
+    column = stack_column(parts, held[0], layer_out)
+    side_x, side_y = gather_sides(column)
+    up_grad, down_grad = ffn_grads(after(h2_all, column), g_all, grad_all, up_weight, (3, 8), held)
+
+    half_x, half_y = lax.optimization_barrier((side_x[2:], side_y[:2], up_grad))[:2]
+    across = shuffle(half_y, lambda i: i ^ 1), shuffle(half_x, lambda i: i ^ 2)
+    home = after(home, up_grad).reshape(heads_here, 3 * HEAD, rows)
+    home = after(home, half_x, half_y)
+    grad_one = go_home(home, (query_weight, value_weight, key_weight))
     input_grad, norm_part = input_back(
         tokens, grad_one, over_core(grad_one), first_gain, grad_middle, second_sums, count
     )
-    norm_parts = lax.all_to_all(norm_part, "blk", 0, 0, tiled=True)
-
-    parts = send_column(output_slice)
-    up_grad, down_grad = ffn_grads(
-        after(h2_all, norm_part, *heads), g_all, grad_all, up_weight, (4, 8), held
-    )
-    rest = gather_plane(stack_column(parts, up_grad, norm_parts))
-    norm_sums = jnp.sum(after(norm_parts, up_grad), axis=0)
-    heads = (after(heads[0], up_grad),) + heads[1:]
+    norm_parts = lax.all_to_all(after(norm_part, *across), "blk", 0, 0, tiled=True)
+    heads = (after(column, norm_part), side_x, side_y) + across
     query_grad, value_grad, key_grad = finish_heads(ids, heads, width, columns)
-    output_grad = finish_rows(ids, rest, width, columns)
+    output_grad = finish_rows(ids, (after(heads[0], query_grad),) + heads[1:], width, columns)
+    norm_sums = jnp.sum(after(norm_parts, output_grad), axis=0)
     return (
         layer_out,
         input_grad,

time: 253 us -> 239 us (0.945)
  starting transfers between devices: 61.6 us -> 53.4 us
  waiting for transfers between devices: 39.3 us -> 32 us
    ppermute x21 -> x16, starting transfers between devices: 36.6 us -> 22.9 us  [shuffle(): return lax.ppermute(block, 'blk', [(i, target(i)) for i in range(16)])]
    all_to_all x1 -> x2, starting transfers between devices: 5.39 us -> 15.4 us  [the longest x1 7.81 us: fast_body(): lax.all_to_all(after(norm_part, *across), 'blk', 0, 0, tiled=True)]
    ppermute x21 -> x16, waiting for transfers between devices: 31 us -> 24.2 us  [shuffle(): return lax.ppermute(block, 'blk', [(i, target(i)) for i in range(16)])]
    all_to_all x1, starting transfers between devices: 11.7 us -> 5.52 us  [fast_body(): lax.all_to_all(parcel, 'blk', 0, 0, tiled=True, axis_index_groups=alike)]
    pallas_call x3 -> x4, Pallas kernels: 8.04 us -> 8.04 us  [the longest x1 3.81 us: go_home(): pl.pallas_call(home_kernel, in_specs=[NEAR] * 4, out_specs=NEAR, out_shap...]
  transfers between devices with their start and end apart: 34 -> 30, of which waited for: 14 -> 15; matrix products, arithmetic and copies ran while one was open for 6% -> 7% of each run, Pallas kernels for 45% -> 49%
where the time goes in v5:
time: 239 us; the launch traced here: 238 us
  Pallas kernels  116 us (49%)
  starting transfers between devices  53.4 us (22%)
  waiting for transfers between devices  32 us (13%)
  between operations  14.6 us (6%)
  local copies, waits for them, and re-layouts  12.8 us (5%)
  other arithmetic  9.31 us (4%)
    pallas_call x2, Pallas kernels, ffn_grads(): pl.pallas_call(ffn_kernel, grid=(last - first,), in_specs=[tokens, tokens...  39.2 us
    ppermute x16, waiting for transfers between devices, shuffle(): return lax.ppermute(block, 'blk', [(i, target(i)) for i in range(16)])  24.2 us
    ppermute x16, starting transfers between devices, shuffle(): return lax.ppermute(block, 'blk', [(i, target(i)) for i in range(16)])  22.9 us
    pallas_call x4, Pallas kernels, project_blocks(): pl.pallas_call(lambda *refs: project_kernel(flip, *refs), in_specs=[SCALA...  14.8 us
    pallas_call x1, Pallas kernels, through(): pl.pallas_call(through_kernel, grid=(hidden // tile,), in_specs=[pl.Block...  13.5 us
    pallas_call x1, Pallas kernels, back(): pl.pallas_call(back_kernel, grid_spec=pltpu.PrefetchScalarGridSpec(num_sc...  9.88 us
    all_to_all x1, starting transfers between devices, fast_body(): lax.all_to_all(to_heads, 'blk', 0, 0, tiled=True, axis_index_groups=alike)  8.64 us
    pallas_call x1, Pallas kernels, own_ffn(): pl.pallas_call(own_kernel, grid=(hidden // tile,), in_specs=[NEAR, NEAR]...  7.89 us
  transfers between devices with their start and end apart: 30, of which 15 were waited for; matrix products, arithmetic and copies ran while one was open for 7% of the time, Pallas kernels for 49%

profile of v5, /device:TPU:0, one launch (start us, length us, event | category | flops | bytes accessed | tf_op | source)
XLA Modules:
  0.0 238.0 jit_solution(7919915513411422789)
XLA Ops:
  7.3 1.7 constant_dynamic-slice_fusion.1
  9.0 0.9 constant_dynamic-slice_fusion.4
  10.0 4.1 %collective-permute-start.1 = (bf16[64,1024]{1,0:T(8,128)(2,1)S(1)}, bf16[64,1024]{1,0:T(8,128)(2,1)S(1)}, u32[]{:S(2)}, u32[]{:S(2)}) collective-permute-start(bf16[64,1024]{1,0:T(8,128)(2,1)S(1)} %constant_dynamic-slice_fusion.4), channel_id=1, source_target_pairs={{0,16},{2,18},{4,20},{6,22},{8,24},{10,26},{12,28},{14,30},{16,0},... | collective-permute-start | bytes 393224 | tf_op jit(solution)/shard_map/ppermute | solution.py:898
  14.1 1.6 collective-permute-start
  15.7 2.2 collective-permute-start.2
  17.9 0.9 fusion.2
  18.8 1.3 dynamic-slice_multiply_fusion
  20.1 4.0 %collective-permute-done.1 = bf16[64,1024]{1,0:T(8,128)(2,1)S(1)} collective-permute-done((bf16[64,1024]{1,0:T(8,128)(2,1)S(1)}, bf16[64,1024]{1,0:T(8,128)(2,1)S(1)}, u32[]{:S(2)}, u32[]{:S(2)}) %collective-permute-start.1) | collective-permute-done | bytes 131104 | tf_op jit(solution)/shard_map/ppermute | solution.py:898
  24.1 0.7 collective-permute-done.2
  24.9 1.6 collective-permute-start.7
  26.5 1.5 collective-permute-start.3
  28.0 1.1 constant_dynamic-slice_fusion.3
  29.1 0.7 copy-done.21
  29.8 1.0 maximum_bitcast_fusion
  30.8 1.2 copy.42.refs_7_
  32.2 1.4 maximum_maximum_fusion.refs_8_
  33.7 3.4 %project_blocks.4 = (bf16[16,128,1024]{2,1,0:T(8,128)(2,1)S(1)}, bf16[16,128,512]{2,1,0:T(8,128)(2,1)S(1)}, bf16[16,128,512]{2,1,0:T(8,128)(2,1)S(1)}, bf16[16,1...) custom-call(s32[2]{0:T(128)S(1)} %pad_add_fusion.refs_0_.ids_ref, bf16[4,64,1024]{2,1,0:T(8,128)(2,1)S(1)} %pad_maximum_fusion.1.refs_1_, ...), custom_call_target="tpu_custom_call" | custom-call | flops 1 | bytes 1 | tf_op jit(solution)/shard_map/project_blocks/pallas_call | solution.py:351
  37.1 3.8 %collective-permute-done.3.refs_1_ = bf16[4,64,1024]{2,1,0:T(8,128)(2,1)} collective-permute-done((bf16[4,64,1024]{2,1,0:T(8,128)(2,1)S(1)}, bf16[4,64,1024]{2,1,0:T(8,128)(2,1)}, u32[]{:S(2)}, u32[]{:S(2)}) %collective-permute-start.3) | collective-permute-done | bytes 524320 | tf_op jit(solution)/shard_map/ppermute | solution.py:898
  41.9 1.1 collective-permute-done.8.refs_2_
  43.0 4.0 %project_blocks.5 = (bf16[16,128,1024]{2,1,0:T(8,128)(2,1)S(1)}, bf16[16,128,512]{2,1,0:T(8,128)(2,1)S(1)}, bf16[16,128,512]{2,1,0:T(8,128)(2,1)S(1)}, bf16[16,1...) custom-call(s32[2]{0:T(128)S(1)} %pad_add_fusion.refs_0_.ids_ref, ...), custom_call_target="tpu_custom_call", output_to_operand_aliasing={{0}: (9, {}), {1}: (10, {}), {2}: (11, {}), {3}: (12, {}), ... | custom-call | flops 1 | bytes 1 | tf_op jit(solution)/shard_map/project_blocks/pallas_call | solution.py:351
  47.0 4.0 %project_blocks.6 = (bf16[16,128,1024]{2,1,0:T(8,128)(2,1)S(1)}, bf16[16,128,512]{2,1,0:T(8,128)(2,1)S(1)}, bf16[16,128,512]{2,1,0:T(8,128)(2,1)S(1)}, bf16[16,1...) custom-call(s32[2]{0:T(128)S(1)} %pad_add_fusion.refs_0_.ids_ref, ...), custom_call_target="tpu_custom_call", output_to_operand_aliasing={{0}: (9, {}), {1}: (10, {}), {2}: (11, {}), {3}: (12, {}), ... | custom-call | flops 1 | bytes 1 | tf_op jit(solution)/shard_map/project_blocks/pallas_call | solution.py:351
  51.0 5.6 %collective-permute-done.5.refs_1_ = bf16[4,64,1024]{2,1,0:T(8,128)(2,1)S(1)} collective-permute-done((bf16[4,64,1024]{2,1,0:T(8,128)(2,1)}, bf16[4,64,1024]{2,1,0:T(8,128)(2,1)S(1)}, u32[]{:S(2)}, u32[]{:S(2)}) %collective-permute-start.5) | collective-permute-done | bytes 524320 | tf_op jit(solution)/shard_map/ppermute | solution.py:898
  56.6 1.9 collective-permute-done.9.refs_2_
  58.5 3.4 %project_blocks.7 = (bf16[16,128,1024]{2,1,0:T(8,128)(2,1)S(1)}, bf16[16,128,512]{2,1,0:T(8,128)(2,1)S(1)}, bf16[16,128,512]{2,1,0:T(8,128)(2,1)S(1)}, bf16[16,1...) custom-call(s32[2]{0:T(128)S(1)} %pad_add_fusion.refs_0_.ids_ref, ...), custom_call_target="tpu_custom_call", output_to_operand_aliasing={{0}: (9, {}), {1}: (10, {}), {2}: (11, {}), {3}: (12, {}), ... | custom-call | flops 1 | bytes 1 | tf_op jit(solution)/shard_map/project_blocks/pallas_call | solution.py:351
  62.1 6.5 %attend.1 = (bf16[128,512]{1,0:T(8,128)(2,1)S(1)}, bf16[128,1024]{1,0:T(8,128)(2,1)S(1)}) custom-call(s32[2]{0:T(128)S(1)} %pad_add_fusion.refs_0_.ids_ref, s32[4]{0:T(128)S(1)} %copy-done.19, bf16[16,128,1024]{2,1,0:T(8,128)(2,1)S(1)} %get-tuple-element.101.h_ref, bf16[2048,512]{1,0:T(8,128)(2,1)S(1)} %bitcast.25, bf16[2048,512]{1,0:T(8,128)(2,1)S(1)} %bitcast.26, ...), custom_call_target="tpu_custom_call" | custom-call | flops 1 | bytes 1 | tf_op jit(solution)/shard_map/attend/pallas_call | solution.py:397
  68.8 1.4 collective-permute-done.10
  70.8 0.7 constant_dynamic-slice_fusion
  71.5 7.9 %own_ffn.1 = (bf16[128,1024]{1,0:T(8,128)(2,1)}, bf16[128,1024]{1,0:T(8,128)(2,1)}) custom-call(bf16[128,1024]{1,0:T(8,128)(2,1)S(1)} %add_convert_fusion.2.h_ref, bf16[128,1024]{1,0:T(8,128)(2,1)S(1)} %copy-done.9, bf16[1024,2048]{1,0:T(8,128)(2,1)} %up_ref.5, bf16[1024,2048]{1,0:T(8,128)(2,1)} %down_ref.3), custom_call_target="tpu_custom_call" | custom-call | flops 1 | bytes 1 | tf_op jit(solution)/shard_map/own_ffn/pallas_call | solution.py:446
  79.5 1.6 collective-permute-done.11.other_ref
  81.1 0.9 copy-done.13
  82.1 1.5 norm_back.1
  83.6 1.0 share_output.1
  84.9 8.6 %all-to-all-start = ((bf16[8,64,128]{2,1,0:T(8,128)(2,1)}), bf16[8,64,128]{2,1,0:T(8,128)(2,1)S(1)}, u32[]{:S(2)}, u32[]{:S(2)}) async-start(bf16[8,64,128]{2,1,0:T(8,128)(2,1)} %get-tuple-element.108), calls=%async_computation | async-start | bytes 262144 | tf_op jit(solution)/shard_map/all_to_all | solution.py:986
  93.6 6.2 %prepare.1.p_ref = bf16[4,2048,256]{2,1,0:T(8,128)(2,1)} custom-call(s32[2]{0:T(128)} %copy-done.17, s32[4]{0:T(128)} %len_ref.5, bf16[16,192,128]{2,1,0:T(8,128)(2,1)} %copy-done.4, bf16[2048,256]{1,0:T(8,128)(2,1)} %bitcast.27), custom_call_target="tpu_custom_call" | custom-call | flops 1 | bytes 1 | tf_op jit(solution)/shard_map/prepare/pallas_call | solution.py:539
  99.8 2.0 add_convert_fusion
  101.9 7.6 %all-to-all-start.1 = ((bf16[8,64,512]{2,1,0:T(8,128)(2,1)}), bf16[8,64,512]{2,1,0:T(8,128)(2,1)S(1)}, u32[]{:S(2)}, u32[]{:S(2)}) async-start(bf16[8,64,512]{2,1,0:T(8,128)(2,1)} %add_convert_fusion), calls=%async_computation.1 | async-start | bytes 1048576 | tf_op jit(solution)/shard_map/all_to_all | solution.py:992
  109.5 9.9 %back.1 = (bf16[8,64,128]{2,1,0:T(8,128)(2,1)}, f32[8,128,128]{2,1,0:T(8,128)}, bf16[8,128,128]{2,1,0:T(8,128)(2,1)}, f32[192,512]{1,0:T(8,128)}, bf16[192,512]{1,0:T(8,128)(2,1)}) custom-call(s32[2]{0:T(128)} %copy-done.17, s32[4]{0:T(128)} %len_ref.5, bf16[4,2048,256]{2,1,0:T(8,128)(2,1)} %prepare.1.p_ref, bf16[8,64,128]{2,1,0:T(8,128)(2,1)} %copy-done.27, ...), custom_call_target="tpu_custom_call" | custom-call | flops 1 | bytes 1 | tf_op jit(solution)/shard_map/back/pallas_call | solution.py:631
  119.6 13.5 %through.1.grad_ref = bf16[2048,2048]{1,0:T(8,128)(2,1)} custom-call(bf16[2048,1024]{1,0:T(8,128)(2,1)} %all-gather.3.cloned.1.call-done.g_ref, bf16[1024,2048]{1,0:T(8,128)(2,1)} %down_ref.3), custom_call_target="tpu_custom_call" | custom-call | flops 8589934592 | bytes 16777216 | tf_op jit(solution)/shard_map/through/pallas_call | solution.py:775
  133.2 1.9 collective-permute-start.15
  135.1 3.8 %collective-permute-start.18 = (bf16[256,512]{1,0:T(8,128)(2,1)S(1)}, bf16[256,512]{1,0:T(8,128)(2,1)S(1)}, u32[]{:S(2)}, u32[]{:S(2)}) collective-permute-start(bf16[256,512]{1,0:T(8,128)(2,1)S(1)} %make_unit.1), channel_id=1, source_target_pairs={{0,24},{2,26},{4,28},{6,30},{8,0},{10,2},{12,4},{14,6},{16,8},{18,... | collective-permute-start | bytes 786440 | tf_op jit(solution)/shard_map/ppermute | solution.py:898
  138.9 1.1 collective-permute-start.16
  140.0 1.5 collective-permute-done.15.given_ref
  141.5 0.8 merge.1
  142.3 5.5 %all-to-all-start.2 = ((bf16[8,192,128]{2,1,0:T(8,128)(2,1)}), bf16[8,192,128]{2,1,0:T(8,128)(2,1)S(1)}, u32[]{:S(2)}, u32[]{:S(2)}) async-start(bf16[8,192,128]{2,1,0:T(8,128)(2,1)} %merge.1), calls=%async_computation.2 | async-start | bytes 786432 | tf_op jit(solution)/shard_map/all_to_all | solution.py:1003
  147.8 1.7 add_convert_fusion.1
  149.6 16.0 %ffn_grads.2 = (f32[1024,2048]{1,0:T(8,128)}, f32[1024,2048]{1,0:T(8,128)}) custom-call(bf16[2048,1024]{1,0:T(8,128)(2,1)} %all-gather.5.cloned.1.call-done.h_ref, bf16[2048,1024]{1,0:T(8,128)(2,1)} %all-gather.3.cloned.1.call-done.g_ref, bf16[2048,2048]{1,0:T(8,128)(2,1)} %through.1.grad_ref, bf16[1024,2048]{1,0:T(8,128)(2,1)} %up_ref.5), custom_call_target="tpu_custom_call" | custom-call | flops 9663676416 | bytes 8388608 | tf_op jit(solution)/shard_map/ffn_grads/pallas_call | solution.py:820
  165.6 4.6 %collective-permute-done.17 = bf16[256,512]{1,0:T(8,128)(2,1)S(1)} collective-permute-done((bf16[256,512]{1,0:T(8,128)(2,1)S(1)}, bf16[256,512]{1,0:T(8,128)(2,1)S(1)}, u32[]{:S(2)}, u32[]{:S(2)}) %collective-permute-start.17) | collective-permute-done | bytes 262176 | tf_op jit(solution)/shard_map/ppermute | solution.py:898
  170.2 1.1 pad_maximum_fusion.refs_0_
  171.3 1.5 collective-permute-start.20
  173.4 23.2 %ffn_grads.3 = (f32[1024,2048]{1,0:T(8,128)}, f32[1024,2048]{1,0:T(8,128)}) custom-call(bf16[2048,1024]{1,0:T(8,128)(2,1)} %all-gather.5.cloned.1.call-done.h_ref, bf16[2048,1024]{1,0:T(8,128)(2,1)} %all-gather.3.cloned.1.call-done.g_ref, bf16[2048,2048]{1,0:T(8,128)(2,1)} %through.1.grad_ref, ...), custom_call_target="tpu_custom_call", output_to_operand_aliasing={{0}: (4, {}), {1}: (5, {})} | custom-call | flops 16106127360 | bytes 8388608 | tf_op jit(solution)/shard_map/ffn_grads/pallas_call | solution.py:820
  196.7 1.1 slice.25
  197.9 1.1 slice.24
  199.0 1.4 collective-permute-start.23
  200.9 0.7 copy-done.26
  201.6 3.8 %go_home.1.mine_ref = bf16[128,1024]{1,0:T(8,128)(2,1)} custom-call(bf16[8,192,128]{2,1,0:T(8,128)(2,1)} %copy-done.26, bf16[1024,512]{1,0:T(8,128)(2,1)} %q_ref.3, bf16[1024,512]{1,0:T(8,128)(2,1)} %v_ref.1, bf16[1024,512]{1,0:T(8,128)(2,1)} %k_ref.1), custom_call_target="tpu_custom_call" | custom-call | flops 1 | bytes 1 | tf_op jit(solution)/shard_map/go_home/pallas_call | solution.py:726
  205.4 1.7 collective-permute-done.21.other_ref
  207.2 0.9 copy-done.10
  208.1 1.3 input_back.1
  209.5 2.6 %collective-permute-done.23.refs_4_ = bf16[2,256,512]{2,1,0:T(8,128)(2,1)S(1)} collective-permute-done((bf16[2,256,512]{2,1,0:T(8,128)(2,1)S(1)}, bf16[2,256,512]{2,1,0:T(8,128)(2,1)S(1)}, u32[]{:S(2)}, u32[]{:S(2)}) %collective-permute-start.23) | collective-permute-done | bytes 524320 | tf_op jit(solution)/shard_map/ppermute | solution.py:898
  212.0 1.2 collective-permute-done.22.refs_3_
  213.2 7.8 %all-to-all-start.3 = ((f32[16,4,1024]{2,1,0:T(4,128)}), f32[16,4,1024]{2,1,0:T(4,128)S(1)}, u32[]{:S(2)}, u32[]{:S(2)}) async-start(f32[16,4,1024]{2,1,0:T(4,128)} %get-tuple-element.146), calls=%async_computation.3 | async-start | bytes 524288 | tf_op jit(solution)/shard_map/all_to_all | solution.py:1017
  221.1 6.1 %finish_heads.1 = (f32[1024,512]{1,0:T(8,128)}, f32[1024,512]{1,0:T(8,128)}, f32[1024,512]{1,0:T(8,128)}) custom-call(s32[2]{0:T(128)} %copy-done.17, bf16[4,256,512]{2,1,0:T(8,128)(2,1)} %copy-done.20, bf16[4,256,512]{2,1,0:T(8,128)(2,1)} %collective-permute-done.19.refs_1_, bf16[4,256,512]{2,1,0:T(8,128)(2,1)} %collective-permute-done.20.refs_2_, ...), custom_call_target="tpu_custom_call" | custom-call | flops 1 | bytes 1 | tf_op jit(solution)/shard_map/finish_heads/pallas_call | solution.py:883
  227.2 3.3 %finish_rows.1 = f32[1024,512]{1,0:T(8,128)} custom-call(s32[2]{0:T(128)} %copy-done.17, bf16[4,256,512]{2,1,0:T(8,128)(2,1)} %copy-done.20, bf16[4,256,512]{2,1,0:T(8,128)(2,1)} %collective-permute-done.19.refs_1_, bf16[4,256,512]{2,1,0:T(8,128)(2,1)} %collective-permute-done.20.refs_2_, bf16[2,256,512]{2,1,0:T(8,128)(2,1)} %copy-done.25, ...), custom_call_target="tpu_custom_call" | custom-call | flops 1 | bytes 1 | tf_op jit(solution)/shard_map/finish_rows/pallas_call | solution.py:861
  230.5 0.6 fusion.1
  (100 shorter events, 4.3 us)
Async XLA Ops:
  7.2 26.5 %copy-start.2 = (bf16[1024,512]{1,0:T(8,128)(2,1)S(1)}, bf16[1024,512]{1,0:T(8,128)(2,1)}, u32[]{:S(2)}) copy-start(bf16[1024,512]{1,0:T(8,128)(2,1)} %v_ref.1) | copy-start | bytes 3145732
  7.2 26.5 %copy-start.1 = (bf16[1024,512]{1,0:T(8,128)(2,1)S(1)}, bf16[1024,512]{1,0:T(8,128)(2,1)}, u32[]{:S(2)}) copy-start(bf16[1024,512]{1,0:T(8,128)(2,1)} %k_ref.1) | copy-start | bytes 3145732
  7.2 26.5 %copy-start.16 = (f32[1024]{0:T(1024)S(1)}, f32[1024]{0:T(1024)}, u32[]{:S(2)}) copy-start(f32[1024]{0:T(1024)} %param.15) | copy-start | bytes 12292
  7.2 26.5 %copy-start.15 = (f32[1024]{0:T(1024)S(1)}, f32[1024]{0:T(1024)}, u32[]{:S(2)}) copy-start(f32[1024]{0:T(1024)} %param.14) | copy-start | bytes 12292
  7.2 86.4 %all-gather.3.cloned.1.call-start = ((), (), s32[]{:S(2)}) async-start(), calls=%async_computation.4 | async-start | bytes 4325376 | tf_op jit(solution)/shard_map/all_gather | solution.py:955
  9.0 140.6 %all-gather.5.cloned.1.call-start = ((), (), s32[]{:S(2)}) async-start(), calls=%async_computation.5 | async-start | bytes 4325376 | tf_op jit(solution)/shard_map/all_gather | solution.py:980
  10.0 14.1 %collective-permute-start.1 = (bf16[64,1024]{1,0:T(8,128)(2,1)S(1)}, bf16[64,1024]{1,0:T(8,128)(2,1)S(1)}, u32[]{:S(2)}, u32[]{:S(2)}) collective-permute-start(bf16[64,1024]{1,0:T(8,128)(2,1)S(1)} %constant_dynamic-slice_fusion.4), channel_id=1, source_target_pairs={{0,16},{2,18},{4,20},{6,22},{8,24},{10,26},{12,28},{14,30},{16,0},... | collective-permute-start | bytes 393224 | tf_op jit(solution)/shard_map/ppermute | solution.py:898
  14.1 10.0 %collective-permute-start = (bf16[64,1024]{1,0:T(8,128)(2,1)S(1)}, bf16[64,1024]{1,0:T(8,128)(2,1)S(1)}, u32[]{:S(2)}, u32[]{:S(2)}) collective-permute-start(bf16[64,1024]{1,0:T(8,128)(2,1)S(1)} %constant_dynamic-slice_fusion.4), channel_id=1, source_target_pairs={{0,8},{2,10},{4,12},{6,14},{8,16},{10,18},{12,20},{14,22},{16,24},... | collective-permute-start | bytes 393224 | tf_op jit(solution)/shard_map/ppermute | solution.py:898
  15.7 9.1 %collective-permute-start.2 = (bf16[64,1024]{1,0:T(8,128)(2,1)S(1)}, bf16[64,1024]{1,0:T(8,128)(2,1)S(1)}, u32[]{:S(2)}, u32[]{:S(2)}) collective-permute-start(bf16[64,1024]{1,0:T(8,128)(2,1)S(1)} %constant_dynamic-slice_fusion.4), channel_id=1, source_target_pairs={{0,24},{2,26},{4,28},{6,30},{8,0},{10,2},{12,4},{14,6},{16,8},{18,... | collective-permute-start | bytes 393224 | tf_op jit(solution)/shard_map/ppermute | solution.py:898
  20.1 9.0 %copy-start.22 = (bf16[1024,64]{1,0:T(8,128)(2,1)}, bf16[1024,64]{1,0:T(8,128)(2,1)S(1)}, u32[]{:S(2)}) copy-start(bf16[1024,64]{1,0:T(8,128)(2,1)S(1)} %get-tuple-element.160) | copy-start | bytes 393220
  20.1 9.0 %copy-start.23 = (bf16[1024,64]{1,0:T(8,128)(2,1)}, bf16[1024,64]{1,0:T(8,128)(2,1)S(1)}, u32[]{:S(2)}) copy-start(bf16[1024,64]{1,0:T(8,128)(2,1)S(1)} %get-tuple-element.161) | copy-start | bytes 393220
  24.9 16.1 %collective-permute-start.7 = (bf16[4,64,1024]{2,1,0:T(8,128)(2,1)S(1)}, bf16[4,64,1024]{2,1,0:T(8,128)(2,1)}, u32[]{:S(2)}, u32[]{:S(2)}) collective-permute-start(bf16[4,64,1024]{2,1,0:T(8,128)(2,1)S(1)} %pad_maximum_fusion.1.refs_1_), channel_id=1, source_target_pairs={{0,2},{2,0},{4,6},{6,4},{8,10},{10,8},{12,14},{14,12},{16,18},{18,... | collective-permute-start | bytes 1572872 | tf_op jit(solution)/shard_map/ppermute | solution.py:898
  26.5 7.2 %collective-permute-start.4 = (bf16[4,64,1024]{2,1,0:T(8,128)(2,1)S(1)}, bf16[4,64,1024]{2,1,0:T(8,128)(2,1)S(1)}, u32[]{:S(2)}, u32[]{:S(2)}) collective-permute-start(bf16[4,64,1024]{2,1,0:T(8,128)(2,1)S(1)} %pad_maximum_fusion.1.refs_1_), channel_id=1, source_target_pairs={{0,1},{1,0},{2,3},{3,2},{4,5},{5,4},{6,7},{7,6},{8,9},{9,8},{10,11... | collective-permute-start | bytes 1572872 | tf_op jit(solution)/shard_map/ppermute | solution.py:902
  26.5 14.4 %collective-permute-start.3 = (bf16[4,64,1024]{2,1,0:T(8,128)(2,1)S(1)}, bf16[4,64,1024]{2,1,0:T(8,128)(2,1)}, u32[]{:S(2)}, u32[]{:S(2)}) collective-permute-start(bf16[4,64,1024]{2,1,0:T(8,128)(2,1)S(1)} %pad_maximum_fusion.1.refs_1_), channel_id=1, source_target_pairs={{0,4},{2,6},{4,0},{6,2},{8,12},{10,14},{12,8},{14,10},{16,20},{18,... | collective-permute-start | bytes 1572872 | tf_op jit(solution)/shard_map/ppermute | solution.py:898
  29.1 0.7 copy-start.21
  32.2 51.4 %copy-start.17 = (s32[2]{0:T(128)}, s32[2]{0:T(128)S(1)}, u32[]{:S(2)}) copy-start(s32[2]{0:T(128)S(1)} %pad_add_fusion.refs_0_.ids_ref) | copy-start | bytes 28
  40.9 2.1 collective-permute-start.8
  40.9 6.1 %collective-permute-start.6 = (bf16[4,64,1024]{2,1,0:T(8,128)(2,1)}, bf16[4,64,1024]{2,1,0:T(8,128)(2,1)S(1)}, u32[]{:S(2)}, u32[]{:S(2)}) collective-permute-start(bf16[4,64,1024]{2,1,0:T(8,128)(2,1)} %collective-permute-done.3.refs_1_), channel_id=1, source_target_pairs={{0,1},{1,0},{2,3},{3,2},{4,5},{5,4},{6,7},{7,6},{8,9},{9,8},{10,11... | collective-permute-start | bytes 1572872 | tf_op jit(solution)/shard_map/ppermute | solution.py:902
  41.4 15.2 %collective-permute-start.5 = (bf16[4,64,1024]{2,1,0:T(8,128)(2,1)}, bf16[4,64,1024]{2,1,0:T(8,128)(2,1)S(1)}, u32[]{:S(2)}, u32[]{:S(2)}) collective-permute-start(bf16[4,64,1024]{2,1,0:T(8,128)(2,1)} %collective-permute-done.3.refs_1_), channel_id=1, source_target_pairs={{0,2},{2,0},{4,6},{6,4},{8,10},{10,8},{12,14},{14,12},{16,18},{18,... | collective-permute-start | bytes 1572872 | tf_op jit(solution)/shard_map/ppermute | solution.py:898
  56.6 1.9 collective-permute-start.9
  58.5 3.5 %copy-start.5 = (bf16[1024,512]{1,0:T(8,128)(2,1)S(1)}, bf16[1024,512]{1,0:T(8,128)(2,1)}, u32[]{:S(2)}) copy-start(bf16[1024,512]{1,0:T(8,128)(2,1)} %q_ref.3) | copy-start | bytes 3145732
  58.5 3.5 %copy-start.6 = (bf16[1024,512]{1,0:T(8,128)(2,1)S(1)}, bf16[1024,512]{1,0:T(8,128)(2,1)}, u32[]{:S(2)}) copy-start(bf16[1024,512]{1,0:T(8,128)(2,1)} %o_ref.3) | copy-start | bytes 3145732
  58.5 3.5 %copy-start.19 = (s32[4]{0:T(128)S(1)}, s32[4]{0:T(128)}, u32[]{:S(2)}) copy-start(s32[4]{0:T(128)} %len_ref.5) | copy-start | bytes 52
  62.0 6.6 %copy-start = (bf16[16,128,1024]{2,1,0:T(8,128)(2,1)}, bf16[16,128,1024]{2,1,0:T(8,128)(2,1)S(1)}, u32[]{:S(2)}) copy-start(bf16[16,128,1024]{2,1,0:T(8,128)(2,1)S(1)} %get-tuple-element.101.h_ref) | copy-start | bytes 12582916
  62.0 6.6 %copy-start.3 = (bf16[16,128,256]{2,1,0:T(8,128)(2,1)}, bf16[16,128,256]{2,1,0:T(8,128)(2,1)S(1)}, u32[]{:S(2)}) copy-start(bf16[16,128,256]{2,1,0:T(8,128)(2,1)S(1)} %get-tuple-element.114) | copy-start | bytes 3145732
  62.0 6.6 %copy-start.4 = (bf16[16,192,128]{2,1,0:T(8,128)(2,1)}, bf16[16,192,128]{2,1,0:T(8,128)(2,1)S(1)}, u32[]{:S(2)}) copy-start(bf16[16,192,128]{2,1,0:T(8,128)(2,1)S(1)} %get-tuple-element.113.t_ref) | copy-start | bytes 2359300
  62.0 8.2 %copy-start.8 = (bf16[128,1024]{1,0:T(8,128)(2,1)S(1)}, bf16[128,1024]{1,0:T(8,128)(2,1)}, u32[]{:S(2)}) copy-start(bf16[128,1024]{1,0:T(8,128)(2,1)} %x_ref.1) | copy-start | bytes 786436
  62.1 8.6 %copy-start.18 = (f32[1024]{0:T(1024)S(1)}, f32[1024]{0:T(1024)}, u32[]{:S(2)}) copy-start(f32[1024]{0:T(1024)} %param.16) | copy-start | bytes 12292
  62.1 8.6 %copy-start.28 = (f32[1024]{0:T(1024)S(1)}, f32[1024]{0:T(1024)}, u32[]{:S(2)}) copy-start(f32[1024]{0:T(1024)} %param.17) | copy-start | bytes 12292
  62.1 9.4 %copy-start.9 = (bf16[128,1024]{1,0:T(8,128)(2,1)S(1)}, bf16[128,1024]{1,0:T(8,128)(2,1)}, u32[]{:S(2)}) copy-start(bf16[128,1024]{1,0:T(8,128)(2,1)} %g_ref.3) | copy-start | bytes 786436
  68.6 1.6 collective-permute-start.10
  71.5 9.6 %copy-start.7 = (bf16[1024,512]{1,0:T(8,128)(2,1)S(1)}, bf16[1024,512]{1,0:T(8,128)(2,1)}, u32[]{:S(2)}) copy-start(bf16[1024,512]{1,0:T(8,128)(2,1)} %o_ref.3) | copy-start | bytes 3145732
  79.4 1.7 collective-permute-start.11
  81.1 1.0 copy-start.13
  84.6 15.2 %collective-permute-start.13 = (bf16[8,64,512]{2,1,0:T(8,128)(2,1)S(1)}, bf16[8,64,512]{2,1,0:T(8,128)(2,1)}, u32[]{:S(2)}, u32[]{:S(2)}) collective-permute-start(bf16[8,64,512]{2,1,0:T(8,128)(2,1)S(1)} %get-tuple-element.112), channel_id=1, source_target_pairs={{0,2},{2,0},{4,6},{6,4},{8,10},{10,8},{12,14},{14,12},{16,18},{18,... | collective-permute-start | bytes 1572872 | tf_op jit(solution)/shard_map/ppermute | solution.py:898
  84.9 16.9 %all-to-all-start = ((bf16[8,64,128]{2,1,0:T(8,128)(2,1)}), bf16[8,64,128]{2,1,0:T(8,128)(2,1)S(1)}, u32[]{:S(2)}, u32[]{:S(2)}) async-start(bf16[8,64,128]{2,1,0:T(8,128)(2,1)} %get-tuple-element.108), calls=%async_computation | async-start | bytes 262144 | tf_op jit(solution)/shard_map/all_to_all | solution.py:986
  101.9 7.6 %copy-start.27 = (bf16[8,64,128]{2,1,0:T(8,128)(2,1)}, bf16[8,64,128]{2,1,0:T(8,128)(2,1)S(1)}, u32[]{:S(2)}) copy-start(bf16[8,64,128]{2,1,0:T(8,128)(2,1)S(1)} %all-to-all-done.ga_ref) | copy-start | bytes 393220
  101.9 31.2 %all-to-all-start.1 = ((bf16[8,64,512]{2,1,0:T(8,128)(2,1)}), bf16[8,64,512]{2,1,0:T(8,128)(2,1)S(1)}, u32[]{:S(2)}, u32[]{:S(2)}) async-start(bf16[8,64,512]{2,1,0:T(8,128)(2,1)} %add_convert_fusion), calls=%async_computation.1 | async-start | bytes 1048576 | tf_op jit(solution)/shard_map/all_to_all | solution.py:992
  119.3 13.7 %copy-start.12 = (f32[192,512]{1,0:T(8,128)S(1)}, f32[192,512]{1,0:T(8,128)}, u32[]{:S(2)}) copy-start(f32[192,512]{1,0:T(8,128)} %get-tuple-element.118.mine_ref) | copy-start | bytes 1179652
  119.4 22.1 %copy-start.11 = (f32[8,128,128]{2,1,0:T(8,128)S(1)}, f32[8,128,128]{2,1,0:T(8,128)}, u32[]{:S(2)}) copy-start(f32[8,128,128]{2,1,0:T(8,128)} %get-tuple-element.126.kept_ref) | copy-start | bytes 1572868
  119.4 22.1 %copy-start.14 = (bf16[8,64,128]{2,1,0:T(8,128)(2,1)S(1)}, bf16[8,64,128]{2,1,0:T(8,128)(2,1)}, u32[]{:S(2)}) copy-start(bf16[8,64,128]{2,1,0:T(8,128)(2,1)} %get-tuple-element.125.gq_ref) | copy-start | bytes 393220
  119.4 13.7 %collective-permute-start.12 = (bf16[192,512]{1,0:T(8,128)(2,1)}, bf16[192,512]{1,0:T(8,128)(2,1)S(1)}, u32[]{:S(2)}, u32[]{:S(2)}) collective-permute-start(bf16[192,512]{1,0:T(8,128)(2,1)} %get-tuple-element.119), channel_id=1, source_target_pairs={{0,2},{2,0},{4,6},{6,4},{8,10},{10,8},{12,14},{14,12},{16,18},{18,... | collective-permute-start | bytes 589832 | tf_op jit(solution)/shard_map/ppermute | solution.py:898
  133.2 8.3 %collective-permute-start.15 = (bf16[8,128,128]{2,1,0:T(8,128)(2,1)}, bf16[8,128,128]{2,1,0:T(8,128)(2,1)S(1)}, u32[]{:S(2)}, u32[]{:S(2)}) collective-permute-start(bf16[8,128,128]{2,1,0:T(8,128)(2,1)} %get-tuple-element.128), channel_id=1, source_target_pairs={{0,2},{2,0},{4,6},{6,4},{8,10},{10,8},{12,14},{14,12},{16,18},{18,... | collective-permute-start | bytes 786440 | tf_op jit(solution)/shard_map/ppermute | solution.py:898
  135.1 12.8 %collective-permute-start.14 = (bf16[128,1024]{1,0:T(8,128)(2,1)}, bf16[128,1024]{1,0:T(8,128)(2,1)S(1)}, u32[]{:S(2)}, u32[]{:S(2)}) collective-permute-start(bf16[128,1024]{1,0:T(8,128)(2,1)} %get-tuple-element.124), channel_id=1, source_target_pairs={{0,1},{1,0},{2,3},{3,2},{4,5},{5,4},{6,7},{7,6},{8,9},{9,8},{10,11... | collective-permute-start | bytes 786440 | tf_op jit(solution)/shard_map/ppermute | solution.py:902
  135.1 30.5 %collective-permute-start.18 = (bf16[256,512]{1,0:T(8,128)(2,1)S(1)}, bf16[256,512]{1,0:T(8,128)(2,1)S(1)}, u32[]{:S(2)}, u32[]{:S(2)}) collective-permute-start(bf16[256,512]{1,0:T(8,128)(2,1)S(1)} %make_unit.1), channel_id=1, source_target_pairs={{0,24},{2,26},{4,28},{6,30},{8,0},{10,2},{12,4},{14,6},{16,8},{18,... | collective-permute-start | bytes 786440 | tf_op jit(solution)/shard_map/ppermute | solution.py:898
  138.9 31.4 %collective-permute-start.17 = (bf16[256,512]{1,0:T(8,128)(2,1)S(1)}, bf16[256,512]{1,0:T(8,128)(2,1)S(1)}, u32[]{:S(2)}, u32[]{:S(2)}) collective-permute-start(bf16[256,512]{1,0:T(8,128)(2,1)S(1)} %make_unit.1), channel_id=1, source_target_pairs={{0,16},{2,18},{4,20},{6,22},{8,24},{10,26},{12,28},{14,30},{16,0},... | collective-permute-start | bytes 786440 | tf_op jit(solution)/shard_map/ppermute | solution.py:898
  138.9 31.4 %collective-permute-start.16 = (bf16[256,512]{1,0:T(8,128)(2,1)S(1)}, bf16[256,512]{1,0:T(8,128)(2,1)}, u32[]{:S(2)}, u32[]{:S(2)}) collective-permute-start(bf16[256,512]{1,0:T(8,128)(2,1)S(1)} %make_unit.1), channel_id=1, source_target_pairs={{0,8},{2,10},{4,12},{6,14},{8,16},{10,18},{12,20},{14,22},{16,24},... | collective-permute-start | bytes 786440 | tf_op jit(solution)/shard_map/ppermute | solution.py:898
  142.3 58.6 %all-to-all-start.2 = ((bf16[8,192,128]{2,1,0:T(8,128)(2,1)}), bf16[8,192,128]{2,1,0:T(8,128)(2,1)S(1)}, u32[]{:S(2)}, u32[]{:S(2)}) async-start(bf16[8,192,128]{2,1,0:T(8,128)(2,1)} %merge.1), calls=%async_computation.2 | async-start | bytes 786432 | tf_op jit(solution)/shard_map/all_to_all | solution.py:1003
  171.3 25.3 %copy-start.20 = (bf16[4,256,512]{2,1,0:T(8,128)(2,1)}, bf16[4,256,512]{2,1,0:T(8,128)(2,1)S(1)}, u32[]{:S(2)}) copy-start(bf16[4,256,512]{2,1,0:T(8,128)(2,1)S(1)} %pad_maximum_fusion.refs_0_) | copy-start | bytes 3145732
  171.3 25.3 %collective-permute-start.20 = (bf16[4,256,512]{2,1,0:T(8,128)(2,1)S(1)}, bf16[4,256,512]{2,1,0:T(8,128)(2,1)}, u32[]{:S(2)}, u32[]{:S(2)}) collective-permute-start(bf16[4,256,512]{2,1,0:T(8,128)(2,1)S(1)} %pad_maximum_fusion.refs_0_), channel_id=1, source_target_pairs={{0,4},{2,6},{4,0},{6,2},{8,12},{10,14},{12,8},{14,10},{16,20},{18,... | collective-permute-start | bytes 3145736 | tf_op jit(solution)/shard_map/ppermute | solution.py:898
  172.9 25.0 %collective-permute-start.19 = (bf16[4,256,512]{2,1,0:T(8,128)(2,1)S(1)}, bf16[4,256,512]{2,1,0:T(8,128)(2,1)}, u32[]{:S(2)}, u32[]{:S(2)}) collective-permute-start(bf16[4,256,512]{2,1,0:T(8,128)(2,1)S(1)} %pad_maximum_fusion.refs_0_), channel_id=1, source_target_pairs={{0,2},{2,0},{4,6},{6,4},{8,10},{10,8},{12,14},{14,12},{16,18},{18,... | collective-permute-start | bytes 3145736 | tf_op jit(solution)/shard_map/ppermute | solution.py:898
  199.0 13.1 %collective-permute-start.23 = (bf16[2,256,512]{2,1,0:T(8,128)(2,1)S(1)}, bf16[2,256,512]{2,1,0:T(8,128)(2,1)S(1)}, u32[]{:S(2)}, u32[]{:S(2)}) collective-permute-start(bf16[2,256,512]{2,1,0:T(8,128)(2,1)S(1)} %slice.24), channel_id=1, source_target_pairs={{0,4},{2,6},{4,0},{6,2},{8,12},{10,14},{12,8},{14,10},{16,20},{18,... | collective-permute-start | bytes 1572872 | tf_op jit(solution)/shard_map/ppermute | solution.py:898
  200.4 12.8 %collective-permute-start.22 = (bf16[2,256,512]{2,1,0:T(8,128)(2,1)S(1)}, bf16[2,256,512]{2,1,0:T(8,128)(2,1)S(1)}, u32[]{:S(2)}, u32[]{:S(2)}) collective-permute-start(bf16[2,256,512]{2,1,0:T(8,128)(2,1)S(1)} %slice.25), channel_id=1, source_target_pairs={{0,2},{2,0},{4,6},{6,4},{8,10},{10,8},{12,14},{14,12},{16,18},{18,... | collective-permute-start | bytes 1572872 | tf_op jit(solution)/shard_map/ppermute | solution.py:898
  200.9 0.7 copy-start.26
  205.4 1.7 collective-permute-start.21
  207.2 1.0 copy-start.10
  212.0 9.0 %copy-start.24 = (bf16[2,256,512]{2,1,0:T(8,128)(2,1)}, bf16[2,256,512]{2,1,0:T(8,128)(2,1)S(1)}, u32[]{:S(2)}) copy-start(bf16[2,256,512]{2,1,0:T(8,128)(2,1)S(1)} %collective-permute-done.23.refs_4_) | copy-start | bytes 1572868
  213.2 7.8 %copy-start.25 = (bf16[2,256,512]{2,1,0:T(8,128)(2,1)}, bf16[2,256,512]{2,1,0:T(8,128)(2,1)S(1)}, u32[]{:S(2)}) copy-start(bf16[2,256,512]{2,1,0:T(8,128)(2,1)S(1)} %collective-permute-done.22.refs_3_) | copy-start | bytes 1572868
  213.2 17.2 %all-to-all-start.3 = ((f32[16,4,1024]{2,1,0:T(4,128)}), f32[16,4,1024]{2,1,0:T(4,128)S(1)}, u32[]{:S(2)}, u32[]{:S(2)}) async-start(f32[16,4,1024]{2,1,0:T(4,128)} %get-tuple-element.146), calls=%async_computation.3 | async-start | bytes 524288 | tf_op jit(solution)/shard_map/all_to_all | solution.py:1017
Sparse Core Ops, SparseCore 0:
  11.5 66.3 all-gather.2
  80.7 66.0 all-gather.4

commit v6 on v5

--- a/solution.py
+++ b/solution.py
@@ -831,66 +831,51 @@
     )(h, g, grad, up_weight, *held)
 
 
-def finish_heads_kernel(ids_ref, *refs):
-    heads, outs = refs[:5], refs[5:]
+def finish_kernel(ids_ref, *refs):
+    pieces, outs = refs[:5], refs[5:]
     row, part = (ids_ref[0] >> 1) & 1, ids_ref[0] & 1
-    wide = heads[0].shape[2]
+    wide = pieces[0].shape[2]
     early = pl.program_id(0) < 2
+
+    def rows_of(k, span):
+        if k < 3:
+            return pieces[k][0, span, :]
+        return jnp.where(early, pieces[3][0, span, :], pieces[4][0, span, :])
+
     for k, x in ((0, part), (1, 1 - part)):
         rows = pl.ds(pl.multiple_of(x * wide, wide), wide)
         for i in range(3):
             span = slice(i * HEAD, (i + 1) * HEAD)
-            this = heads[k][0, span, :]
-            that = heads[2][0, span, :] if k == 0 else jnp.where(early, heads[3][0, span, :], heads[4][0, span, :])
+            this, that = rows_of(k, span), rows_of(k + 2, span)
             pair = [jnp.where(row == 0, this, that), jnp.where(row == 0, that, this)]
             outs[i][rows, :] = jnp.concatenate(pair, axis=0).T.astype(f32)
-
-
-def finish_rows_kernel(ids_ref, *refs):
-    pieces, out_ref = refs[:5], refs[5]
-    slots = pieces[0].shape[1]
+    slots = pieces[0].shape[1] - 3 * HEAD
     for k in range(4):
-        for s in range(4):
-            piece = pieces[k][s] if k < 3 else pieces[3 + s // 2][s % 2]
-            at = pl.multiple_of((((ids_ref[0] - 4 * s) & 15) ^ k) * slots, slots)
-            out_ref[pl.ds(at, slots), :] = piece.astype(f32)
-
-
-def finish_rows(ids, pieces, width, columns):
-    slots = width // 16
-    return pl.pallas_call(
-        finish_rows_kernel,
-        grid_spec=pltpu.PrefetchScalarGridSpec(
-            num_scalar_prefetch=1,
-            grid=(1,),
-            in_specs=[
-                pl.BlockSpec((p.shape[0], slots, columns), lambda i, ids: (0, 3 * HEAD // slots, 0)) for p in pieces
-            ],
-            out_specs=full((width, columns)),
-        ),
-        out_shape=jax.ShapeDtypeStruct((width, columns), f32),
-        cost_estimate=HINT,
-        name="finish_rows",
-    )(ids, *pieces)
-
-
-def finish_heads(ids, pieces, width, columns):
-    block = pl.BlockSpec((width, columns // 4), lambda s, ids: (0, ((ids[0] - 4 * s) & 15) >> 2))
-    shape = (1, 3 * HEAD, pieces[0].shape[2])
+        at = pl.multiple_of(((ids_ref[0] & 3) ^ k) * slots, slots)
+        outs[3][pl.ds(at, slots), :] = rows_of(k, slice(3 * HEAD, None)).astype(f32)
+
+
+def finish(ids, pieces, width, columns):
+    def plane(s, ids):
+        return ((ids[0] - 4 * s) & 15) >> 2
+
+    shape = (1,) + pieces[0].shape[1:]
     whole = pl.BlockSpec(shape, lambda s, ids: (s, 0, 0))
     early = pl.BlockSpec(shape, lambda s, ids: (jnp.minimum(s, 1), 0, 0))
     late = pl.BlockSpec(shape, lambda s, ids: (jnp.maximum(s - 2, 0), 0, 0))
-    return pl.pallas_call(
-        finish_heads_kernel,
+    across = pl.BlockSpec((width, columns // 4), lambda s, ids: (0, plane(s, ids)))
+    down = pl.BlockSpec((width // 4, columns), lambda s, ids: (plane(s, ids), 0))
+    return pl.pallas_call(
+        finish_kernel,
         grid_spec=pltpu.PrefetchScalarGridSpec(
             num_scalar_prefetch=1,
             grid=(4,),
             in_specs=[whole, whole, whole, early, late],
-            out_specs=[block] * 3,
-        ),
-        out_shape=[jax.ShapeDtypeStruct((width, columns), f32)] * 3,
-        cost_estimate=HINT,
-        name="finish_heads",
+            out_specs=[across] * 3 + [down],
+        ),
+        out_shape=[jax.ShapeDtypeStruct((width, columns), f32)] * 4,
+        cost_estimate=HINT,
+        name="finish",
     )(ids, *pieces)
 
 
@@ -1014,10 +999,9 @@
     input_grad, norm_part = input_back(
         tokens, grad_one, over_core(grad_one), first_gain, grad_middle, second_sums, count
     )
-    norm_parts = lax.all_to_all(after(norm_part, *across), "blk", 0, 0, tiled=True)
+    norm_parts = lax.all_to_all(norm_part, "blk", 0, 0, tiled=True)
     heads = (after(column, norm_part), side_x, side_y) + across
-    query_grad, value_grad, key_grad = finish_heads(ids, heads, width, columns)
-    output_grad = finish_rows(ids, (after(heads[0], query_grad),) + heads[1:], width, columns)
+    query_grad, value_grad, key_grad, output_grad = finish(ids, heads, width, columns)
     norm_sums = jnp.sum(after(norm_parts, output_grad), axis=0)
     return (
         layer_out,

time: 239 us -> 237 us (level)
  Pallas kernels: 116 us -> 113 us
    pallas_call x2 -> x1, Pallas kernels: 9.41 us -> 6.65 us  [finish(): pl.pallas_call(finish_kernel, grid_spec=pltpu.PrefetchScalarGridSpec(num_...]
  transfers between devices with their start and end apart: 30 -> 30, of which waited for: 15 -> 12; matrix products, arithmetic and copies ran while one was open for 7% -> 7% of each run, Pallas kernels for 49% -> 47%
where the time goes in v6:
time: 237 us; the launch traced here: 234 us
  Pallas kernels  113 us (48%)
  starting transfers between devices  53 us (22%)
  waiting for transfers between devices  30.9 us (13%)
  between operations  14.6 us (6%)
  local copies, waits for them, and re-layouts  13.1 us (6%)
  other arithmetic  9.31 us (4%)
    pallas_call x2, Pallas kernels, ffn_grads(): pl.pallas_call(ffn_kernel, grid=(last - first,), in_specs=[tokens, tokens...  39.2 us
    ppermute x16, waiting for transfers between devices, shuffle(): return lax.ppermute(block, 'blk', [(i, target(i)) for i in range(16)])  24.7 us
    ppermute x16, starting transfers between devices, shuffle(): return lax.ppermute(block, 'blk', [(i, target(i)) for i in range(16)])  23.1 us
    pallas_call x4, Pallas kernels, project_blocks(): pl.pallas_call(lambda *refs: project_kernel(flip, *refs), in_specs=[SCALA...  14.8 us
    pallas_call x1, Pallas kernels, through(): pl.pallas_call(through_kernel, grid=(hidden // tile,), in_specs=[pl.Block...  13.4 us
    pallas_call x1, Pallas kernels, back(): pl.pallas_call(back_kernel, grid_spec=pltpu.PrefetchScalarGridSpec(num_sc...  9.88 us
    all_to_all x1, starting transfers between devices, fast_body(): lax.all_to_all(to_heads, 'blk', 0, 0, tiled=True, axis_index_groups=alike)  8.64 us
    pallas_call x1, Pallas kernels, own_ffn(): pl.pallas_call(own_kernel, grid=(hidden // tile,), in_specs=[NEAR, NEAR]...  7.89 us
  transfers between devices with their start and end apart: 30, of which 12 were waited for; matrix products, arithmetic and copies ran while one was open for 7% of the time, Pallas kernels for 47%

profile of v6, /device:TPU:0, one launch (start us, length us, event | category | flops | bytes accessed | tf_op | source)
XLA Modules:
  0.0 233.9 jit_solution(3611111377806717772)
XLA Ops:
  7.3 1.7 constant_dynamic-slice_fusion.1
  9.0 0.9 constant_dynamic-slice_fusion.4
  10.0 4.1 %collective-permute-start.1 = (bf16[64,1024]{1,0:T(8,128)(2,1)S(1)}, bf16[64,1024]{1,0:T(8,128)(2,1)S(1)}, u32[]{:S(2)}, u32[]{:S(2)}) collective-permute-start(bf16[64,1024]{1,0:T(8,128)(2,1)S(1)} %constant_dynamic-slice_fusion.4), channel_id=1, source_target_pairs={{0,16},{2,18},{4,20},{6,22},{8,24},{10,26},{12,28},{14,30},{16,0},... | collective-permute-start | bytes 393224 | tf_op jit(solution)/shard_map/ppermute | solution.py:883
  14.1 1.6 collective-permute-start
  15.7 2.2 collective-permute-start.2
  17.9 0.9 fusion.2
  18.8 1.3 dynamic-slice_multiply_fusion
  20.1 4.0 %collective-permute-done.1 = bf16[64,1024]{1,0:T(8,128)(2,1)S(1)} collective-permute-done((bf16[64,1024]{1,0:T(8,128)(2,1)S(1)}, bf16[64,1024]{1,0:T(8,128)(2,1)S(1)}, u32[]{:S(2)}, u32[]{:S(2)}) %collective-permute-start.1) | collective-permute-done | bytes 131104 | tf_op jit(solution)/shard_map/ppermute | solution.py:883
  24.1 0.7 collective-permute-done.2
  24.9 1.6 collective-permute-start.7
  26.5 1.5 collective-permute-start.3
  28.0 1.1 constant_dynamic-slice_fusion.3
  29.1 0.7 copy-done.21
  29.8 1.0 maximum_bitcast_fusion
  30.8 1.2 copy.42.refs_7_
  32.2 1.4 maximum_maximum_fusion.refs_8_
  33.7 3.4 %project_blocks.4 = (bf16[16,128,1024]{2,1,0:T(8,128)(2,1)S(1)}, bf16[16,128,512]{2,1,0:T(8,128)(2,1)S(1)}, bf16[16,128,512]{2,1,0:T(8,128)(2,1)S(1)}, bf16[16,1...) custom-call(s32[2]{0:T(128)S(1)} %pad_add_fusion.refs_0_.ids_ref, bf16[4,64,1024]{2,1,0:T(8,128)(2,1)S(1)} %pad_maximum_fusion.1.refs_1_, ...), custom_call_target="tpu_custom_call" | custom-call | flops 1 | bytes 1 | tf_op jit(solution)/shard_map/project_blocks/pallas_call | solution.py:351
  37.1 3.8 %collective-permute-done.3.refs_1_ = bf16[4,64,1024]{2,1,0:T(8,128)(2,1)} collective-permute-done((bf16[4,64,1024]{2,1,0:T(8,128)(2,1)S(1)}, bf16[4,64,1024]{2,1,0:T(8,128)(2,1)}, u32[]{:S(2)}, u32[]{:S(2)}) %collective-permute-start.3) | collective-permute-done | bytes 524320 | tf_op jit(solution)/shard_map/ppermute | solution.py:883
  41.9 1.1 collective-permute-done.8.refs_2_
  43.0 4.0 %project_blocks.5 = (bf16[16,128,1024]{2,1,0:T(8,128)(2,1)S(1)}, bf16[16,128,512]{2,1,0:T(8,128)(2,1)S(1)}, bf16[16,128,512]{2,1,0:T(8,128)(2,1)S(1)}, bf16[16,1...) custom-call(s32[2]{0:T(128)S(1)} %pad_add_fusion.refs_0_.ids_ref, ...), custom_call_target="tpu_custom_call", output_to_operand_aliasing={{0}: (9, {}), {1}: (10, {}), {2}: (11, {}), {3}: (12, {}), ... | custom-call | flops 1 | bytes 1 | tf_op jit(solution)/shard_map/project_blocks/pallas_call | solution.py:351
  47.0 4.0 %project_blocks.6 = (bf16[16,128,1024]{2,1,0:T(8,128)(2,1)S(1)}, bf16[16,128,512]{2,1,0:T(8,128)(2,1)S(1)}, bf16[16,128,512]{2,1,0:T(8,128)(2,1)S(1)}, bf16[16,1...) custom-call(s32[2]{0:T(128)S(1)} %pad_add_fusion.refs_0_.ids_ref, ...), custom_call_target="tpu_custom_call", output_to_operand_aliasing={{0}: (9, {}), {1}: (10, {}), {2}: (11, {}), {3}: (12, {}), ... | custom-call | flops 1 | bytes 1 | tf_op jit(solution)/shard_map/project_blocks/pallas_call | solution.py:351
  51.0 5.6 %collective-permute-done.5.refs_1_ = bf16[4,64,1024]{2,1,0:T(8,128)(2,1)S(1)} collective-permute-done((bf16[4,64,1024]{2,1,0:T(8,128)(2,1)}, bf16[4,64,1024]{2,1,0:T(8,128)(2,1)S(1)}, u32[]{:S(2)}, u32[]{:S(2)}) %collective-permute-start.5) | collective-permute-done | bytes 524320 | tf_op jit(solution)/shard_map/ppermute | solution.py:883
  56.6 1.9 collective-permute-done.9.refs_2_
  58.5 3.4 %project_blocks.7 = (bf16[16,128,1024]{2,1,0:T(8,128)(2,1)S(1)}, bf16[16,128,512]{2,1,0:T(8,128)(2,1)S(1)}, bf16[16,128,512]{2,1,0:T(8,128)(2,1)S(1)}, bf16[16,1...) custom-call(s32[2]{0:T(128)S(1)} %pad_add_fusion.refs_0_.ids_ref, ...), custom_call_target="tpu_custom_call", output_to_operand_aliasing={{0}: (9, {}), {1}: (10, {}), {2}: (11, {}), {3}: (12, {}), ... | custom-call | flops 1 | bytes 1 | tf_op jit(solution)/shard_map/project_blocks/pallas_call | solution.py:351
  62.1 6.5 %attend.1 = (bf16[128,512]{1,0:T(8,128)(2,1)S(1)}, bf16[128,1024]{1,0:T(8,128)(2,1)S(1)}) custom-call(s32[2]{0:T(128)S(1)} %pad_add_fusion.refs_0_.ids_ref, s32[4]{0:T(128)S(1)} %copy-done.19, bf16[16,128,1024]{2,1,0:T(8,128)(2,1)S(1)} %get-tuple-element.100.h_ref, bf16[2048,512]{1,0:T(8,128)(2,1)S(1)} %bitcast.25, bf16[2048,512]{1,0:T(8,128)(2,1)S(1)} %bitcast.26, ...), custom_call_target="tpu_custom_call" | custom-call | flops 1 | bytes 1 | tf_op jit(solution)/shard_map/attend/pallas_call | solution.py:397
  68.8 1.4 collective-permute-done.10
  70.8 0.7 constant_dynamic-slice_fusion
  71.5 7.9 %own_ffn.1 = (bf16[128,1024]{1,0:T(8,128)(2,1)}, bf16[128,1024]{1,0:T(8,128)(2,1)}) custom-call(bf16[128,1024]{1,0:T(8,128)(2,1)S(1)} %add_convert_fusion.2.h_ref, bf16[128,1024]{1,0:T(8,128)(2,1)S(1)} %copy-done.9, bf16[1024,2048]{1,0:T(8,128)(2,1)} %up_ref.5, bf16[1024,2048]{1,0:T(8,128)(2,1)} %down_ref.3), custom_call_target="tpu_custom_call" | custom-call | flops 1 | bytes 1 | tf_op jit(solution)/shard_map/own_ffn/pallas_call | solution.py:446
  79.5 1.6 collective-permute-done.11.other_ref
  81.1 0.9 copy-done.13
  82.1 1.5 norm_back.1
  83.6 1.0 share_output.1
  84.9 8.6 %all-to-all-start = ((bf16[8,64,128]{2,1,0:T(8,128)(2,1)}), bf16[8,64,128]{2,1,0:T(8,128)(2,1)S(1)}, u32[]{:S(2)}, u32[]{:S(2)}) async-start(bf16[8,64,128]{2,1,0:T(8,128)(2,1)} %get-tuple-element.107), calls=%async_computation | async-start | bytes 262144 | tf_op jit(solution)/shard_map/all_to_all | solution.py:971
  93.6 6.2 %prepare.1.p_ref = bf16[4,2048,256]{2,1,0:T(8,128)(2,1)} custom-call(s32[2]{0:T(128)} %copy-done.17, s32[4]{0:T(128)} %len_ref.5, bf16[16,192,128]{2,1,0:T(8,128)(2,1)} %copy-done.4, bf16[2048,256]{1,0:T(8,128)(2,1)} %bitcast.27), custom_call_target="tpu_custom_call" | custom-call | flops 1 | bytes 1 | tf_op jit(solution)/shard_map/prepare/pallas_call | solution.py:539
  99.8 2.0 add_convert_fusion
  101.9 7.6 %all-to-all-start.1 = ((bf16[8,64,512]{2,1,0:T(8,128)(2,1)}), bf16[8,64,512]{2,1,0:T(8,128)(2,1)S(1)}, u32[]{:S(2)}, u32[]{:S(2)}) async-start(bf16[8,64,512]{2,1,0:T(8,128)(2,1)} %add_convert_fusion), calls=%async_computation.1 | async-start | bytes 1048576 | tf_op jit(solution)/shard_map/all_to_all | solution.py:977
  109.5 9.9 %back.1 = (bf16[8,64,128]{2,1,0:T(8,128)(2,1)}, f32[8,128,128]{2,1,0:T(8,128)}, bf16[8,128,128]{2,1,0:T(8,128)(2,1)}, f32[192,512]{1,0:T(8,128)}, bf16[192,512]{1,0:T(8,128)(2,1)}) custom-call(s32[2]{0:T(128)} %copy-done.17, s32[4]{0:T(128)} %len_ref.5, bf16[4,2048,256]{2,1,0:T(8,128)(2,1)} %prepare.1.p_ref, bf16[8,64,128]{2,1,0:T(8,128)(2,1)} %copy-done.25, ...), custom_call_target="tpu_custom_call" | custom-call | flops 1 | bytes 1 | tf_op jit(solution)/shard_map/back/pallas_call | solution.py:631
  119.4 0.8 collective-permute-start.12
  120.1 13.4 %through.1.grad_ref = bf16[2048,2048]{1,0:T(8,128)(2,1)} custom-call(bf16[2048,1024]{1,0:T(8,128)(2,1)} %all-gather.3.cloned.1.call-done.g_ref, bf16[1024,2048]{1,0:T(8,128)(2,1)} %down_ref.3), custom_call_target="tpu_custom_call" | custom-call | flops 8589934592 | bytes 16777216 | tf_op jit(solution)/shard_map/through/pallas_call | solution.py:775
  133.7 1.4 collective-permute-start.15
  135.1 3.8 %collective-permute-start.18 = (bf16[256,512]{1,0:T(8,128)(2,1)S(1)}, bf16[256,512]{1,0:T(8,128)(2,1)S(1)}, u32[]{:S(2)}, u32[]{:S(2)}) collective-permute-start(bf16[256,512]{1,0:T(8,128)(2,1)S(1)} %make_unit.1), channel_id=1, source_target_pairs={{0,24},{2,26},{4,28},{6,30},{8,0},{10,2},{12,4},{14,6},{16,8},{18,... | collective-permute-start | bytes 786440 | tf_op jit(solution)/shard_map/ppermute | solution.py:883
  138.9 1.1 collective-permute-start.16
  140.0 1.5 collective-permute-done.15.given_ref
  141.5 0.8 merge.1
  142.3 5.7 %all-to-all-start.2 = ((bf16[8,192,128]{2,1,0:T(8,128)(2,1)}), bf16[8,192,128]{2,1,0:T(8,128)(2,1)S(1)}, u32[]{:S(2)}, u32[]{:S(2)}) async-start(bf16[8,192,128]{2,1,0:T(8,128)(2,1)} %merge.1), calls=%async_computation.2 | async-start | bytes 786432 | tf_op jit(solution)/shard_map/all_to_all | solution.py:988
  148.0 1.7 add_convert_fusion.1
  149.8 16.0 %ffn_grads.2 = (f32[1024,2048]{1,0:T(8,128)}, f32[1024,2048]{1,0:T(8,128)}) custom-call(bf16[2048,1024]{1,0:T(8,128)(2,1)} %all-gather.5.cloned.1.call-done.h_ref, bf16[2048,1024]{1,0:T(8,128)(2,1)} %all-gather.3.cloned.1.call-done.g_ref, bf16[2048,2048]{1,0:T(8,128)(2,1)} %through.1.grad_ref, bf16[1024,2048]{1,0:T(8,128)(2,1)} %up_ref.5), custom_call_target="tpu_custom_call" | custom-call | flops 9663676416 | bytes 8388608 | tf_op jit(solution)/shard_map/ffn_grads/pallas_call | solution.py:820
  165.8 4.4 %collective-permute-done.17 = bf16[256,512]{1,0:T(8,128)(2,1)S(1)} collective-permute-done((bf16[256,512]{1,0:T(8,128)(2,1)S(1)}, bf16[256,512]{1,0:T(8,128)(2,1)S(1)}, u32[]{:S(2)}, u32[]{:S(2)}) %collective-permute-start.17) | collective-permute-done | bytes 262176 | tf_op jit(solution)/shard_map/ppermute | solution.py:883
  170.2 1.1 pad_maximum_fusion.refs_0_
  171.3 1.5 collective-permute-start.20
  172.9 0.6 collective-permute-start.19
  173.5 23.2 %ffn_grads.3 = (f32[1024,2048]{1,0:T(8,128)}, f32[1024,2048]{1,0:T(8,128)}) custom-call(bf16[2048,1024]{1,0:T(8,128)(2,1)} %all-gather.5.cloned.1.call-done.h_ref, bf16[2048,1024]{1,0:T(8,128)(2,1)} %all-gather.3.cloned.1.call-done.g_ref, bf16[2048,2048]{1,0:T(8,128)(2,1)} %through.1.grad_ref, ...), custom_call_target="tpu_custom_call", output_to_operand_aliasing={{0}: (4, {}), {1}: (5, {})} | custom-call | flops 16106127360 | bytes 8388608 | tf_op jit(solution)/shard_map/ffn_grads/pallas_call | solution.py:820
  196.7 1.2 slice.25
  197.9 1.1 slice.24
  199.0 3.8 %go_home.1.mine_ref = bf16[128,1024]{1,0:T(8,128)(2,1)} custom-call(bf16[8,192,128]{2,1,0:T(8,128)(2,1)} %copy-done.24, bf16[1024,512]{1,0:T(8,128)(2,1)} %q_ref.3, bf16[1024,512]{1,0:T(8,128)(2,1)} %v_ref.1, bf16[1024,512]{1,0:T(8,128)(2,1)} %k_ref.1), custom_call_target="tpu_custom_call" | custom-call | flops 1 | bytes 1 | tf_op jit(solution)/shard_map/go_home/pallas_call | solution.py:726
  202.9 1.3 collective-permute-start.23
  204.2 0.7 collective-permute-start.22
  204.8 0.9 copy-done.10
  205.8 1.3 input_back.1
  207.1 7.1 %all-to-all-start.3 = ((f32[16,4,1024]{2,1,0:T(4,128)}), f32[16,4,1024]{2,1,0:T(4,128)S(1)}, u32[]{:S(2)}, u32[]{:S(2)}) async-start(f32[16,4,1024]{2,1,0:T(4,128)} %get-tuple-element.144), calls=%async_computation.3 | async-start | bytes 524288 | tf_op jit(solution)/shard_map/all_to_all | solution.py:1002
  214.2 3.2 %collective-permute-done.23.refs_4_ = bf16[2,256,512]{2,1,0:T(8,128)(2,1)S(1)} collective-permute-done((bf16[2,256,512]{2,1,0:T(8,128)(2,1)S(1)}, bf16[2,256,512]{2,1,0:T(8,128)(2,1)S(1)}, u32[]{:S(2)}, u32[]{:S(2)}) %collective-permute-start.23) | collective-permute-done | bytes 524320 | tf_op jit(solution)/shard_map/ppermute | solution.py:883
  217.4 1.5 collective-permute-done.22.refs_3_
  218.9 0.8 copy-done.27
  219.8 6.7 %finish.1 = (f32[1024,512]{1,0:T(8,128)}, f32[1024,512]{1,0:T(8,128)}, f32[1024,512]{1,0:T(8,128)}, f32[1024,512]{1,0:T(8,128)}) custom-call(s32[2]{0:T(128)} %copy-done.17, bf16[4,256,512]{2,1,0:T(8,128)(2,1)} %copy-done.20, bf16[4,256,512]{2,1,0:T(8,128)(2,1)} %collective-permute-done.19.refs_1_, bf16[4,256,512]{2,1,0:T(8,128)(2,1)} %collective-permute-done.20.refs_2_, ...), custom_call_target="tpu_custom_call" | custom-call | flops 1 | bytes 1 | tf_op jit(solution)/shard_map/finish/pallas_call | solution.py:868
  (99 shorter events, 3.5 us)
Async XLA Ops:
  7.2 26.5 %copy-start.2 = (bf16[1024,512]{1,0:T(8,128)(2,1)S(1)}, bf16[1024,512]{1,0:T(8,128)(2,1)}, u32[]{:S(2)}) copy-start(bf16[1024,512]{1,0:T(8,128)(2,1)} %v_ref.1) | copy-start | bytes 3145732
  7.2 26.5 %copy-start.1 = (bf16[1024,512]{1,0:T(8,128)(2,1)S(1)}, bf16[1024,512]{1,0:T(8,128)(2,1)}, u32[]{:S(2)}) copy-start(bf16[1024,512]{1,0:T(8,128)(2,1)} %k_ref.1) | copy-start | bytes 3145732
  7.2 26.5 %copy-start.16 = (f32[1024]{0:T(1024)S(1)}, f32[1024]{0:T(1024)}, u32[]{:S(2)}) copy-start(f32[1024]{0:T(1024)} %param.15) | copy-start | bytes 12292
  7.2 26.5 %copy-start.15 = (f32[1024]{0:T(1024)S(1)}, f32[1024]{0:T(1024)}, u32[]{:S(2)}) copy-start(f32[1024]{0:T(1024)} %param.14) | copy-start | bytes 12292
  7.2 86.4 %all-gather.3.cloned.1.call-start = ((), (), s32[]{:S(2)}) async-start(), calls=%async_computation.4 | async-start | bytes 4325376 | tf_op jit(solution)/shard_map/all_gather | solution.py:940
  9.0 140.8 %all-gather.5.cloned.1.call-start = ((), (), s32[]{:S(2)}) async-start(), calls=%async_computation.5 | async-start | bytes 4325376 | tf_op jit(solution)/shard_map/all_gather | solution.py:965
  10.0 14.1 %collective-permute-start.1 = (bf16[64,1024]{1,0:T(8,128)(2,1)S(1)}, bf16[64,1024]{1,0:T(8,128)(2,1)S(1)}, u32[]{:S(2)}, u32[]{:S(2)}) collective-permute-start(bf16[64,1024]{1,0:T(8,128)(2,1)S(1)} %constant_dynamic-slice_fusion.4), channel_id=1, source_target_pairs={{0,16},{2,18},{4,20},{6,22},{8,24},{10,26},{12,28},{14,30},{16,0},... | collective-permute-start | bytes 393224 | tf_op jit(solution)/shard_map/ppermute | solution.py:883
  14.1 10.0 %collective-permute-start = (bf16[64,1024]{1,0:T(8,128)(2,1)S(1)}, bf16[64,1024]{1,0:T(8,128)(2,1)S(1)}, u32[]{:S(2)}, u32[]{:S(2)}) collective-permute-start(bf16[64,1024]{1,0:T(8,128)(2,1)S(1)} %constant_dynamic-slice_fusion.4), channel_id=1, source_target_pairs={{0,8},{2,10},{4,12},{6,14},{8,16},{10,18},{12,20},{14,22},{16,24},... | collective-permute-start | bytes 393224 | tf_op jit(solution)/shard_map/ppermute | solution.py:883
  15.7 9.1 %collective-permute-start.2 = (bf16[64,1024]{1,0:T(8,128)(2,1)S(1)}, bf16[64,1024]{1,0:T(8,128)(2,1)S(1)}, u32[]{:S(2)}, u32[]{:S(2)}) collective-permute-start(bf16[64,1024]{1,0:T(8,128)(2,1)S(1)} %constant_dynamic-slice_fusion.4), channel_id=1, source_target_pairs={{0,24},{2,26},{4,28},{6,30},{8,0},{10,2},{12,4},{14,6},{16,8},{18,... | collective-permute-start | bytes 393224 | tf_op jit(solution)/shard_map/ppermute | solution.py:883
  20.1 9.0 %copy-start.22 = (bf16[1024,64]{1,0:T(8,128)(2,1)}, bf16[1024,64]{1,0:T(8,128)(2,1)S(1)}, u32[]{:S(2)}) copy-start(bf16[1024,64]{1,0:T(8,128)(2,1)S(1)} %get-tuple-element.158) | copy-start | bytes 393220
  20.1 9.0 %copy-start.23 = (bf16[1024,64]{1,0:T(8,128)(2,1)}, bf16[1024,64]{1,0:T(8,128)(2,1)S(1)}, u32[]{:S(2)}) copy-start(bf16[1024,64]{1,0:T(8,128)(2,1)S(1)} %get-tuple-element.159) | copy-start | bytes 393220
  24.9 16.1 %collective-permute-start.7 = (bf16[4,64,1024]{2,1,0:T(8,128)(2,1)S(1)}, bf16[4,64,1024]{2,1,0:T(8,128)(2,1)}, u32[]{:S(2)}, u32[]{:S(2)}) collective-permute-start(bf16[4,64,1024]{2,1,0:T(8,128)(2,1)S(1)} %pad_maximum_fusion.1.refs_1_), channel_id=1, source_target_pairs={{0,2},{2,0},{4,6},{6,4},{8,10},{10,8},{12,14},{14,12},{16,18},{18,... | collective-permute-start | bytes 1572872 | tf_op jit(solution)/shard_map/ppermute | solution.py:883
  26.5 7.2 %collective-permute-start.4 = (bf16[4,64,1024]{2,1,0:T(8,128)(2,1)S(1)}, bf16[4,64,1024]{2,1,0:T(8,128)(2,1)S(1)}, u32[]{:S(2)}, u32[]{:S(2)}) collective-permute-start(bf16[4,64,1024]{2,1,0:T(8,128)(2,1)S(1)} %pad_maximum_fusion.1.refs_1_), channel_id=1, source_target_pairs={{0,1},{1,0},{2,3},{3,2},{4,5},{5,4},{6,7},{7,6},{8,9},{9,8},{10,11... | collective-permute-start | bytes 1572872 | tf_op jit(solution)/shard_map/ppermute | solution.py:887
  26.5 14.4 %collective-permute-start.3 = (bf16[4,64,1024]{2,1,0:T(8,128)(2,1)S(1)}, bf16[4,64,1024]{2,1,0:T(8,128)(2,1)}, u32[]{:S(2)}, u32[]{:S(2)}) collective-permute-start(bf16[4,64,1024]{2,1,0:T(8,128)(2,1)S(1)} %pad_maximum_fusion.1.refs_1_), channel_id=1, source_target_pairs={{0,4},{2,6},{4,0},{6,2},{8,12},{10,14},{12,8},{14,10},{16,20},{18,... | collective-permute-start | bytes 1572872 | tf_op jit(solution)/shard_map/ppermute | solution.py:883
  29.1 0.7 copy-start.21
  32.2 51.4 %copy-start.17 = (s32[2]{0:T(128)}, s32[2]{0:T(128)S(1)}, u32[]{:S(2)}) copy-start(s32[2]{0:T(128)S(1)} %pad_add_fusion.refs_0_.ids_ref) | copy-start | bytes 28
  40.9 2.1 collective-permute-start.8
  40.9 6.1 %collective-permute-start.6 = (bf16[4,64,1024]{2,1,0:T(8,128)(2,1)}, bf16[4,64,1024]{2,1,0:T(8,128)(2,1)S(1)}, u32[]{:S(2)}, u32[]{:S(2)}) collective-permute-start(bf16[4,64,1024]{2,1,0:T(8,128)(2,1)} %collective-permute-done.3.refs_1_), channel_id=1, source_target_pairs={{0,1},{1,0},{2,3},{3,2},{4,5},{5,4},{6,7},{7,6},{8,9},{9,8},{10,11... | collective-permute-start | bytes 1572872 | tf_op jit(solution)/shard_map/ppermute | solution.py:887
  41.4 15.2 %collective-permute-start.5 = (bf16[4,64,1024]{2,1,0:T(8,128)(2,1)}, bf16[4,64,1024]{2,1,0:T(8,128)(2,1)S(1)}, u32[]{:S(2)}, u32[]{:S(2)}) collective-permute-start(bf16[4,64,1024]{2,1,0:T(8,128)(2,1)} %collective-permute-done.3.refs_1_), channel_id=1, source_target_pairs={{0,2},{2,0},{4,6},{6,4},{8,10},{10,8},{12,14},{14,12},{16,18},{18,... | collective-permute-start | bytes 1572872 | tf_op jit(solution)/shard_map/ppermute | solution.py:883
  56.6 1.9 collective-permute-start.9
  58.5 3.5 %copy-start.5 = (bf16[1024,512]{1,0:T(8,128)(2,1)S(1)}, bf16[1024,512]{1,0:T(8,128)(2,1)}, u32[]{:S(2)}) copy-start(bf16[1024,512]{1,0:T(8,128)(2,1)} %q_ref.3) | copy-start | bytes 3145732
  58.5 3.5 %copy-start.6 = (bf16[1024,512]{1,0:T(8,128)(2,1)S(1)}, bf16[1024,512]{1,0:T(8,128)(2,1)}, u32[]{:S(2)}) copy-start(bf16[1024,512]{1,0:T(8,128)(2,1)} %o_ref.3) | copy-start | bytes 3145732
  58.5 3.5 %copy-start.19 = (s32[4]{0:T(128)S(1)}, s32[4]{0:T(128)}, u32[]{:S(2)}) copy-start(s32[4]{0:T(128)} %len_ref.5) | copy-start | bytes 52
  62.0 6.6 %copy-start = (bf16[16,128,1024]{2,1,0:T(8,128)(2,1)}, bf16[16,128,1024]{2,1,0:T(8,128)(2,1)S(1)}, u32[]{:S(2)}) copy-start(bf16[16,128,1024]{2,1,0:T(8,128)(2,1)S(1)} %get-tuple-element.100.h_ref) | copy-start | bytes 12582916
  62.0 6.6 %copy-start.3 = (bf16[16,128,256]{2,1,0:T(8,128)(2,1)}, bf16[16,128,256]{2,1,0:T(8,128)(2,1)S(1)}, u32[]{:S(2)}) copy-start(bf16[16,128,256]{2,1,0:T(8,128)(2,1)S(1)} %get-tuple-element.113) | copy-start | bytes 3145732
  62.0 6.6 %copy-start.4 = (bf16[16,192,128]{2,1,0:T(8,128)(2,1)}, bf16[16,192,128]{2,1,0:T(8,128)(2,1)S(1)}, u32[]{:S(2)}) copy-start(bf16[16,192,128]{2,1,0:T(8,128)(2,1)S(1)} %get-tuple-element.112.t_ref) | copy-start | bytes 2359300
  62.0 8.2 %copy-start.8 = (bf16[128,1024]{1,0:T(8,128)(2,1)S(1)}, bf16[128,1024]{1,0:T(8,128)(2,1)}, u32[]{:S(2)}) copy-start(bf16[128,1024]{1,0:T(8,128)(2,1)} %x_ref.1) | copy-start | bytes 786436
  62.1 8.6 %copy-start.18 = (f32[1024]{0:T(1024)S(1)}, f32[1024]{0:T(1024)}, u32[]{:S(2)}) copy-start(f32[1024]{0:T(1024)} %param.16) | copy-start | bytes 12292
  62.1 8.6 %copy-start.28 = (f32[1024]{0:T(1024)S(1)}, f32[1024]{0:T(1024)}, u32[]{:S(2)}) copy-start(f32[1024]{0:T(1024)} %param.17) | copy-start | bytes 12292
  62.1 9.4 %copy-start.9 = (bf16[128,1024]{1,0:T(8,128)(2,1)S(1)}, bf16[128,1024]{1,0:T(8,128)(2,1)}, u32[]{:S(2)}) copy-start(bf16[128,1024]{1,0:T(8,128)(2,1)} %g_ref.3) | copy-start | bytes 786436
  68.6 1.6 collective-permute-start.10
  71.5 9.6 %copy-start.7 = (bf16[1024,512]{1,0:T(8,128)(2,1)S(1)}, bf16[1024,512]{1,0:T(8,128)(2,1)}, u32[]{:S(2)}) copy-start(bf16[1024,512]{1,0:T(8,128)(2,1)} %o_ref.3) | copy-start | bytes 3145732
  79.4 1.7 collective-permute-start.11
  81.1 1.0 copy-start.13
  84.6 15.2 %collective-permute-start.13 = (bf16[8,64,512]{2,1,0:T(8,128)(2,1)S(1)}, bf16[8,64,512]{2,1,0:T(8,128)(2,1)}, u32[]{:S(2)}, u32[]{:S(2)}) collective-permute-start(bf16[8,64,512]{2,1,0:T(8,128)(2,1)S(1)} %get-tuple-element.111), channel_id=1, source_target_pairs={{0,2},{2,0},{4,6},{6,4},{8,10},{10,8},{12,14},{14,12},{16,18},{18,... | collective-permute-start | bytes 1572872 | tf_op jit(solution)/shard_map/ppermute | solution.py:883
  84.9 16.9 %all-to-all-start = ((bf16[8,64,128]{2,1,0:T(8,128)(2,1)}), bf16[8,64,128]{2,1,0:T(8,128)(2,1)S(1)}, u32[]{:S(2)}, u32[]{:S(2)}) async-start(bf16[8,64,128]{2,1,0:T(8,128)(2,1)} %get-tuple-element.107), calls=%async_computation | async-start | bytes 262144 | tf_op jit(solution)/shard_map/all_to_all | solution.py:971
  101.9 7.6 %copy-start.25 = (bf16[8,64,128]{2,1,0:T(8,128)(2,1)}, bf16[8,64,128]{2,1,0:T(8,128)(2,1)S(1)}, u32[]{:S(2)}) copy-start(bf16[8,64,128]{2,1,0:T(8,128)(2,1)S(1)} %all-to-all-done.ga_ref) | copy-start | bytes 393220
  101.9 31.7 %all-to-all-start.1 = ((bf16[8,64,512]{2,1,0:T(8,128)(2,1)}), bf16[8,64,512]{2,1,0:T(8,128)(2,1)S(1)}, u32[]{:S(2)}, u32[]{:S(2)}) async-start(bf16[8,64,512]{2,1,0:T(8,128)(2,1)} %add_convert_fusion), calls=%async_computation.1 | async-start | bytes 1048576 | tf_op jit(solution)/shard_map/all_to_all | solution.py:977
  119.3 14.2 %copy-start.12 = (f32[192,512]{1,0:T(8,128)S(1)}, f32[192,512]{1,0:T(8,128)}, u32[]{:S(2)}) copy-start(f32[192,512]{1,0:T(8,128)} %get-tuple-element.117.mine_ref) | copy-start | bytes 1179652
  119.4 22.2 %copy-start.11 = (f32[8,128,128]{2,1,0:T(8,128)S(1)}, f32[8,128,128]{2,1,0:T(8,128)}, u32[]{:S(2)}) copy-start(f32[8,128,128]{2,1,0:T(8,128)} %get-tuple-element.125.kept_ref) | copy-start | bytes 1572868
  119.4 22.2 %copy-start.14 = (bf16[8,64,128]{2,1,0:T(8,128)(2,1)S(1)}, bf16[8,64,128]{2,1,0:T(8,128)(2,1)}, u32[]{:S(2)}) copy-start(bf16[8,64,128]{2,1,0:T(8,128)(2,1)} %get-tuple-element.124.gq_ref) | copy-start | bytes 393220
  119.4 14.2 %collective-permute-start.12 = (bf16[192,512]{1,0:T(8,128)(2,1)}, bf16[192,512]{1,0:T(8,128)(2,1)S(1)}, u32[]{:S(2)}, u32[]{:S(2)}) collective-permute-start(bf16[192,512]{1,0:T(8,128)(2,1)} %get-tuple-element.118), channel_id=1, source_target_pairs={{0,2},{2,0},{4,6},{6,4},{8,10},{10,8},{12,14},{14,12},{16,18},{18,... | collective-permute-start | bytes 589832 | tf_op jit(solution)/shard_map/ppermute | solution.py:883
  133.7 7.8 %collective-permute-start.15 = (bf16[8,128,128]{2,1,0:T(8,128)(2,1)}, bf16[8,128,128]{2,1,0:T(8,128)(2,1)S(1)}, u32[]{:S(2)}, u32[]{:S(2)}) collective-permute-start(bf16[8,128,128]{2,1,0:T(8,128)(2,1)} %get-tuple-element.127), channel_id=1, source_target_pairs={{0,2},{2,0},{4,6},{6,4},{8,10},{10,8},{12,14},{14,12},{16,18},{18,... | collective-permute-start | bytes 786440 | tf_op jit(solution)/shard_map/ppermute | solution.py:883
  135.1 13.0 %collective-permute-start.14 = (bf16[128,1024]{1,0:T(8,128)(2,1)}, bf16[128,1024]{1,0:T(8,128)(2,1)S(1)}, u32[]{:S(2)}, u32[]{:S(2)}) collective-permute-start(bf16[128,1024]{1,0:T(8,128)(2,1)} %get-tuple-element.123), channel_id=1, source_target_pairs={{0,1},{1,0},{2,3},{3,2},{4,5},{5,4},{6,7},{7,6},{8,9},{9,8},{10,11... | collective-permute-start | bytes 786440 | tf_op jit(solution)/shard_map/ppermute | solution.py:887
  135.1 30.7 %collective-permute-start.18 = (bf16[256,512]{1,0:T(8,128)(2,1)S(1)}, bf16[256,512]{1,0:T(8,128)(2,1)S(1)}, u32[]{:S(2)}, u32[]{:S(2)}) collective-permute-start(bf16[256,512]{1,0:T(8,128)(2,1)S(1)} %make_unit.1), channel_id=1, source_target_pairs={{0,24},{2,26},{4,28},{6,30},{8,0},{10,2},{12,4},{14,6},{16,8},{18,... | collective-permute-start | bytes 786440 | tf_op jit(solution)/shard_map/ppermute | solution.py:883
  138.9 31.4 %collective-permute-start.17 = (bf16[256,512]{1,0:T(8,128)(2,1)S(1)}, bf16[256,512]{1,0:T(8,128)(2,1)S(1)}, u32[]{:S(2)}, u32[]{:S(2)}) collective-permute-start(bf16[256,512]{1,0:T(8,128)(2,1)S(1)} %make_unit.1), channel_id=1, source_target_pairs={{0,16},{2,18},{4,20},{6,22},{8,24},{10,26},{12,28},{14,30},{16,0},... | collective-permute-start | bytes 786440 | tf_op jit(solution)/shard_map/ppermute | solution.py:883
  138.9 31.4 %collective-permute-start.16 = (bf16[256,512]{1,0:T(8,128)(2,1)S(1)}, bf16[256,512]{1,0:T(8,128)(2,1)}, u32[]{:S(2)}, u32[]{:S(2)}) collective-permute-start(bf16[256,512]{1,0:T(8,128)(2,1)S(1)} %make_unit.1), channel_id=1, source_target_pairs={{0,8},{2,10},{4,12},{6,14},{8,16},{10,18},{12,20},{14,22},{16,24},... | collective-permute-start | bytes 786440 | tf_op jit(solution)/shard_map/ppermute | solution.py:883
  142.3 54.4 %all-to-all-start.2 = ((bf16[8,192,128]{2,1,0:T(8,128)(2,1)}), bf16[8,192,128]{2,1,0:T(8,128)(2,1)S(1)}, u32[]{:S(2)}, u32[]{:S(2)}) async-start(bf16[8,192,128]{2,1,0:T(8,128)(2,1)} %merge.1), calls=%async_computation.2 | async-start | bytes 786432 | tf_op jit(solution)/shard_map/all_to_all | solution.py:988
  171.3 25.4 %copy-start.20 = (bf16[4,256,512]{2,1,0:T(8,128)(2,1)}, bf16[4,256,512]{2,1,0:T(8,128)(2,1)S(1)}, u32[]{:S(2)}) copy-start(bf16[4,256,512]{2,1,0:T(8,128)(2,1)S(1)} %pad_maximum_fusion.refs_0_) | copy-start | bytes 3145732
  171.3 25.4 %collective-permute-start.20 = (bf16[4,256,512]{2,1,0:T(8,128)(2,1)S(1)}, bf16[4,256,512]{2,1,0:T(8,128)(2,1)}, u32[]{:S(2)}, u32[]{:S(2)}) collective-permute-start(bf16[4,256,512]{2,1,0:T(8,128)(2,1)S(1)} %pad_maximum_fusion.refs_0_), channel_id=1, source_target_pairs={{0,4},{2,6},{4,0},{6,2},{8,12},{10,14},{12,8},{14,10},{16,20},{18,... | collective-permute-start | bytes 3145736 | tf_op jit(solution)/shard_map/ppermute | solution.py:883
  172.9 25.1 %collective-permute-start.19 = (bf16[4,256,512]{2,1,0:T(8,128)(2,1)S(1)}, bf16[4,256,512]{2,1,0:T(8,128)(2,1)}, u32[]{:S(2)}, u32[]{:S(2)}) collective-permute-start(bf16[4,256,512]{2,1,0:T(8,128)(2,1)S(1)} %pad_maximum_fusion.refs_0_), channel_id=1, source_target_pairs={{0,2},{2,0},{4,6},{6,4},{8,10},{10,8},{12,14},{14,12},{16,18},{18,... | collective-permute-start | bytes 3145736 | tf_op jit(solution)/shard_map/ppermute | solution.py:883
  196.7 2.3 copy-start.24
  202.9 2.0 collective-permute-start.21
  202.9 14.5 %collective-permute-start.23 = (bf16[2,256,512]{2,1,0:T(8,128)(2,1)S(1)}, bf16[2,256,512]{2,1,0:T(8,128)(2,1)S(1)}, u32[]{:S(2)}, u32[]{:S(2)}) collective-permute-start(bf16[2,256,512]{2,1,0:T(8,128)(2,1)S(1)} %slice.24), channel_id=1, source_target_pairs={{0,4},{2,6},{4,0},{6,2},{8,12},{10,14},{12,8},{14,10},{16,20},{18,... | collective-permute-start | bytes 1572872 | tf_op jit(solution)/shard_map/ppermute | solution.py:883
  204.2 14.8 %collective-permute-start.22 = (bf16[2,256,512]{2,1,0:T(8,128)(2,1)S(1)}, bf16[2,256,512]{2,1,0:T(8,128)(2,1)S(1)}, u32[]{:S(2)}, u32[]{:S(2)}) collective-permute-start(bf16[2,256,512]{2,1,0:T(8,128)(2,1)S(1)} %slice.25), channel_id=1, source_target_pairs={{0,2},{2,0},{4,6},{6,4},{8,10},{10,8},{12,14},{14,12},{16,18},{18,... | collective-permute-start | bytes 1572872 | tf_op jit(solution)/shard_map/ppermute | solution.py:883
  204.8 1.0 copy-start.10
  207.1 19.3 %all-to-all-start.3 = ((f32[16,4,1024]{2,1,0:T(4,128)}), f32[16,4,1024]{2,1,0:T(4,128)S(1)}, u32[]{:S(2)}, u32[]{:S(2)}) async-start(f32[16,4,1024]{2,1,0:T(4,128)} %get-tuple-element.144), calls=%async_computation.3 | async-start | bytes 524288 | tf_op jit(solution)/shard_map/all_to_all | solution.py:1002
  217.4 1.5 copy-start.26
  218.9 0.8 copy-start.27
Sparse Core Ops, SparseCore 0:
  11.5 66.3 all-gather.2
  80.7 65.9 all-gather.4

commit v7 on v6

--- a/solution.py
+++ b/solution.py
@@ -771,15 +771,15 @@
 def through(g, weight):
     total, width = g.shape
     hidden = weight.shape[1]
-    tile = 2 * FT
+    rows, tile = TT // 2, hidden // 2
     return pl.pallas_call(
         through_kernel,
-        grid=(hidden // tile,),
+        grid=(hidden // tile, total // rows),
         in_specs=[
-            pl.BlockSpec((total, width), lambda i: (0, 0), pipeline_mode=pl.Buffered(1)),
-            pl.BlockSpec((width, tile), lambda i: (0, i)),
+            pl.BlockSpec((rows, width), lambda i, j: (j, 0)),
+            pl.BlockSpec((width, tile), lambda i, j: (0, i)),
         ],
-        out_specs=pl.BlockSpec((total, tile), lambda i: (0, i)),
+        out_specs=pl.BlockSpec((rows, tile), lambda i, j: (j, i)),
         out_shape=jax.ShapeDtypeStruct((total, hidden), bf16),
         cost_estimate=pl.CostEstimate(
             flops=2 * total * width * hidden, bytes_accessed=8 * total * width, transcendentals=0

time: 237 us -> 236 us (level)
  Pallas kernels: 113 us -> 118 us
  starting transfers between devices: 53 us -> 50.3 us
  transfers between devices with their start and end apart: 30 -> 30, of which waited for: 12 -> 12; matrix products, arithmetic and copies ran while one was open for 7% -> 7% of each run, Pallas kernels for 47% -> 49%
where the time goes in v7:
time: 236 us; the launch traced here: 235 us
  Pallas kernels  118 us (50%)
  starting transfers between devices  50.3 us (21%)
  waiting for transfers between devices  29.8 us (13%)
  between operations  14.6 us (6%)
  local copies, waits for them, and re-layouts  13.1 us (6%)
  other arithmetic  9.31 us (4%)
    pallas_call x2, Pallas kernels, ffn_grads(): pl.pallas_call(ffn_kernel, grid=(last - first,), in_specs=[tokens, tokens...  39.2 us
    ppermute x16, waiting for transfers between devices, shuffle(): return lax.ppermute(block, 'blk', [(i, target(i)) for i in range(16)])  23.7 us
    ppermute x16, starting transfers between devices, shuffle(): return lax.ppermute(block, 'blk', [(i, target(i)) for i in range(16)])  23 us
    pallas_call x1, Pallas kernels, through(): pl.pallas_call(through_kernel, grid=(hidden // tile, total // rows), in_s...  15.2 us
    pallas_call x4, Pallas kernels, project_blocks(): pl.pallas_call(lambda *refs: project_kernel(flip, *refs), in_specs=[SCALA...  14.8 us
    pallas_call x1, Pallas kernels, back(): pl.pallas_call(back_kernel, grid_spec=pltpu.PrefetchScalarGridSpec(num_sc...  11.8 us
    all_to_all x1, starting transfers between devices, fast_body(): lax.all_to_all(to_heads, 'blk', 0, 0, tiled=True, axis_index_groups=alike)  8.64 us
    pallas_call x1, Pallas kernels, own_ffn(): pl.pallas_call(own_kernel, grid=(hidden // tile,), in_specs=[NEAR, NEAR]...  7.89 us
  transfers between devices with their start and end apart: 30, of which 12 were waited for; matrix products, arithmetic and copies ran while one was open for 7% of the time, Pallas kernels for 49%

profile of v7, /device:TPU:0, one launch (start us, length us, event | category | flops | bytes accessed | tf_op | source)
XLA Modules:
  0.0 235.0 jit_solution(17078376217961676952)
XLA Ops:
  7.3 1.7 constant_dynamic-slice_fusion.1
  9.0 0.9 constant_dynamic-slice_fusion.4
  10.0 4.1 %collective-permute-start.1 = (bf16[64,1024]{1,0:T(8,128)(2,1)S(1)}, bf16[64,1024]{1,0:T(8,128)(2,1)S(1)}, u32[]{:S(2)}, u32[]{:S(2)}) collective-permute-start(bf16[64,1024]{1,0:T(8,128)(2,1)S(1)} %constant_dynamic-slice_fusion.4), channel_id=1, source_target_pairs={{0,16},{2,18},{4,20},{6,22},{8,24},{10,26},{12,28},{14,30},{16,0},... | collective-permute-start | bytes 393224 | tf_op jit(solution)/shard_map/ppermute | solution.py:883
  14.1 1.6 collective-permute-start
  15.7 2.2 collective-permute-start.2
  17.9 0.9 fusion.2
  18.8 1.3 dynamic-slice_multiply_fusion
  20.1 4.0 %collective-permute-done.1 = bf16[64,1024]{1,0:T(8,128)(2,1)S(1)} collective-permute-done((bf16[64,1024]{1,0:T(8,128)(2,1)S(1)}, bf16[64,1024]{1,0:T(8,128)(2,1)S(1)}, u32[]{:S(2)}, u32[]{:S(2)}) %collective-permute-start.1) | collective-permute-done | bytes 131104 | tf_op jit(solution)/shard_map/ppermute | solution.py:883
  24.1 0.7 collective-permute-done.2
  24.9 1.6 collective-permute-start.7
  26.5 1.5 collective-permute-start.3
  28.0 1.1 constant_dynamic-slice_fusion.3
  29.1 0.7 copy-done.21
  29.8 1.0 maximum_bitcast_fusion
  30.8 1.2 copy.42.refs_7_
  32.2 1.4 maximum_maximum_fusion.refs_8_
  33.7 3.4 %project_blocks.4 = (bf16[16,128,1024]{2,1,0:T(8,128)(2,1)S(1)}, bf16[16,128,512]{2,1,0:T(8,128)(2,1)S(1)}, bf16[16,128,512]{2,1,0:T(8,128)(2,1)S(1)}, bf16[16,1...) custom-call(s32[2]{0:T(128)S(1)} %pad_add_fusion.refs_0_.ids_ref, bf16[4,64,1024]{2,1,0:T(8,128)(2,1)S(1)} %pad_maximum_fusion.1.refs_1_, ...), custom_call_target="tpu_custom_call" | custom-call | flops 1 | bytes 1 | tf_op jit(solution)/shard_map/project_blocks/pallas_call | solution.py:351
  37.1 3.8 %collective-permute-done.3.refs_1_ = bf16[4,64,1024]{2,1,0:T(8,128)(2,1)} collective-permute-done((bf16[4,64,1024]{2,1,0:T(8,128)(2,1)S(1)}, bf16[4,64,1024]{2,1,0:T(8,128)(2,1)}, u32[]{:S(2)}, u32[]{:S(2)}) %collective-permute-start.3) | collective-permute-done | bytes 524320 | tf_op jit(solution)/shard_map/ppermute | solution.py:883
  41.9 1.1 collective-permute-done.8.refs_2_
  43.0 4.0 %project_blocks.5 = (bf16[16,128,1024]{2,1,0:T(8,128)(2,1)S(1)}, bf16[16,128,512]{2,1,0:T(8,128)(2,1)S(1)}, bf16[16,128,512]{2,1,0:T(8,128)(2,1)S(1)}, bf16[16,1...) custom-call(s32[2]{0:T(128)S(1)} %pad_add_fusion.refs_0_.ids_ref, ...), custom_call_target="tpu_custom_call", output_to_operand_aliasing={{0}: (9, {}), {1}: (10, {}), {2}: (11, {}), {3}: (12, {}), ... | custom-call | flops 1 | bytes 1 | tf_op jit(solution)/shard_map/project_blocks/pallas_call | solution.py:351
  47.0 4.0 %project_blocks.6 = (bf16[16,128,1024]{2,1,0:T(8,128)(2,1)S(1)}, bf16[16,128,512]{2,1,0:T(8,128)(2,1)S(1)}, bf16[16,128,512]{2,1,0:T(8,128)(2,1)S(1)}, bf16[16,1...) custom-call(s32[2]{0:T(128)S(1)} %pad_add_fusion.refs_0_.ids_ref, ...), custom_call_target="tpu_custom_call", output_to_operand_aliasing={{0}: (9, {}), {1}: (10, {}), {2}: (11, {}), {3}: (12, {}), ... | custom-call | flops 1 | bytes 1 | tf_op jit(solution)/shard_map/project_blocks/pallas_call | solution.py:351
  51.0 5.6 %collective-permute-done.5.refs_1_ = bf16[4,64,1024]{2,1,0:T(8,128)(2,1)S(1)} collective-permute-done((bf16[4,64,1024]{2,1,0:T(8,128)(2,1)}, bf16[4,64,1024]{2,1,0:T(8,128)(2,1)S(1)}, u32[]{:S(2)}, u32[]{:S(2)}) %collective-permute-start.5) | collective-permute-done | bytes 524320 | tf_op jit(solution)/shard_map/ppermute | solution.py:883
  56.6 1.9 collective-permute-done.9.refs_2_
  58.5 3.4 %project_blocks.7 = (bf16[16,128,1024]{2,1,0:T(8,128)(2,1)S(1)}, bf16[16,128,512]{2,1,0:T(8,128)(2,1)S(1)}, bf16[16,128,512]{2,1,0:T(8,128)(2,1)S(1)}, bf16[16,1...) custom-call(s32[2]{0:T(128)S(1)} %pad_add_fusion.refs_0_.ids_ref, ...), custom_call_target="tpu_custom_call", output_to_operand_aliasing={{0}: (9, {}), {1}: (10, {}), {2}: (11, {}), {3}: (12, {}), ... | custom-call | flops 1 | bytes 1 | tf_op jit(solution)/shard_map/project_blocks/pallas_call | solution.py:351
  62.1 6.5 %attend.1 = (bf16[128,512]{1,0:T(8,128)(2,1)S(1)}, bf16[128,1024]{1,0:T(8,128)(2,1)S(1)}) custom-call(s32[2]{0:T(128)S(1)} %pad_add_fusion.refs_0_.ids_ref, s32[4]{0:T(128)S(1)} %copy-done.19, bf16[16,128,1024]{2,1,0:T(8,128)(2,1)S(1)} %get-tuple-element.100.h_ref, bf16[2048,512]{1,0:T(8,128)(2,1)S(1)} %bitcast.25, bf16[2048,512]{1,0:T(8,128)(2,1)S(1)} %bitcast.26, ...), custom_call_target="tpu_custom_call" | custom-call | flops 1 | bytes 1 | tf_op jit(solution)/shard_map/attend/pallas_call | solution.py:397
  68.8 1.4 collective-permute-done.10
  70.8 0.7 constant_dynamic-slice_fusion
  71.5 7.9 %own_ffn.1 = (bf16[128,1024]{1,0:T(8,128)(2,1)}, bf16[128,1024]{1,0:T(8,128)(2,1)}) custom-call(bf16[128,1024]{1,0:T(8,128)(2,1)S(1)} %add_convert_fusion.2.h_ref, bf16[128,1024]{1,0:T(8,128)(2,1)S(1)} %copy-done.9, bf16[1024,2048]{1,0:T(8,128)(2,1)} %up_ref.5, bf16[1024,2048]{1,0:T(8,128)(2,1)} %down_ref.3), custom_call_target="tpu_custom_call" | custom-call | flops 1 | bytes 1 | tf_op jit(solution)/shard_map/own_ffn/pallas_call | solution.py:446
  79.5 1.6 collective-permute-done.11.other_ref
  81.1 0.9 copy-done.13
  82.1 1.5 norm_back.1
  83.6 1.0 share_output.1
  84.9 8.6 %all-to-all-start = ((bf16[8,64,128]{2,1,0:T(8,128)(2,1)}), bf16[8,64,128]{2,1,0:T(8,128)(2,1)S(1)}, u32[]{:S(2)}, u32[]{:S(2)}) async-start(bf16[8,64,128]{2,1,0:T(8,128)(2,1)} %get-tuple-element.107), calls=%async_computation | async-start | bytes 262144 | tf_op jit(solution)/shard_map/all_to_all | solution.py:971
  93.6 7.4 %prepare.1.p_ref = bf16[4,2048,256]{2,1,0:T(8,128)(2,1)} custom-call(s32[2]{0:T(128)} %copy-done.17, s32[4]{0:T(128)} %len_ref.5, bf16[16,192,128]{2,1,0:T(8,128)(2,1)} %copy-done.4, bf16[2048,256]{1,0:T(8,128)(2,1)} %bitcast.27), custom_call_target="tpu_custom_call" | custom-call | flops 1 | bytes 1 | tf_op jit(solution)/shard_map/prepare/pallas_call | solution.py:539
  101.0 2.0 add_convert_fusion
  103.0 6.4 %all-to-all-start.1 = ((bf16[8,64,512]{2,1,0:T(8,128)(2,1)}), bf16[8,64,512]{2,1,0:T(8,128)(2,1)S(1)}, u32[]{:S(2)}, u32[]{:S(2)}) async-start(bf16[8,64,512]{2,1,0:T(8,128)(2,1)} %add_convert_fusion), calls=%async_computation.1 | async-start | bytes 1048576 | tf_op jit(solution)/shard_map/all_to_all | solution.py:977
  109.5 11.8 %back.1 = (bf16[8,64,128]{2,1,0:T(8,128)(2,1)}, f32[8,128,128]{2,1,0:T(8,128)}, bf16[8,128,128]{2,1,0:T(8,128)(2,1)}, f32[192,512]{1,0:T(8,128)}, bf16[192,512]{1,0:T(8,128)(2,1)}) custom-call(s32[2]{0:T(128)} %copy-done.17, s32[4]{0:T(128)} %len_ref.5, bf16[4,2048,256]{2,1,0:T(8,128)(2,1)} %prepare.1.p_ref, bf16[8,64,128]{2,1,0:T(8,128)(2,1)} %copy-done.25, ...), custom_call_target="tpu_custom_call" | custom-call | flops 1 | bytes 1 | tf_op jit(solution)/shard_map/back/pallas_call | solution.py:631
  121.3 0.8 collective-permute-start.12
  122.1 15.2 %through.1.grad_ref = bf16[2048,2048]{1,0:T(8,128)(2,1)} custom-call(bf16[2048,1024]{1,0:T(8,128)(2,1)} %all-gather.3.cloned.1.call-done.g_ref, bf16[1024,2048]{1,0:T(8,128)(2,1)} %down_ref.3), custom_call_target="tpu_custom_call" | custom-call | flops 8589934592 | bytes 16777216 | tf_op jit(solution)/shard_map/through/pallas_call | solution.py:775
  137.4 1.1 collective-permute-start.15
  138.5 4.1 %collective-permute-start.18 = (bf16[256,512]{1,0:T(8,128)(2,1)S(1)}, bf16[256,512]{1,0:T(8,128)(2,1)S(1)}, u32[]{:S(2)}, u32[]{:S(2)}) collective-permute-start(bf16[256,512]{1,0:T(8,128)(2,1)S(1)} %make_unit.1), channel_id=1, source_target_pairs={{0,24},{2,26},{4,28},{6,30},{8,0},{10,2},{12,4},{14,6},{16,8},{18,... | collective-permute-start | bytes 786440 | tf_op jit(solution)/shard_map/ppermute | solution.py:883
  142.6 1.1 collective-permute-start.16
  143.7 1.3 collective-permute-done.15.given_ref
  145.0 0.8 merge.1
  145.8 5.7 %all-to-all-start.2 = ((bf16[8,192,128]{2,1,0:T(8,128)(2,1)}), bf16[8,192,128]{2,1,0:T(8,128)(2,1)S(1)}, u32[]{:S(2)}, u32[]{:S(2)}) async-start(bf16[8,192,128]{2,1,0:T(8,128)(2,1)} %merge.1), calls=%async_computation.2 | async-start | bytes 786432 | tf_op jit(solution)/shard_map/all_to_all | solution.py:988
  151.5 1.7 add_convert_fusion.1
  153.3 16.0 %ffn_grads.2 = (f32[1024,2048]{1,0:T(8,128)}, f32[1024,2048]{1,0:T(8,128)}) custom-call(bf16[2048,1024]{1,0:T(8,128)(2,1)} %all-gather.5.cloned.1.call-done.h_ref, bf16[2048,1024]{1,0:T(8,128)(2,1)} %all-gather.3.cloned.1.call-done.g_ref, bf16[2048,2048]{1,0:T(8,128)(2,1)} %through.1.grad_ref, bf16[1024,2048]{1,0:T(8,128)(2,1)} %up_ref.5), custom_call_target="tpu_custom_call" | custom-call | flops 9663676416 | bytes 8388608 | tf_op jit(solution)/shard_map/ffn_grads/pallas_call | solution.py:820
  169.3 1.4 collective-permute-done.17
  170.7 1.1 pad_maximum_fusion.refs_0_
  171.8 1.5 collective-permute-start.20
  173.3 0.7 collective-permute-start.19
  173.9 23.2 %ffn_grads.3 = (f32[1024,2048]{1,0:T(8,128)}, f32[1024,2048]{1,0:T(8,128)}) custom-call(bf16[2048,1024]{1,0:T(8,128)(2,1)} %all-gather.5.cloned.1.call-done.h_ref, bf16[2048,1024]{1,0:T(8,128)(2,1)} %all-gather.3.cloned.1.call-done.g_ref, bf16[2048,2048]{1,0:T(8,128)(2,1)} %through.1.grad_ref, ...), custom_call_target="tpu_custom_call", output_to_operand_aliasing={{0}: (4, {}), {1}: (5, {})} | custom-call | flops 16106127360 | bytes 8388608 | tf_op jit(solution)/shard_map/ffn_grads/pallas_call | solution.py:820
  197.1 1.2 slice.25
  198.4 1.1 slice.24
  199.5 3.8 %go_home.1.mine_ref = bf16[128,1024]{1,0:T(8,128)(2,1)} custom-call(bf16[8,192,128]{2,1,0:T(8,128)(2,1)} %copy-done.24, bf16[1024,512]{1,0:T(8,128)(2,1)} %q_ref.3, bf16[1024,512]{1,0:T(8,128)(2,1)} %v_ref.1, bf16[1024,512]{1,0:T(8,128)(2,1)} %k_ref.1), custom_call_target="tpu_custom_call" | custom-call | flops 1 | bytes 1 | tf_op jit(solution)/shard_map/go_home/pallas_call | solution.py:726
  203.3 0.9 collective-permute-start.23
  204.2 1.1 collective-permute-start.22
  205.3 0.9 copy-done.10
  206.2 1.3 input_back.1
  207.5 5.5 %all-to-all-start.3 = ((f32[16,4,1024]{2,1,0:T(4,128)}), f32[16,4,1024]{2,1,0:T(4,128)S(1)}, u32[]{:S(2)}, u32[]{:S(2)}) async-start(f32[16,4,1024]{2,1,0:T(4,128)} %get-tuple-element.144), calls=%async_computation.3 | async-start | bytes 524288 | tf_op jit(solution)/shard_map/all_to_all | solution.py:1002
  213.1 5.5 %collective-permute-done.23.refs_4_ = bf16[2,256,512]{2,1,0:T(8,128)(2,1)S(1)} collective-permute-done((bf16[2,256,512]{2,1,0:T(8,128)(2,1)S(1)}, bf16[2,256,512]{2,1,0:T(8,128)(2,1)S(1)}, u32[]{:S(2)}, u32[]{:S(2)}) %collective-permute-start.23) | collective-permute-done | bytes 524320 | tf_op jit(solution)/shard_map/ppermute | solution.py:883
  218.6 1.4 collective-permute-done.22.refs_3_
  220.0 0.8 copy-done.27
  220.8 6.7 %finish.1 = (f32[1024,512]{1,0:T(8,128)}, f32[1024,512]{1,0:T(8,128)}, f32[1024,512]{1,0:T(8,128)}, f32[1024,512]{1,0:T(8,128)}) custom-call(s32[2]{0:T(128)} %copy-done.17, bf16[4,256,512]{2,1,0:T(8,128)(2,1)} %copy-done.20, bf16[4,256,512]{2,1,0:T(8,128)(2,1)} %collective-permute-done.19.refs_1_, bf16[4,256,512]{2,1,0:T(8,128)(2,1)} %collective-permute-done.20.refs_2_, ...), custom_call_target="tpu_custom_call" | custom-call | flops 1 | bytes 1 | tf_op jit(solution)/shard_map/finish/pallas_call | solution.py:868
  (99 shorter events, 3.5 us)
Async XLA Ops:
  7.2 26.5 %copy-start.2 = (bf16[1024,512]{1,0:T(8,128)(2,1)S(1)}, bf16[1024,512]{1,0:T(8,128)(2,1)}, u32[]{:S(2)}) copy-start(bf16[1024,512]{1,0:T(8,128)(2,1)} %v_ref.1) | copy-start | bytes 3145732
  7.2 26.5 %copy-start.1 = (bf16[1024,512]{1,0:T(8,128)(2,1)S(1)}, bf16[1024,512]{1,0:T(8,128)(2,1)}, u32[]{:S(2)}) copy-start(bf16[1024,512]{1,0:T(8,128)(2,1)} %k_ref.1) | copy-start | bytes 3145732
  7.2 26.5 %copy-start.16 = (f32[1024]{0:T(1024)S(1)}, f32[1024]{0:T(1024)}, u32[]{:S(2)}) copy-start(f32[1024]{0:T(1024)} %param.15) | copy-start | bytes 12292
  7.2 26.5 %copy-start.15 = (f32[1024]{0:T(1024)S(1)}, f32[1024]{0:T(1024)}, u32[]{:S(2)}) copy-start(f32[1024]{0:T(1024)} %param.14) | copy-start | bytes 12292
  7.2 86.4 %all-gather.3.cloned.1.call-start = ((), (), s32[]{:S(2)}) async-start(), calls=%async_computation.4 | async-start | bytes 4325376 | tf_op jit(solution)/shard_map/all_gather | solution.py:940
  9.0 144.3 %all-gather.5.cloned.1.call-start = ((), (), s32[]{:S(2)}) async-start(), calls=%async_computation.5 | async-start | bytes 4325376 | tf_op jit(solution)/shard_map/all_gather | solution.py:965
  10.0 14.1 %collective-permute-start.1 = (bf16[64,1024]{1,0:T(8,128)(2,1)S(1)}, bf16[64,1024]{1,0:T(8,128)(2,1)S(1)}, u32[]{:S(2)}, u32[]{:S(2)}) collective-permute-start(bf16[64,1024]{1,0:T(8,128)(2,1)S(1)} %constant_dynamic-slice_fusion.4), channel_id=1, source_target_pairs={{0,16},{2,18},{4,20},{6,22},{8,24},{10,26},{12,28},{14,30},{16,0},... | collective-permute-start | bytes 393224 | tf_op jit(solution)/shard_map/ppermute | solution.py:883
  14.1 10.0 %collective-permute-start = (bf16[64,1024]{1,0:T(8,128)(2,1)S(1)}, bf16[64,1024]{1,0:T(8,128)(2,1)S(1)}, u32[]{:S(2)}, u32[]{:S(2)}) collective-permute-start(bf16[64,1024]{1,0:T(8,128)(2,1)S(1)} %constant_dynamic-slice_fusion.4), channel_id=1, source_target_pairs={{0,8},{2,10},{4,12},{6,14},{8,16},{10,18},{12,20},{14,22},{16,24},... | collective-permute-start | bytes 393224 | tf_op jit(solution)/shard_map/ppermute | solution.py:883
  15.7 9.1 %collective-permute-start.2 = (bf16[64,1024]{1,0:T(8,128)(2,1)S(1)}, bf16[64,1024]{1,0:T(8,128)(2,1)S(1)}, u32[]{:S(2)}, u32[]{:S(2)}) collective-permute-start(bf16[64,1024]{1,0:T(8,128)(2,1)S(1)} %constant_dynamic-slice_fusion.4), channel_id=1, source_target_pairs={{0,24},{2,26},{4,28},{6,30},{8,0},{10,2},{12,4},{14,6},{16,8},{18,... | collective-permute-start | bytes 393224 | tf_op jit(solution)/shard_map/ppermute | solution.py:883
  20.1 9.0 %copy-start.22 = (bf16[1024,64]{1,0:T(8,128)(2,1)}, bf16[1024,64]{1,0:T(8,128)(2,1)S(1)}, u32[]{:S(2)}) copy-start(bf16[1024,64]{1,0:T(8,128)(2,1)S(1)} %get-tuple-element.158) | copy-start | bytes 393220
  20.1 9.0 %copy-start.23 = (bf16[1024,64]{1,0:T(8,128)(2,1)}, bf16[1024,64]{1,0:T(8,128)(2,1)S(1)}, u32[]{:S(2)}) copy-start(bf16[1024,64]{1,0:T(8,128)(2,1)S(1)} %get-tuple-element.159) | copy-start | bytes 393220
  24.9 16.1 %collective-permute-start.7 = (bf16[4,64,1024]{2,1,0:T(8,128)(2,1)S(1)}, bf16[4,64,1024]{2,1,0:T(8,128)(2,1)}, u32[]{:S(2)}, u32[]{:S(2)}) collective-permute-start(bf16[4,64,1024]{2,1,0:T(8,128)(2,1)S(1)} %pad_maximum_fusion.1.refs_1_), channel_id=1, source_target_pairs={{0,2},{2,0},{4,6},{6,4},{8,10},{10,8},{12,14},{14,12},{16,18},{18,... | collective-permute-start | bytes 1572872 | tf_op jit(solution)/shard_map/ppermute | solution.py:883
  26.5 7.2 %collective-permute-start.4 = (bf16[4,64,1024]{2,1,0:T(8,128)(2,1)S(1)}, bf16[4,64,1024]{2,1,0:T(8,128)(2,1)S(1)}, u32[]{:S(2)}, u32[]{:S(2)}) collective-permute-start(bf16[4,64,1024]{2,1,0:T(8,128)(2,1)S(1)} %pad_maximum_fusion.1.refs_1_), channel_id=1, source_target_pairs={{0,1},{1,0},{2,3},{3,2},{4,5},{5,4},{6,7},{7,6},{8,9},{9,8},{10,11... | collective-permute-start | bytes 1572872 | tf_op jit(solution)/shard_map/ppermute | solution.py:887
  26.5 14.4 %collective-permute-start.3 = (bf16[4,64,1024]{2,1,0:T(8,128)(2,1)S(1)}, bf16[4,64,1024]{2,1,0:T(8,128)(2,1)}, u32[]{:S(2)}, u32[]{:S(2)}) collective-permute-start(bf16[4,64,1024]{2,1,0:T(8,128)(2,1)S(1)} %pad_maximum_fusion.1.refs_1_), channel_id=1, source_target_pairs={{0,4},{2,6},{4,0},{6,2},{8,12},{10,14},{12,8},{14,10},{16,20},{18,... | collective-permute-start | bytes 1572872 | tf_op jit(solution)/shard_map/ppermute | solution.py:883
  29.1 0.7 copy-start.21
  32.2 51.4 %copy-start.17 = (s32[2]{0:T(128)}, s32[2]{0:T(128)S(1)}, u32[]{:S(2)}) copy-start(s32[2]{0:T(128)S(1)} %pad_add_fusion.refs_0_.ids_ref) | copy-start | bytes 28
  40.9 2.1 collective-permute-start.8
  40.9 6.1 %collective-permute-start.6 = (bf16[4,64,1024]{2,1,0:T(8,128)(2,1)}, bf16[4,64,1024]{2,1,0:T(8,128)(2,1)S(1)}, u32[]{:S(2)}, u32[]{:S(2)}) collective-permute-start(bf16[4,64,1024]{2,1,0:T(8,128)(2,1)} %collective-permute-done.3.refs_1_), channel_id=1, source_target_pairs={{0,1},{1,0},{2,3},{3,2},{4,5},{5,4},{6,7},{7,6},{8,9},{9,8},{10,11... | collective-permute-start | bytes 1572872 | tf_op jit(solution)/shard_map/ppermute | solution.py:887
  41.4 15.2 %collective-permute-start.5 = (bf16[4,64,1024]{2,1,0:T(8,128)(2,1)}, bf16[4,64,1024]{2,1,0:T(8,128)(2,1)S(1)}, u32[]{:S(2)}, u32[]{:S(2)}) collective-permute-start(bf16[4,64,1024]{2,1,0:T(8,128)(2,1)} %collective-permute-done.3.refs_1_), channel_id=1, source_target_pairs={{0,2},{2,0},{4,6},{6,4},{8,10},{10,8},{12,14},{14,12},{16,18},{18,... | collective-permute-start | bytes 1572872 | tf_op jit(solution)/shard_map/ppermute | solution.py:883
  56.6 1.9 collective-permute-start.9
  58.5 3.5 %copy-start.5 = (bf16[1024,512]{1,0:T(8,128)(2,1)S(1)}, bf16[1024,512]{1,0:T(8,128)(2,1)}, u32[]{:S(2)}) copy-start(bf16[1024,512]{1,0:T(8,128)(2,1)} %q_ref.3) | copy-start | bytes 3145732
  58.5 3.5 %copy-start.6 = (bf16[1024,512]{1,0:T(8,128)(2,1)S(1)}, bf16[1024,512]{1,0:T(8,128)(2,1)}, u32[]{:S(2)}) copy-start(bf16[1024,512]{1,0:T(8,128)(2,1)} %o_ref.3) | copy-start | bytes 3145732
  58.5 3.5 %copy-start.19 = (s32[4]{0:T(128)S(1)}, s32[4]{0:T(128)}, u32[]{:S(2)}) copy-start(s32[4]{0:T(128)} %len_ref.5) | copy-start | bytes 52
  62.0 6.6 %copy-start = (bf16[16,128,1024]{2,1,0:T(8,128)(2,1)}, bf16[16,128,1024]{2,1,0:T(8,128)(2,1)S(1)}, u32[]{:S(2)}) copy-start(bf16[16,128,1024]{2,1,0:T(8,128)(2,1)S(1)} %get-tuple-element.100.h_ref) | copy-start | bytes 12582916
  62.0 6.6 %copy-start.3 = (bf16[16,128,256]{2,1,0:T(8,128)(2,1)}, bf16[16,128,256]{2,1,0:T(8,128)(2,1)S(1)}, u32[]{:S(2)}) copy-start(bf16[16,128,256]{2,1,0:T(8,128)(2,1)S(1)} %get-tuple-element.113) | copy-start | bytes 3145732
  62.0 6.6 %copy-start.4 = (bf16[16,192,128]{2,1,0:T(8,128)(2,1)}, bf16[16,192,128]{2,1,0:T(8,128)(2,1)S(1)}, u32[]{:S(2)}) copy-start(bf16[16,192,128]{2,1,0:T(8,128)(2,1)S(1)} %get-tuple-element.112.t_ref) | copy-start | bytes 2359300
  62.0 8.2 %copy-start.8 = (bf16[128,1024]{1,0:T(8,128)(2,1)S(1)}, bf16[128,1024]{1,0:T(8,128)(2,1)}, u32[]{:S(2)}) copy-start(bf16[128,1024]{1,0:T(8,128)(2,1)} %x_ref.1) | copy-start | bytes 786436
  62.1 8.6 %copy-start.18 = (f32[1024]{0:T(1024)S(1)}, f32[1024]{0:T(1024)}, u32[]{:S(2)}) copy-start(f32[1024]{0:T(1024)} %param.16) | copy-start | bytes 12292
  62.1 8.6 %copy-start.28 = (f32[1024]{0:T(1024)S(1)}, f32[1024]{0:T(1024)}, u32[]{:S(2)}) copy-start(f32[1024]{0:T(1024)} %param.17) | copy-start | bytes 12292
  62.1 9.4 %copy-start.9 = (bf16[128,1024]{1,0:T(8,128)(2,1)S(1)}, bf16[128,1024]{1,0:T(8,128)(2,1)}, u32[]{:S(2)}) copy-start(bf16[128,1024]{1,0:T(8,128)(2,1)} %g_ref.3) | copy-start | bytes 786436
  68.6 1.6 collective-permute-start.10
  71.5 9.6 %copy-start.7 = (bf16[1024,512]{1,0:T(8,128)(2,1)S(1)}, bf16[1024,512]{1,0:T(8,128)(2,1)}, u32[]{:S(2)}) copy-start(bf16[1024,512]{1,0:T(8,128)(2,1)} %o_ref.3) | copy-start | bytes 3145732
  79.4 1.7 collective-permute-start.11
  81.1 1.0 copy-start.13
  84.6 16.4 %collective-permute-start.13 = (bf16[8,64,512]{2,1,0:T(8,128)(2,1)S(1)}, bf16[8,64,512]{2,1,0:T(8,128)(2,1)}, u32[]{:S(2)}, u32[]{:S(2)}) collective-permute-start(bf16[8,64,512]{2,1,0:T(8,128)(2,1)S(1)} %get-tuple-element.111), channel_id=1, source_target_pairs={{0,2},{2,0},{4,6},{6,4},{8,10},{10,8},{12,14},{14,12},{16,18},{18,... | collective-permute-start | bytes 1572872 | tf_op jit(solution)/shard_map/ppermute | solution.py:883
  84.9 18.1 %all-to-all-start = ((bf16[8,64,128]{2,1,0:T(8,128)(2,1)}), bf16[8,64,128]{2,1,0:T(8,128)(2,1)S(1)}, u32[]{:S(2)}, u32[]{:S(2)}) async-start(bf16[8,64,128]{2,1,0:T(8,128)(2,1)} %get-tuple-element.107), calls=%async_computation | async-start | bytes 262144 | tf_op jit(solution)/shard_map/all_to_all | solution.py:971
  103.0 6.4 %copy-start.25 = (bf16[8,64,128]{2,1,0:T(8,128)(2,1)}, bf16[8,64,128]{2,1,0:T(8,128)(2,1)S(1)}, u32[]{:S(2)}) copy-start(bf16[8,64,128]{2,1,0:T(8,128)(2,1)S(1)} %all-to-all-done.ga_ref) | copy-start | bytes 393220
  103.0 34.3 %all-to-all-start.1 = ((bf16[8,64,512]{2,1,0:T(8,128)(2,1)}), bf16[8,64,512]{2,1,0:T(8,128)(2,1)S(1)}, u32[]{:S(2)}, u32[]{:S(2)}) async-start(bf16[8,64,512]{2,1,0:T(8,128)(2,1)} %add_convert_fusion), calls=%async_computation.1 | async-start | bytes 1048576 | tf_op jit(solution)/shard_map/all_to_all | solution.py:977
  121.3 16.1 %copy-start.12 = (f32[192,512]{1,0:T(8,128)S(1)}, f32[192,512]{1,0:T(8,128)}, u32[]{:S(2)}) copy-start(f32[192,512]{1,0:T(8,128)} %get-tuple-element.117.mine_ref) | copy-start | bytes 1179652
  121.3 23.7 %copy-start.11 = (f32[8,128,128]{2,1,0:T(8,128)S(1)}, f32[8,128,128]{2,1,0:T(8,128)}, u32[]{:S(2)}) copy-start(f32[8,128,128]{2,1,0:T(8,128)} %get-tuple-element.125.kept_ref) | copy-start | bytes 1572868
  121.3 23.7 %copy-start.14 = (bf16[8,64,128]{2,1,0:T(8,128)(2,1)S(1)}, bf16[8,64,128]{2,1,0:T(8,128)(2,1)}, u32[]{:S(2)}) copy-start(bf16[8,64,128]{2,1,0:T(8,128)(2,1)} %get-tuple-element.124.gq_ref) | copy-start | bytes 393220
  121.3 16.0 %collective-permute-start.12 = (bf16[192,512]{1,0:T(8,128)(2,1)}, bf16[192,512]{1,0:T(8,128)(2,1)S(1)}, u32[]{:S(2)}, u32[]{:S(2)}) collective-permute-start(bf16[192,512]{1,0:T(8,128)(2,1)} %get-tuple-element.118), channel_id=1, source_target_pairs={{0,2},{2,0},{4,6},{6,4},{8,10},{10,8},{12,14},{14,12},{16,18},{18,... | collective-permute-start | bytes 589832 | tf_op jit(solution)/shard_map/ppermute | solution.py:883
  137.4 7.6 %collective-permute-start.15 = (bf16[8,128,128]{2,1,0:T(8,128)(2,1)}, bf16[8,128,128]{2,1,0:T(8,128)(2,1)S(1)}, u32[]{:S(2)}, u32[]{:S(2)}) collective-permute-start(bf16[8,128,128]{2,1,0:T(8,128)(2,1)} %get-tuple-element.127), channel_id=1, source_target_pairs={{0,2},{2,0},{4,6},{6,4},{8,10},{10,8},{12,14},{14,12},{16,18},{18,... | collective-permute-start | bytes 786440 | tf_op jit(solution)/shard_map/ppermute | solution.py:883
  138.5 13.0 %collective-permute-start.14 = (bf16[128,1024]{1,0:T(8,128)(2,1)}, bf16[128,1024]{1,0:T(8,128)(2,1)S(1)}, u32[]{:S(2)}, u32[]{:S(2)}) collective-permute-start(bf16[128,1024]{1,0:T(8,128)(2,1)} %get-tuple-element.123), channel_id=1, source_target_pairs={{0,1},{1,0},{2,3},{3,2},{4,5},{5,4},{6,7},{7,6},{8,9},{9,8},{10,11... | collective-permute-start | bytes 786440 | tf_op jit(solution)/shard_map/ppermute | solution.py:887
  138.5 30.8 %collective-permute-start.18 = (bf16[256,512]{1,0:T(8,128)(2,1)S(1)}, bf16[256,512]{1,0:T(8,128)(2,1)S(1)}, u32[]{:S(2)}, u32[]{:S(2)}) collective-permute-start(bf16[256,512]{1,0:T(8,128)(2,1)S(1)} %make_unit.1), channel_id=1, source_target_pairs={{0,24},{2,26},{4,28},{6,30},{8,0},{10,2},{12,4},{14,6},{16,8},{18,... | collective-permute-start | bytes 786440 | tf_op jit(solution)/shard_map/ppermute | solution.py:883
  142.6 28.1 %collective-permute-start.17 = (bf16[256,512]{1,0:T(8,128)(2,1)S(1)}, bf16[256,512]{1,0:T(8,128)(2,1)S(1)}, u32[]{:S(2)}, u32[]{:S(2)}) collective-permute-start(bf16[256,512]{1,0:T(8,128)(2,1)S(1)} %make_unit.1), channel_id=1, source_target_pairs={{0,16},{2,18},{4,20},{6,22},{8,24},{10,26},{12,28},{14,30},{16,0},... | collective-permute-start | bytes 786440 | tf_op jit(solution)/shard_map/ppermute | solution.py:883
  142.6 28.1 %collective-permute-start.16 = (bf16[256,512]{1,0:T(8,128)(2,1)S(1)}, bf16[256,512]{1,0:T(8,128)(2,1)}, u32[]{:S(2)}, u32[]{:S(2)}) collective-permute-start(bf16[256,512]{1,0:T(8,128)(2,1)S(1)} %make_unit.1), channel_id=1, source_target_pairs={{0,8},{2,10},{4,12},{6,14},{8,16},{10,18},{12,20},{14,22},{16,24},... | collective-permute-start | bytes 786440 | tf_op jit(solution)/shard_map/ppermute | solution.py:883
  145.8 51.3 %all-to-all-start.2 = ((bf16[8,192,128]{2,1,0:T(8,128)(2,1)}), bf16[8,192,128]{2,1,0:T(8,128)(2,1)S(1)}, u32[]{:S(2)}, u32[]{:S(2)}) async-start(bf16[8,192,128]{2,1,0:T(8,128)(2,1)} %merge.1), calls=%async_computation.2 | async-start | bytes 786432 | tf_op jit(solution)/shard_map/all_to_all | solution.py:988
  171.7 25.4 %copy-start.20 = (bf16[4,256,512]{2,1,0:T(8,128)(2,1)}, bf16[4,256,512]{2,1,0:T(8,128)(2,1)S(1)}, u32[]{:S(2)}) copy-start(bf16[4,256,512]{2,1,0:T(8,128)(2,1)S(1)} %pad_maximum_fusion.refs_0_) | copy-start | bytes 3145732
  171.8 25.4 %collective-permute-start.20 = (bf16[4,256,512]{2,1,0:T(8,128)(2,1)S(1)}, bf16[4,256,512]{2,1,0:T(8,128)(2,1)}, u32[]{:S(2)}, u32[]{:S(2)}) collective-permute-start(bf16[4,256,512]{2,1,0:T(8,128)(2,1)S(1)} %pad_maximum_fusion.refs_0_), channel_id=1, source_target_pairs={{0,4},{2,6},{4,0},{6,2},{8,12},{10,14},{12,8},{14,10},{16,20},{18,... | collective-permute-start | bytes 3145736 | tf_op jit(solution)/shard_map/ppermute | solution.py:883
  173.3 25.1 %collective-permute-start.19 = (bf16[4,256,512]{2,1,0:T(8,128)(2,1)S(1)}, bf16[4,256,512]{2,1,0:T(8,128)(2,1)}, u32[]{:S(2)}, u32[]{:S(2)}) collective-permute-start(bf16[4,256,512]{2,1,0:T(8,128)(2,1)S(1)} %pad_maximum_fusion.refs_0_), channel_id=1, source_target_pairs={{0,2},{2,0},{4,6},{6,4},{8,10},{10,8},{12,14},{14,12},{16,18},{18,... | collective-permute-start | bytes 3145736 | tf_op jit(solution)/shard_map/ppermute | solution.py:883
  197.1 2.3 copy-start.24
  203.3 2.0 collective-permute-start.21
  203.3 15.3 %collective-permute-start.23 = (bf16[2,256,512]{2,1,0:T(8,128)(2,1)S(1)}, bf16[2,256,512]{2,1,0:T(8,128)(2,1)S(1)}, u32[]{:S(2)}, u32[]{:S(2)}) collective-permute-start(bf16[2,256,512]{2,1,0:T(8,128)(2,1)S(1)} %slice.24), channel_id=1, source_target_pairs={{0,4},{2,6},{4,0},{6,2},{8,12},{10,14},{12,8},{14,10},{16,20},{18,... | collective-permute-start | bytes 1572872 | tf_op jit(solution)/shard_map/ppermute | solution.py:883
  204.2 15.8 %collective-permute-start.22 = (bf16[2,256,512]{2,1,0:T(8,128)(2,1)S(1)}, bf16[2,256,512]{2,1,0:T(8,128)(2,1)S(1)}, u32[]{:S(2)}, u32[]{:S(2)}) collective-permute-start(bf16[2,256,512]{2,1,0:T(8,128)(2,1)S(1)} %slice.25), channel_id=1, source_target_pairs={{0,2},{2,0},{4,6},{6,4},{8,10},{10,8},{12,14},{14,12},{16,18},{18,... | collective-permute-start | bytes 1572872 | tf_op jit(solution)/shard_map/ppermute | solution.py:883
  205.2 1.0 copy-start.10
  207.5 20.0 %all-to-all-start.3 = ((f32[16,4,1024]{2,1,0:T(4,128)}), f32[16,4,1024]{2,1,0:T(4,128)S(1)}, u32[]{:S(2)}, u32[]{:S(2)}) async-start(f32[16,4,1024]{2,1,0:T(4,128)} %get-tuple-element.144), calls=%async_computation.3 | async-start | bytes 524288 | tf_op jit(solution)/shard_map/all_to_all | solution.py:1002
  218.5 1.4 copy-start.26
  220.0 0.8 copy-start.27
Sparse Core Ops, SparseCore 0:
  11.5 66.3 all-gather.2
  80.7 64.5 all-gather.4
